TPU v7x, 32 devices: a whole 2x2x4 slice. The times are simulated.
32 devices in a mesh: space: 8 (over y, x, core), chan: 4 (over z).
Axes of the slice: x: 2, y: 2, z: 4, core: 2. Of those that a mesh axis runs over, the one named last changes fastest.
Arguments:
- members: bfloat16 [8, 96, 8, 17280], P(None, 'space', 'chan'), may hold values from -400 to 400, as said below
- gain: float32 [768], P('chan'), may hold values from 0.5 to 1.5
- shift: float32 [768], P('chan'), may hold values from -3 to 3
- w_first: bfloat16 [2, 8, 96, 96], P(None, 'chan'), may hold values from -0.4375 to 0.4375
- b_first: float32 [2, 8, 96], P(None, 'chan'), may hold values from -3 to 3
- w_second: bfloat16 [2, 8, 96, 96], P(None, 'chan'), may hold values from -0.4375 to 0.4375
- b_second: float32 [2, 8, 96], P(None, 'chan'), may hold values from -3 to 3
- cotangent: bfloat16 [8, 96, 8, 17280], P(None, 'space', 'chan'), may hold values from -6 to 6
Outputs:
- mixed: bfloat16 [8, 96, 8, 17280], P(None, 'space', 'chan')
- grad_input: bfloat16 [8, 96, 8, 17280], P(None, 'space', 'chan')
- grad_w_first: float32 [2, 8, 96, 96], P(None, 'chan')
- grad_b_first: float32 [2, 8, 96], P(None, 'chan')
- grad_w_second: float32 [2, 8, 96, 96], P(None, 'chan')
- grad_b_second: float32 [2, 8, 96], P(None, 'chan')
- grad_gain: float32 [768], P('chan')
- grad_shift: float32 [768], P('chan')
Inputs may be any that keep to these rules, and one draw needn't show every extreme that they name: `members`: real values of varying channel scale.
All inputs are finite; a program needn't handle non-finite values.
Results may differ from a plain program's by a relative error of at most 0.019.
The roundings to bfloat16 on the way count: a program that leaves them out, or rounds other values in their place, can miss the bound.
Values may be sent and summed in bfloat16 or wider, within the bound.
No kernel may reach another device: no remote copies, remote signals or barrier semaphores. Data moves between devices by JAX's collectives and lax.ppermute only.
A program may use at most 192 MiB of HBM per device.

v0:
```python
import functools
import math

import jax
import jax.numpy as jnp
import numpy as np
from jax import lax
from jax.experimental import pallas as pl
from jax.experimental.pallas import tpu as pltpu
from jax.sharding import PartitionSpec as P


MW = 64
LANES = 128
PACK = 4

shrink_level = 0.05
norm_epsilon = 1e-05
gelu_scale = 0.7978845608
gelu_cubic = 0.044715

half = jnp.bfloat16
single = jnp.float32
VMEM_LIMIT = 60 * 1024 * 1024
CHUNKS = 2

TN = (((0,), (0,)), ((), ()))
NT = (((1,), (1,)), ((), ()))


def mul(first_op, second_op, dims=(((1,), (0,)), ((), ()))):
    return lax.dot_general(first_op, second_op, dims, preferred_element_type=single)


def trig(length, columns):
    angles = (np.arange(length)[:, None] * np.arange(columns)[None, :] % length).astype(np.float32)
    angles = (angles * np.float32(2.0 * math.pi / length)).astype(np.float64)
    cast = lambda table: table.astype(np.float32).astype(half).astype(np.float32)
    return cast(np.cos(angles)), cast(np.sin(angles))


class Plan:
    def __init__(self, members, width, space, chan):
        self.batch, self.rows, self.groups, self.long = members.shape
        self.width, self.space, self.chan = width, space, chan
        self.lon = self.long // width
        self.lat = self.rows * space
        self.modes = MW // space
        self.stack = PACK // self.groups
        self.packs = self.batch // self.stack
        self.lanes = PACK * width
        self.tiles = self.lanes // LANES
        self.turn = self.lon // PACK
        self.turn_pad = -(-self.turn // 16) * 16
        self.words = self.long // LANES
        self.line = self.rows * self.groups
        self.word_pad = self.tiles * self.turn_pad
        self.channels = self.groups * width * chan


def moved_lanes(p, fetch, from_start, to_start, tile):
    pieces = []
    for slot in range(PACK):
        low = max(to_start(slot), tile * LANES)
        high = min(to_start(slot) + p.width, (tile + 1) * LANES)
        at = low
        while at < high:
            source = at - to_start(slot) + from_start(slot)
            stop = min(high, at + LANES - source % LANES)
            shift = (at - source) % LANES
            pieces.append((stop - tile * LANES, fetch(slot, source // LANES, shift)))
            at = stop
    return pieces


def merged(pieces, lane):
    value = pieces[-1][1]
    for stop, piece in reversed(pieces[:-1]):
        value = jnp.where(lane < stop, piece, value)
    return value


def rolled(value, shift):
    return value if shift == 0 else pltpu.roll(value, shift, 1)


def spread(p, stored_ref, words_ref):
    for s in range(p.stack):
        for t in range(p.words):
            part = stored_ref[s, :, :, t * LANES : (t + 1) * LANES]
            words_ref[s, t * p.line : (t + 1) * p.line, :] = part.reshape(p.line, LANES).astype(single)


def gather_row(p, words_ref, h, put):
    lane = lax.broadcasted_iota(jnp.int32, (p.turn_pad, LANES), 1)
    source = {}
    for q in range(PACK):
        s, n = divmod(q, p.groups)
        for i in range(p.tiles):
            start = i * p.line + h * p.groups + n
            source[q, i] = words_ref[s, pl.ds(start, p.turn_pad, stride=p.tiles * p.line), :]
    for r in range(PACK):
        cache = {}

        def fetch(q, i, shift):
            key = (q, i, shift)
            if key not in cache:
                cache[key] = rolled(source[q, i], shift)
            return cache[key]

        for c in range(p.tiles):
            pieces = moved_lanes(p, fetch, lambda q: r * p.width, lambda q: q * p.width, c)
            put(r, c, merged(pieces, lane))


def scatter_row(p, tokens, words_ref, h):
    lane = lax.broadcasted_iota(jnp.int32, (p.turn_pad, LANES), 1)
    for q in range(PACK):
        s, n = divmod(q, p.groups)

        def fetch(r, c, shift):
            part = tokens[r * p.turn_pad : (r + 1) * p.turn_pad, c * LANES : (c + 1) * LANES]
            return rolled(part, shift)

        for i in range(p.tiles):
            pieces = moved_lanes(p, fetch, lambda r: q * p.width, lambda r: r * p.width, i)
            start = i * p.line + h * p.groups + n
            words_ref[s, pl.ds(start, p.turn_pad, stride=p.tiles * p.line), :] = merged(pieces, lane)


def store_words(p, words_ref, stored_ref):
    for s in range(p.stack):
        for t in range(p.words):
            part = words_ref[s, t * p.line : (t + 1) * p.line, :]
            stored_ref[s, :, :, t * LANES : (t + 1) * LANES] = part.reshape(
                p.rows, p.groups, LANES
            ).astype(half)


def clear_tail(p, words_ref):
    @pl.when(pl.program_id(0) == 0)
    def _():
        tail = (p.word_pad - p.words) * p.line
        words_ref[:, p.words * p.line :, :] = jnp.zeros((p.stack, tail, LANES), single)


def analyse(p, tokens, table, scale, turn_ref, h):
    spectrum = mul(table, tokens) * scale
    for c in range(p.tiles):
        for ri in range(2):
            turn_ref[c, pl.ds(ri * p.rows + h, MW, stride=2 * p.rows), :] = spectrum[
                ri * MW : (ri + 1) * MW, c * LANES : (c + 1) * LANES
            ]


def send_turn(p, turn_ref, out_ref, outer, inner):
    count = outer * inner
    for d in range(p.space):
        for c in range(p.tiles):
            part = turn_ref[c, d * count : (d + 1) * count, :].reshape(outer, inner, LANES)
            out_ref[d, 0, :, :, c * LANES : (c + 1) * LANES] = part.astype(half)


def split_three(value):
    high = value.astype(half).astype(single)
    rest = value - high
    middle = rest.astype(half).astype(single)
    return high, middle, rest - middle


def expand(parts, spread_table):
    stacked = jnp.concatenate(split_three(parts), axis=0).astype(half)
    return mul(stacked, spread_table, TN)


def summed(table, value):
    high = value.astype(half)
    low = (value - high.astype(single)).astype(half)
    return mul(table, high, NT) + mul(table, low, NT)


def cotangent_kernel(p, stored_ref, table_ref, scale_ref, out_ref, words_ref, turn_ref, tokens_ref):
    clear_tail(p, words_ref)
    spread(p, stored_ref, words_ref)

    def row(h, carry):
        def put(r, c, value):
            tokens_ref[r * p.turn_pad : (r + 1) * p.turn_pad, c * LANES : (c + 1) * LANES] = (
                value.astype(half)
            )

        gather_row(p, words_ref, h, put)
        analyse(p, tokens_ref[...], table_ref[...], scale_ref[...], turn_ref, h)
        return carry

    lax.fori_loop(0, p.rows, row, 0)
    send_turn(p, turn_ref, out_ref, p.modes, 2 * p.rows)


def stats_kernel(p, stored_ref, sum_ref, tokens_ref, stat_ref, words_ref, rows_ref):
    clear_tail(p, words_ref)
    spread(p, stored_ref, words_ref)
    count = 2 * p.stack

    def row(h, carry):
        def put(r, c, value):
            tokens_ref[
                0, h, r * p.turn_pad : (r + 1) * p.turn_pad, c * LANES : (c + 1) * LANES
            ] = value.astype(half)

        gather_row(p, words_ref, h, put)
        tokens = tokens_ref[0, h]
        wide = tokens.astype(single)
        plain = mul(sum_ref[0], tokens, NT)
        rows_ref[h] = plain + summed(sum_ref[1], wide * wide)
        return carry

    lax.fori_loop(0, p.rows, row, 0)
    for h in range(p.rows):
        stat_ref[0, h * count : (h + 1) * count, :] = rows_ref[h, :count, :]


def moments(p, stat_refs, rows_ref):
    count = 2 * p.stack
    total = stat_refs[0][0]
    for ref in stat_refs[1:]:
        total = total + ref[0]
    for h in range(p.rows):
        part = total[h * count : (h + 1) * count] * (1.0 / p.channels)
        mean, square = part[: p.stack], part[p.stack :]
        inverse = lax.rsqrt(square - mean * mean + norm_epsilon)
        rows_ref[h, : p.stack, :] = mean
        rows_ref[h, p.stack : count, :] = inverse
        if count < 8:
            rows_ref[h, count:, :] = jnp.zeros((8 - count, p.turn_pad * PACK), single)


def normalise_kernel(p, *refs):
    stat_refs = refs[: p.chan]
    tokens_ref, gain_ref, shift_ref, table_ref, scale_ref, wide_ref = refs[p.chan : p.chan + 6]
    out_ref, rows_ref, turn_ref = refs[p.chan + 6 :]
    moments(p, stat_refs, rows_ref)

    def row(h, carry):
        each = expand(rows_ref[h], wide_ref[...])
        wide = tokens_ref[0, h].astype(single)
        centred = (wide - each[:, : p.lanes]) * each[:, p.lanes :]
        normed = (centred * gain_ref[...] + shift_ref[...]).astype(half)
        analyse(p, normed, table_ref[...], scale_ref[...], turn_ref, h)
        return carry

    lax.fori_loop(0, p.rows, row, 0)
    send_turn(p, turn_ref, out_ref, p.modes, 2 * p.rows)


def gelu_both(values):
    inner = jnp.tanh(gelu_scale * (values + gelu_cubic * values * values * values))
    hidden = 0.5 * values * (1.0 + inner)
    slope = 0.5 * (1.0 + inner) + 0.5 * values * (1.0 - inner * inner) * gelu_scale * (
        1.0 + 3.0 * gelu_cubic * values * values
    )
    return hidden, slope


BAND = 16


def spectral_kernel(
    p,
    step_modes,
    x_ref,
    g_ref,
    there_ref,
    back_ref,
    w1_ref,
    w2_ref,
    bias_ref,
    y_ref,
    dx_ref,
    gw_ref,
    gb_ref,
    lat_ref,
    hid_ref,
    gpost_ref,
    gpre_ref,
    wide_ref,
    slope_ref,
    gsh_ref,
    shr_ref,
    turn_y_ref,
    turn_x_ref,
    acc1_ref,
    acc2_ref,
):
    pack, group = pl.program_id(0), pl.program_id(1)
    count = step_modes * p.lat
    factor = 1.0 / math.sqrt(p.lat)
    base = pl.multiple_of(group * count, count)

    @pl.when((pack == 0) & (group == 0))
    def _():
        gb_ref[...] = jnp.zeros_like(gb_ref)
        acc1_ref[...] = jnp.zeros_like(acc1_ref)
        acc2_ref[...] = jnp.zeros_like(acc2_ref)

    def there(ref, into, offset):
        for m in range(step_modes):
            block = ref[:, 0, m].reshape(2 * p.lat, p.lanes)
            out = (mul(there_ref[...], block) * factor).astype(half)
            at = pl.ds(offset + m * p.lat, p.lat)
            into[at, : p.lanes] = out[: p.lat]
            into[at, p.lanes :] = out[p.lat :]

    def back(value_of, turn_ref):
        for m in range(step_modes):
            rows = slice(m * p.lat, (m + 1) * p.lat)
            both = jnp.concatenate([value_of(rows, 0), value_of(rows, 1)], axis=0)
            out = mul(back_ref[...], both) * factor
            mode = group * step_modes + m
            for ri in range(2):
                for c in range(p.tiles):
                    turn_ref[c, pl.ds(ri * p.modes + mode, p.lat, stride=2 * p.modes), :] = out[
                        ri * p.lat : (ri + 1) * p.lat, c * LANES : (c + 1) * LANES
                    ]

    there(x_ref, lat_ref, base)
    there(g_ref, gsh_ref, 0)
    wide_ref[...] = mul(lat_ref[pl.ds(base, count), :], w1_ref[...])

    def first(i, carry):
        at = pl.ds(pl.multiple_of(i * BAND, BAND), BAND)
        hidden, slope = gelu_both(wide_ref[at, :] + bias_ref[0:1, :])
        hid_ref[pl.ds(pl.multiple_of(base + i * BAND, BAND), BAND), :] = hidden.astype(half)
        slope_ref[at, :] = slope
        return carry

    lax.fori_loop(0, count // BAND, first, 0)
    wide_ref[...] = mul(hid_ref[pl.ds(base, count), :], w2_ref[...])

    def second(i, carry):
        at = pl.ds(pl.multiple_of(i * BAND, BAND), BAND)
        post = wide_ref[at, :] + bias_ref[1:2, :]
        inner = jnp.tanh(post * (1.0 / shrink_level))
        shr_ref[at, :] = (post - shrink_level * inner).astype(half)
        gpost = (gsh_ref[at, :].astype(single) * (inner * inner)).astype(half)
        gpost_ref[pl.ds(pl.multiple_of(base + i * BAND, BAND), BAND), :] = gpost
        gb_ref[8:16, :] += gpost.astype(single).reshape(BAND // 8, 8, 2 * p.lanes).sum(0)
        return carry

    lax.fori_loop(0, count // BAND, second, 0)
    back(lambda rows, ri: shr_ref[rows, ri * p.lanes : (ri + 1) * p.lanes], turn_y_ref)
    wide_ref[...] = mul(gpost_ref[pl.ds(base, count), :], w2_ref[...], NT)

    def third(i, carry):
        at = pl.ds(pl.multiple_of(i * BAND, BAND), BAND)
        gpre = (wide_ref[at, :] * slope_ref[at, :]).astype(half)
        gpre_ref[pl.ds(pl.multiple_of(base + i * BAND, BAND), BAND), :] = gpre
        gb_ref[0:8, :] += gpre.astype(single).reshape(BAND // 8, 8, 2 * p.lanes).sum(0)
        return carry

    lax.fori_loop(0, count // BAND, third, 0)
    shr_ref[...] = mul(gpre_ref[pl.ds(base, count), :], w1_ref[...], NT).astype(half)
    back(lambda rows, ri: shr_ref[rows, ri * p.lanes : (ri + 1) * p.lanes], turn_x_ref)

    @pl.when(group == pl.num_programs(1) - 1)
    def _():
        send_turn(p, turn_y_ref, y_ref, p.rows, 2 * p.modes)
        send_turn(p, turn_x_ref, dx_ref, p.rows, 2 * p.modes)
        acc1_ref[...] += mul(lat_ref[...], gpre_ref[...], TN)
        acc2_ref[...] += mul(hid_ref[...], gpost_ref[...], TN)

    @pl.when((group == pl.num_programs(1) - 1) & (pack == pl.num_programs(0) - 1))
    def _():
        for which, acc in enumerate((acc1_ref, acc2_ref)):
            for n in range(p.groups):
                for part in range(2):
                    total = jnp.zeros((p.width, LANES), single)
                    for s in range(p.stack):
                        q = s * p.groups + n
                        for row_ri, col_ri, sign in (((0, 0, 1), (1, 1, 1)), ((0, 1, 1), (1, 0, -1)))[part]:
                            top = row_ri * p.lanes + q * p.width
                            left = col_ri * p.lanes + q * p.width
                            tile = left // LANES
                            value = rolled(
                                acc[top : top + p.width, tile * LANES : (tile + 1) * LANES],
                                -left % LANES,
                            )
                            if left % LANES + p.width > LANES:
                                nxt = acc[
                                    top : top + p.width, (tile + 1) * LANES : (tile + 2) * LANES
                                ]
                                lane = lax.broadcasted_iota(jnp.int32, (p.width, LANES), 1)
                                value = jnp.where(
                                    lane < LANES - left % LANES, value, rolled(nxt, -left % LANES)
                                )
                            total = total + sign * value
                    gw_ref[which, part, n] = total


def mixed_kernel(p, rows_ref, table_ref, out_ref, words_ref):
    factor = 1.0 / math.sqrt(p.lon)

    def row(h, carry):
        block = rows_ref[:, 0, h].reshape(2 * MW, p.lanes)
        tokens = mul(table_ref[...], block) * factor
        scatter_row(p, tokens, words_ref, h)
        return carry

    lax.fori_loop(0, p.rows, row, 0)
    store_words(p, words_ref, out_ref)


def slope_sums_kernel(p, *refs):
    stat_refs = refs[: p.chan]
    rows_in_ref, tokens_ref, gain_ref, table_ref, wide_ref, sum_ref = refs[p.chan : p.chan + 6]
    sums_ref, param_ref, rows_ref, part_ref = refs[p.chan + 6 :]
    factor = 1.0 / math.sqrt(p.lon)
    count = 2 * p.stack
    moments(p, stat_refs, rows_ref)

    @pl.when(pl.program_id(0) == 0)
    def _():
        param_ref[...] = jnp.zeros_like(param_ref)

    def row(h, carry):
        block = rows_in_ref[:, 0, h].reshape(2 * MW, p.lanes)
        normed_grad = mul(table_ref[...], block) * factor
        each = expand(rows_ref[h], wide_ref[...])
        wide = tokens_ref[0, h].astype(single)
        centred = (wide - each[:, : p.lanes]) * each[:, p.lanes :]
        product = normed_grad * centred
        folds = (PACK * p.turn_pad // 8, 8, p.lanes)
        param_ref[0:8, :] += product.reshape(folds).sum(0)
        param_ref[8:16, :] += normed_grad.reshape(folds).sum(0)
        gain = gain_ref[...]
        part_ref[h] = summed(sum_ref[0], normed_grad * gain) + summed(sum_ref[1], product * gain)
        return carry

    lax.fori_loop(0, p.rows, row, 0)
    for h in range(p.rows):
        sums_ref[0, h * count : (h + 1) * count, :] = part_ref[h, :count, :]


def input_grad_kernel(p, *refs):
    stat_refs, part_refs = refs[: p.chan], refs[p.chan : 2 * p.chan]
    rows_in_ref, tokens_ref, gain_ref, table_ref, wide_ref = refs[2 * p.chan : 2 * p.chan + 5]
    out_ref, rows_ref, part_ref, words_ref = refs[2 * p.chan + 5 :]
    factor = 1.0 / math.sqrt(p.lon)
    count = 2 * p.stack
    moments(p, stat_refs, rows_ref)
    total = part_refs[0][0].astype(single)
    for ref in part_refs[1:]:
        total = total + ref[0].astype(single)
    for h in range(p.rows):
        part_ref[h, :count, :] = total[h * count : (h + 1) * count] * (1.0 / p.channels)
        if count < 8:
            part_ref[h, count:, :] = jnp.zeros((8 - count, p.turn_pad * PACK), single)

    def row(h, carry):
        block = rows_in_ref[:, 0, h].reshape(2 * MW, p.lanes)
        normed_grad = mul(table_ref[...], block) * factor
        each = expand(rows_ref[h], wide_ref[...])
        means = expand(part_ref[h], wide_ref[...])
        inverse = each[:, p.lanes :]
        centred = (tokens_ref[0, h].astype(single) - each[:, : p.lanes]) * inverse
        grad = inverse * (
            normed_grad * gain_ref[...] - means[:, : p.lanes] - centred * means[:, p.lanes :]
        )
        scatter_row(p, grad, words_ref, h)
        return carry

    lax.fori_loop(0, p.rows, row, 0)
    store_words(p, words_ref, out_ref)


def whole_spec(value):
    dims = value.shape
    return pl.BlockSpec(dims, lambda *_: (0,) * len(dims))


def pack_spec(value, offset=0):
    dims = (1,) + value.shape[1:]
    return pl.BlockSpec(dims, lambda b, *_: (b + offset,) + (0,) * (len(dims) - 1))


def peer_spec(value):
    dims = (value.shape[0], 1) + value.shape[2:]
    return pl.BlockSpec(dims, lambda b, *_: (0, b) + (0,) * (len(dims) - 2))


def stored_spec(p, offset):
    return pl.BlockSpec(
        (p.stack, p.rows, p.groups, p.long), lambda b, *_: (b + offset, 0, 0, 0)
    )


def call(body, grid, ins, in_specs, outs, out_specs, scratch, flops, aliases=None):
    moved = sum(v.size * v.dtype.itemsize for v in ins) + sum(
        math.prod(o.shape) * o.dtype.itemsize for o in outs
    )
    return _call(body, grid, ins, in_specs, outs, out_specs, scratch, flops, moved, aliases)


def _call(body, grid, ins, in_specs, outs, out_specs, scratch, flops, moved, aliases):
    return pl.pallas_call(
        body,
        grid=grid,
        in_specs=in_specs,
        out_specs=out_specs,
        out_shape=outs,
        scratch_shapes=scratch,
        input_output_aliases=aliases or {},
        compiler_params=pltpu.CompilerParams(vmem_limit_bytes=VMEM_LIMIT),
        cost_estimate=pl.CostEstimate(flops=flops, bytes_accessed=moved, transcendentals=0),
    )(*ins)


def lon_tables(p):
    cos_lon, sin_lon = trig(p.lon, MW)
    wave = np.concatenate([cos_lon, -sin_lon], axis=1)
    turned = np.zeros((PACK, p.turn_pad, 2 * MW), np.float32)
    turned[:, : p.turn] = wave.reshape(p.turn, PACK, 2 * MW).transpose(1, 0, 2)
    turned = turned.reshape(PACK * p.turn_pad, 2 * MW)
    doubling = np.where(np.arange(MW) == 0, 1.0, 2.0).astype(np.float32)
    factor = np.float32(1.0 / math.sqrt(p.lon))
    plain_scale = np.full((2 * MW, 1), factor, np.float32)
    double_scale = (factor * np.tile(doubling, 2))[:, None].astype(np.float32)
    owner = turned.reshape(-1, 2, p.space, p.modes).transpose(0, 2, 1, 3).reshape(-1, 2 * MW)
    twice = np.tile(doubling.reshape(p.space, 1, p.modes), (1, 2, 1)).reshape(1, 2 * MW)
    to_half = lambda value: jnp.asarray(value, half)
    return (
        to_half(turned.T),
        jnp.asarray(plain_scale),
        jnp.asarray(double_scale),
        to_half(owner * twice),
        to_half(owner),
    )


def lat_tables(p):
    cos_lat, sin_lat = trig(p.lat, p.lat)
    there = np.block([[cos_lat, sin_lat], [-sin_lat, cos_lat]])
    there = there.reshape(2 * p.lat, 2, p.space, p.rows).transpose(0, 2, 1, 3)
    back = np.block([[cos_lat.T, -sin_lat.T], [sin_lat.T, cos_lat.T]])
    return jnp.asarray(there.reshape(2 * p.lat, 2 * p.lat), half), jnp.asarray(back, half)


def sum_tables(p):
    owner = np.arange(PACK) // p.groups
    lane_owner = np.repeat(owner, p.width)
    sums = np.zeros((2, 8, p.lanes), np.float32)
    wide = np.zeros((3, 8, 2, p.lanes), np.float32)
    for s in range(p.stack):
        sums[0, s] = lane_owner == s
        sums[1, p.stack + s] = lane_owner == s
        wide[:, s, 0] = lane_owner == s
        wide[:, p.stack + s, 1] = lane_owner == s
    return jnp.asarray(sums, half), jnp.asarray(wide.reshape(24, 2 * p.lanes), half)


def block_weights(p, weights):
    each = jnp.tile(weights, (1, p.stack, 1, 1))
    eye = jnp.eye(PACK, dtype=weights.dtype)
    wide = (each[:, :, :, None, :] * eye[None, :, None, :, None]).reshape(2, p.lanes, p.lanes)
    top = jnp.concatenate([wide[0], wide[1]], axis=1)
    bottom = jnp.concatenate([-wide[1], wide[0]], axis=1)
    return jnp.concatenate([top, bottom], axis=0)


def lane_vector(p, vector):
    return jnp.tile(vector, p.stack)[None, :]


def exchange(value):
    return lax.all_to_all(value, "space", 0, 0, tiled=True)


def around(value, axis, size):
    gathered = [value]
    for step in range(1, size):
        gathered.append(
            lax.ppermute(value, axis, [(i, (i + step) % size) for i in range(size)])
        )
    return gathered


def reduced(p, value, kind):
    step = 1
    while step < p.space:
        own = value.astype(kind)
        other = lax.ppermute(own, "space", [(i, i ^ step) for i in range(p.space)])
        value = own.astype(single) + other.astype(single)
        step *= 2
    return value


def on_device(space, chan, members, gain, shift, w_first, b_first, w_second, b_second, cotangent):
    p = Plan(members, w_first.shape[-1], space, chan)
    chunks = CHUNKS if p.packs % CHUNKS == 0 else 1
    size = p.packs // chunks
    grid = (size,)
    table, plain_scale, double_scale, mixed_table, slope_table = lon_tables(p)
    there_table, back_table = lat_tables(p)
    sum_table, wide_table = sum_tables(p)
    gain_lanes, shift_lanes = lane_vector(p, gain), lane_vector(p, shift)
    w1, w2 = block_weights(p, w_first), block_weights(p, w_second)
    bias = jnp.stack(
        [jnp.tile(b.reshape(2, -1), (1, p.stack)).reshape(-1) for b in (b_first, b_second)]
    )
    tokens_rows = PACK * p.turn_pad
    dft_flops = 2 * size * p.rows * tokens_rows * 2 * MW * p.lanes
    words = pltpu.VMEM((p.stack, p.word_pad * p.line, LANES), single)
    turn_in = pltpu.VMEM((p.tiles, MW * 2 * p.rows, LANES), single)
    rows_scratch = pltpu.VMEM((p.rows, 8, tokens_rows), single)
    sent = jax.ShapeDtypeStruct((space, size, p.modes, 2 * p.rows, p.lanes), half)
    returned = jax.ShapeDtypeStruct((space, size, p.rows, 2 * p.modes, p.lanes), half)
    count = 2 * p.stack * p.rows
    stored = jax.ShapeDtypeStruct(members.shape, half)

    def cotangent_chunk(c):
        ins = (cotangent, table, double_scale)
        return call(
            functools.partial(cotangent_kernel, p), grid, ins,
            [stored_spec(p, c * size), whole_spec(table), whole_spec(double_scale)],
            [sent], [peer_spec(sent)],
            [words, turn_in, pltpu.VMEM((tokens_rows, p.lanes), half)], dft_flops,
        )[0]

    def stats_chunk(c):
        ins = (members, sum_table)
        outs = [
            jax.ShapeDtypeStruct((size, p.rows, tokens_rows, p.lanes), half),
            jax.ShapeDtypeStruct((size, count, tokens_rows), single),
        ]
        return call(
            functools.partial(stats_kernel, p), grid, ins,
            [stored_spec(p, c * size), whole_spec(sum_table)],
            outs, [pack_spec(o) for o in outs], [words, rows_scratch], dft_flops // 4,
        )

    def normalise_chunk(stats, tokens):
        tail = (gain_lanes, shift_lanes, table, plain_scale, wide_table)
        return call(
            functools.partial(normalise_kernel, p), grid, (*stats, tokens, *tail),
            [pack_spec(s) for s in stats] + [pack_spec(tokens)] + [whole_spec(v) for v in tail],
            [sent], [peer_spec(sent)], [rows_scratch, turn_in], dft_flops,
        )[0]

    step_modes = 2 if p.modes % 2 == 0 else 1
    wide_lanes = 2 * p.lanes

    def spectral_chunk(x_in, g_in):
        tail = (there_table, back_table, w1, w2, bias)
        mode_spec = pl.BlockSpec(
            (space, 1, step_modes, 2 * p.rows, p.lanes), lambda b, m: (0, b, m, 0, 0)
        )
        grads = jax.ShapeDtypeStruct((2, 2, p.groups, p.width, LANES), single)
        bias_grads = jax.ShapeDtypeStruct((16, wide_lanes), single)
        kept = pltpu.VMEM((p.modes * p.lat, wide_lanes), half)
        held = pltpu.VMEM((step_modes * p.lat, wide_lanes), single)
        brief = pltpu.VMEM((step_modes * p.lat, wide_lanes), half)
        turn_out = pltpu.VMEM((p.tiles, p.lat * 2 * p.modes, LANES), single)
        return call(
            functools.partial(spectral_kernel, p, step_modes),
            (size, p.modes // step_modes), (x_in, g_in, *tail),
            [mode_spec, mode_spec] + [whole_spec(v) for v in tail],
            [returned, returned, grads, bias_grads],
            [peer_spec(returned), peer_spec(returned), whole_spec(grads), whole_spec(bias_grads)],
            [kept] * 4 + [held] * 2 + [brief] * 2 + [turn_out] * 2
            + [pltpu.VMEM((wide_lanes, wide_lanes), single)] * 2,
            12 * size * p.modes * p.lat * wide_lanes * wide_lanes,
        )

    def out_call(body, c, ins, specs, scratch, before, flops):
        ins, specs = list(ins), list(specs)
        aliases = {}
        inner = body
        if before is not None:
            place = len(ins)
            inner = lambda *refs: body(*refs[:place], *refs[place + 1 :])
            ins.append(before)
            specs.append(pl.BlockSpec(memory_space=pl.ANY))
            aliases = {place: 0}
        return call(
            inner, grid, tuple(ins), specs, [stored], [stored_spec(p, c * size)],
            scratch, flops, aliases,
        )[0]

    def mixed_chunk(c, rows_in, before):
        return out_call(
            functools.partial(mixed_kernel, p), c, (rows_in, mixed_table),
            [peer_spec(rows_in), whole_spec(mixed_table)], [words], before, dft_flops,
        )

    def slope_sums_chunk(stats, rows_in, tokens):
        tail = (gain_lanes, slope_table, wide_table, sum_table)
        outs = [
            jax.ShapeDtypeStruct((size, count, tokens_rows), single),
            jax.ShapeDtypeStruct((16, p.lanes), single),
        ]
        return call(
            functools.partial(slope_sums_kernel, p), grid,
            (*stats, rows_in, tokens, *tail),
            [pack_spec(s) for s in stats] + [peer_spec(rows_in), pack_spec(tokens)]
            + [whole_spec(v) for v in tail],
            outs, [pack_spec(outs[0]), whole_spec(outs[1])], [rows_scratch, rows_scratch],
            dft_flops,
        )

    def input_grad_chunk(c, stats, parts, rows_in, tokens, before):
        tail = (gain_lanes, slope_table, wide_table)
        return out_call(
            functools.partial(input_grad_kernel, p), c,
            (*stats, *parts, rows_in, tokens, *tail),
            [pack_spec(s) for s in (*stats, *parts)] + [peer_spec(rows_in), pack_spec(tokens)]
            + [whole_spec(v) for v in tail],
            [rows_scratch, rows_scratch, words], before, dft_flops,
        )

    everyone = range(chunks)
    g_in = [exchange(cotangent_chunk(c)) for c in everyone]
    first = [stats_chunk(c) for c in everyone]
    stats = [around(s, "chan", chan) for _, s in first]
    x_in = [exchange(normalise_chunk(stats[c], first[c][0])) for c in everyone]
    mixed = grad_input = None
    weight_grads = bias_grads = param_grads = 0.0
    spectra = [spectral_chunk(x_in[c], g_in[c]) for c in everyone]
    for c in everyone:
        y_out, dx_out, gw, gb = spectra[c]
        weight_grads, bias_grads = weight_grads + gw, bias_grads + gb
        dx_rows = exchange(dx_out)
        y_rows = exchange(y_out)
        sums, params = slope_sums_chunk(stats[c], dx_rows, first[c][0])
        param_grads = param_grads + params
        parts = around(sums.astype(half), "chan", chan)
        grad_input = input_grad_chunk(c, stats[c], parts, dx_rows, first[c][0], grad_input)
        mixed = mixed_chunk(c, y_rows, mixed)

    def by_channel(rows):
        return rows.reshape(-1, p.stack, p.groups * p.width).sum(1)

    weights = weight_grads.reshape(-1, LANES)
    flat_bias = bias_grads.reshape(2, 8, 2, p.stack, p.groups * p.width).sum((1, 3))
    flat_params = by_channel(param_grads.reshape(2, 8, p.lanes).sum(1))
    grads = reduced(p, weights, half).reshape(weight_grads.shape)[..., : p.width]
    flat_bias = reduced(p, flat_bias, single).reshape((2,) + b_first.shape)
    both = reduced(p, flat_params, single)
    return (mixed, grad_input, grads[0], flat_bias[0], grads[1], flat_bias[1], both[0], both[1])


def solution(mesh):
    tokens = P(None, "space", "chan", None)
    weights = P(None, "chan", None, None)
    biases = P(None, "chan", None)
    placed = (tokens, P("chan"), P("chan"), weights, biases, weights, biases, tokens)
    return jax.shard_map(
        functools.partial(on_device, mesh.shape["space"], mesh.shape["chan"]),
        mesh=mesh,
        in_specs=placed,
        out_specs=(tokens, tokens, weights, biases, weights, biases, P("chan"), P("chan")),
        check_vma=False,
    )
```

profile of v0, /device:TPU:0, one launch (start us, length us, event | category | flops | bytes accessed | tf_op | source)
XLA Modules:
  0.0 474.6 jit_solution(13648847663792330817)
XLA Ops:
  0.6 12.7 %shard_map.230 = bf16[8,2,8,24,384]{4,3,2,1,0:T(8,128)(2,1)} custom-call(bf16[8,12,2,17280]{3,2,1,0:T(2,128)(2,1)} %stored_ref.7, bf16[128,192]{1,0:T(8,128)(2,1)} %constant.20.clone.refs_7_.table_ref, f32[128,1]{1,0:T(8,128)} %constant.22.clone.scale_ref), custom_call_target="tpu_custom_call" | custom-call | flops 452984832 | bytes 9044480 | tf_op jit(solution)/shard_map/pallas_call | solution.py:505
  13.3 5.2 %all-to-all-start.4 = ((bf16[8,2,8,24,384]{4,3,2,1,0:T(8,128)(2,1)}), bf16[8,2,8,24,384]{4,3,2,1,0:T(8,128)(2,1)S(1)}, u32[]{:S(2)}, u32[]{:S(2)}) async-start(bf16[8,2,8,24,384]{4,3,2,1,0:T(8,128)(2,1)} %shard_map.230), calls=%async_computation.4 | async-start | bytes 4718592 | tf_op jit(solution)/shard_map/all_to_all | solution.py:575
  18.5 12.7 %shard_map.226 = bf16[8,2,8,24,384]{4,3,2,1,0:T(8,128)(2,1)} custom-call(bf16[8,12,2,17280]{3,2,1,0:T(2,128)(2,1)} %stored_ref.7, bf16[128,192]{1,0:T(8,128)(2,1)} %constant.20.clone.refs_7_.table_ref, f32[128,1]{1,0:T(8,128)} %constant.22.clone.scale_ref), custom_call_target="tpu_custom_call" | custom-call | flops 452984832 | bytes 9044480 | tf_op jit(solution)/shard_map/pallas_call | solution.py:505
  31.2 16.7 %all-to-all-done.4.g_ref = bf16[8,2,8,24,384]{4,3,2,1,0:T(8,128)(2,1)S(1)} async-done(((bf16[8,2,8,24,384]{4,3,2,1,0:T(8,128)(2,1)}), bf16[8,2,8,24,384]{4,3,2,1,0:T(8,128)(2,1)S(1)}, u32[]{:S(2)}, u32[]{:S(2)}) %all-to-all-start.4) | async-done | bytes 2359328 | tf_op jit(solution)/shard_map/all_to_all | solution.py:575
  48.0 1.5 copy-done.3
  49.4 3.6 all-to-all-start.1
  53.1 14.1 %shard_map.228 = (bf16[2,12,192,384]{3,2,1,0:T(8,128)(2,1)}, f32[2,48,192]{2,1,0:T(8,128)}) custom-call(bf16[8,12,2,17280]{3,2,1,0:T(2,128)(2,1)} %stored_ref.6, bf16[2,8,384]{2,1,0:T(8,128)(2,1)} %constant.27.clone.sum_ref.refs_9_), custom_call_target="tpu_custom_call" | custom-call | flops 113246208 | bytes 10260480 | tf_op jit(solution)/shard_map/pallas_call | solution.py:505
  67.1 1.6 collective-permute-start.3
  68.7 2.6 collective-permute-start.4
  74.9 3.7 collective-permute-done.4.refs_2_
  79.3 14.6 %shard_map.229 = bf16[8,2,8,24,384]{4,3,2,1,0:T(8,128)(2,1)} custom-call(f32[2,48,192]{2,1,0:T(8,128)} %get-tuple-element.27.refs_0_, f32[2,48,192]{2,1,0:T(8,128)} %copy-done.6, f32[2,48,192]{2,1,0:T(8,128)} %copy-done.7, f32[2,48,192]{2,1,0:T(8,128)} %copy-done.8, bf16[2,12,192,384]{3,2,1,0:T(8,128)(2,1)} %get-tuple-element.28.refs_4_.refs_5_.refs_9_, ...), custom_call_target="tpu_custom_call" | custom-call | flops 452984832 | bytes 6282752 | tf_op jit(solution)/shard_map/pallas_call | solution.py:505
  93.9 1.4 copy-done.2
  95.3 4.4 all-to-all-start.3
  99.7 14.1 %shard_map.224 = (bf16[2,12,192,384]{3,2,1,0:T(8,128)(2,1)}, f32[2,48,192]{2,1,0:T(8,128)}) custom-call(bf16[8,12,2,17280]{3,2,1,0:T(2,128)(2,1)} %stored_ref.6, bf16[2,8,384]{2,1,0:T(8,128)(2,1)} %constant.27.clone.sum_ref.refs_9_), custom_call_target="tpu_custom_call" | custom-call | flops 113246208 | bytes 10260480 | tf_op jit(solution)/shard_map/pallas_call | solution.py:505
  113.8 2.6 collective-permute-start
  116.4 1.7 collective-permute-start.1
  118.7 2.8 collective-permute-done.refs_1_
  121.6 3.7 collective-permute-done.1.refs_2_
  126.0 14.6 %shard_map.225 = bf16[8,2,8,24,384]{4,3,2,1,0:T(8,128)(2,1)} custom-call(f32[2,48,192]{2,1,0:T(8,128)} %get-tuple-element.24.refs_0_, f32[2,48,192]{2,1,0:T(8,128)} %copy-done.9, f32[2,48,192]{2,1,0:T(8,128)} %copy-done.10, f32[2,48,192]{2,1,0:T(8,128)} %copy-done.11, bf16[2,12,192,384]{3,2,1,0:T(8,128)(2,1)} %get-tuple-element.25.refs_4_.refs_5_.refs_9_, ...), custom_call_target="tpu_custom_call" | custom-call | flops 452984832 | bytes 6282752 | tf_op jit(solution)/shard_map/pallas_call | solution.py:505
  140.5 4.0 all-to-all-start
  145.5 1.5 fusion.1
  149.2 2.0 squeeze.36
  155.3 2.3 maximum_maximum_fusion.1.w2_ref
  157.6 2.2 maximum_maximum_fusion.w1_ref
  159.8 41.6 %shard_map.231 = (bf16[8,2,12,16,384]{4,3,2,1,0:T(8,128)(2,1)}, bf16[8,2,12,16,384]{4,3,2,1,0:T(8,128)(2,1)}, f32[2,2,2,96,128]{4,3,2,1,0:T(8,128)}, f32[16,768]{1,0:T(8,128)}) custom-call(bf16[8,2,8,24,384]{4,3,2,1,0:T(8,128)(2,1)} %all-to-all-done.3.x_ref, bf16[8,2,8,24,384]{4,3,2,1,0:T(8,128)(2,1)} %copy-done.3, ...), custom_call_target="tpu_custom_call" | custom-call | flops 10871635968 | bytes 12392448 | tf_op jit(solution)/shard_map/pallas_call | solution.py:505
  202.8 4.2 all-to-all-start.7
  207.0 41.6 %shard_map.227 = (bf16[8,2,12,16,384]{4,3,2,1,0:T(8,128)(2,1)}, bf16[8,2,12,16,384]{4,3,2,1,0:T(8,128)(2,1)}, f32[2,2,2,96,128]{4,3,2,1,0:T(8,128)}, f32[16,768]{1,0:T(8,128)}) custom-call(bf16[8,2,8,24,384]{4,3,2,1,0:T(8,128)(2,1)} %copy-done.4, bf16[8,2,8,24,384]{4,3,2,1,0:T(8,128)(2,1)} %copy-done.2, bf16[192,192]{1,0:T(8,128)(2,1)} %constant.25.clone.there_ref, ...), custom_call_target="tpu_custom_call" | custom-call | flops 10871635968 | bytes 12392448 | tf_op jit(solution)/shard_map/pallas_call | solution.py:505
  248.7 34.2 %all_to_all.40.refs_4_.refs_8_ = bf16[8,2,12,16,384]{4,3,2,1,0:T(8,128)(2,1)} all-to-all(bf16[8,2,12,16,384]{4,3,2,1,0:T(8,128)(2,1)} %get-tuple-element.30), channel_id=1, replica_groups=mesh['space'=8,'chan'=4] {'space'}, dimensions={0} | all-to-all | bytes 4718592 | tf_op jit(solution)/shard_map/all_to_all | solution.py:575
  282.9 32.6 %all_to_all.41.rows_ref = bf16[8,2,12,16,384]{4,3,2,1,0:T(8,128)(2,1)} all-to-all(bf16[8,2,12,16,384]{4,3,2,1,0:T(8,128)(2,1)S(1)} %copy-done.5), channel_id=1, replica_groups=mesh['space'=8,'chan'=4] {'space'}, dimensions={0} | all-to-all | bytes 4718592 | tf_op jit(solution)/shard_map/all_to_all | solution.py:575
  315.4 3.8 all-to-all-start.2
  319.7 1.4 collective-permute-done.12
  321.2 1.7 collective-permute-start.13
  324.7 27.2 %collective-permute-done.16 = f32[2,2,192]{2,1,0:T(2,128)S(1)} collective-permute-done((f32[2,2,192]{2,1,0:T(2,128)S(1)}, f32[2,2,192]{2,1,0:T(2,128)S(1)}, u32[]{:S(2)}, u32[]{:S(2)}) %collective-permute-start.16) | collective-permute-done | bytes 3104 | tf_op jit(solution)/shard_map/ppermute | solution.py:591
  351.9 1.5 collective-permute-start.17
  353.4 2.1 collective-permute-done.17
  355.6 1.6 collective-permute-start.14
  358.5 2.9 collective-permute-done.14
  361.4 16.9 %shard_map.235 = (f32[2,48,192]{2,1,0:T(8,128)}, f32[16,384]{1,0:T(8,128)}) custom-call(f32[2,48,192]{2,1,0:T(8,128)} %get-tuple-element.27.refs_0_, f32[2,48,192]{2,1,0:T(8,128)} %copy-done.6, f32[2,48,192]{2,1,0:T(8,128)} %copy-done.7, f32[2,48,192]{2,1,0:T(8,128)} %copy-done.8, bf16[8,2,12,16,384]{4,3,2,1,0:T(8,128)(2,1)} %copy-done, ...), custom_call_target="tpu_custom_call" | custom-call | flops 452984832 | bytes 6391296 | tf_op jit(solution)/shard_map/pallas_call | solution.py:505
  378.3 16.9 %shard_map.234 = (f32[2,48,192]{2,1,0:T(8,128)}, f32[16,384]{1,0:T(8,128)}) custom-call(f32[2,48,192]{2,1,0:T(8,128)} %get-tuple-element.24.refs_0_, f32[2,48,192]{2,1,0:T(8,128)} %copy-done.9, f32[2,48,192]{2,1,0:T(8,128)} %copy-done.10, f32[2,48,192]{2,1,0:T(8,128)} %copy-done.11, bf16[8,2,12,16,384]{4,3,2,1,0:T(8,128)(2,1)} %all_to_all.40.refs_4_.refs_8_, ...), custom_call_target="tpu_custom_call" | custom-call | flops 452984832 | bytes 6391296 | tf_op jit(solution)/shard_map/pallas_call | solution.py:505
  396.9 1.7 collective-permute-start.10
  398.6 3.3 collective-permute-start.11
  404.2 12.7 %shard_map.232.refs_2_ = bf16[8,12,2,17280]{3,2,1,0:T(2,128)(2,1)} custom-call(bf16[8,2,12,16,384]{4,3,2,1,0:T(8,128)(2,1)} %all_to_all.41.rows_ref, bf16[192,128]{1,0:T(8,128)(2,1)} %constant.23.clone.table_ref.refs_1_), custom_call_target="tpu_custom_call" | custom-call | flops 452984832 | bytes 9043968 | tf_op jit(solution)/shard_map/pallas_call | solution.py:505
  416.9 1.7 collective-permute-start.20
  418.6 1.4 copy-done.1
  420.0 12.7 %shard_map.233 = bf16[8,12,2,17280]{3,2,1,0:T(2,128)(2,1)} custom-call(bf16[8,2,12,16,384]{4,3,2,1,0:T(8,128)(2,1)} %copy-done.1, bf16[192,128]{1,0:T(8,128)(2,1)} %constant.23.clone.table_ref.refs_1_, bf16[8,12,2,17280]{3,2,1,0:T(2,128)(2,1)} %shard_map.232.refs_2_), custom_call_target="tpu_custom_call", output_to_operand_aliasing={{}: (2, {})} | custom-call | flops 452984832 | bytes 15679488 | tf_op jit(solution)/shard_map/pallas_call | solution.py:505
  432.7 3.4 collective-permute-start.7
  438.2 17.5 %shard_map.236.refs_13_ = bf16[8,12,2,17280]{3,2,1,0:T(2,128)(2,1)} custom-call(f32[2,48,192]{2,1,0:T(8,128)} %get-tuple-element.27.refs_0_, f32[2,48,192]{2,1,0:T(8,128)} %copy-done.6, f32[2,48,192]{2,1,0:T(8,128)} %copy-done.7, f32[2,48,192]{2,1,0:T(8,128)} %copy-done.8, bf16[2,48,192]{2,1,0:T(8,128)(2,1)} %copy-done.14, bf16[2,48,192]{2,1,0:T(8,128)(2,1)} %copy-done.21, ...), custom_call_target="tpu_custom_call" | custom-call | flops 452984832 | bytes 13063680 | tf_op jit(solution)/shard_map/pallas_call | solution.py:505
  457.0 17.5 %shard_map.237 = bf16[8,12,2,17280]{3,2,1,0:T(2,128)(2,1)} custom-call(f32[2,48,192]{2,1,0:T(8,128)} %get-tuple-element.24.refs_0_, f32[2,48,192]{2,1,0:T(8,128)} %copy-done.9, f32[2,48,192]{2,1,0:T(8,128)} %copy-done.10, f32[2,48,192]{2,1,0:T(8,128)} %copy-done.11, bf16[2,48,192]{2,1,0:T(8,128)(2,1)} %copy-done.15, ...), custom_call_target="tpu_custom_call", output_to_operand_aliasing={{}: (13, {})} | custom-call | flops 452984832 | bytes 19699200 | tf_op jit(solution)/shard_map/pallas_call | solution.py:505
  (134 shorter events, 25.4 us)
Async XLA Ops:
  13.3 34.6 %all-to-all-start.4 = ((bf16[8,2,8,24,384]{4,3,2,1,0:T(8,128)(2,1)}), bf16[8,2,8,24,384]{4,3,2,1,0:T(8,128)(2,1)S(1)}, u32[]{:S(2)}, u32[]{:S(2)}) async-start(bf16[8,2,8,24,384]{4,3,2,1,0:T(8,128)(2,1)} %shard_map.230), calls=%async_computation.4 | async-start | bytes 4718592 | tf_op jit(solution)/shard_map/all_to_all | solution.py:575
  48.0 1.5 copy-start.3
  49.4 44.5 %all-to-all-start.1 = ((bf16[8,2,8,24,384]{4,3,2,1,0:T(8,128)(2,1)}), bf16[8,2,8,24,384]{4,3,2,1,0:T(8,128)(2,1)S(1)}, u32[]{:S(2)}, u32[]{:S(2)}) async-start(bf16[8,2,8,24,384]{4,3,2,1,0:T(8,128)(2,1)} %shard_map.226), calls=%async_computation.1 | async-start | bytes 4718592 | tf_op jit(solution)/shard_map/all_to_all | solution.py:575
  53.0 19.6 %copy-start.30 = (f32[192]{0:T(256)S(1)}, f32[192]{0:T(256)}, u32[]{:S(2)}) copy-start(f32[192]{0:T(256)} %param.18) | copy-start | bytes 2308
  53.1 20.3 %copy-start.31 = (f32[192]{0:T(256)S(1)}, f32[192]{0:T(256)}, u32[]{:S(2)}) copy-start(f32[192]{0:T(256)} %param.19) | copy-start | bytes 2308
  67.1 7.8 %collective-permute-start.3 = (f32[2,48,192]{2,1,0:T(8,128)}, f32[2,48,192]{2,1,0:T(8,128)S(1)}, u32[]{:S(2)}, u32[]{:S(2)}) collective-permute-start(f32[2,48,192]{2,1,0:T(8,128)} %get-tuple-element.27.refs_0_), channel_id=1, source_target_pairs={{0,1},{1,2},{2,3},{3,0},{4,5},{5,6},{6,7},{7,4},{8,9},{9,10},{10,1... | collective-permute-start | bytes 221192 | tf_op jit(solution)/shard_map/ppermute | solution.py:582
  68.7 9.9 %collective-permute-start.4 = (f32[2,48,192]{2,1,0:T(8,128)}, f32[2,48,192]{2,1,0:T(8,128)S(1)}, u32[]{:S(2)}, u32[]{:S(2)}) collective-permute-start(f32[2,48,192]{2,1,0:T(8,128)} %get-tuple-element.27.refs_0_), channel_id=1, source_target_pairs={{0,2},{1,3},{2,0},{3,1},{4,6},{5,7},{6,4},{7,5},{8,10},{9,11},{10,... | collective-permute-start | bytes 221192 | tf_op jit(solution)/shard_map/ppermute | solution.py:582
  71.3 7.3 %collective-permute-start.5 = (f32[2,48,192]{2,1,0:T(8,128)}, f32[2,48,192]{2,1,0:T(8,128)S(1)}, u32[]{:S(2)}, u32[]{:S(2)}) collective-permute-start(f32[2,48,192]{2,1,0:T(8,128)} %get-tuple-element.27.refs_0_), channel_id=1, source_target_pairs={{0,3},{1,0},{2,1},{3,2},{4,7},{5,4},{6,5},{7,6},{8,11},{9,8},{10,9... | collective-permute-start | bytes 221192 | tf_op jit(solution)/shard_map/ppermute | solution.py:582
  74.9 4.4 copy-start.6
  93.9 1.4 copy-start.2
  95.3 45.2 %all-to-all-start.3 = ((bf16[8,2,8,24,384]{4,3,2,1,0:T(8,128)(2,1)}), bf16[8,2,8,24,384]{4,3,2,1,0:T(8,128)(2,1)}, u32[]{:S(2)}, u32[]{:S(2)}) async-start(bf16[8,2,8,24,384]{4,3,2,1,0:T(8,128)(2,1)} %shard_map.229), calls=%async_computation.3 | async-start | bytes 4718592 | tf_op jit(solution)/shard_map/all_to_all | solution.py:575
  113.8 7.8 %collective-permute-start = (f32[2,48,192]{2,1,0:T(8,128)}, f32[2,48,192]{2,1,0:T(8,128)S(1)}, u32[]{:S(2)}, u32[]{:S(2)}) collective-permute-start(f32[2,48,192]{2,1,0:T(8,128)} %get-tuple-element.24.refs_0_), channel_id=1, source_target_pairs={{0,1},{1,2},{2,3},{3,0},{4,5},{5,6},{6,7},{7,4},{8,9},{9,10},{10,1... | collective-permute-start | bytes 221192 | tf_op jit(solution)/shard_map/ppermute | solution.py:582
  116.4 8.9 %collective-permute-start.1 = (f32[2,48,192]{2,1,0:T(8,128)}, f32[2,48,192]{2,1,0:T(8,128)S(1)}, u32[]{:S(2)}, u32[]{:S(2)}) collective-permute-start(f32[2,48,192]{2,1,0:T(8,128)} %get-tuple-element.24.refs_0_), channel_id=1, source_target_pairs={{0,2},{1,3},{2,0},{3,1},{4,6},{5,7},{6,4},{7,5},{8,10},{9,11},{10,... | collective-permute-start | bytes 221192 | tf_op jit(solution)/shard_map/ppermute | solution.py:582
  118.0 7.3 %collective-permute-start.2 = (f32[2,48,192]{2,1,0:T(8,128)}, f32[2,48,192]{2,1,0:T(8,128)S(1)}, u32[]{:S(2)}, u32[]{:S(2)}) collective-permute-start(f32[2,48,192]{2,1,0:T(8,128)} %get-tuple-element.24.refs_0_), channel_id=1, source_target_pairs={{0,3},{1,0},{2,1},{3,2},{4,7},{5,4},{6,5},{7,6},{8,11},{9,8},{10,9... | collective-permute-start | bytes 221192 | tf_op jit(solution)/shard_map/ppermute | solution.py:582
  121.6 3.7 copy-start.9
  140.5 4.1 copy-start.17
  140.5 4.1 copy-start.18
  140.5 60.9 %all-to-all-start = ((bf16[8,2,8,24,384]{4,3,2,1,0:T(8,128)(2,1)}), bf16[8,2,8,24,384]{4,3,2,1,0:T(8,128)(2,1)S(1)}, u32[]{:S(2)}, u32[]{:S(2)}) async-start(bf16[8,2,8,24,384]{4,3,2,1,0:T(8,128)(2,1)} %shard_map.225), calls=%async_computation | async-start | bytes 4718592 | tf_op jit(solution)/shard_map/all_to_all | solution.py:575
  147.1 7.3 %copy-start.28 = (f32[2,2,96]{2,1,0:T(2,128)S(1)}, f32[2,2,96]{2,1,0:T(2,128)}, u32[]{:S(2)}) copy-start(f32[2,2,96]{2,1,0:T(2,128)} %param.21) | copy-start | bytes 4612
  147.1 7.5 %copy-start.29 = (f32[2,2,96]{2,1,0:T(2,128)S(1)}, f32[2,2,96]{2,1,0:T(2,128)}, u32[]{:S(2)}) copy-start(f32[2,2,96]{2,1,0:T(2,128)} %param.23) | copy-start | bytes 4612
  201.4 1.4 copy-start.4
  202.8 45.8 %all-to-all-start.7 = ((bf16[8,2,12,16,384]{4,3,2,1,0:T(8,128)(2,1)}), bf16[8,2,12,16,384]{4,3,2,1,0:T(8,128)(2,1)S(1)}, u32[]{:S(2)}, u32[]{:S(2)}) async-start(bf16[8,2,12,16,384]{4,3,2,1,0:T(8,128)(2,1)} %get-tuple-element.32), calls=%async_computation.7 | async-start | bytes 4718592 | tf_op jit(solution)/shard_map/all_to_all | solution.py:575
  248.6 34.2 %copy-start = (bf16[8,2,12,16,384]{4,3,2,1,0:T(8,128)(2,1)}, bf16[8,2,12,16,384]{4,3,2,1,0:T(8,128)(2,1)S(1)}, u32[]{:S(2)}) copy-start(bf16[8,2,12,16,384]{4,3,2,1,0:T(8,128)(2,1)S(1)} %all-to-all-done.7.refs_4_.refs_8_) | copy-start | bytes 7077892
  248.6 34.2 %copy-start.5 = (bf16[8,2,12,16,384]{4,3,2,1,0:T(8,128)(2,1)S(1)}, bf16[8,2,12,16,384]{4,3,2,1,0:T(8,128)(2,1)}, u32[]{:S(2)}) copy-start(bf16[8,2,12,16,384]{4,3,2,1,0:T(8,128)(2,1)} %get-tuple-element.29) | copy-start | bytes 7077892
  315.4 3.8 copy-start.12
  315.4 3.8 copy-start.13
  315.4 7.5 %copy-start.22 = (f32[16,768]{1,0:T(8,128)S(1)}, f32[16,768]{1,0:T(8,128)}, u32[]{:S(2)}) copy-start(f32[16,768]{1,0:T(8,128)} %get-tuple-element.36) | copy-start | bytes 147460
  315.4 7.5 %copy-start.23 = (f32[16,768]{1,0:T(8,128)S(1)}, f32[16,768]{1,0:T(8,128)}, u32[]{:S(2)}) copy-start(f32[16,768]{1,0:T(8,128)} %get-tuple-element.37) | copy-start | bytes 147460
  315.4 103.2 %all-to-all-start.2 = ((bf16[8,2,12,16,384]{4,3,2,1,0:T(8,128)(2,1)}), bf16[8,2,12,16,384]{4,3,2,1,0:T(8,128)(2,1)S(1)}, u32[]{:S(2)}, u32[]{:S(2)}) async-start(bf16[8,2,12,16,384]{4,3,2,1,0:T(8,128)(2,1)} %get-tuple-element.26), calls=%async_computation.2 | async-start | bytes 4718592 | tf_op jit(solution)/shard_map/all_to_all | solution.py:575
  319.3 1.9 collective-permute-start.12
  321.2 34.3 %collective-permute-start.13 = (bf16[768,128]{1,0:T(8,128)(2,1)S(1)}, bf16[768,128]{1,0:T(8,128)(2,1)S(1)}, u32[]{:S(2)}, u32[]{:S(2)}) collective-permute-start(bf16[768,128]{1,0:T(8,128)(2,1)S(1)} %add_convert_fusion.1), channel_id=1, source_target_pairs={{0,8},{4,12},{8,0},{12,4},{16,24},{20,28},{24,16},{28,20},{1,9},{5... | collective-permute-start | bytes 589832 | tf_op jit(solution)/shard_map/ppermute | solution.py:591
  323.1 1.2 collective-permute-start.15
  324.4 27.5 %collective-permute-start.16 = (f32[2,2,192]{2,1,0:T(2,128)S(1)}, f32[2,2,192]{2,1,0:T(2,128)S(1)}, u32[]{:S(2)}, u32[]{:S(2)}) collective-permute-start(f32[2,2,192]{2,1,0:T(2,128)S(1)} %add.41), channel_id=1, source_target_pairs={{0,8},{4,12},{8,0},{12,4},{16,24},{20,28},{24,16},{28,20},{1,9},{5... | collective-permute-start | bytes 9224 | tf_op jit(solution)/shard_map/ppermute | solution.py:591
  351.9 3.6 collective-permute-start.17
  355.6 5.7 %collective-permute-start.14 = (bf16[768,128]{1,0:T(8,128)(2,1)S(1)}, bf16[768,128]{1,0:T(8,128)(2,1)S(1)}, u32[]{:S(2)}, u32[]{:S(2)}) collective-permute-start(bf16[768,128]{1,0:T(8,128)(2,1)S(1)} %add_convert_fusion), channel_id=1, source_target_pairs={{0,16},{4,20},{8,24},{12,28},{16,0},{20,4},{24,8},{28,12},{1,17},{... | collective-permute-start | bytes 589832 | tf_op jit(solution)/shard_map/ppermute | solution.py:591
  378.2 16.9 %copy-start.27 = (f32[16,384]{1,0:T(8,128)S(1)}, f32[16,384]{1,0:T(8,128)}, u32[]{:S(2)}) copy-start(f32[16,384]{1,0:T(8,128)} %get-tuple-element.38) | copy-start | bytes 73732
  378.2 18.6 %copy-start.16 = (f32[2,48,192]{2,1,0:T(8,128)S(1)}, f32[2,48,192]{2,1,0:T(8,128)}, u32[]{:S(2)}) copy-start(f32[2,48,192]{2,1,0:T(8,128)} %get-tuple-element.33) | copy-start | bytes 221188
  396.0 7.7 %collective-permute-start.18 = (f32[2,192]{1,0:T(2,128)S(1)}, f32[2,192]{1,0:T(2,128)S(1)}, u32[]{:S(2)}, u32[]{:S(2)}) collective-permute-start(f32[2,192]{1,0:T(2,128)S(1)} %reduce_sum.29), channel_id=1, source_target_pairs={{0,4},{4,0},{8,12},{12,8},{16,20},{20,16},{24,28},{28,24},{1,5},{5... | collective-permute-start | bytes 4616 | tf_op jit(solution)/shard_map/ppermute | solution.py:591
  396.9 20.0 %copy-start.14 = (bf16[2,48,192]{2,1,0:T(8,128)(2,1)}, bf16[2,48,192]{2,1,0:T(8,128)(2,1)S(1)}, u32[]{:S(2)}) copy-start(bf16[2,48,192]{2,1,0:T(8,128)(2,1)S(1)} %convert_element_type.48.refs_4_) | copy-start | bytes 110596
  396.9 39.8 %collective-permute-start.10 = (bf16[2,48,192]{2,1,0:T(8,128)(2,1)S(1)}, bf16[2,48,192]{2,1,0:T(8,128)(2,1)S(1)}, u32[]{:S(2)}, u32[]{:S(2)}) collective-permute-start(bf16[2,48,192]{2,1,0:T(8,128)(2,1)S(1)} %convert_element_type.48.refs_4_), channel_id=1, source_target_pairs={{0,2},{1,3},{2,0},{3,1},{4,6},{5,7},{6,4},{7,5},{8,10},{9,11},{10,... | collective-permute-start | bytes 110600 | tf_op jit(solution)/shard_map/ppermute | solution.py:582
  398.6 38.4 %collective-permute-start.11 = (bf16[2,48,192]{2,1,0:T(8,128)(2,1)S(1)}, bf16[2,48,192]{2,1,0:T(8,128)(2,1)S(1)}, u32[]{:S(2)}, u32[]{:S(2)}) collective-permute-start(bf16[2,48,192]{2,1,0:T(8,128)(2,1)S(1)} %convert_element_type.48.refs_4_), channel_id=1, source_target_pairs={{0,3},{1,0},{2,1},{3,2},{4,7},{5,4},{6,5},{7,6},{8,11},{9,8},{10,9... | collective-permute-start | bytes 110600 | tf_op jit(solution)/shard_map/ppermute | solution.py:582
  401.8 35.2 %collective-permute-start.9 = (bf16[2,48,192]{2,1,0:T(8,128)(2,1)S(1)}, bf16[2,48,192]{2,1,0:T(8,128)(2,1)S(1)}, u32[]{:S(2)}, u32[]{:S(2)}) collective-permute-start(bf16[2,48,192]{2,1,0:T(8,128)(2,1)S(1)} %convert_element_type.48.refs_4_), channel_id=1, source_target_pairs={{0,1},{1,2},{2,3},{3,0},{4,5},{5,6},{6,7},{7,4},{8,9},{9,10},{10,1... | collective-permute-start | bytes 110600 | tf_op jit(solution)/shard_map/ppermute | solution.py:582
  402.7 33.9 %copy-start.15 = (bf16[2,48,192]{2,1,0:T(8,128)(2,1)}, bf16[2,48,192]{2,1,0:T(8,128)(2,1)S(1)}, u32[]{:S(2)}) copy-start(bf16[2,48,192]{2,1,0:T(8,128)(2,1)S(1)} %convert_element_type.47.refs_4_) | copy-start | bytes 110596
  402.7 53.0 %collective-permute-start.6 = (bf16[2,48,192]{2,1,0:T(8,128)(2,1)S(1)}, bf16[2,48,192]{2,1,0:T(8,128)(2,1)S(1)}, u32[]{:S(2)}, u32[]{:S(2)}) collective-permute-start(bf16[2,48,192]{2,1,0:T(8,128)(2,1)S(1)} %convert_element_type.47.refs_4_), channel_id=1, source_target_pairs={{0,1},{1,2},{2,3},{3,0},{4,5},{5,6},{6,7},{7,4},{8,9},{9,10},{10,1... | collective-permute-start | bytes 110600 | tf_op jit(solution)/shard_map/ppermute | solution.py:582
  403.8 13.1 %collective-permute-start.19 = (f32[2,192]{1,0:T(2,128)S(1)}, f32[2,192]{1,0:T(2,128)S(1)}, u32[]{:S(2)}, u32[]{:S(2)}) collective-permute-start(f32[2,192]{1,0:T(2,128)S(1)} %add.45), channel_id=1, source_target_pairs={{0,8},{4,12},{8,0},{12,4},{16,24},{20,28},{24,16},{28,20},{1,9},{5... | collective-permute-start | bytes 4616 | tf_op jit(solution)/shard_map/ppermute | solution.py:591
  416.9 15.8 %collective-permute-start.20 = (f32[2,192]{1,0:T(2,128)S(1)}, f32[2,192]{1,0:T(2,128)S(1)}, u32[]{:S(2)}, u32[]{:S(2)}) collective-permute-start(f32[2,192]{1,0:T(2,128)S(1)} %add.46), channel_id=1, source_target_pairs={{0,16},{4,20},{8,24},{12,28},{16,0},{20,4},{24,8},{28,12},{1,17},{... | collective-permute-start | bytes 4616 | tf_op jit(solution)/shard_map/ppermute | solution.py:591
  432.7 23.1 %collective-permute-start.7 = (bf16[2,48,192]{2,1,0:T(8,128)(2,1)S(1)}, bf16[2,48,192]{2,1,0:T(8,128)(2,1)S(1)}, u32[]{:S(2)}, u32[]{:S(2)}) collective-permute-start(bf16[2,48,192]{2,1,0:T(8,128)(2,1)S(1)} %convert_element_type.47.refs_4_), channel_id=1, source_target_pairs={{0,2},{1,3},{2,0},{3,1},{4,6},{5,7},{6,4},{7,5},{8,10},{9,11},{10,... | collective-permute-start | bytes 110600 | tf_op jit(solution)/shard_map/ppermute | solution.py:582
  436.7 19.1 %collective-permute-start.8 = (bf16[2,48,192]{2,1,0:T(8,128)(2,1)S(1)}, bf16[2,48,192]{2,1,0:T(8,128)(2,1)S(1)}, u32[]{:S(2)}, u32[]{:S(2)}) collective-permute-start(bf16[2,48,192]{2,1,0:T(8,128)(2,1)S(1)} %convert_element_type.47.refs_4_), channel_id=1, source_target_pairs={{0,3},{1,0},{2,1},{3,2},{4,7},{5,4},{6,5},{7,6},{8,11},{9,8},{10,9... | collective-permute-start | bytes 110600 | tf_op jit(solution)/shard_map/ppermute | solution.py:582
  (11 other events, 7.8 us)
where the time goes:
time: 476 us; the launch traced here: 475 us
  Pallas kernels  260 us (55%)
  blocking collectives  66.7 us (14%)
  waiting for transfers between devices  62.6 us (13%)
  starting transfers between devices  53.3 us (11%)
  local copies, waits for them, and re-layouts  21.3 us (4%)
  other arithmetic  9.51 us (2%)
    pallas_call x14, Pallas kernels, _call(): pl.pallas_call(body, grid=grid, in_specs=in_specs, out_specs=out_specs, o...  260 us
    all_to_all x2, blocking collectives, exchange(): return lax.all_to_all(value, 'space', 0, 0, tiled=True)  66.7 us
    ppermute x9, waiting for transfers between devices, reduced(): other = lax.ppermute(own, 'space', [(i, i ^ step) for i in range(p.space)])  34.7 us
    all_to_all x6, starting transfers between devices, exchange(): return lax.all_to_all(value, 'space', 0, 0, tiled=True)  25.2 us
    ppermute x12, starting transfers between devices, around(): lax.ppermute(value, axis, [(i, (i + step) % size) for i in range(size)])  20.2 us
    all_to_all x6, waiting for transfers between devices, exchange(): return lax.all_to_all(value, 'space', 0, 0, tiled=True)  16.7 us
    ppermute x12, waiting for transfers between devices, around(): lax.ppermute(value, axis, [(i, (i + step) % size) for i in range(size)])  11.2 us
  transfers between devices with their start and end apart: 27, of which 10 were waited for; matrix products, arithmetic and copies ran while one was open for 5% of the time, Pallas kernels for 48%

commit v1 on v0

--- a/solution.py
+++ b/solution.py
@@ -21,8 +21,8 @@
 
 half = jnp.bfloat16
 single = jnp.float32
-VMEM_LIMIT = 60 * 1024 * 1024
-CHUNKS = 2
+VMEM_LIMIT = 36 * 1024 * 1024
+SLOTS = 2
 
 TN = (((0,), (0,)), ((), ()))
 NT = (((1,), (1,)), ((), ()))
@@ -53,7 +53,6 @@
         self.turn = self.lon // PACK
         self.turn_pad = -(-self.turn // 16) * 16
         self.words = self.long // LANES
-        self.line = self.rows * self.groups
         self.word_pad = self.tiles * self.turn_pad
         self.channels = self.groups * width * chan
 
@@ -84,21 +83,19 @@
     return value if shift == 0 else pltpu.roll(value, shift, 1)
 
 
-def spread(p, stored_ref, words_ref):
-    for s in range(p.stack):
-        for t in range(p.words):
-            part = stored_ref[s, :, :, t * LANES : (t + 1) * LANES]
-            words_ref[s, t * p.line : (t + 1) * p.line, :] = part.reshape(p.line, LANES).astype(single)
-
-
-def gather_row(p, words_ref, h, put):
+def spread(p, stored_ref, words_ref, h):
+    for q in range(PACK):
+        line = stored_ref[q // p.groups, h, q % p.groups, :]
+        words_ref[q, : p.words, :] = line.reshape(p.words, LANES).astype(single)
+
+
+def gather_row(p, words_ref):
     lane = lax.broadcasted_iota(jnp.int32, (p.turn_pad, LANES), 1)
     source = {}
     for q in range(PACK):
-        s, n = divmod(q, p.groups)
         for i in range(p.tiles):
-            start = i * p.line + h * p.groups + n
-            source[q, i] = words_ref[s, pl.ds(start, p.turn_pad, stride=p.tiles * p.line), :]
+            source[q, i] = words_ref[q, pl.ds(i, p.turn_pad, stride=p.tiles), :]
+    rows = []
     for r in range(PACK):
         cache = {}
 
@@ -108,12 +105,15 @@
                 cache[key] = rolled(source[q, i], shift)
             return cache[key]
 
+        tiles = []
         for c in range(p.tiles):
             pieces = moved_lanes(p, fetch, lambda q: r * p.width, lambda q: q * p.width, c)
-            put(r, c, merged(pieces, lane))
-
-
-def scatter_row(p, tokens, words_ref, h):
+            tiles.append(merged(pieces, lane).astype(half))
+        rows.append(jnp.concatenate(tiles, axis=1))
+    return jnp.concatenate(rows, axis=0)
+
+
+def scatter_row(p, tokens, words_ref, stored_ref, h):
     lane = lax.broadcasted_iota(jnp.int32, (p.turn_pad, LANES), 1)
     for q in range(PACK):
         s, n = divmod(q, p.groups)
@@ -124,24 +124,32 @@
 
         for i in range(p.tiles):
             pieces = moved_lanes(p, fetch, lambda r: q * p.width, lambda r: r * p.width, i)
-            start = i * p.line + h * p.groups + n
-            words_ref[s, pl.ds(start, p.turn_pad, stride=p.tiles * p.line), :] = merged(pieces, lane)
-
-
-def store_words(p, words_ref, stored_ref):
+            at = pl.ds(i * p.groups + n, p.turn_pad, stride=p.tiles * p.groups)
+            words_ref[s, at, :] = merged(pieces, lane)
     for s in range(p.stack):
+        lines = words_ref[s, : p.words * p.groups, :].astype(half)
         for t in range(p.words):
-            part = words_ref[s, t * p.line : (t + 1) * p.line, :]
-            stored_ref[s, :, :, t * LANES : (t + 1) * LANES] = part.reshape(
-                p.rows, p.groups, LANES
-            ).astype(half)
+            stored_ref[s, h, :, t * LANES : (t + 1) * LANES] = lines[
+                t * p.groups : (t + 1) * p.groups, :
+            ]
 
 
 def clear_tail(p, words_ref):
     @pl.when(pl.program_id(0) == 0)
     def _():
-        tail = (p.word_pad - p.words) * p.line
-        words_ref[:, p.words * p.line :, :] = jnp.zeros((p.stack, tail, LANES), single)
+        tail = p.word_pad - p.words
+        words_ref[:, :, p.words :, :] = jnp.zeros(words_ref.shape[:2] + (tail, LANES), single)
+
+
+def each_row(p, body):
+    side = SLOTS if p.rows % SLOTS == 0 else 1
+
+    def step(i, carry):
+        for slot in range(side):
+            body(i * side + slot, slot)
+        return carry
+
+    lax.fori_loop(0, p.rows // side, step, 0)
 
 
 def analyse(p, tokens, table, scale, turn_ref, h):
@@ -153,12 +161,12 @@
             ]
 
 
-def send_turn(p, turn_ref, out_ref, outer, inner):
+def send_turn(p, turn_ref, out_ref, outer, inner, which=0):
     count = outer * inner
     for d in range(p.space):
         for c in range(p.tiles):
             part = turn_ref[c, d * count : (d + 1) * count, :].reshape(outer, inner, LANES)
-            out_ref[d, 0, :, :, c * LANES : (c + 1) * LANES] = part.astype(half)
+            out_ref[d, which, 0, :, :, c * LANES : (c + 1) * LANES] = part.astype(half)
 
 
 def split_three(value):
@@ -179,43 +187,30 @@
     return mul(table, high, NT) + mul(table, low, NT)
 
 
-def cotangent_kernel(p, stored_ref, table_ref, scale_ref, out_ref, words_ref, turn_ref, tokens_ref):
+def cotangent_kernel(p, stored_ref, table_ref, scale_ref, out_ref, words_ref, turn_ref):
     clear_tail(p, words_ref)
-    spread(p, stored_ref, words_ref)
-
-    def row(h, carry):
-        def put(r, c, value):
-            tokens_ref[r * p.turn_pad : (r + 1) * p.turn_pad, c * LANES : (c + 1) * LANES] = (
-                value.astype(half)
-            )
-
-        gather_row(p, words_ref, h, put)
-        analyse(p, tokens_ref[...], table_ref[...], scale_ref[...], turn_ref, h)
-        return carry
-
-    lax.fori_loop(0, p.rows, row, 0)
+
+    def row(h, slot):
+        spread(p, stored_ref, words_ref.at[slot], h)
+        tokens = gather_row(p, words_ref.at[slot])
+        analyse(p, tokens, table_ref[...], scale_ref[...], turn_ref, h)
+
+    each_row(p, row)
     send_turn(p, turn_ref, out_ref, p.modes, 2 * p.rows)
 
 
 def stats_kernel(p, stored_ref, sum_ref, tokens_ref, stat_ref, words_ref, rows_ref):
     clear_tail(p, words_ref)
-    spread(p, stored_ref, words_ref)
     count = 2 * p.stack
 
-    def row(h, carry):
-        def put(r, c, value):
-            tokens_ref[
-                0, h, r * p.turn_pad : (r + 1) * p.turn_pad, c * LANES : (c + 1) * LANES
-            ] = value.astype(half)
-
-        gather_row(p, words_ref, h, put)
-        tokens = tokens_ref[0, h]
+    def row(h, slot):
+        spread(p, stored_ref, words_ref.at[slot], h)
+        tokens = gather_row(p, words_ref.at[slot])
+        tokens_ref[0, h] = tokens
         wide = tokens.astype(single)
-        plain = mul(sum_ref[0], tokens, NT)
-        rows_ref[h] = plain + summed(sum_ref[1], wide * wide)
-        return carry
-
-    lax.fori_loop(0, p.rows, row, 0)
+        rows_ref[h] = mul(sum_ref[0], tokens, NT) + summed(sum_ref[1], wide * wide)
+
+    each_row(p, row)
     for h in range(p.rows):
         stat_ref[0, h * count : (h + 1) * count, :] = rows_ref[h, :count, :]
 
@@ -241,42 +236,65 @@
     out_ref, rows_ref, turn_ref = refs[p.chan + 6 :]
     moments(p, stat_refs, rows_ref)
 
-    def row(h, carry):
+    def row(h, slot):
         each = expand(rows_ref[h], wide_ref[...])
         wide = tokens_ref[0, h].astype(single)
         centred = (wide - each[:, : p.lanes]) * each[:, p.lanes :]
         normed = (centred * gain_ref[...] + shift_ref[...]).astype(half)
         analyse(p, normed, table_ref[...], scale_ref[...], turn_ref, h)
-        return carry
-
-    lax.fori_loop(0, p.rows, row, 0)
+
+    each_row(p, row)
     send_turn(p, turn_ref, out_ref, p.modes, 2 * p.rows)
 
 
 def gelu_both(values):
-    inner = jnp.tanh(gelu_scale * (values + gelu_cubic * values * values * values))
-    hidden = 0.5 * values * (1.0 + inner)
-    slope = 0.5 * (1.0 + inner) + 0.5 * values * (1.0 - inner * inner) * gelu_scale * (
-        1.0 + 3.0 * gelu_cubic * values * values
+    square = values * values
+    inner = jnp.tanh(values * (gelu_scale + gelu_scale * gelu_cubic * square))
+    upper = 0.5 + 0.5 * inner
+    hidden = values * upper
+    slope = upper + hidden * (1.0 - upper) * (
+        2.0 * gelu_scale + 6.0 * gelu_scale * gelu_cubic * square
     )
     return hidden, slope
 
 
 BAND = 16
+
+
+def place_weights(p, w_ref, out_refs):
+    lane = lax.broadcasted_iota(jnp.int32, (p.width, LANES), 1)
+    for which, out_ref in enumerate(out_refs):
+        for q in range(PACK):
+            at, shift = divmod(q * p.width, LANES)
+            for part in range(2):
+                value = w_ref[which, part, q % p.groups].astype(single)
+                turned = rolled(value, shift)
+                tiles = [jnp.zeros_like(value) for _ in range(p.tiles)]
+                tiles[at] = jnp.where(lane >= shift, turned, 0.0)
+                if shift + p.width > LANES:
+                    tiles[at + 1] = jnp.where(lane < shift + p.width - LANES, turned, 0.0)
+                wide = jnp.concatenate(tiles, axis=1)
+                for row_ri, col_ri, sign in (((0, 0, 1), (1, 1, 1)), ((0, 1, 1), (1, 0, -1)))[part]:
+                    top = row_ri * p.lanes + q * p.width
+                    out_ref[top : top + p.width, col_ri * p.lanes : (col_ri + 1) * p.lanes] = (
+                        sign * wide
+                    ).astype(half)
 
 
 def spectral_kernel(
     p,
     step_modes,
+    joined,
     x_ref,
     g_ref,
     there_ref,
     back_ref,
-    w1_ref,
-    w2_ref,
+    w_ref,
     bias_ref,
-    y_ref,
-    dx_ref,
+    *refs,
+):
+    out_refs = refs[: 1 if joined else 2]
+    (
     gw_ref,
     gb_ref,
     lat_ref,
@@ -291,7 +309,9 @@
     turn_x_ref,
     acc1_ref,
     acc2_ref,
-):
+    w1_ref,
+    w2_ref,
+    ) = refs[len(out_refs) :]
     pack, group = pl.program_id(0), pl.program_id(1)
     count = step_modes * p.lat
     factor = 1.0 / math.sqrt(p.lat)
@@ -299,13 +319,14 @@
 
     @pl.when((pack == 0) & (group == 0))
     def _():
+        place_weights(p, w_ref, (w1_ref, w2_ref))
         gb_ref[...] = jnp.zeros_like(gb_ref)
         acc1_ref[...] = jnp.zeros_like(acc1_ref)
         acc2_ref[...] = jnp.zeros_like(acc2_ref)
 
     def there(ref, into, offset):
         for m in range(step_modes):
-            block = ref[:, 0, m].reshape(2 * p.lat, p.lanes)
+            block = ref[:, 0, 0, m].reshape(2 * p.lat, p.lanes)
             out = (mul(there_ref[...], block) * factor).astype(half)
             at = pl.ds(offset + m * p.lat, p.lat)
             into[at, : p.lanes] = out[: p.lat]
@@ -364,8 +385,8 @@
 
     @pl.when(group == pl.num_programs(1) - 1)
     def _():
-        send_turn(p, turn_y_ref, y_ref, p.rows, 2 * p.modes)
-        send_turn(p, turn_x_ref, dx_ref, p.rows, 2 * p.modes)
+        send_turn(p, turn_y_ref, out_refs[0], p.rows, 2 * p.modes)
+        send_turn(p, turn_x_ref, out_refs[-1], p.rows, 2 * p.modes, len(out_refs) % 2)
         acc1_ref[...] += mul(lat_ref[...], gpre_ref[...], TN)
         acc2_ref[...] += mul(hid_ref[...], gpost_ref[...], TN)
 
@@ -400,14 +421,12 @@
 def mixed_kernel(p, rows_ref, table_ref, out_ref, words_ref):
     factor = 1.0 / math.sqrt(p.lon)
 
-    def row(h, carry):
-        block = rows_ref[:, 0, h].reshape(2 * MW, p.lanes)
+    def row(h, slot):
+        block = rows_ref[:, 0, 0, h].reshape(2 * MW, p.lanes)
         tokens = mul(table_ref[...], block) * factor
-        scatter_row(p, tokens, words_ref, h)
-        return carry
-
-    lax.fori_loop(0, p.rows, row, 0)
-    store_words(p, words_ref, out_ref)
+        scatter_row(p, tokens, words_ref.at[slot], out_ref, h)
+
+    each_row(p, row)
 
 
 def slope_sums_kernel(p, *refs):
@@ -422,8 +441,8 @@
     def _():
         param_ref[...] = jnp.zeros_like(param_ref)
 
-    def row(h, carry):
-        block = rows_in_ref[:, 0, h].reshape(2 * MW, p.lanes)
+    def row(h, slot):
+        block = rows_in_ref[:, 0, 0, h].reshape(2 * MW, p.lanes)
         normed_grad = mul(table_ref[...], block) * factor
         each = expand(rows_ref[h], wide_ref[...])
         wide = tokens_ref[0, h].astype(single)
@@ -434,9 +453,8 @@
         param_ref[8:16, :] += normed_grad.reshape(folds).sum(0)
         gain = gain_ref[...]
         part_ref[h] = summed(sum_ref[0], normed_grad * gain) + summed(sum_ref[1], product * gain)
-        return carry
-
-    lax.fori_loop(0, p.rows, row, 0)
+
+    each_row(p, row)
     for h in range(p.rows):
         sums_ref[0, h * count : (h + 1) * count, :] = part_ref[h, :count, :]
 
@@ -456,8 +474,8 @@
         if count < 8:
             part_ref[h, count:, :] = jnp.zeros((8 - count, p.turn_pad * PACK), single)
 
-    def row(h, carry):
-        block = rows_in_ref[:, 0, h].reshape(2 * MW, p.lanes)
+    def row(h, slot):
+        block = rows_in_ref[:, 0, 0, h].reshape(2 * MW, p.lanes)
         normed_grad = mul(table_ref[...], block) * factor
         each = expand(rows_ref[h], wide_ref[...])
         means = expand(part_ref[h], wide_ref[...])
@@ -466,11 +484,9 @@
         grad = inverse * (
             normed_grad * gain_ref[...] - means[:, : p.lanes] - centred * means[:, p.lanes :]
         )
-        scatter_row(p, grad, words_ref, h)
-        return carry
-
-    lax.fori_loop(0, p.rows, row, 0)
-    store_words(p, words_ref, out_ref)
+        scatter_row(p, grad, words_ref.at[slot], out_ref, h)
+
+    each_row(p, row)
 
 
 def whole_spec(value):
@@ -483,9 +499,9 @@
     return pl.BlockSpec(dims, lambda b, *_: (b + offset,) + (0,) * (len(dims) - 1))
 
 
-def peer_spec(value):
-    dims = (value.shape[0], 1) + value.shape[2:]
-    return pl.BlockSpec(dims, lambda b, *_: (0, b) + (0,) * (len(dims) - 2))
+def peer_spec(value, which=0, wide=1):
+    dims = (value.shape[0], wide, 1) + value.shape[3:]
+    return pl.BlockSpec(dims, lambda b, *_: (0, which, b) + (0,) * (len(dims) - 3))
 
 
 def stored_spec(p, offset):
@@ -558,15 +574,6 @@
     return jnp.asarray(sums, half), jnp.asarray(wide.reshape(24, 2 * p.lanes), half)
 
 
-def block_weights(p, weights):
-    each = jnp.tile(weights, (1, p.stack, 1, 1))
-    eye = jnp.eye(PACK, dtype=weights.dtype)
-    wide = (each[:, :, :, None, :] * eye[None, :, None, :, None]).reshape(2, p.lanes, p.lanes)
-    top = jnp.concatenate([wide[0], wide[1]], axis=1)
-    bottom = jnp.concatenate([-wide[1], wide[0]], axis=1)
-    return jnp.concatenate([top, bottom], axis=0)
-
-
 def lane_vector(p, vector):
     return jnp.tile(vector, p.stack)[None, :]
 
@@ -596,35 +603,52 @@
 
 def on_device(space, chan, members, gain, shift, w_first, b_first, w_second, b_second, cotangent):
     p = Plan(members, w_first.shape[-1], space, chan)
-    chunks = CHUNKS if p.packs % CHUNKS == 0 else 1
-    size = p.packs // chunks
+    size = p.packs // 2
     grid = (size,)
     table, plain_scale, double_scale, mixed_table, slope_table = lon_tables(p)
     there_table, back_table = lat_tables(p)
     sum_table, wide_table = sum_tables(p)
     gain_lanes, shift_lanes = lane_vector(p, gain), lane_vector(p, shift)
-    w1, w2 = block_weights(p, w_first), block_weights(p, w_second)
-    bias = jnp.stack(
-        [jnp.tile(b.reshape(2, -1), (1, p.stack)).reshape(-1) for b in (b_first, b_second)]
+    both_weights = jnp.pad(
+        jnp.stack([w_first, w_second]), ((0, 0),) * 4 + ((0, LANES - p.width),)
     )
+    bias = jnp.concatenate(
+        [b[ri].reshape(-1) for b in (b_first, b_second) for ri in range(2) for _ in range(p.stack)]
+    ).reshape(2, 2 * p.lanes)
     tokens_rows = PACK * p.turn_pad
     dft_flops = 2 * size * p.rows * tokens_rows * 2 * MW * p.lanes
-    words = pltpu.VMEM((p.stack, p.word_pad * p.line, LANES), single)
+    words = pltpu.VMEM((SLOTS, PACK, p.word_pad, LANES), single)
+    lines = pltpu.VMEM((SLOTS, p.stack, p.word_pad * p.groups, LANES), single)
     turn_in = pltpu.VMEM((p.tiles, MW * 2 * p.rows, LANES), single)
     rows_scratch = pltpu.VMEM((p.rows, 8, tokens_rows), single)
-    sent = jax.ShapeDtypeStruct((space, size, p.modes, 2 * p.rows, p.lanes), half)
-    returned = jax.ShapeDtypeStruct((space, size, p.rows, 2 * p.modes, p.lanes), half)
+
+    def sent(wide):
+        return jax.ShapeDtypeStruct((space, wide, size, p.modes, 2 * p.rows, p.lanes), half)
+
+    def returned(wide):
+        return jax.ShapeDtypeStruct((space, wide, size, p.rows, 2 * p.modes, p.lanes), half)
+
     count = 2 * p.stack * p.rows
     stored = jax.ShapeDtypeStruct(members.shape, half)
 
-    def cotangent_chunk(c):
-        ins = (cotangent, table, double_scale)
-        return call(
-            functools.partial(cotangent_kernel, p), grid, ins,
+    def out_call(body, ins, specs, out, out_spec, scratch, flops, before):
+        ins, specs = list(ins), list(specs)
+        aliases = {}
+        inner = body
+        if before is not None:
+            place = len(ins)
+            inner = lambda *refs: body(*refs[:place], *refs[place + 1 :])
+            ins.append(before)
+            specs.append(pl.BlockSpec(memory_space=pl.ANY))
+            aliases = {place: 0}
+        return call(inner, grid, tuple(ins), specs, [out], [out_spec], scratch, flops, aliases)[0]
+
+    def cotangent_chunk(c, wide):
+        return out_call(
+            functools.partial(cotangent_kernel, p), (cotangent, table, double_scale),
             [stored_spec(p, c * size), whole_spec(table), whole_spec(double_scale)],
-            [sent], [peer_spec(sent)],
-            [words, turn_in, pltpu.VMEM((tokens_rows, p.lanes), half)], dft_flops,
-        )[0]
+            sent(wide), peer_spec(sent(wide)), [words, turn_in], dft_flops, None,
+        )
 
     def stats_chunk(c):
         ins = (members, sum_table)
@@ -638,22 +662,29 @@
             outs, [pack_spec(o) for o in outs], [words, rows_scratch], dft_flops // 4,
         )
 
-    def normalise_chunk(stats, tokens):
+    def normalise_chunk(stats, tokens, before):
         tail = (gain_lanes, shift_lanes, table, plain_scale, wide_table)
-        return call(
-            functools.partial(normalise_kernel, p), grid, (*stats, tokens, *tail),
+        out = sent(1 if before is None else 2)
+        return out_call(
+            functools.partial(normalise_kernel, p), (*stats, tokens, *tail),
             [pack_spec(s) for s in stats] + [pack_spec(tokens)] + [whole_spec(v) for v in tail],
-            [sent], [peer_spec(sent)], [rows_scratch, turn_in], dft_flops,
-        )[0]
+            out, peer_spec(out, out.shape[1] - 1), [rows_scratch, turn_in], dft_flops, before,
+        )
 
     step_modes = 2 if p.modes % 2 == 0 else 1
     wide_lanes = 2 * p.lanes
 
-    def spectral_chunk(x_in, g_in):
-        tail = (there_table, back_table, w1, w2, bias)
-        mode_spec = pl.BlockSpec(
-            (space, 1, step_modes, 2 * p.rows, p.lanes), lambda b, m: (0, b, m, 0, 0)
-        )
+    def spectral_chunk(x_in, x_which, g_in, joined):
+        tail = (there_table, back_table, both_weights, bias)
+
+        def mode_spec(which):
+            return pl.BlockSpec(
+                (space, 1, 1, step_modes, 2 * p.rows, p.lanes),
+                lambda b, m: (0, which, b, m, 0, 0),
+            )
+
+        outs = [returned(2)] if joined else [returned(1), returned(1)]
+        out_specs = [peer_spec(o, 0, o.shape[1]) for o in outs]
         grads = jax.ShapeDtypeStruct((2, 2, p.groups, p.width, LANES), single)
         bias_grads = jax.ShapeDtypeStruct((16, wide_lanes), single)
         kept = pltpu.VMEM((p.modes * p.lat, wide_lanes), half)
@@ -661,38 +692,25 @@
         brief = pltpu.VMEM((step_modes * p.lat, wide_lanes), half)
         turn_out = pltpu.VMEM((p.tiles, p.lat * 2 * p.modes, LANES), single)
         return call(
-            functools.partial(spectral_kernel, p, step_modes),
+            functools.partial(spectral_kernel, p, step_modes, joined),
             (size, p.modes // step_modes), (x_in, g_in, *tail),
-            [mode_spec, mode_spec] + [whole_spec(v) for v in tail],
-            [returned, returned, grads, bias_grads],
-            [peer_spec(returned), peer_spec(returned), whole_spec(grads), whole_spec(bias_grads)],
+            [mode_spec(x_which), mode_spec(0)] + [whole_spec(v) for v in tail],
+            [*outs, grads, bias_grads],
+            [*out_specs, whole_spec(grads), whole_spec(bias_grads)],
             [kept] * 4 + [held] * 2 + [brief] * 2 + [turn_out] * 2
-            + [pltpu.VMEM((wide_lanes, wide_lanes), single)] * 2,
+            + [pltpu.VMEM((wide_lanes, wide_lanes), single)] * 2
+            + [pltpu.VMEM((wide_lanes, wide_lanes), half)] * 2,
             12 * size * p.modes * p.lat * wide_lanes * wide_lanes,
         )
 
-    def out_call(body, c, ins, specs, scratch, before, flops):
-        ins, specs = list(ins), list(specs)
-        aliases = {}
-        inner = body
-        if before is not None:
-            place = len(ins)
-            inner = lambda *refs: body(*refs[:place], *refs[place + 1 :])
-            ins.append(before)
-            specs.append(pl.BlockSpec(memory_space=pl.ANY))
-            aliases = {place: 0}
-        return call(
-            inner, grid, tuple(ins), specs, [stored], [stored_spec(p, c * size)],
-            scratch, flops, aliases,
-        )[0]
-
-    def mixed_chunk(c, rows_in, before):
+    def mixed_chunk(c, rows_in, which, before):
         return out_call(
-            functools.partial(mixed_kernel, p), c, (rows_in, mixed_table),
-            [peer_spec(rows_in), whole_spec(mixed_table)], [words], before, dft_flops,
-        )
-
-    def slope_sums_chunk(stats, rows_in, tokens):
+            functools.partial(mixed_kernel, p), (rows_in, mixed_table),
+            [peer_spec(rows_in, which), whole_spec(mixed_table)], stored, stored_spec(p, c * size),
+            [lines], dft_flops, before,
+        )
+
+    def slope_sums_chunk(stats, rows_in, which, tokens):
         tail = (gain_lanes, slope_table, wide_table, sum_table)
         outs = [
             jax.ShapeDtypeStruct((size, count, tokens_rows), single),
@@ -701,40 +719,48 @@
         return call(
             functools.partial(slope_sums_kernel, p), grid,
             (*stats, rows_in, tokens, *tail),
-            [pack_spec(s) for s in stats] + [peer_spec(rows_in), pack_spec(tokens)]
+            [pack_spec(s) for s in stats] + [peer_spec(rows_in, which), pack_spec(tokens)]
             + [whole_spec(v) for v in tail],
             outs, [pack_spec(outs[0]), whole_spec(outs[1])], [rows_scratch, rows_scratch],
             dft_flops,
         )
 
-    def input_grad_chunk(c, stats, parts, rows_in, tokens, before):
+    def input_grad_chunk(c, stats, parts, rows_in, which, tokens, before):
         tail = (gain_lanes, slope_table, wide_table)
         return out_call(
-            functools.partial(input_grad_kernel, p), c,
+            functools.partial(input_grad_kernel, p),
             (*stats, *parts, rows_in, tokens, *tail),
-            [pack_spec(s) for s in (*stats, *parts)] + [peer_spec(rows_in), pack_spec(tokens)]
-            + [whole_spec(v) for v in tail],
-            [rows_scratch, rows_scratch, words], before, dft_flops,
-        )
-
-    everyone = range(chunks)
-    g_in = [exchange(cotangent_chunk(c)) for c in everyone]
-    first = [stats_chunk(c) for c in everyone]
-    stats = [around(s, "chan", chan) for _, s in first]
-    x_in = [exchange(normalise_chunk(stats[c], first[c][0])) for c in everyone]
-    mixed = grad_input = None
-    weight_grads = bias_grads = param_grads = 0.0
-    spectra = [spectral_chunk(x_in[c], g_in[c]) for c in everyone]
-    for c in everyone:
-        y_out, dx_out, gw, gb = spectra[c]
-        weight_grads, bias_grads = weight_grads + gw, bias_grads + gb
-        dx_rows = exchange(dx_out)
-        y_rows = exchange(y_out)
-        sums, params = slope_sums_chunk(stats[c], dx_rows, first[c][0])
-        param_grads = param_grads + params
-        parts = around(sums.astype(half), "chan", chan)
-        grad_input = input_grad_chunk(c, stats[c], parts, dx_rows, first[c][0], grad_input)
-        mixed = mixed_chunk(c, y_rows, mixed)
+            [pack_spec(s) for s in (*stats, *parts)]
+            + [peer_spec(rows_in, which), pack_spec(tokens)] + [whole_spec(v) for v in tail],
+            stored, stored_spec(p, c * size), [rows_scratch, rows_scratch, lines], dft_flops,
+            before,
+        )
+
+    def channel_sums(value):
+        return around(value, "chan", chan)
+
+    g0 = exchange(cotangent_chunk(0, 1))
+    tokens0, sums = stats_chunk(0)
+    stats0 = channel_sums(sums)
+    x0 = exchange(normalise_chunk(stats0, tokens0, None))
+    both1 = cotangent_chunk(1, 2)
+    tokens1, sums = stats_chunk(1)
+    stats1 = channel_sums(sums)
+    both1 = exchange(normalise_chunk(stats1, tokens1, both1))
+    out0, gw0, gb0 = spectral_chunk(x0, 0, g0, True)
+    rows0 = exchange(out0)
+    y1, dx1, gw1, gb1 = spectral_chunk(both1, 1, both1, False)
+    dx1 = exchange(dx1)
+    y1 = exchange(y1)
+    sums, params0 = slope_sums_chunk(stats0, rows0, 1, tokens0)
+    parts = channel_sums(sums.astype(half))
+    grad_input = input_grad_chunk(0, stats0, parts, rows0, 1, tokens0, None)
+    mixed = mixed_chunk(0, rows0, 0, None)
+    sums, params1 = slope_sums_chunk(stats1, dx1, 0, tokens1)
+    parts = channel_sums(sums.astype(half))
+    grad_input = input_grad_chunk(1, stats1, parts, dx1, 0, tokens1, grad_input)
+    mixed = mixed_chunk(1, y1, 0, mixed)
+    weight_grads, bias_grads, param_grads = gw0 + gw1, gb0 + gb1, params0 + params1
 
     def by_channel(rows):
         return rows.reshape(-1, p.stack, p.groups * p.width).sum(1)
@@ -742,8 +768,10 @@
     weights = weight_grads.reshape(-1, LANES)
     flat_bias = bias_grads.reshape(2, 8, 2, p.stack, p.groups * p.width).sum((1, 3))
     flat_params = by_channel(param_grads.reshape(2, 8, p.lanes).sum(1))
-    grads = reduced(p, weights, half).reshape(weight_grads.shape)[..., : p.width]
-    flat_bias = reduced(p, flat_bias, single).reshape((2,) + b_first.shape)
+    flat = jnp.concatenate([weights, flat_bias.reshape(-1, LANES)])
+    flat = reduced(p, flat, half)
+    grads = flat[: weights.shape[0]].reshape(weight_grads.shape)[..., : p.width]
+    flat_bias = flat[weights.shape[0] :].reshape((2,) + b_first.shape)
     both = reduced(p, flat_params, single)
     return (mixed, grad_input, grads[0], flat_bias[0], grads[1], flat_bias[1], both[0], both[1])
 

time: 476 us -> 386 us (0.81)
  Pallas kernels: 260 us -> 191 us
  blocking collectives: 66.7 us -> 0 us
  local copies, waits for them, and re-layouts: 21.3 us -> 61.9 us
    pallas_call x14, Pallas kernels: 260 us -> 191 us  [_call(): pl.pallas_call(body, grid=grid, in_specs=in_specs, out_specs=out_specs, o...]
    all_to_all x2 -> x0, blocking collectives: 66.7 us -> none  [exchange(): return lax.all_to_all(value, 'space', 0, 0, tiled=True)]
    unnamed x64 -> x116, local copies, waits for them, and re-layouts: 8.87 us -> 41 us
    all_to_all x6, waiting for transfers between devices: 16.7 us -> 29.8 us  [exchange(): return lax.all_to_all(value, 'space', 0, 0, tiled=True)]
    ppermute x12, waiting for transfers between devices: 11.2 us -> 2.12 us  [around(): lax.ppermute(value, axis, [(i, (i + step) % size) for i in range(size)])]
    squeeze x4 -> x0, local copies, waits for them, and re-layouts: 5.69 us -> none  [block_weights(): top = jnp.concatenate([wide[0], wide[1]], axis=1)]
    ppermute x9 -> x6, waiting for transfers between devices: 34.7 us -> 33.2 us  [reduced(): other = lax.ppermute(own, 'space', [(i, i ^ step) for i in range(p.space)])]
  transfers between devices with their start and end apart: 27 -> 24, of which waited for: 10 -> 6; matrix products, arithmetic and copies ran while one was open for 5% -> 8% of each run, Pallas kernels for 48% -> 45%
where the time goes in v1:
time: 386 us; the launch traced here: 384 us
  Pallas kernels  191 us (49%)
  waiting for transfers between devices  65.1 us (17%)
  local copies, waits for them, and re-layouts  61.9 us (16%)
  starting transfers between devices  53.4 us (14%)
  other arithmetic  11.6 us (3%)
    pallas_call x14, Pallas kernels, _call(): pl.pallas_call(body, grid=grid, in_specs=in_specs, out_specs=out_specs, o...  191 us
    unnamed x116, local copies, waits for them, and re-layouts  41 us
    ppermute x6, waiting for transfers between devices, reduced(): other = lax.ppermute(own, 'space', [(i, i ^ step) for i in range(p.space)])  33.2 us
    all_to_all x6, waiting for transfers between devices, exchange(): return lax.all_to_all(value, 'space', 0, 0, tiled=True)  29.8 us
    all_to_all x6, starting transfers between devices, exchange(): return lax.all_to_all(value, 'space', 0, 0, tiled=True)  28 us
    ppermute x12, starting transfers between devices, around(): lax.ppermute(value, axis, [(i, (i + step) % size) for i in range(size)])  19.3 us
  transfers between devices with their start and end apart: 24, of which 6 were waited for; matrix products, arithmetic and copies ran while one was open for 8% of the time, Pallas kernels for 45%

profile of v1, /device:TPU:0, one launch (start us, length us, event | category | flops | bytes accessed | tf_op | source)
XLA Modules:
  0.0 384.0 jit_solution(8616485985347434001)
XLA Ops:
  0.7 2.9 copy-done.6
  5.2 6.2 %shard_map.230 = bf16[8,1,2,8,24,384]{5,4,3,2,1,0:T(8,128)(2,1)} custom-call(bf16[8,12,2,17280]{3,2,1,0:T(2,128)(2,1)S(1)} %copy-done.6, bf16[128,192]{1,0:T(8,128)(2,1)S(1)} %copy-done.16, f32[128,1]{1,0:T(8,128)S(1)} %copy-done.37), custom_call_target="tpu_custom_call" | custom-call | flops 452984832 | bytes 9044480 | tf_op jit(solution)/shard_map/pallas_call | solution.py:521
  11.4 5.3 %all-to-all-start.3 = ((bf16[8,1,2,8,24,384]{5,4,3,2,1,0:T(8,128)(2,1)}), bf16[8,1,2,8,24,384]{5,4,3,2,1,0:T(8,128)(2,1)}, u32[]{:S(2)}, u32[]{:S(2)}) async-start(bf16[8,1,2,8,24,384]{5,4,3,2,1,0:T(8,128)(2,1)} %shard_map.230), calls=%async_computation.3 | async-start | bytes 4718592 | tf_op jit(solution)/shard_map/all_to_all | solution.py:582
  16.8 2.9 copy-done.4
  19.7 8.0 %shard_map.228 = (bf16[2,12,192,384]{3,2,1,0:T(8,128)(2,1)S(1)}, f32[2,48,192]{2,1,0:T(8,128)}) custom-call(bf16[8,12,2,17280]{3,2,1,0:T(2,128)(2,1)S(1)} %copy-done.4, bf16[2,8,384]{2,1,0:T(8,128)(2,1)S(1)} %copy-done.43), custom_call_target="tpu_custom_call" | custom-call | flops 113246208 | bytes 10260480 | tf_op jit(solution)/shard_map/pallas_call | solution.py:521
  27.7 2.2 collective-permute-start.3
  29.9 2.6 collective-permute-start.4
  37.8 2.1 collective-permute-done.4.refs_2_
  42.2 9.8 %shard_map.229 = bf16[8,1,2,8,24,384]{5,4,3,2,1,0:T(8,128)(2,1)S(1)} custom-call(f32[2,48,192]{2,1,0:T(8,128)} %get-tuple-element.26.refs_0_, f32[2,48,192]{2,1,0:T(8,128)} %collective-permute-done.3.refs_1_, f32[2,48,192]{2,1,0:T(8,128)} %collective-permute-done.4.refs_2_, f32[2,48,192]{2,1,0:T(8,128)} %collective-permute-done.5.refs_3_, ...), custom_call_target="tpu_custom_call" | custom-call | flops 452984832 | bytes 6282752 | tf_op jit(solution)/shard_map/pallas_call | solution.py:521
  52.0 1.4 copy-done.8
  54.0 4.4 %all-to-all-start.2 = ((bf16[8,1,2,8,24,384]{5,4,3,2,1,0:T(8,128)(2,1)}), bf16[8,1,2,8,24,384]{5,4,3,2,1,0:T(8,128)(2,1)}, u32[]{:S(2)}, u32[]{:S(2)}) async-start(bf16[8,1,2,8,24,384]{5,4,3,2,1,0:T(8,128)(2,1)} %copy-done.8), calls=%async_computation.2 | async-start | bytes 4718592 | tf_op jit(solution)/shard_map/all_to_all | solution.py:582
  58.5 2.9 copy-done.5
  61.3 7.4 %shard_map.224 = (bf16[2,12,192,384]{3,2,1,0:T(8,128)(2,1)S(1)}, f32[2,48,192]{2,1,0:T(8,128)S(1)}) custom-call(bf16[8,12,2,17280]{3,2,1,0:T(2,128)(2,1)S(1)} %copy-done.5, bf16[2,8,384]{2,1,0:T(8,128)(2,1)S(1)} %copy-done.43), custom_call_target="tpu_custom_call" | custom-call | flops 113246208 | bytes 10260480 | tf_op jit(solution)/shard_map/pallas_call | solution.py:521
  68.8 2.6 collective-permute-start
  71.4 1.6 collective-permute-start.1
  73.9 2.9 copy-done.7
  76.7 5.4 %shard_map.225.refs_10_ = bf16[8,2,2,8,24,384]{5,4,3,2,1,0:T(8,128)(2,1)S(1)} custom-call(bf16[8,12,2,17280]{3,2,1,0:T(2,128)(2,1)S(1)} %copy-done.7, bf16[128,192]{1,0:T(8,128)(2,1)S(1)} %copy-done.18, f32[128,1]{1,0:T(8,128)S(1)} %copy-done.38), custom_call_target="tpu_custom_call" | custom-call | flops 452984832 | bytes 11403776 | tf_op jit(solution)/shard_map/pallas_call | solution.py:521
  82.3 8.9 %shard_map.226 = bf16[8,2,2,8,24,384]{5,4,3,2,1,0:T(8,128)(2,1)S(1)} custom-call(f32[2,48,192]{2,1,0:T(8,128)S(1)} %get-tuple-element.23.refs_0_, f32[2,48,192]{2,1,0:T(8,128)S(1)} %collective-permute-done.refs_1_, f32[2,48,192]{2,1,0:T(8,128)S(1)} %collective-permute-done.1.refs_2_, ...), custom_call_target="tpu_custom_call", output_to_operand_aliasing={{}: (10, {})} | custom-call | flops 452984832 | bytes 13360640 | tf_op jit(solution)/shard_map/pallas_call | solution.py:521
  91.2 2.2 copy-done
  95.4 4.6 %all-to-all-start = ((bf16[8,2,2,8,24,384]{5,4,3,2,1,0:T(8,128)(2,1)}), bf16[8,2,2,8,24,384]{5,4,3,2,1,0:T(8,128)(2,1)}, u32[]{:S(2)}, u32[]{:S(2)}) async-start(bf16[8,2,2,8,24,384]{5,4,3,2,1,0:T(8,128)(2,1)} %copy-done), calls=%async_computation | async-start | bytes 9437184 | tf_op jit(solution)/shard_map/all_to_all | solution.py:582
  107.8 1.5 concatenate.7
  114.0 38.8 %shard_map.231 = (bf16[8,2,2,12,16,384]{5,4,3,2,1,0:T(8,128)(2,1)S(1)}, f32[2,2,2,96,128]{4,3,2,1,0:T(8,128)S(1)}, f32[16,768]{1,0:T(8,128)S(1)}) custom-call(bf16[8,1,2,8,24,384]{5,4,3,2,1,0:T(8,128)(2,1)} %all-to-all-done.2.x_ref, bf16[8,1,2,8,24,384]{5,4,3,2,1,0:T(8,128)(2,1)} %all-to-all-done.3.g_ref, bf16[192,192]{1,0:T(8,128)(2,1)S(1)} %copy-done.52, ...), custom_call_target="tpu_custom_call" | custom-call | flops 10871635968 | bytes 10229760 | tf_op jit(solution)/shard_map/pallas_call | solution.py:521
  152.9 2.2 copy-done.9
  157.1 4.8 %all-to-all-start.4 = ((bf16[8,2,2,12,16,384]{5,4,3,2,1,0:T(8,128)(2,1)}), bf16[8,2,2,12,16,384]{5,4,3,2,1,0:T(8,128)(2,1)}, u32[]{:S(2)}, u32[]{:S(2)}) async-start(bf16[8,2,2,12,16,384]{5,4,3,2,1,0:T(8,128)(2,1)} %copy-done.9), calls=%async_computation.4 | async-start | bytes 9437184 | tf_op jit(solution)/shard_map/all_to_all | solution.py:582
  165.3 38.9 %shard_map.227 = (bf16[8,1,2,12,16,384]{5,4,3,2,1,0:T(8,128)(2,1)S(1)}, bf16[8,1,2,12,16,384]{5,4,3,2,1,0:T(8,128)(2,1)S(1)}, f32[2,2,2,96,128]{4,3,2,1,0:T(8,128)S(1)}, f32[16,768]{1,0:T(8,128)S(1)}) custom-call(bf16[8,2,2,8,24,384]{5,4,3,2,1,0:T(8,128)(2,1)} %all-to-all-done.x_ref.g_ref, bf16[8,2,2,8,24,384]{5,4,3,2,1,0:T(8,128)(2,1)} %all-to-all-done.x_ref.g_ref, ...), custom_call_target="tpu_custom_call" | custom-call | flops 10871635968 | bytes 14948352 | tf_op jit(solution)/shard_map/pallas_call | solution.py:521
  205.6 1.5 copy-done.11
  208.5 8.0 %all-to-all-done.4.rows_ref.refs_4_.refs_8_ = bf16[8,2,2,12,16,384]{5,4,3,2,1,0:T(8,128)(2,1)} async-done(((bf16[8,2,2,12,16,384]{5,4,3,2,1,0:T(8,128)(2,1)}), bf16[8,2,2,12,16,384]{5,4,3,2,1,0:T(8,128)(2,1)}, u32[]{:S(2)}, u32[]{:S(2)}) %all-to-all-start.4) | async-done | bytes 4718624 | tf_op jit(solution)/shard_map/all_to_all | solution.py:582
  216.5 4.4 %all-to-all-start.5 = ((bf16[8,1,2,12,16,384]{5,4,3,2,1,0:T(8,128)(2,1)}), bf16[8,1,2,12,16,384]{5,4,3,2,1,0:T(8,128)(2,1)}, u32[]{:S(2)}, u32[]{:S(2)}) async-start(bf16[8,1,2,12,16,384]{5,4,3,2,1,0:T(8,128)(2,1)} %copy-done.11), calls=%async_computation.5 | async-start | bytes 4718592 | tf_op jit(solution)/shard_map/all_to_all | solution.py:582
  220.9 1.5 add.30
  222.3 1.5 reshape.48
  223.8 1.5 reduce_sum.27
  226.6 1.8 add_convert_fusion.2
  228.5 21.8 %all-to-all-done.5.refs_4_.refs_8_ = bf16[8,1,2,12,16,384]{5,4,3,2,1,0:T(8,128)(2,1)} async-done(((bf16[8,1,2,12,16,384]{5,4,3,2,1,0:T(8,128)(2,1)}), bf16[8,1,2,12,16,384]{5,4,3,2,1,0:T(8,128)(2,1)}, u32[]{:S(2)}, u32[]{:S(2)}) %all-to-all-start.5) | async-done | bytes 2359328 | tf_op jit(solution)/shard_map/all_to_all | solution.py:582
  250.3 4.4 %all-to-all-start.1 = ((bf16[8,1,2,12,16,384]{5,4,3,2,1,0:T(8,128)(2,1)}), bf16[8,1,2,12,16,384]{5,4,3,2,1,0:T(8,128)(2,1)}, u32[]{:S(2)}, u32[]{:S(2)}) async-start(bf16[8,1,2,12,16,384]{5,4,3,2,1,0:T(8,128)(2,1)} %copy-done.10), calls=%async_computation.1 | async-start | bytes 4718592 | tf_op jit(solution)/shard_map/all_to_all | solution.py:582
  258.2 2.0 collective-permute-start.13
  260.2 27.2 %collective-permute-done.13 = bf16[774,128]{1,0:T(8,128)(2,1)S(1)} collective-permute-done((bf16[774,128]{1,0:T(8,128)(2,1)S(1)}, bf16[774,128]{1,0:T(8,128)(2,1)S(1)}, u32[]{:S(2)}, u32[]{:S(2)}) %collective-permute-start.13) | collective-permute-done | bytes 198176 | tf_op jit(solution)/shard_map/ppermute | solution.py:598
  287.5 1.6 collective-permute-start.14
  289.0 4.9 %collective-permute-done.14 = bf16[774,128]{1,0:T(8,128)(2,1)S(1)} collective-permute-done((bf16[774,128]{1,0:T(8,128)(2,1)S(1)}, bf16[774,128]{1,0:T(8,128)(2,1)S(1)}, u32[]{:S(2)}, u32[]{:S(2)}) %collective-permute-start.14) | collective-permute-done | bytes 198176 | tf_op jit(solution)/shard_map/ppermute | solution.py:598
  297.5 11.4 %shard_map.235 = (f32[2,48,192]{2,1,0:T(8,128)S(1)}, f32[16,384]{1,0:T(8,128)S(1)}) custom-call(f32[2,48,192]{2,1,0:T(8,128)} %get-tuple-element.26.refs_0_, f32[2,48,192]{2,1,0:T(8,128)} %collective-permute-done.3.refs_1_, f32[2,48,192]{2,1,0:T(8,128)} %collective-permute-done.4.refs_2_, f32[2,48,192]{2,1,0:T(8,128)} %collective-permute-done.5.refs_3_, ...), custom_call_target="tpu_custom_call" | custom-call | flops 452984832 | bytes 8750592 | tf_op jit(solution)/shard_map/pallas_call | solution.py:521
  309.0 11.2 %shard_map.234 = (f32[2,48,192]{2,1,0:T(8,128)S(1)}, f32[16,384]{1,0:T(8,128)S(1)}) custom-call(f32[2,48,192]{2,1,0:T(8,128)S(1)} %copy-done.20, f32[2,48,192]{2,1,0:T(8,128)S(1)} %copy-done.23, f32[2,48,192]{2,1,0:T(8,128)S(1)} %copy-done.26, f32[2,48,192]{2,1,0:T(8,128)S(1)} %copy-done.29, bf16[8,1,2,12,16,384]{5,4,3,2,1,0:T(8,128)(2,1)} %all-to-all-done.5.refs_4_.refs_8_, ...), custom_call_target="tpu_custom_call" | custom-call | flops 452984832 | bytes 6391296 | tf_op jit(solution)/shard_map/pallas_call | solution.py:521
  323.2 1.5 convert_element_type.34.refs_4_
  325.5 2.8 collective-permute-start.11
  328.3 1.5 convert_element_type.33.refs_4_
  333.0 8.9 %shard_map.232.refs_2_ = bf16[8,12,2,17280]{3,2,1,0:T(2,128)(2,1)} custom-call(bf16[8,2,2,12,16,384]{5,4,3,2,1,0:T(8,128)(2,1)} %all-to-all-done.4.rows_ref.refs_4_.refs_8_, bf16[192,128]{1,0:T(8,128)(2,1)S(1)} %copy-done.39), custom_call_target="tpu_custom_call" | custom-call | flops 452984832 | bytes 11403264 | tf_op jit(solution)/shard_map/pallas_call | solution.py:521
  344.1 8.9 %shard_map.233 = bf16[8,12,2,17280]{3,2,1,0:T(2,128)(2,1)} custom-call(bf16[8,1,2,12,16,384]{5,4,3,2,1,0:T(8,128)(2,1)} %all-to-all-done.1.refs_0_, bf16[192,128]{1,0:T(8,128)(2,1)S(1)} %copy-done.40, bf16[8,12,2,17280]{3,2,1,0:T(2,128)(2,1)} %shard_map.232.refs_2_), custom_call_target="tpu_custom_call", output_to_operand_aliasing={{}: (2, {})} | custom-call | flops 452984832 | bytes 15679488 | tf_op jit(solution)/shard_map/pallas_call | solution.py:521
  353.0 3.5 collective-permute-start.7
  357.2 13.5 %shard_map.236.refs_13_ = bf16[8,12,2,17280]{3,2,1,0:T(2,128)(2,1)} custom-call(f32[2,48,192]{2,1,0:T(8,128)} %get-tuple-element.26.refs_0_, f32[2,48,192]{2,1,0:T(8,128)} %collective-permute-done.3.refs_1_, f32[2,48,192]{2,1,0:T(8,128)} %collective-permute-done.4.refs_2_, f32[2,48,192]{2,1,0:T(8,128)} %collective-permute-done.5.refs_3_, ...), custom_call_target="tpu_custom_call" | custom-call | flops 452984832 | bytes 15422976 | tf_op jit(solution)/shard_map/pallas_call | solution.py:521
  370.8 13.2 %shard_map.237 = bf16[8,12,2,17280]{3,2,1,0:T(2,128)(2,1)} custom-call(f32[2,48,192]{2,1,0:T(8,128)S(1)} %copy-done.21, f32[2,48,192]{2,1,0:T(8,128)S(1)} %copy-done.24, f32[2,48,192]{2,1,0:T(8,128)S(1)} %copy-done.27, f32[2,48,192]{2,1,0:T(8,128)S(1)} %copy-done.30, ...), custom_call_target="tpu_custom_call", output_to_operand_aliasing={{}: (13, {})} | custom-call | flops 452984832 | bytes 19699200 | tf_op jit(solution)/shard_map/pallas_call | solution.py:521
  (167 shorter events, 51.7 us)
Async XLA Ops:
  0.6 16.1 %copy-start.43 = (bf16[2,8,384]{2,1,0:T(8,128)(2,1)S(1)}, bf16[2,8,384]{2,1,0:T(8,128)(2,1)}, u32[]{:S(2)}) copy-start(bf16[2,8,384]{2,1,0:T(8,128)(2,1)} %constant.30.clone.sum_ref.refs_9_) | copy-start | bytes 36868
  0.6 2.9 copy-start.6
  11.4 22.4 %copy-start.57 = (f32[192]{0:T(256)S(1)}, f32[192]{0:T(256)}, u32[]{:S(2)}) copy-start(f32[192]{0:T(256)} %param.18) | copy-start | bytes 2308
  11.4 42.6 %all-to-all-start.3 = ((bf16[8,1,2,8,24,384]{5,4,3,2,1,0:T(8,128)(2,1)}), bf16[8,1,2,8,24,384]{5,4,3,2,1,0:T(8,128)(2,1)}, u32[]{:S(2)}, u32[]{:S(2)}) async-start(bf16[8,1,2,8,24,384]{5,4,3,2,1,0:T(8,128)(2,1)} %shard_map.230), calls=%async_computation.3 | async-start | bytes 4718592 | tf_op jit(solution)/shard_map/all_to_all | solution.py:582
  16.8 2.9 copy-start.4
  27.7 10.1 %collective-permute-start.3 = (f32[2,48,192]{2,1,0:T(8,128)}, f32[2,48,192]{2,1,0:T(8,128)}, u32[]{:S(2)}, u32[]{:S(2)}) collective-permute-start(f32[2,48,192]{2,1,0:T(8,128)} %get-tuple-element.26.refs_0_), channel_id=1, source_target_pairs={{0,1},{1,2},{2,3},{3,0},{4,5},{5,6},{6,7},{7,4},{8,9},{9,10},{10,1... | collective-permute-start | bytes 221192 | tf_op jit(solution)/shard_map/ppermute | solution.py:589
  29.9 10.0 %collective-permute-start.4 = (f32[2,48,192]{2,1,0:T(8,128)}, f32[2,48,192]{2,1,0:T(8,128)}, u32[]{:S(2)}, u32[]{:S(2)}) collective-permute-start(f32[2,48,192]{2,1,0:T(8,128)} %get-tuple-element.26.refs_0_), channel_id=1, source_target_pairs={{0,2},{1,3},{2,0},{3,1},{4,6},{5,7},{6,4},{7,5},{8,10},{9,11},{10,... | collective-permute-start | bytes 221192 | tf_op jit(solution)/shard_map/ppermute | solution.py:589
  32.5 7.4 %collective-permute-start.5 = (f32[2,48,192]{2,1,0:T(8,128)}, f32[2,48,192]{2,1,0:T(8,128)}, u32[]{:S(2)}, u32[]{:S(2)}) collective-permute-start(f32[2,48,192]{2,1,0:T(8,128)} %get-tuple-element.26.refs_0_), channel_id=1, source_target_pairs={{0,3},{1,0},{2,1},{3,2},{4,7},{5,4},{6,5},{7,6},{8,11},{9,8},{10,9... | collective-permute-start | bytes 221192 | tf_op jit(solution)/shard_map/ppermute | solution.py:589
  54.0 41.3 %all-to-all-start.2 = ((bf16[8,1,2,8,24,384]{5,4,3,2,1,0:T(8,128)(2,1)}), bf16[8,1,2,8,24,384]{5,4,3,2,1,0:T(8,128)(2,1)}, u32[]{:S(2)}, u32[]{:S(2)}) async-start(bf16[8,1,2,8,24,384]{5,4,3,2,1,0:T(8,128)(2,1)} %copy-done.8), calls=%async_computation.2 | async-start | bytes 4718592 | tf_op jit(solution)/shard_map/all_to_all | solution.py:582
  61.3 12.5 %copy-start.18 = (bf16[128,192]{1,0:T(8,128)(2,1)S(1)}, bf16[128,192]{1,0:T(8,128)(2,1)}, u32[]{:S(2)}) copy-start(bf16[128,192]{1,0:T(8,128)(2,1)} %constant.23.clone.table_ref.refs_7_) | copy-start | bytes 147460
  61.3 12.5 %copy-start.38 = (f32[128,1]{1,0:T(8,128)S(1)}, f32[128,1]{1,0:T(8,128)}, u32[]{:S(2)}) copy-start(f32[128,1]{1,0:T(8,128)} %constant.25.clone.scale_ref) | copy-start | bytes 1540
  61.3 20.9 %copy-start.13 = (bf16[24,768]{1,0:T(8,128)(2,1)S(1)}, bf16[24,768]{1,0:T(8,128)(2,1)}, u32[]{:S(2)}) copy-start(bf16[24,768]{1,0:T(8,128)(2,1)} %constant.31.clone.refs_9_.refs_8_.refs_12_) | copy-start | bytes 110596
  61.3 20.9 %copy-start.34 = (f32[128,1]{1,0:T(8,128)S(1)}, f32[128,1]{1,0:T(8,128)}, u32[]{:S(2)}) copy-start(f32[128,1]{1,0:T(8,128)} %copy-done.33) | copy-start | bytes 1540
  68.8 13.5 %copy-start.1 = (bf16[2,12,192,384]{3,2,1,0:T(8,128)(2,1)}, bf16[2,12,192,384]{3,2,1,0:T(8,128)(2,1)S(1)}, u32[]{:S(2)}) copy-start(bf16[2,12,192,384]{3,2,1,0:T(8,128)(2,1)S(1)} %get-tuple-element.24.refs_4_.refs_5_.refs_9_) | copy-start | bytes 10616836
  68.8 13.5 %copy-start.19 = (f32[2,48,192]{2,1,0:T(8,128)}, f32[2,48,192]{2,1,0:T(8,128)S(1)}, u32[]{:S(2)}) copy-start(f32[2,48,192]{2,1,0:T(8,128)S(1)} %get-tuple-element.23.refs_0_) | copy-start | bytes 221188
  68.8 13.5 %copy-start.49 = (f32[1,384]{1,0:T(1,128)S(1)}, f32[1,384]{1,0:T(1,128)}, u32[]{:S(2)}) copy-start(f32[1,384]{1,0:T(1,128)} %broadcast_in_dim_tile.7.refs_6_) | copy-start | bytes 4612
  68.8 13.4 %collective-permute-start = (f32[2,48,192]{2,1,0:T(8,128)S(1)}, f32[2,48,192]{2,1,0:T(8,128)S(1)}, u32[]{:S(2)}, u32[]{:S(2)}) collective-permute-start(f32[2,48,192]{2,1,0:T(8,128)S(1)} %get-tuple-element.23.refs_0_), channel_id=1, source_target_pairs={{0,1},{1,2},{2,3},{3,0},{4,5},{5,6},{6,7},{7,4},{8,9},{9,10},{10,1... | collective-permute-start | bytes 221192 | tf_op jit(solution)/shard_map/ppermute | solution.py:589
  71.4 10.8 %collective-permute-start.1 = (f32[2,48,192]{2,1,0:T(8,128)S(1)}, f32[2,48,192]{2,1,0:T(8,128)S(1)}, u32[]{:S(2)}, u32[]{:S(2)}) collective-permute-start(f32[2,48,192]{2,1,0:T(8,128)S(1)} %get-tuple-element.23.refs_0_), channel_id=1, source_target_pairs={{0,2},{1,3},{2,0},{3,1},{4,6},{5,7},{6,4},{7,5},{8,10},{9,11},{10,... | collective-permute-start | bytes 221192 | tf_op jit(solution)/shard_map/ppermute | solution.py:589
  73.1 9.2 %collective-permute-start.2 = (f32[2,48,192]{2,1,0:T(8,128)S(1)}, f32[2,48,192]{2,1,0:T(8,128)S(1)}, u32[]{:S(2)}, u32[]{:S(2)}) collective-permute-start(f32[2,48,192]{2,1,0:T(8,128)S(1)} %get-tuple-element.23.refs_0_), channel_id=1, source_target_pairs={{0,3},{1,0},{2,1},{3,2},{4,7},{5,4},{6,5},{7,6},{8,11},{9,8},{10,9... | collective-permute-start | bytes 221192 | tf_op jit(solution)/shard_map/ppermute | solution.py:589
  95.4 61.7 %all-to-all-start = ((bf16[8,2,2,8,24,384]{5,4,3,2,1,0:T(8,128)(2,1)}), bf16[8,2,2,8,24,384]{5,4,3,2,1,0:T(8,128)(2,1)}, u32[]{:S(2)}, u32[]{:S(2)}) async-start(bf16[8,2,2,8,24,384]{5,4,3,2,1,0:T(8,128)(2,1)} %copy-done), calls=%async_computation | async-start | bytes 9437184 | tf_op jit(solution)/shard_map/all_to_all | solution.py:582
  157.1 59.4 %all-to-all-start.4 = ((bf16[8,2,2,12,16,384]{5,4,3,2,1,0:T(8,128)(2,1)}), bf16[8,2,2,12,16,384]{5,4,3,2,1,0:T(8,128)(2,1)}, u32[]{:S(2)}, u32[]{:S(2)}) async-start(bf16[8,2,2,12,16,384]{5,4,3,2,1,0:T(8,128)(2,1)} %copy-done.9), calls=%async_computation.4 | async-start | bytes 9437184 | tf_op jit(solution)/shard_map/all_to_all | solution.py:582
  216.5 33.8 %all-to-all-start.5 = ((bf16[8,1,2,12,16,384]{5,4,3,2,1,0:T(8,128)(2,1)}), bf16[8,1,2,12,16,384]{5,4,3,2,1,0:T(8,128)(2,1)}, u32[]{:S(2)}, u32[]{:S(2)}) async-start(bf16[8,1,2,12,16,384]{5,4,3,2,1,0:T(8,128)(2,1)} %copy-done.11), calls=%async_computation.5 | async-start | bytes 4718592 | tf_op jit(solution)/shard_map/all_to_all | solution.py:582
  250.3 93.0 %all-to-all-start.1 = ((bf16[8,1,2,12,16,384]{5,4,3,2,1,0:T(8,128)(2,1)}), bf16[8,1,2,12,16,384]{5,4,3,2,1,0:T(8,128)(2,1)}, u32[]{:S(2)}, u32[]{:S(2)}) async-start(bf16[8,1,2,12,16,384]{5,4,3,2,1,0:T(8,128)(2,1)} %copy-done.10), calls=%async_computation.1 | async-start | bytes 4718592 | tf_op jit(solution)/shard_map/all_to_all | solution.py:582
  255.7 1.5 collective-permute-start.12
  258.2 29.2 %collective-permute-start.13 = (bf16[774,128]{1,0:T(8,128)(2,1)S(1)}, bf16[774,128]{1,0:T(8,128)(2,1)S(1)}, u32[]{:S(2)}, u32[]{:S(2)}) collective-permute-start(bf16[774,128]{1,0:T(8,128)(2,1)S(1)} %add_convert_fusion.1), channel_id=1, source_target_pairs={{0,8},{4,12},{8,0},{12,4},{16,24},{20,28},{24,16},{28,20},{1,9},{5... | collective-permute-start | bytes 594440 | tf_op jit(solution)/shard_map/ppermute | solution.py:598
  287.5 6.5 %collective-permute-start.14 = (bf16[774,128]{1,0:T(8,128)(2,1)S(1)}, bf16[774,128]{1,0:T(8,128)(2,1)S(1)}, u32[]{:S(2)}, u32[]{:S(2)}) collective-permute-start(bf16[774,128]{1,0:T(8,128)(2,1)S(1)} %add_convert_fusion), channel_id=1, source_target_pairs={{0,16},{4,20},{8,24},{12,28},{16,0},{20,4},{24,8},{28,12},{1,17},{... | collective-permute-start | bytes 594440 | tf_op jit(solution)/shard_map/ppermute | solution.py:598
  294.7 14.2 %copy-start.2 = (bf16[2,12,192,384]{3,2,1,0:T(8,128)(2,1)S(1)}, bf16[2,12,192,384]{3,2,1,0:T(8,128)(2,1)}, u32[]{:S(2)}) copy-start(bf16[2,12,192,384]{3,2,1,0:T(8,128)(2,1)} %copy-done.1) | copy-start | bytes 10616836
  297.5 11.4 %copy-start.20 = (f32[2,48,192]{2,1,0:T(8,128)S(1)}, f32[2,48,192]{2,1,0:T(8,128)}, u32[]{:S(2)}) copy-start(f32[2,48,192]{2,1,0:T(8,128)} %copy-done.19) | copy-start | bytes 221188
  297.5 11.5 %copy-start.23 = (f32[2,48,192]{2,1,0:T(8,128)S(1)}, f32[2,48,192]{2,1,0:T(8,128)}, u32[]{:S(2)}) copy-start(f32[2,48,192]{2,1,0:T(8,128)} %copy-done.22) | copy-start | bytes 221188
  297.5 11.5 %copy-start.26 = (f32[2,48,192]{2,1,0:T(8,128)S(1)}, f32[2,48,192]{2,1,0:T(8,128)}, u32[]{:S(2)}) copy-start(f32[2,48,192]{2,1,0:T(8,128)} %copy-done.25) | copy-start | bytes 221188
  297.5 11.5 %copy-start.29 = (f32[2,48,192]{2,1,0:T(8,128)S(1)}, f32[2,48,192]{2,1,0:T(8,128)}, u32[]{:S(2)}) copy-start(f32[2,48,192]{2,1,0:T(8,128)} %copy-done.28) | copy-start | bytes 221188
  309.0 11.3 %copy-start.45 = (f32[2,48,192]{2,1,0:T(8,128)}, f32[2,48,192]{2,1,0:T(8,128)S(1)}, u32[]{:S(2)}) copy-start(f32[2,48,192]{2,1,0:T(8,128)S(1)} %get-tuple-element.31) | copy-start | bytes 221188
  321.0 9.7 %collective-permute-start.15 = (f32[2,192]{1,0:T(2,128)S(1)}, f32[2,192]{1,0:T(2,128)}, u32[]{:S(2)}, u32[]{:S(2)}) collective-permute-start(f32[2,192]{1,0:T(2,128)S(1)} %reduce_sum.29), channel_id=1, source_target_pairs={{0,4},{4,0},{8,12},{12,8},{16,20},{20,16},{24,28},{28,24},{1,5},{5... | collective-permute-start | bytes 4616 | tf_op jit(solution)/shard_map/ppermute | solution.py:598
  324.7 32.4 %collective-permute-start.10 = (bf16[2,48,192]{2,1,0:T(8,128)(2,1)}, bf16[2,48,192]{2,1,0:T(8,128)(2,1)}, u32[]{:S(2)}, u32[]{:S(2)}) collective-permute-start(bf16[2,48,192]{2,1,0:T(8,128)(2,1)} %convert_element_type.34.refs_4_), channel_id=1, source_target_pairs={{0,2},{1,3},{2,0},{3,1},{4,6},{5,7},{6,4},{7,5},{8,10},{9,11},{10,... | collective-permute-start | bytes 110600 | tf_op jit(solution)/shard_map/ppermute | solution.py:589
  325.5 31.6 %collective-permute-start.11 = (bf16[2,48,192]{2,1,0:T(8,128)(2,1)}, bf16[2,48,192]{2,1,0:T(8,128)(2,1)}, u32[]{:S(2)}, u32[]{:S(2)}) collective-permute-start(bf16[2,48,192]{2,1,0:T(8,128)(2,1)} %convert_element_type.34.refs_4_), channel_id=1, source_target_pairs={{0,3},{1,0},{2,1},{3,2},{4,7},{5,4},{6,5},{7,6},{8,11},{9,8},{10,9... | collective-permute-start | bytes 110600 | tf_op jit(solution)/shard_map/ppermute | solution.py:589
  328.3 28.9 %collective-permute-start.9 = (bf16[2,48,192]{2,1,0:T(8,128)(2,1)}, bf16[2,48,192]{2,1,0:T(8,128)(2,1)}, u32[]{:S(2)}, u32[]{:S(2)}) collective-permute-start(bf16[2,48,192]{2,1,0:T(8,128)(2,1)} %convert_element_type.34.refs_4_), channel_id=1, source_target_pairs={{0,1},{1,2},{2,3},{3,0},{4,5},{5,6},{6,7},{7,4},{8,9},{9,10},{10,1... | collective-permute-start | bytes 110600 | tf_op jit(solution)/shard_map/ppermute | solution.py:589
  329.8 40.9 %collective-permute-start.6 = (bf16[2,48,192]{2,1,0:T(8,128)(2,1)}, bf16[2,48,192]{2,1,0:T(8,128)(2,1)}, u32[]{:S(2)}, u32[]{:S(2)}) collective-permute-start(bf16[2,48,192]{2,1,0:T(8,128)(2,1)} %convert_element_type.33.refs_4_), channel_id=1, source_target_pairs={{0,1},{1,2},{2,3},{3,0},{4,5},{5,6},{6,7},{7,4},{8,9},{9,10},{10,1... | collective-permute-start | bytes 110600 | tf_op jit(solution)/shard_map/ppermute | solution.py:589
  331.4 10.5 %collective-permute-start.16 = (f32[2,192]{1,0:T(2,128)S(1)}, f32[2,192]{1,0:T(2,128)S(1)}, u32[]{:S(2)}, u32[]{:S(2)}) collective-permute-start(f32[2,192]{1,0:T(2,128)S(1)} %add.35), channel_id=1, source_target_pairs={{0,8},{4,12},{8,0},{12,4},{16,24},{20,28},{24,16},{28,20},{1,9},{5... | collective-permute-start | bytes 4616 | tf_op jit(solution)/shard_map/ppermute | solution.py:598
  341.9 11.1 %collective-permute-start.17 = (f32[2,192]{1,0:T(2,128)S(1)}, f32[2,192]{1,0:T(2,128)S(1)}, u32[]{:S(2)}, u32[]{:S(2)}) collective-permute-start(f32[2,192]{1,0:T(2,128)S(1)} %add.36), channel_id=1, source_target_pairs={{0,16},{4,20},{8,24},{12,28},{16,0},{20,4},{24,8},{28,12},{1,17},{... | collective-permute-start | bytes 4616 | tf_op jit(solution)/shard_map/ppermute | solution.py:598
  344.1 13.1 %copy-start.15 = (bf16[24,768]{1,0:T(8,128)(2,1)S(1)}, bf16[24,768]{1,0:T(8,128)(2,1)}, u32[]{:S(2)}) copy-start(bf16[24,768]{1,0:T(8,128)(2,1)} %constant.31.clone.refs_9_.refs_8_.refs_12_) | copy-start | bytes 110596
  344.1 13.1 %copy-start.32 = (bf16[192,128]{1,0:T(8,128)(2,1)S(1)}, bf16[192,128]{1,0:T(8,128)(2,1)}, u32[]{:S(2)}) copy-start(bf16[192,128]{1,0:T(8,128)(2,1)} %constant.27.clone.refs_7_.refs_11_) | copy-start | bytes 147460
  353.0 17.7 %collective-permute-start.7 = (bf16[2,48,192]{2,1,0:T(8,128)(2,1)}, bf16[2,48,192]{2,1,0:T(8,128)(2,1)S(1)}, u32[]{:S(2)}, u32[]{:S(2)}) collective-permute-start(bf16[2,48,192]{2,1,0:T(8,128)(2,1)} %convert_element_type.33.refs_4_), channel_id=1, source_target_pairs={{0,2},{1,3},{2,0},{3,1},{4,6},{5,7},{6,4},{7,5},{8,10},{9,11},{10,... | collective-permute-start | bytes 110600 | tf_op jit(solution)/shard_map/ppermute | solution.py:589
  357.1 13.7 %copy-start.3 = (bf16[2,12,192,384]{3,2,1,0:T(8,128)(2,1)S(1)}, bf16[2,12,192,384]{3,2,1,0:T(8,128)(2,1)}, u32[]{:S(2)}) copy-start(bf16[2,12,192,384]{3,2,1,0:T(8,128)(2,1)} %copy-done.1) | copy-start | bytes 10616836
  357.1 13.7 %copy-start.21 = (f32[2,48,192]{2,1,0:T(8,128)S(1)}, f32[2,48,192]{2,1,0:T(8,128)}, u32[]{:S(2)}) copy-start(f32[2,48,192]{2,1,0:T(8,128)} %copy-done.19) | copy-start | bytes 221188
  357.1 13.7 %copy-start.24 = (f32[2,48,192]{2,1,0:T(8,128)S(1)}, f32[2,48,192]{2,1,0:T(8,128)}, u32[]{:S(2)}) copy-start(f32[2,48,192]{2,1,0:T(8,128)} %copy-done.22) | copy-start | bytes 221188
  357.1 13.7 %copy-start.27 = (f32[2,48,192]{2,1,0:T(8,128)S(1)}, f32[2,48,192]{2,1,0:T(8,128)}, u32[]{:S(2)}) copy-start(f32[2,48,192]{2,1,0:T(8,128)} %copy-done.25) | copy-start | bytes 221188
  357.1 13.7 %copy-start.30 = (f32[2,48,192]{2,1,0:T(8,128)S(1)}, f32[2,48,192]{2,1,0:T(8,128)}, u32[]{:S(2)}) copy-start(f32[2,48,192]{2,1,0:T(8,128)} %copy-done.28) | copy-start | bytes 221188
  357.1 13.6 %collective-permute-start.8 = (bf16[2,48,192]{2,1,0:T(8,128)(2,1)}, bf16[2,48,192]{2,1,0:T(8,128)(2,1)S(1)}, u32[]{:S(2)}, u32[]{:S(2)}) collective-permute-start(bf16[2,48,192]{2,1,0:T(8,128)(2,1)} %convert_element_type.33.refs_4_), channel_id=1, source_target_pairs={{0,3},{1,0},{2,1},{3,2},{4,7},{5,4},{6,5},{7,6},{8,11},{9,8},{10,9... | collective-permute-start | bytes 110600 | tf_op jit(solution)/shard_map/ppermute | solution.py:589
  (34 other events, 35.3 us)

commit v2 on v1

--- a/solution.py
+++ b/solution.py
@@ -21,7 +21,7 @@
 
 half = jnp.bfloat16
 single = jnp.float32
-VMEM_LIMIT = 36 * 1024 * 1024
+VMEM_LIMIT = 67043328
 SLOTS = 2
 
 TN = (((0,), (0,)), ((), ()))
@@ -232,15 +232,15 @@
 
 def normalise_kernel(p, *refs):
     stat_refs = refs[: p.chan]
-    tokens_ref, gain_ref, shift_ref, table_ref, scale_ref, wide_ref = refs[p.chan : p.chan + 6]
-    out_ref, rows_ref, turn_ref = refs[p.chan + 6 :]
+    tokens_ref, affine_ref, table_ref, scale_ref, wide_ref = refs[p.chan : p.chan + 5]
+    out_ref, rows_ref, turn_ref = refs[p.chan + 5 :]
     moments(p, stat_refs, rows_ref)
 
     def row(h, slot):
         each = expand(rows_ref[h], wide_ref[...])
         wide = tokens_ref[0, h].astype(single)
         centred = (wide - each[:, : p.lanes]) * each[:, p.lanes :]
-        normed = (centred * gain_ref[...] + shift_ref[...]).astype(half)
+        normed = (centred * affine_ref[0:1, :] + affine_ref[1:2, :]).astype(half)
         analyse(p, normed, table_ref[...], scale_ref[...], turn_ref, h)
 
     each_row(p, row)
@@ -261,24 +261,54 @@
 BAND = 16
 
 
-def place_weights(p, w_ref, out_refs):
-    lane = lax.broadcasted_iota(jnp.int32, (p.width, LANES), 1)
-    for which, out_ref in enumerate(out_refs):
+def widened(p, value):
+    blank = jnp.zeros((value.shape[0], LANES - p.width), single)
+    return jnp.concatenate([value.astype(single), blank], axis=1)
+
+
+def placed_slot(p, value, q):
+    lane = lax.broadcasted_iota(jnp.int32, value.shape, 1)
+    at, shift = divmod(q * p.width, LANES)
+    turned = rolled(value, shift)
+    tiles = [jnp.zeros_like(value) for _ in range(p.tiles)]
+    tiles[at] = jnp.where(lane >= shift, turned, 0.0)
+    if shift + p.width > LANES:
+        tiles[at + 1] = jnp.where(lane < shift + p.width - LANES, turned, 0.0)
+    return jnp.concatenate(tiles, axis=1)
+
+
+def taken_slot(p, read, q):
+    at, shift = divmod(q * p.width, LANES)
+    value = rolled(read(at), -shift % LANES)
+    if shift + p.width > LANES:
+        lane = lax.broadcasted_iota(jnp.int32, value.shape, 1)
+        value = jnp.where(lane < LANES - shift, value, rolled(read(at + 1), -shift % LANES))
+    return value
+
+
+PARTS = (((0, 0, 1), (1, 1, 1)), ((0, 1, 1), (1, 0, -1)))
+
+
+def place_weights(p, w_refs, out_refs):
+    for w_ref, out_ref in zip(w_refs, out_refs):
         for q in range(PACK):
-            at, shift = divmod(q * p.width, LANES)
             for part in range(2):
-                value = w_ref[which, part, q % p.groups].astype(single)
-                turned = rolled(value, shift)
-                tiles = [jnp.zeros_like(value) for _ in range(p.tiles)]
-                tiles[at] = jnp.where(lane >= shift, turned, 0.0)
-                if shift + p.width > LANES:
-                    tiles[at + 1] = jnp.where(lane < shift + p.width - LANES, turned, 0.0)
-                wide = jnp.concatenate(tiles, axis=1)
-                for row_ri, col_ri, sign in (((0, 0, 1), (1, 1, 1)), ((0, 1, 1), (1, 0, -1)))[part]:
+                wide = placed_slot(p, widened(p, w_ref[part, q % p.groups]), q)
+                for row_ri, col_ri, sign in PARTS[part]:
                     top = row_ri * p.lanes + q * p.width
                     out_ref[top : top + p.width, col_ri * p.lanes : (col_ri + 1) * p.lanes] = (
                         sign * wide
                     ).astype(half)
+
+
+def place_biases(p, b_refs, out_ref):
+    for which, b_ref in enumerate(b_refs):
+        for ri in range(2):
+            row = jnp.zeros((1, p.lanes), single)
+            for q in range(PACK):
+                n = q % p.groups
+                row = row + placed_slot(p, widened(p, b_ref[ri, n : n + 1, :]), q)
+            out_ref[which : which + 1, ri * p.lanes : (ri + 1) * p.lanes] = row
 
 
 def spectral_kernel(
@@ -289,14 +319,20 @@
     g_ref,
     there_ref,
     back_ref,
-    w_ref,
-    bias_ref,
+    w_first_ref,
+    w_second_ref,
+    b_first_ref,
+    b_second_ref,
     *refs,
 ):
+    before_ref = None
+    if not joined:
+        before_ref, refs = refs[0], refs[1:]
     out_refs = refs[: 1 if joined else 2]
     (
-    gw_ref,
+    total_ref,
     gb_ref,
+    bias_ref,
     lat_ref,
     hid_ref,
     gpost_ref,
@@ -319,7 +355,8 @@
 
     @pl.when((pack == 0) & (group == 0))
     def _():
-        place_weights(p, w_ref, (w1_ref, w2_ref))
+        place_weights(p, (w_first_ref, w_second_ref), (w1_ref, w2_ref))
+        place_biases(p, (b_first_ref, b_second_ref), bias_ref)
         gb_ref[...] = jnp.zeros_like(gb_ref)
         acc1_ref[...] = jnp.zeros_like(acc1_ref)
         acc2_ref[...] = jnp.zeros_like(acc2_ref)
@@ -392,30 +429,45 @@
 
     @pl.when((group == pl.num_programs(1) - 1) & (pack == pl.num_programs(0) - 1))
     def _():
-        for which, acc in enumerate((acc1_ref, acc2_ref)):
-            for n in range(p.groups):
-                for part in range(2):
+        def keep(top, rows, value):
+            at = slice(top, top + rows)
+            if before_ref is not None:
+                value = value + before_ref[at, :]
+            total_ref[at, :] = value.astype(total_ref.dtype)
+
+        place = 0
+        for acc in (acc1_ref, acc2_ref):
+            for part in range(2):
+                for n in range(p.groups):
                     total = jnp.zeros((p.width, LANES), single)
                     for s in range(p.stack):
                         q = s * p.groups + n
-                        for row_ri, col_ri, sign in (((0, 0, 1), (1, 1, 1)), ((0, 1, 1), (1, 0, -1)))[part]:
-                            top = row_ri * p.lanes + q * p.width
-                            left = col_ri * p.lanes + q * p.width
-                            tile = left // LANES
-                            value = rolled(
-                                acc[top : top + p.width, tile * LANES : (tile + 1) * LANES],
-                                -left % LANES,
-                            )
-                            if left % LANES + p.width > LANES:
-                                nxt = acc[
-                                    top : top + p.width, (tile + 1) * LANES : (tile + 2) * LANES
-                                ]
-                                lane = lax.broadcasted_iota(jnp.int32, (p.width, LANES), 1)
-                                value = jnp.where(
-                                    lane < LANES - left % LANES, value, rolled(nxt, -left % LANES)
-                                )
-                            total = total + sign * value
-                    gw_ref[which, part, n] = total
+                        for row_ri, col_ri, sign in PARTS[part]:
+                            rows = slice(row_ri * p.lanes + q * p.width, row_ri * p.lanes + (q + 1) * p.width)
+
+                            def read(tile):
+                                left = col_ri * p.lanes + tile * LANES
+                                return acc[rows, left : left + LANES]
+
+                            total = total + sign * taken_slot(p, read, q)
+                    keep(place, p.width, total)
+                    place += p.width
+        rows = []
+        for which in range(2):
+            sums = gb_ref[which * 8 : (which + 1) * 8, :].sum(0, keepdims=True)
+            for ri in range(2):
+                for n in range(p.groups):
+                    row = jnp.zeros((1, LANES), single)
+                    for s in range(p.stack):
+
+                        def read(tile):
+                            left = ri * p.lanes + tile * LANES
+                            return sums[:, left : left + LANES]
+
+                        row = row + taken_slot(p, read, s * p.groups + n)
+                    rows.append(row)
+        rows += [jnp.zeros((1, LANES), single)] * (-len(rows) % 8)
+        keep(place, len(rows), jnp.concatenate(rows, axis=0))
 
 
 def mixed_kernel(p, rows_ref, table_ref, out_ref, words_ref):
@@ -431,8 +483,8 @@
 
 def slope_sums_kernel(p, *refs):
     stat_refs = refs[: p.chan]
-    rows_in_ref, tokens_ref, gain_ref, table_ref, wide_ref, sum_ref = refs[p.chan : p.chan + 6]
-    sums_ref, param_ref, rows_ref, part_ref = refs[p.chan + 6 :]
+    rows_in_ref, tokens_ref, affine_ref, table_ref, wide_ref, sum_ref = refs[p.chan : p.chan + 6]
+    sums_ref, param_ref, rows_ref, part_ref, dense_ref = refs[p.chan + 6 :]
     factor = 1.0 / math.sqrt(p.lon)
     count = 2 * p.stack
     moments(p, stat_refs, rows_ref)
@@ -451,17 +503,18 @@
         folds = (PACK * p.turn_pad // 8, 8, p.lanes)
         param_ref[0:8, :] += product.reshape(folds).sum(0)
         param_ref[8:16, :] += normed_grad.reshape(folds).sum(0)
-        gain = gain_ref[...]
+        gain = affine_ref[0:1, :]
         part_ref[h] = summed(sum_ref[0], normed_grad * gain) + summed(sum_ref[1], product * gain)
 
     each_row(p, row)
     for h in range(p.rows):
-        sums_ref[0, h * count : (h + 1) * count, :] = part_ref[h, :count, :]
+        dense_ref[h * count : (h + 1) * count, :] = part_ref[h, :count, :]
+    sums_ref[0] = dense_ref[...].astype(half)
 
 
 def input_grad_kernel(p, *refs):
     stat_refs, part_refs = refs[: p.chan], refs[p.chan : 2 * p.chan]
-    rows_in_ref, tokens_ref, gain_ref, table_ref, wide_ref = refs[2 * p.chan : 2 * p.chan + 5]
+    rows_in_ref, tokens_ref, affine_ref, table_ref, wide_ref = refs[2 * p.chan : 2 * p.chan + 5]
     out_ref, rows_ref, part_ref, words_ref = refs[2 * p.chan + 5 :]
     factor = 1.0 / math.sqrt(p.lon)
     count = 2 * p.stack
@@ -482,7 +535,7 @@
         inverse = each[:, p.lanes :]
         centred = (tokens_ref[0, h].astype(single) - each[:, : p.lanes]) * inverse
         grad = inverse * (
-            normed_grad * gain_ref[...] - means[:, : p.lanes] - centred * means[:, p.lanes :]
+            normed_grad * affine_ref[0:1, :] - means[:, : p.lanes] - centred * means[:, p.lanes :]
         )
         scatter_row(p, grad, words_ref.at[slot], out_ref, h)
 
@@ -574,10 +627,6 @@
     return jnp.asarray(sums, half), jnp.asarray(wide.reshape(24, 2 * p.lanes), half)
 
 
-def lane_vector(p, vector):
-    return jnp.tile(vector, p.stack)[None, :]
-
-
 def exchange(value):
     return lax.all_to_all(value, "space", 0, 0, tiled=True)
 
@@ -608,13 +657,7 @@
     table, plain_scale, double_scale, mixed_table, slope_table = lon_tables(p)
     there_table, back_table = lat_tables(p)
     sum_table, wide_table = sum_tables(p)
-    gain_lanes, shift_lanes = lane_vector(p, gain), lane_vector(p, shift)
-    both_weights = jnp.pad(
-        jnp.stack([w_first, w_second]), ((0, 0),) * 4 + ((0, LANES - p.width),)
-    )
-    bias = jnp.concatenate(
-        [b[ri].reshape(-1) for b in (b_first, b_second) for ri in range(2) for _ in range(p.stack)]
-    ).reshape(2, 2 * p.lanes)
+    affine = jnp.concatenate([gain] * p.stack + [shift] * p.stack).reshape(2, p.lanes)
     tokens_rows = PACK * p.turn_pad
     dft_flops = 2 * size * p.rows * tokens_rows * 2 * MW * p.lanes
     words = pltpu.VMEM((SLOTS, PACK, p.word_pad, LANES), single)
@@ -663,7 +706,7 @@
         )
 
     def normalise_chunk(stats, tokens, before):
-        tail = (gain_lanes, shift_lanes, table, plain_scale, wide_table)
+        tail = (affine, table, plain_scale, wide_table)
         out = sent(1 if before is None else 2)
         return out_call(
             functools.partial(normalise_kernel, p), (*stats, tokens, *tail),
@@ -674,8 +717,10 @@
     step_modes = 2 if p.modes % 2 == 0 else 1
     wide_lanes = 2 * p.lanes
 
-    def spectral_chunk(x_in, x_which, g_in, joined):
-        tail = (there_table, back_table, both_weights, bias)
+    def spectral_chunk(x_in, x_which, g_in, before):
+        joined = before is None
+        tail = (there_table, back_table, w_first, w_second, b_first, b_second)
+        tail += () if joined else (before,)
 
         def mode_spec(which):
             return pl.BlockSpec(
@@ -685,8 +730,10 @@
 
         outs = [returned(2)] if joined else [returned(1), returned(1)]
         out_specs = [peer_spec(o, 0, o.shape[1]) for o in outs]
-        grads = jax.ShapeDtypeStruct((2, 2, p.groups, p.width, LANES), single)
-        bias_grads = jax.ShapeDtypeStruct((16, wide_lanes), single)
+        bias_rows = -(-4 * p.groups // 8) * 8
+        totals = jax.ShapeDtypeStruct(
+            (4 * p.groups * p.width + bias_rows, LANES), single if joined else half
+        )
         kept = pltpu.VMEM((p.modes * p.lat, wide_lanes), half)
         held = pltpu.VMEM((step_modes * p.lat, wide_lanes), single)
         brief = pltpu.VMEM((step_modes * p.lat, wide_lanes), half)
@@ -695,9 +742,10 @@
             functools.partial(spectral_kernel, p, step_modes, joined),
             (size, p.modes // step_modes), (x_in, g_in, *tail),
             [mode_spec(x_which), mode_spec(0)] + [whole_spec(v) for v in tail],
-            [*outs, grads, bias_grads],
-            [*out_specs, whole_spec(grads), whole_spec(bias_grads)],
-            [kept] * 4 + [held] * 2 + [brief] * 2 + [turn_out] * 2
+            [*outs, totals],
+            [*out_specs, whole_spec(totals)],
+            [pltpu.VMEM((16, wide_lanes), single), pltpu.VMEM((2, wide_lanes), single)]
+            + [kept] * 4 + [held] * 2 + [brief] * 2 + [turn_out] * 2
             + [pltpu.VMEM((wide_lanes, wide_lanes), single)] * 2
             + [pltpu.VMEM((wide_lanes, wide_lanes), half)] * 2,
             12 * size * p.modes * p.lat * wide_lanes * wide_lanes,
@@ -711,9 +759,9 @@
         )
 
     def slope_sums_chunk(stats, rows_in, which, tokens):
-        tail = (gain_lanes, slope_table, wide_table, sum_table)
+        tail = (affine, slope_table, wide_table, sum_table)
         outs = [
-            jax.ShapeDtypeStruct((size, count, tokens_rows), single),
+            jax.ShapeDtypeStruct((size, count, tokens_rows), half),
             jax.ShapeDtypeStruct((16, p.lanes), single),
         ]
         return call(
@@ -721,12 +769,13 @@
             (*stats, rows_in, tokens, *tail),
             [pack_spec(s) for s in stats] + [peer_spec(rows_in, which), pack_spec(tokens)]
             + [whole_spec(v) for v in tail],
-            outs, [pack_spec(outs[0]), whole_spec(outs[1])], [rows_scratch, rows_scratch],
+            outs, [pack_spec(outs[0]), whole_spec(outs[1])],
+            [rows_scratch, rows_scratch, pltpu.VMEM((count, tokens_rows), single)],
             dft_flops,
         )
 
     def input_grad_chunk(c, stats, parts, rows_in, which, tokens, before):
-        tail = (gain_lanes, slope_table, wide_table)
+        tail = (affine, slope_table, wide_table)
         return out_call(
             functools.partial(input_grad_kernel, p),
             (*stats, *parts, rows_in, tokens, *tail),
@@ -747,33 +796,28 @@
     tokens1, sums = stats_chunk(1)
     stats1 = channel_sums(sums)
     both1 = exchange(normalise_chunk(stats1, tokens1, both1))
-    out0, gw0, gb0 = spectral_chunk(x0, 0, g0, True)
+    out0, totals = spectral_chunk(x0, 0, g0, None)
     rows0 = exchange(out0)
-    y1, dx1, gw1, gb1 = spectral_chunk(both1, 1, both1, False)
+    y1, dx1, totals = spectral_chunk(both1, 1, both1, totals)
     dx1 = exchange(dx1)
     y1 = exchange(y1)
     sums, params0 = slope_sums_chunk(stats0, rows0, 1, tokens0)
-    parts = channel_sums(sums.astype(half))
+    parts = channel_sums(sums)
     grad_input = input_grad_chunk(0, stats0, parts, rows0, 1, tokens0, None)
     mixed = mixed_chunk(0, rows0, 0, None)
     sums, params1 = slope_sums_chunk(stats1, dx1, 0, tokens1)
-    parts = channel_sums(sums.astype(half))
+    parts = channel_sums(sums)
     grad_input = input_grad_chunk(1, stats1, parts, dx1, 0, tokens1, grad_input)
     mixed = mixed_chunk(1, y1, 0, mixed)
-    weight_grads, bias_grads, param_grads = gw0 + gw1, gb0 + gb1, params0 + params1
-
-    def by_channel(rows):
-        return rows.reshape(-1, p.stack, p.groups * p.width).sum(1)
-
-    weights = weight_grads.reshape(-1, LANES)
-    flat_bias = bias_grads.reshape(2, 8, 2, p.stack, p.groups * p.width).sum((1, 3))
-    flat_params = by_channel(param_grads.reshape(2, 8, p.lanes).sum(1))
-    flat = jnp.concatenate([weights, flat_bias.reshape(-1, LANES)])
-    flat = reduced(p, flat, half)
-    grads = flat[: weights.shape[0]].reshape(weight_grads.shape)[..., : p.width]
-    flat_bias = flat[weights.shape[0] :].reshape((2,) + b_first.shape)
-    both = reduced(p, flat_params, single)
-    return (mixed, grad_input, grads[0], flat_bias[0], grads[1], flat_bias[1], both[0], both[1])
+    size_w = p.groups * p.width
+    flat = reduced(p, totals, half)[:, : p.width]
+    grads = flat[: 4 * size_w].reshape((2,) + w_first.shape)
+    bias_grads = flat[4 * size_w : 4 * size_w + 4 * p.groups].reshape((2,) + b_first.shape)
+    params = reduced(p, params0 + params1, single)
+    params = params.reshape(2, 8, p.stack, size_w).sum((1, 2))
+    return (
+        mixed, grad_input, grads[0], bias_grads[0], grads[1], bias_grads[1], params[0], params[1]
+    )
 
 
 def solution(mesh):

time: 386 us -> 411 us (1.065)
  blocking collectives: 0 us -> 91.9 us
  local copies, waits for them, and re-layouts: 61.9 us -> 3.25 us
  Pallas kernels: 191 us -> 211 us
  waiting for transfers between devices: 65.1 us -> 53.9 us
  starting transfers between devices: 53.4 us -> 44.1 us
  other arithmetic: 11.6 us -> 5.91 us
    all_to_all x0 -> x2, blocking collectives: none -> 91.9 us  [exchange(): return lax.all_to_all(value, 'space', 0, 0, tiled=True)]
    unnamed x116 -> x4, local copies, waits for them, and re-layouts: 41 us -> 0.01 us
    pallas_call x14, Pallas kernels: 191 us -> 211 us  [_call(): pl.pallas_call(body, grid=grid, in_specs=in_specs, out_specs=out_specs, o...]
    all_to_all x6 -> x4, waiting for transfers between devices: 29.8 us -> 13.9 us  [exchange(): return lax.all_to_all(value, 'space', 0, 0, tiled=True)]
    all_to_all x6 -> x4, starting transfers between devices: 28 us -> 18.9 us  [exchange(): return lax.all_to_all(value, 'space', 0, 0, tiled=True)]
    another operation x9 -> x1, local copies, waits for them, and re-layouts: 9.21 us -> 0.64 us  [the longest x4 5.28 us: on_device(): b[ri].reshape(-1)]
  transfers between devices with their start and end apart: 24 -> 22, of which waited for: 6 -> 6; matrix products, arithmetic and copies ran while one was open for 8% -> 2% of each run, Pallas kernels for 45% -> 39%
where the time goes in v2:
time: 411 us; the launch traced here: 410 us
  Pallas kernels  211 us (51%)
  blocking collectives  91.9 us (22%)
  waiting for transfers between devices  53.9 us (13%)
  starting transfers between devices  44.1 us (11%)
  other arithmetic  5.91 us (1%)
    pallas_call x14, Pallas kernels, _call(): pl.pallas_call(body, grid=grid, in_specs=in_specs, out_specs=out_specs, o...  211 us
    all_to_all x2, blocking collectives, exchange(): return lax.all_to_all(value, 'space', 0, 0, tiled=True)  91.9 us
    ppermute x6, waiting for transfers between devices, reduced(): other = lax.ppermute(own, 'space', [(i, i ^ step) for i in range(p.space)])  35.4 us
    ppermute x12, starting transfers between devices, around(): lax.ppermute(value, axis, [(i, (i + step) % size) for i in range(size)])  19.4 us
    all_to_all x4, starting transfers between devices, exchange(): return lax.all_to_all(value, 'space', 0, 0, tiled=True)  18.9 us
    all_to_all x4, waiting for transfers between devices, exchange(): return lax.all_to_all(value, 'space', 0, 0, tiled=True)  13.9 us
  transfers between devices with their start and end apart: 22, of which 6 were waited for; matrix products, arithmetic and copies ran while one was open for 2% of the time, Pallas kernels for 39%

profile of v2, /device:TPU:0, one launch (start us, length us, event | category | flops | bytes accessed | tf_op | source)
XLA Modules:
  0.0 410.4 jit_solution(7024781500301525710)
XLA Ops:
  0.6 7.7 %shard_map.229 = bf16[8,1,2,8,24,384]{5,4,3,2,1,0:T(8,128)(2,1)} custom-call(bf16[8,12,2,17280]{3,2,1,0:T(2,128)(2,1)} %stored_ref.7, bf16[128,192]{1,0:T(8,128)(2,1)} %constant.20.clone.table_ref.refs_6_, f32[128,1]{1,0:T(8,128)} %constant.22.clone.scale_ref), custom_call_target="tpu_custom_call" | custom-call | flops 452984832 | bytes 9044480 | tf_op jit(solution)/shard_map/pallas_call | solution.py:574
  8.3 5.2 %all-to-all-start.2 = ((bf16[8,1,2,8,24,384]{5,4,3,2,1,0:T(8,128)(2,1)}), bf16[8,1,2,8,24,384]{5,4,3,2,1,0:T(8,128)(2,1)}, u32[]{:S(2)}, u32[]{:S(2)}) async-start(bf16[8,1,2,8,24,384]{5,4,3,2,1,0:T(8,128)(2,1)} %shard_map.229), calls=%async_computation.2 | async-start | bytes 4718592 | tf_op jit(solution)/shard_map/all_to_all | solution.py:631
  13.5 10.1 %shard_map.227 = (bf16[2,12,192,384]{3,2,1,0:T(8,128)(2,1)}, f32[2,48,192]{2,1,0:T(8,128)}) custom-call(bf16[8,12,2,17280]{3,2,1,0:T(2,128)(2,1)} %stored_ref.6, bf16[2,8,384]{2,1,0:T(8,128)(2,1)} %constant.27.clone.sum_ref.refs_9_), custom_call_target="tpu_custom_call" | custom-call | flops 113246208 | bytes 10260480 | tf_op jit(solution)/shard_map/pallas_call | solution.py:574
  23.6 2.2 collective-permute-start.3
  25.8 2.6 collective-permute-start.4
  28.4 1.4 collective-permute-start.5
  29.8 0.8 pad_maximum_fusion
  30.6 0.6 reshape.32.refs_5_.refs_6_.refs_10_
  31.2 0.7 collective-permute-done.3.refs_1_
  31.9 3.9 collective-permute-done.4.refs_2_
  35.8 0.6 jit_solution_.3.refs_7_
  36.4 11.3 %shard_map.228 = bf16[8,1,2,8,24,384]{5,4,3,2,1,0:T(8,128)(2,1)} custom-call(f32[2,48,192]{2,1,0:T(8,128)} %get-tuple-element.23.refs_0_, f32[2,48,192]{2,1,0:T(8,128)} %collective-permute-done.3.refs_1_, f32[2,48,192]{2,1,0:T(8,128)} %collective-permute-done.4.refs_2_, f32[2,48,192]{2,1,0:T(8,128)} %collective-permute-done.5.refs_3_, ...), custom_call_target="tpu_custom_call" | custom-call | flops 452984832 | bytes 6282752 | tf_op jit(solution)/shard_map/pallas_call | solution.py:574
  47.8 4.4 %all-to-all-start.1 = ((bf16[8,1,2,8,24,384]{5,4,3,2,1,0:T(8,128)(2,1)}), bf16[8,1,2,8,24,384]{5,4,3,2,1,0:T(8,128)(2,1)}, u32[]{:S(2)}, u32[]{:S(2)}) async-start(bf16[8,1,2,8,24,384]{5,4,3,2,1,0:T(8,128)(2,1)} %shard_map.228), calls=%async_computation.1 | async-start | bytes 4718592 | tf_op jit(solution)/shard_map/all_to_all | solution.py:631
  52.2 10.2 %shard_map.224 = (bf16[2,12,192,384]{3,2,1,0:T(8,128)(2,1)}, f32[2,48,192]{2,1,0:T(8,128)}) custom-call(bf16[8,12,2,17280]{3,2,1,0:T(2,128)(2,1)} %stored_ref.6, bf16[2,8,384]{2,1,0:T(8,128)(2,1)} %constant.27.clone.sum_ref.refs_9_), custom_call_target="tpu_custom_call" | custom-call | flops 113246208 | bytes 10260480 | tf_op jit(solution)/shard_map/pallas_call | solution.py:574
  62.3 2.6 collective-permute-start
  64.9 1.6 collective-permute-start.1
  66.6 0.7 collective-permute-start.2
  67.3 7.7 %shard_map.225.refs_9_ = bf16[8,2,2,8,24,384]{5,4,3,2,1,0:T(8,128)(2,1)} custom-call(bf16[8,12,2,17280]{3,2,1,0:T(2,128)(2,1)} %stored_ref.7, bf16[128,192]{1,0:T(8,128)(2,1)} %constant.20.clone.table_ref.refs_6_, f32[128,1]{1,0:T(8,128)} %constant.22.clone.scale_ref), custom_call_target="tpu_custom_call" | custom-call | flops 452984832 | bytes 11403776 | tf_op jit(solution)/shard_map/pallas_call | solution.py:574
  75.0 11.4 %shard_map.226 = bf16[8,2,2,8,24,384]{5,4,3,2,1,0:T(8,128)(2,1)} custom-call(f32[2,48,192]{2,1,0:T(8,128)} %get-tuple-element.21.refs_0_, f32[2,48,192]{2,1,0:T(8,128)} %collective-permute-done.refs_1_, f32[2,48,192]{2,1,0:T(8,128)} %collective-permute-done.1.refs_2_, f32[2,48,192]{2,1,0:T(8,128)} %collective-permute-done.2.refs_3_, ...), custom_call_target="tpu_custom_call", output_to_operand_aliasing={{}: (9, {})} | custom-call | flops 452984832 | bytes 13360640 | tf_op jit(solution)/shard_map/pallas_call | solution.py:574
  86.3 4.8 %all-to-all-start = ((bf16[8,2,2,8,24,384]{5,4,3,2,1,0:T(8,128)(2,1)}), bf16[8,2,2,8,24,384]{5,4,3,2,1,0:T(8,128)(2,1)}, u32[]{:S(2)}, u32[]{:S(2)}) async-start(bf16[8,2,2,8,24,384]{5,4,3,2,1,0:T(8,128)(2,1)} %shard_map.226), calls=%async_computation | async-start | bytes 9437184 | tf_op jit(solution)/shard_map/all_to_all | solution.py:631
  91.1 40.7 %shard_map.230 = (bf16[8,2,2,12,16,384]{5,4,3,2,1,0:T(8,128)(2,1)}, f32[776,128]{1,0:T(8,128)}) custom-call(bf16[8,1,2,8,24,384]{5,4,3,2,1,0:T(8,128)(2,1)} %all-to-all-done.1.x_ref, bf16[8,1,2,8,24,384]{5,4,3,2,1,0:T(8,128)(2,1)} %all-to-all-done.2.g_ref, bf16[192,192]{1,0:T(8,128)(2,1)} %constant.25.clone.there_ref, ...), custom_call_target="tpu_custom_call" | custom-call | flops 10871635968 | bytes 10132480 | tf_op jit(solution)/shard_map/pallas_call | solution.py:574
  131.8 13.8 %all-to-all-done.x_ref.g_ref = bf16[8,2,2,8,24,384]{5,4,3,2,1,0:T(8,128)(2,1)} async-done(((bf16[8,2,2,8,24,384]{5,4,3,2,1,0:T(8,128)(2,1)}), bf16[8,2,2,8,24,384]{5,4,3,2,1,0:T(8,128)(2,1)}, u32[]{:S(2)}, u32[]{:S(2)}) %all-to-all-start) | async-done | bytes 4718624 | tf_op jit(solution)/shard_map/all_to_all | solution.py:631
  145.7 40.8 %shard_map.231 = (bf16[8,1,2,12,16,384]{5,4,3,2,1,0:T(8,128)(2,1)}, bf16[8,1,2,12,16,384]{5,4,3,2,1,0:T(8,128)(2,1)}, bf16[776,128]{1,0:T(8,128)(2,1)}) custom-call(bf16[8,2,2,8,24,384]{5,4,3,2,1,0:T(8,128)(2,1)} %all-to-all-done.x_ref.g_ref, bf16[8,2,2,8,24,384]{5,4,3,2,1,0:T(8,128)(2,1)} %all-to-all-done.x_ref.g_ref, ...), custom_call_target="tpu_custom_call" | custom-call | flops 10871635968 | bytes 15049728 | tf_op jit(solution)/shard_map/pallas_call | solution.py:574
  186.5 34.0 %all_to_all.30.refs_4_.refs_8_ = bf16[8,1,2,12,16,384]{5,4,3,2,1,0:T(8,128)(2,1)} all-to-all(bf16[8,1,2,12,16,384]{5,4,3,2,1,0:T(8,128)(2,1)} %get-tuple-element.28), channel_id=1, replica_groups=mesh['space'=8,'chan'=4] {'space'}, dimensions={0} | all-to-all | bytes 4718592 | tf_op jit(solution)/shard_map/all_to_all | solution.py:631
  220.5 57.9 %all_to_all.31.rows_ref.refs_4_.refs_8_ = bf16[8,2,2,12,16,384]{5,4,3,2,1,0:T(8,128)(2,1)} all-to-all(bf16[8,2,2,12,16,384]{5,4,3,2,1,0:T(8,128)(2,1)S(1)} %copy-done), channel_id=1, replica_groups=mesh['space'=8,'chan'=4] {'space'}, dimensions={0} | all-to-all | bytes 9437184 | tf_op jit(solution)/shard_map/all_to_all | solution.py:631
  278.5 4.5 %all-to-all-start.3 = ((bf16[8,1,2,12,16,384]{5,4,3,2,1,0:T(8,128)(2,1)}), bf16[8,1,2,12,16,384]{5,4,3,2,1,0:T(8,128)(2,1)}, u32[]{:S(2)}, u32[]{:S(2)}) async-start(bf16[8,1,2,12,16,384]{5,4,3,2,1,0:T(8,128)(2,1)} %get-tuple-element.26), calls=%async_computation.3 | async-start | bytes 4718592 | tf_op jit(solution)/shard_map/all_to_all | solution.py:631
  283.4 1.6 collective-permute-done.12
  285.0 1.7 collective-permute-start.13
  286.7 28.9 %collective-permute-done.13 = bf16[776,128]{1,0:T(8,128)(2,1)S(1)} collective-permute-done((bf16[776,128]{1,0:T(8,128)(2,1)S(1)}, bf16[776,128]{1,0:T(8,128)(2,1)S(1)}, u32[]{:S(2)}, u32[]{:S(2)}) %collective-permute-start.13) | collective-permute-done | bytes 198688 | tf_op jit(solution)/shard_map/ppermute | solution.py:647
  315.7 1.6 collective-permute-start.14
  317.3 4.9 %collective-permute-done.14 = bf16[776,128]{1,0:T(8,128)(2,1)S(1)} collective-permute-done((bf16[776,128]{1,0:T(8,128)(2,1)S(1)}, bf16[776,128]{1,0:T(8,128)(2,1)S(1)}, u32[]{:S(2)}, u32[]{:S(2)}) %collective-permute-start.14) | collective-permute-done | bytes 198688 | tf_op jit(solution)/shard_map/ppermute | solution.py:647
  322.8 0.8 fusion.1
  323.6 12.5 %shard_map.235 = (bf16[2,48,192]{2,1,0:T(8,128)(2,1)}, f32[16,384]{1,0:T(8,128)}) custom-call(f32[2,48,192]{2,1,0:T(8,128)} %get-tuple-element.23.refs_0_, f32[2,48,192]{2,1,0:T(8,128)} %collective-permute-done.3.refs_1_, f32[2,48,192]{2,1,0:T(8,128)} %collective-permute-done.4.refs_2_, f32[2,48,192]{2,1,0:T(8,128)} %collective-permute-done.5.refs_3_, ...), custom_call_target="tpu_custom_call" | custom-call | flops 452984832 | bytes 8715264 | tf_op jit(solution)/shard_map/pallas_call | solution.py:574
  336.1 1.0 collective-permute-start.10
  337.0 3.0 collective-permute-start.11
  340.0 12.5 %shard_map.234 = (bf16[2,48,192]{2,1,0:T(8,128)(2,1)}, f32[16,384]{1,0:T(8,128)}) custom-call(f32[2,48,192]{2,1,0:T(8,128)} %get-tuple-element.21.refs_0_, f32[2,48,192]{2,1,0:T(8,128)} %collective-permute-done.refs_1_, f32[2,48,192]{2,1,0:T(8,128)} %collective-permute-done.1.refs_2_, f32[2,48,192]{2,1,0:T(8,128)} %collective-permute-done.2.refs_3_, ...), custom_call_target="tpu_custom_call" | custom-call | flops 452984832 | bytes 6355968 | tf_op jit(solution)/shard_map/pallas_call | solution.py:574
  352.5 1.4 add.24
  353.8 1.0 collective-permute-start.6
  354.8 8.9 %shard_map.232.refs_2_ = bf16[8,12,2,17280]{3,2,1,0:T(2,128)(2,1)} custom-call(bf16[8,2,2,12,16,384]{5,4,3,2,1,0:T(8,128)(2,1)} %all_to_all.31.rows_ref.refs_4_.refs_8_, bf16[192,128]{1,0:T(8,128)(2,1)} %constant.23.clone.table_ref.refs_1_), custom_call_target="tpu_custom_call" | custom-call | flops 452984832 | bytes 11403264 | tf_op jit(solution)/shard_map/pallas_call | solution.py:574
  363.7 8.9 %shard_map.233 = bf16[8,12,2,17280]{3,2,1,0:T(2,128)(2,1)} custom-call(bf16[8,1,2,12,16,384]{5,4,3,2,1,0:T(8,128)(2,1)} %all-to-all-done.3.refs_0_, bf16[192,128]{1,0:T(8,128)(2,1)} %constant.23.clone.table_ref.refs_1_, bf16[8,12,2,17280]{3,2,1,0:T(2,128)(2,1)} %shard_map.232.refs_2_), custom_call_target="tpu_custom_call", output_to_operand_aliasing={{}: (2, {})} | custom-call | flops 452984832 | bytes 15679488 | tf_op jit(solution)/shard_map/pallas_call | solution.py:574
  372.7 3.4 collective-permute-start.7
  376.1 1.4 add.25
  377.5 0.8 collective-permute-start.16
  378.3 13.9 %shard_map.236.refs_13_ = bf16[8,12,2,17280]{3,2,1,0:T(2,128)(2,1)} custom-call(f32[2,48,192]{2,1,0:T(8,128)} %get-tuple-element.23.refs_0_, f32[2,48,192]{2,1,0:T(8,128)} %collective-permute-done.3.refs_1_, f32[2,48,192]{2,1,0:T(8,128)} %collective-permute-done.4.refs_2_, f32[2,48,192]{2,1,0:T(8,128)} %collective-permute-done.5.refs_3_, ...), custom_call_target="tpu_custom_call" | custom-call | flops 452984832 | bytes 15424512 | tf_op jit(solution)/shard_map/pallas_call | solution.py:574
  392.2 1.4 add.26
  393.6 1.3 collective-permute-start.17
  394.9 14.0 %shard_map.237 = bf16[8,12,2,17280]{3,2,1,0:T(2,128)(2,1)} custom-call(f32[2,48,192]{2,1,0:T(8,128)} %get-tuple-element.21.refs_0_, f32[2,48,192]{2,1,0:T(8,128)} %collective-permute-done.refs_1_, f32[2,48,192]{2,1,0:T(8,128)} %collective-permute-done.1.refs_2_, f32[2,48,192]{2,1,0:T(8,128)} %collective-permute-done.2.refs_3_, ...), custom_call_target="tpu_custom_call", output_to_operand_aliasing={{}: (13, {})} | custom-call | flops 452984832 | bytes 19700736 | tf_op jit(solution)/shard_map/pallas_call | solution.py:574
  408.9 0.8 add.27
  (31 shorter events, 1.9 us)
Async XLA Ops:
  8.3 39.4 %all-to-all-start.2 = ((bf16[8,1,2,8,24,384]{5,4,3,2,1,0:T(8,128)(2,1)}), bf16[8,1,2,8,24,384]{5,4,3,2,1,0:T(8,128)(2,1)}, u32[]{:S(2)}, u32[]{:S(2)}) async-start(bf16[8,1,2,8,24,384]{5,4,3,2,1,0:T(8,128)(2,1)} %shard_map.229), calls=%async_computation.2 | async-start | bytes 4718592 | tf_op jit(solution)/shard_map/all_to_all | solution.py:631
  23.6 8.3 %collective-permute-start.3 = (f32[2,48,192]{2,1,0:T(8,128)}, f32[2,48,192]{2,1,0:T(8,128)}, u32[]{:S(2)}, u32[]{:S(2)}) collective-permute-start(f32[2,48,192]{2,1,0:T(8,128)} %get-tuple-element.23.refs_0_), channel_id=1, source_target_pairs={{0,1},{1,2},{2,3},{3,0},{4,5},{5,6},{6,7},{7,4},{8,9},{9,10},{10,1... | collective-permute-start | bytes 221192 | tf_op jit(solution)/shard_map/ppermute | solution.py:638
  25.8 9.9 %collective-permute-start.4 = (f32[2,48,192]{2,1,0:T(8,128)}, f32[2,48,192]{2,1,0:T(8,128)}, u32[]{:S(2)}, u32[]{:S(2)}) collective-permute-start(f32[2,48,192]{2,1,0:T(8,128)} %get-tuple-element.23.refs_0_), channel_id=1, source_target_pairs={{0,2},{1,3},{2,0},{3,1},{4,6},{5,7},{6,4},{7,5},{8,10},{9,11},{10,... | collective-permute-start | bytes 221192 | tf_op jit(solution)/shard_map/ppermute | solution.py:638
  28.4 7.4 %collective-permute-start.5 = (f32[2,48,192]{2,1,0:T(8,128)}, f32[2,48,192]{2,1,0:T(8,128)}, u32[]{:S(2)}, u32[]{:S(2)}) collective-permute-start(f32[2,48,192]{2,1,0:T(8,128)} %get-tuple-element.23.refs_0_), channel_id=1, source_target_pairs={{0,3},{1,0},{2,1},{3,2},{4,7},{5,4},{6,5},{7,6},{8,11},{9,8},{10,9... | collective-permute-start | bytes 221192 | tf_op jit(solution)/shard_map/ppermute | solution.py:638
  47.8 38.6 %all-to-all-start.1 = ((bf16[8,1,2,8,24,384]{5,4,3,2,1,0:T(8,128)(2,1)}), bf16[8,1,2,8,24,384]{5,4,3,2,1,0:T(8,128)(2,1)}, u32[]{:S(2)}, u32[]{:S(2)}) async-start(bf16[8,1,2,8,24,384]{5,4,3,2,1,0:T(8,128)(2,1)} %shard_map.228), calls=%async_computation.1 | async-start | bytes 4718592 | tf_op jit(solution)/shard_map/all_to_all | solution.py:631
  62.3 12.6 %collective-permute-start = (f32[2,48,192]{2,1,0:T(8,128)}, f32[2,48,192]{2,1,0:T(8,128)}, u32[]{:S(2)}, u32[]{:S(2)}) collective-permute-start(f32[2,48,192]{2,1,0:T(8,128)} %get-tuple-element.21.refs_0_), channel_id=1, source_target_pairs={{0,1},{1,2},{2,3},{3,0},{4,5},{5,6},{6,7},{7,4},{8,9},{9,10},{10,1... | collective-permute-start | bytes 221192 | tf_op jit(solution)/shard_map/ppermute | solution.py:638
  64.9 10.0 %collective-permute-start.1 = (f32[2,48,192]{2,1,0:T(8,128)}, f32[2,48,192]{2,1,0:T(8,128)}, u32[]{:S(2)}, u32[]{:S(2)}) collective-permute-start(f32[2,48,192]{2,1,0:T(8,128)} %get-tuple-element.21.refs_0_), channel_id=1, source_target_pairs={{0,2},{1,3},{2,0},{3,1},{4,6},{5,7},{6,4},{7,5},{8,10},{9,11},{10,... | collective-permute-start | bytes 221192 | tf_op jit(solution)/shard_map/ppermute | solution.py:638
  66.6 8.4 %collective-permute-start.2 = (f32[2,48,192]{2,1,0:T(8,128)}, f32[2,48,192]{2,1,0:T(8,128)}, u32[]{:S(2)}, u32[]{:S(2)}) collective-permute-start(f32[2,48,192]{2,1,0:T(8,128)} %get-tuple-element.21.refs_0_), channel_id=1, source_target_pairs={{0,3},{1,0},{2,1},{3,2},{4,7},{5,4},{6,5},{7,6},{8,11},{9,8},{10,9... | collective-permute-start | bytes 221192 | tf_op jit(solution)/shard_map/ppermute | solution.py:638
  86.3 59.3 %all-to-all-start = ((bf16[8,2,2,8,24,384]{5,4,3,2,1,0:T(8,128)(2,1)}), bf16[8,2,2,8,24,384]{5,4,3,2,1,0:T(8,128)(2,1)}, u32[]{:S(2)}, u32[]{:S(2)}) async-start(bf16[8,2,2,8,24,384]{5,4,3,2,1,0:T(8,128)(2,1)} %shard_map.226), calls=%async_computation | async-start | bytes 9437184 | tf_op jit(solution)/shard_map/all_to_all | solution.py:631
  186.5 34.0 %copy-start = (bf16[8,2,2,12,16,384]{5,4,3,2,1,0:T(8,128)(2,1)S(1)}, bf16[8,2,2,12,16,384]{5,4,3,2,1,0:T(8,128)(2,1)}, u32[]{:S(2)}) copy-start(bf16[8,2,2,12,16,384]{5,4,3,2,1,0:T(8,128)(2,1)} %get-tuple-element.27) | copy-start | bytes 14155780
  278.5 4.5 %copy-start.1 = (bf16[776,128]{1,0:T(8,128)(2,1)S(1)}, bf16[776,128]{1,0:T(8,128)(2,1)}, u32[]{:S(2)}) copy-start(bf16[776,128]{1,0:T(8,128)(2,1)} %get-tuple-element.31) | copy-start | bytes 595972
  278.5 85.3 %all-to-all-start.3 = ((bf16[8,1,2,12,16,384]{5,4,3,2,1,0:T(8,128)(2,1)}), bf16[8,1,2,12,16,384]{5,4,3,2,1,0:T(8,128)(2,1)}, u32[]{:S(2)}, u32[]{:S(2)}) async-start(bf16[8,1,2,12,16,384]{5,4,3,2,1,0:T(8,128)(2,1)} %get-tuple-element.26), calls=%async_computation.3 | async-start | bytes 4718592 | tf_op jit(solution)/shard_map/all_to_all | solution.py:631
  283.0 1.9 collective-permute-start.12
  285.0 30.7 %collective-permute-start.13 = (bf16[776,128]{1,0:T(8,128)(2,1)S(1)}, bf16[776,128]{1,0:T(8,128)(2,1)S(1)}, u32[]{:S(2)}, u32[]{:S(2)}) collective-permute-start(bf16[776,128]{1,0:T(8,128)(2,1)S(1)} %add_convert_fusion.1), channel_id=1, source_target_pairs={{0,8},{4,12},{8,0},{12,4},{16,24},{20,28},{24,16},{28,20},{1,9},{5... | collective-permute-start | bytes 595976 | tf_op jit(solution)/shard_map/ppermute | solution.py:647
  315.7 6.5 %collective-permute-start.14 = (bf16[776,128]{1,0:T(8,128)(2,1)S(1)}, bf16[776,128]{1,0:T(8,128)(2,1)S(1)}, u32[]{:S(2)}, u32[]{:S(2)}) collective-permute-start(bf16[776,128]{1,0:T(8,128)(2,1)S(1)} %add_convert_fusion), channel_id=1, source_target_pairs={{0,16},{4,20},{8,24},{12,28},{16,0},{20,4},{24,8},{28,12},{1,17},{... | collective-permute-start | bytes 595976 | tf_op jit(solution)/shard_map/ppermute | solution.py:647
  336.1 41.4 %collective-permute-start.10 = (bf16[2,48,192]{2,1,0:T(8,128)(2,1)}, bf16[2,48,192]{2,1,0:T(8,128)(2,1)}, u32[]{:S(2)}, u32[]{:S(2)}) collective-permute-start(bf16[2,48,192]{2,1,0:T(8,128)(2,1)} %get-tuple-element.30.refs_4_), channel_id=1, source_target_pairs={{0,2},{1,3},{2,0},{3,1},{4,6},{5,7},{6,4},{7,5},{8,10},{9,11},{10,... | collective-permute-start | bytes 110600 | tf_op jit(solution)/shard_map/ppermute | solution.py:638
  337.0 40.5 %collective-permute-start.11 = (bf16[2,48,192]{2,1,0:T(8,128)(2,1)}, bf16[2,48,192]{2,1,0:T(8,128)(2,1)}, u32[]{:S(2)}, u32[]{:S(2)}) collective-permute-start(bf16[2,48,192]{2,1,0:T(8,128)(2,1)} %get-tuple-element.30.refs_4_), channel_id=1, source_target_pairs={{0,3},{1,0},{2,1},{3,2},{4,7},{5,4},{6,5},{7,6},{8,11},{9,8},{10,9... | collective-permute-start | bytes 110600 | tf_op jit(solution)/shard_map/ppermute | solution.py:638
  340.0 38.3 %collective-permute-start.9 = (bf16[2,48,192]{2,1,0:T(8,128)(2,1)}, bf16[2,48,192]{2,1,0:T(8,128)(2,1)}, u32[]{:S(2)}, u32[]{:S(2)}) collective-permute-start(bf16[2,48,192]{2,1,0:T(8,128)(2,1)} %get-tuple-element.30.refs_4_), channel_id=1, source_target_pairs={{0,1},{1,2},{2,3},{3,0},{4,5},{5,6},{6,7},{7,4},{8,9},{9,10},{10,1... | collective-permute-start | bytes 110600 | tf_op jit(solution)/shard_map/ppermute | solution.py:638
  353.8 18.8 %collective-permute-start.15 = (f32[16,384]{1,0:T(8,128)}, f32[16,384]{1,0:T(8,128)}, u32[]{:S(2)}, u32[]{:S(2)}) collective-permute-start(f32[16,384]{1,0:T(8,128)} %add.24), channel_id=1, source_target_pairs={{0,4},{4,0},{8,12},{12,8},{16,20},{20,16},{24,28},{28,24},{1,5},{5... | collective-permute-start | bytes 73736 | tf_op jit(solution)/shard_map/ppermute | solution.py:647
  353.8 41.1 %collective-permute-start.6 = (bf16[2,48,192]{2,1,0:T(8,128)(2,1)}, bf16[2,48,192]{2,1,0:T(8,128)(2,1)}, u32[]{:S(2)}, u32[]{:S(2)}) collective-permute-start(bf16[2,48,192]{2,1,0:T(8,128)(2,1)} %get-tuple-element.29.refs_4_), channel_id=1, source_target_pairs={{0,1},{1,2},{2,3},{3,0},{4,5},{5,6},{6,7},{7,4},{8,9},{9,10},{10,1... | collective-permute-start | bytes 110600 | tf_op jit(solution)/shard_map/ppermute | solution.py:638
  372.7 22.3 %collective-permute-start.7 = (bf16[2,48,192]{2,1,0:T(8,128)(2,1)}, bf16[2,48,192]{2,1,0:T(8,128)(2,1)}, u32[]{:S(2)}, u32[]{:S(2)}) collective-permute-start(bf16[2,48,192]{2,1,0:T(8,128)(2,1)} %get-tuple-element.29.refs_4_), channel_id=1, source_target_pairs={{0,2},{1,3},{2,0},{3,1},{4,6},{5,7},{6,4},{7,5},{8,10},{9,11},{10,... | collective-permute-start | bytes 110600 | tf_op jit(solution)/shard_map/ppermute | solution.py:638
  377.5 17.4 %collective-permute-start.8 = (bf16[2,48,192]{2,1,0:T(8,128)(2,1)}, bf16[2,48,192]{2,1,0:T(8,128)(2,1)}, u32[]{:S(2)}, u32[]{:S(2)}) collective-permute-start(bf16[2,48,192]{2,1,0:T(8,128)(2,1)} %get-tuple-element.29.refs_4_), channel_id=1, source_target_pairs={{0,3},{1,0},{2,1},{3,2},{4,7},{5,4},{6,5},{7,6},{8,11},{9,8},{10,9... | collective-permute-start | bytes 110600 | tf_op jit(solution)/shard_map/ppermute | solution.py:638
  377.5 14.7 %collective-permute-start.16 = (f32[16,384]{1,0:T(8,128)}, f32[16,384]{1,0:T(8,128)}, u32[]{:S(2)}, u32[]{:S(2)}) collective-permute-start(f32[16,384]{1,0:T(8,128)} %add.25), channel_id=1, source_target_pairs={{0,8},{4,12},{8,0},{12,4},{16,24},{20,28},{24,16},{28,20},{1,9},{5... | collective-permute-start | bytes 73736 | tf_op jit(solution)/shard_map/ppermute | solution.py:647
  393.6 15.3 %collective-permute-start.17 = (f32[16,384]{1,0:T(8,128)}, f32[16,384]{1,0:T(8,128)}, u32[]{:S(2)}, u32[]{:S(2)}) collective-permute-start(f32[16,384]{1,0:T(8,128)} %add.26), channel_id=1, source_target_pairs={{0,16},{4,20},{8,24},{12,28},{16,0},{20,4},{24,8},{28,12},{1,17},{... | collective-permute-start | bytes 73736 | tf_op jit(solution)/shard_map/ppermute | solution.py:647

commit v3 on v2

--- a/solution.py
+++ b/solution.py
@@ -22,7 +22,7 @@
 half = jnp.bfloat16
 single = jnp.float32
 VMEM_LIMIT = 67043328
-SLOTS = 2
+SLOTS = 4
 
 TN = (((0,), (0,)), ((), ()))
 NT = (((1,), (1,)), ((), ()))
@@ -117,10 +117,13 @@
     lane = lax.broadcasted_iota(jnp.int32, (p.turn_pad, LANES), 1)
     for q in range(PACK):
         s, n = divmod(q, p.groups)
+        cache = {}
 
         def fetch(r, c, shift):
-            part = tokens[r * p.turn_pad : (r + 1) * p.turn_pad, c * LANES : (c + 1) * LANES]
-            return rolled(part, shift)
+            if (r, c, shift) not in cache:
+                part = tokens[r * p.turn_pad : (r + 1) * p.turn_pad, c * LANES : (c + 1) * LANES]
+                cache[r, c, shift] = rolled(part, shift)
+            return cache[r, c, shift]
 
         for i in range(p.tiles):
             pieces = moved_lanes(p, fetch, lambda r: q * p.width, lambda r: r * p.width, i)
@@ -176,9 +179,13 @@
     return high, middle, rest - middle
 
 
-def expand(parts, spread_table):
+def expand(p, parts, wide_ref):
     stacked = jnp.concatenate(split_three(parts), axis=0).astype(half)
-    return mul(stacked, spread_table, TN)
+    pairs = []
+    for c in range(p.tiles):
+        both = mul(stacked, wide_ref[:, 2 * c * LANES : 2 * (c + 1) * LANES], TN)
+        pairs.append((both[:, :LANES], both[:, LANES:]))
+    return pairs
 
 
 def summed(table, value):
@@ -237,10 +244,12 @@
     moments(p, stat_refs, rows_ref)
 
     def row(h, slot):
-        each = expand(rows_ref[h], wide_ref[...])
-        wide = tokens_ref[0, h].astype(single)
-        centred = (wide - each[:, : p.lanes]) * each[:, p.lanes :]
-        normed = (centred * affine_ref[0:1, :] + affine_ref[1:2, :]).astype(half)
+        tiles = []
+        for c, (mean, inverse) in enumerate(expand(p, rows_ref[h], wide_ref)):
+            at = slice(c * LANES, (c + 1) * LANES)
+            centred = (tokens_ref[0, h, :, at].astype(single) - mean) * inverse
+            tiles.append((centred * affine_ref[0:1, at] + affine_ref[1:2, at]).astype(half))
+        normed = jnp.concatenate(tiles, axis=1)
         analyse(p, normed, table_ref[...], scale_ref[...], turn_ref, h)
 
     each_row(p, row)
@@ -258,7 +267,8 @@
     return hidden, slope
 
 
-BAND = 16
+BAND = 32
+COLUMNS = 256
 
 
 def widened(p, value):
@@ -337,10 +347,10 @@
     hid_ref,
     gpost_ref,
     gpre_ref,
-    wide_ref,
     slope_ref,
     gsh_ref,
     shr_ref,
+    glat_ref,
     turn_y_ref,
     turn_x_ref,
     acc1_ref,
@@ -381,44 +391,59 @@
                         ri * p.lat : (ri + 1) * p.lat, c * LANES : (c + 1) * LANES
                     ]
 
+    def bands(columns, body):
+        for low in range(0, count, BAND):
+            at = slice(low, low + BAND)
+            body(at, pl.ds(pl.multiple_of(base + low, BAND), BAND), columns)
+
+    def folded(value):
+        return value.reshape(BAND // 8, 8, value.shape[1]).sum(0)
+
     there(x_ref, lat_ref, base)
     there(g_ref, gsh_ref, 0)
-    wide_ref[...] = mul(lat_ref[pl.ds(base, count), :], w1_ref[...])
-
-    def first(i, carry):
-        at = pl.ds(pl.multiple_of(i * BAND, BAND), BAND)
-        hidden, slope = gelu_both(wide_ref[at, :] + bias_ref[0:1, :])
-        hid_ref[pl.ds(pl.multiple_of(base + i * BAND, BAND), BAND), :] = hidden.astype(half)
-        slope_ref[at, :] = slope
-        return carry
-
-    lax.fori_loop(0, count // BAND, first, 0)
-    wide_ref[...] = mul(hid_ref[pl.ds(base, count), :], w2_ref[...])
-
-    def second(i, carry):
-        at = pl.ds(pl.multiple_of(i * BAND, BAND), BAND)
-        post = wide_ref[at, :] + bias_ref[1:2, :]
-        inner = jnp.tanh(post * (1.0 / shrink_level))
-        shr_ref[at, :] = (post - shrink_level * inner).astype(half)
-        gpost = (gsh_ref[at, :].astype(single) * (inner * inner)).astype(half)
-        gpost_ref[pl.ds(pl.multiple_of(base + i * BAND, BAND), BAND), :] = gpost
-        gb_ref[8:16, :] += gpost.astype(single).reshape(BAND // 8, 8, 2 * p.lanes).sum(0)
-        return carry
-
-    lax.fori_loop(0, count // BAND, second, 0)
+    every = [slice(low, low + COLUMNS) for low in range(0, 2 * p.lanes, COLUMNS)]
+    lat = lat_ref[pl.ds(base, count), :]
+    for columns in every:
+        pre = mul(lat, w1_ref[:, columns])
+
+        def first(at, kept, columns):
+            hidden, slope = gelu_both(pre[at] + bias_ref[0:1, columns])
+            hid_ref[kept, columns] = hidden.astype(half)
+            slope_ref[at, columns] = slope
+
+        bands(columns, first)
+    hid = hid_ref[pl.ds(base, count), :]
+    for columns in every:
+        part = mul(hid, w2_ref[:, columns])
+        sums = [jnp.zeros((8, COLUMNS), single)]
+
+        def second(at, kept, columns):
+            post = part[at] + bias_ref[1:2, columns]
+            inner = jnp.tanh(post * (1.0 / shrink_level))
+            shr_ref[at, columns] = (post - shrink_level * inner).astype(half)
+            gpost = (gsh_ref[at, columns].astype(single) * (inner * inner)).astype(half)
+            gpost_ref[kept, columns] = gpost
+            sums[0] += folded(gpost.astype(single))
+
+        bands(columns, second)
+        gb_ref[8:16, columns] += sums[0]
     back(lambda rows, ri: shr_ref[rows, ri * p.lanes : (ri + 1) * p.lanes], turn_y_ref)
-    wide_ref[...] = mul(gpost_ref[pl.ds(base, count), :], w2_ref[...], NT)
-
-    def third(i, carry):
-        at = pl.ds(pl.multiple_of(i * BAND, BAND), BAND)
-        gpre = (wide_ref[at, :] * slope_ref[at, :]).astype(half)
-        gpre_ref[pl.ds(pl.multiple_of(base + i * BAND, BAND), BAND), :] = gpre
-        gb_ref[0:8, :] += gpre.astype(single).reshape(BAND // 8, 8, 2 * p.lanes).sum(0)
-        return carry
-
-    lax.fori_loop(0, count // BAND, third, 0)
-    shr_ref[...] = mul(gpre_ref[pl.ds(base, count), :], w1_ref[...], NT).astype(half)
-    back(lambda rows, ri: shr_ref[rows, ri * p.lanes : (ri + 1) * p.lanes], turn_x_ref)
+    gpost = gpost_ref[pl.ds(base, count), :]
+    for columns in every:
+        part = mul(gpost, w2_ref[columns, :], NT)
+        sums = [jnp.zeros((8, COLUMNS), single)]
+
+        def third(at, kept, columns):
+            gpre = (part[at] * slope_ref[at, columns]).astype(half)
+            gpre_ref[kept, columns] = gpre
+            sums[0] += folded(gpre.astype(single))
+
+        bands(columns, third)
+        gb_ref[0:8, columns] += sums[0]
+    gpre = gpre_ref[pl.ds(base, count), :]
+    for columns in every:
+        glat_ref[:, columns] = mul(gpre, w1_ref[columns, :], NT).astype(half)
+    back(lambda rows, ri: glat_ref[rows, ri * p.lanes : (ri + 1) * p.lanes], turn_x_ref)
 
     @pl.when(group == pl.num_programs(1) - 1)
     def _():
@@ -484,7 +509,7 @@
 def slope_sums_kernel(p, *refs):
     stat_refs = refs[: p.chan]
     rows_in_ref, tokens_ref, affine_ref, table_ref, wide_ref, sum_ref = refs[p.chan : p.chan + 6]
-    sums_ref, param_ref, rows_ref, part_ref, dense_ref = refs[p.chan + 6 :]
+    sums_ref, total_ref, param_ref, rows_ref, part_ref, dense_ref = refs[p.chan + 6 :]
     factor = 1.0 / math.sqrt(p.lon)
     count = 2 * p.stack
     moments(p, stat_refs, rows_ref)
@@ -495,21 +520,33 @@
 
     def row(h, slot):
         block = rows_in_ref[:, 0, 0, h].reshape(2 * MW, p.lanes)
-        normed_grad = mul(table_ref[...], block) * factor
-        each = expand(rows_ref[h], wide_ref[...])
-        wide = tokens_ref[0, h].astype(single)
-        centred = (wide - each[:, : p.lanes]) * each[:, p.lanes :]
-        product = normed_grad * centred
-        folds = (PACK * p.turn_pad // 8, 8, p.lanes)
-        param_ref[0:8, :] += product.reshape(folds).sum(0)
-        param_ref[8:16, :] += normed_grad.reshape(folds).sum(0)
-        gain = affine_ref[0:1, :]
-        part_ref[h] = summed(sum_ref[0], normed_grad * gain) + summed(sum_ref[1], product * gain)
+        folds = (PACK * p.turn_pad // 8, 8, LANES)
+        plain, scaled = [], []
+        spectrum = mul(table_ref[...], block)
+        for c, (mean, inverse) in enumerate(expand(p, rows_ref[h], wide_ref)):
+            at = slice(c * LANES, (c + 1) * LANES)
+            normed_grad = spectrum[:, at] * factor
+            centred = (tokens_ref[0, h, :, at].astype(single) - mean) * inverse
+            param_ref[0:8, at] += (normed_grad * centred).reshape(folds).sum(0)
+            param_ref[8:16, at] += normed_grad.reshape(folds).sum(0)
+            grad = normed_grad * affine_ref[0:1, at]
+            plain.append(grad.astype(half))
+            scaled.append((grad * centred).astype(half))
+        part_ref[h] = mul(sum_ref[0], jnp.concatenate(plain, axis=1), NT) + mul(
+            sum_ref[1], jnp.concatenate(scaled, axis=1), NT
+        )
 
     each_row(p, row)
     for h in range(p.rows):
         dense_ref[h * count : (h + 1) * count, :] = part_ref[h, :count, :]
     sums_ref[0] = dense_ref[...].astype(half)
+
+    @pl.when(pl.program_id(0) == pl.num_programs(0) - 1)
+    def _():
+        for kind in range(2):
+            total_ref[kind : kind + 1, :] = param_ref[8 * kind : 8 * kind + 8, :].sum(
+                0, keepdims=True
+            )
 
 
 def input_grad_kernel(p, *refs):
@@ -529,14 +566,17 @@
 
     def row(h, slot):
         block = rows_in_ref[:, 0, 0, h].reshape(2 * MW, p.lanes)
-        normed_grad = mul(table_ref[...], block) * factor
-        each = expand(rows_ref[h], wide_ref[...])
-        means = expand(part_ref[h], wide_ref[...])
-        inverse = each[:, p.lanes :]
-        centred = (tokens_ref[0, h].astype(single) - each[:, : p.lanes]) * inverse
-        grad = inverse * (
-            normed_grad * affine_ref[0:1, :] - means[:, : p.lanes] - centred * means[:, p.lanes :]
-        )
+        spectrum = mul(table_ref[...], block)
+        moment = expand(p, rows_ref[h], wide_ref)
+        means = expand(p, part_ref[h], wide_ref)
+        tiles = []
+        for c in range(p.tiles):
+            at = slice(c * LANES, (c + 1) * LANES)
+            (mean, inverse), (first, second) = moment[c], means[c]
+            centred = (tokens_ref[0, h, :, at].astype(single) - mean) * inverse
+            grad = spectrum[:, at] * factor * affine_ref[0:1, at]
+            tiles.append(inverse * (grad - first - centred * second))
+        grad = jnp.concatenate(tiles, axis=1)
         scatter_row(p, grad, words_ref.at[slot], out_ref, h)
 
     each_row(p, row)
@@ -624,6 +664,7 @@
         sums[1, p.stack + s] = lane_owner == s
         wide[:, s, 0] = lane_owner == s
         wide[:, p.stack + s, 1] = lane_owner == s
+    wide = wide.reshape(24, 2, p.tiles, LANES).transpose(0, 2, 1, 3)
     return jnp.asarray(sums, half), jnp.asarray(wide.reshape(24, 2 * p.lanes), half)
 
 
@@ -745,7 +786,7 @@
             [*outs, totals],
             [*out_specs, whole_spec(totals)],
             [pltpu.VMEM((16, wide_lanes), single), pltpu.VMEM((2, wide_lanes), single)]
-            + [kept] * 4 + [held] * 2 + [brief] * 2 + [turn_out] * 2
+            + [kept] * 4 + [held] + [brief] * 3 + [turn_out] * 2
             + [pltpu.VMEM((wide_lanes, wide_lanes), single)] * 2
             + [pltpu.VMEM((wide_lanes, wide_lanes), half)] * 2,
             12 * size * p.modes * p.lat * wide_lanes * wide_lanes,
@@ -762,7 +803,7 @@
         tail = (affine, slope_table, wide_table, sum_table)
         outs = [
             jax.ShapeDtypeStruct((size, count, tokens_rows), half),
-            jax.ShapeDtypeStruct((16, p.lanes), single),
+            jax.ShapeDtypeStruct((2, p.lanes), single),
         ]
         return call(
             functools.partial(slope_sums_kernel, p), grid,
@@ -770,7 +811,10 @@
             [pack_spec(s) for s in stats] + [peer_spec(rows_in, which), pack_spec(tokens)]
             + [whole_spec(v) for v in tail],
             outs, [pack_spec(outs[0]), whole_spec(outs[1])],
-            [rows_scratch, rows_scratch, pltpu.VMEM((count, tokens_rows), single)],
+            [
+                pltpu.VMEM((16, p.lanes), single), rows_scratch, rows_scratch,
+                pltpu.VMEM((count, tokens_rows), single),
+            ],
             dft_flops,
         )
 
@@ -814,7 +858,7 @@
     grads = flat[: 4 * size_w].reshape((2,) + w_first.shape)
     bias_grads = flat[4 * size_w : 4 * size_w + 4 * p.groups].reshape((2,) + b_first.shape)
     params = reduced(p, params0 + params1, single)
-    params = params.reshape(2, 8, p.stack, size_w).sum((1, 2))
+    params = params.reshape(2, p.stack, size_w).sum(1)
     return (
         mixed, grad_input, grads[0], bias_grads[0], grads[1], bias_grads[1], params[0], params[1]
     )

time: 411 us -> 388 us (0.944)
  Pallas kernels: 211 us -> 180 us
  waiting for transfers between devices: 53.9 us -> 60.7 us
    pallas_call x14, Pallas kernels: 211 us -> 180 us  [_call(): pl.pallas_call(body, grid=grid, in_specs=in_specs, out_specs=out_specs, o...]
    all_to_all x4, waiting for transfers between devices: 13.9 us -> 20.7 us  [exchange(): return lax.all_to_all(value, 'space', 0, 0, tiled=True)]
  transfers between devices with their start and end apart: 22 -> 22, of which waited for: 6 -> 7; matrix products, arithmetic and copies ran while one was open for 2% -> 2% of each run, Pallas kernels for 39% -> 33%
where the time goes in v3:
time: 388 us; the launch traced here: 387 us
  Pallas kernels  180 us (46%)
  blocking collectives  91.9 us (24%)
  waiting for transfers between devices  60.7 us (16%)
  starting transfers between devices  45.1 us (12%)
  local copies, waits for them, and re-layouts  4.75 us (1%)
  other arithmetic  4.23 us (1%)
    pallas_call x14, Pallas kernels, _call(): pl.pallas_call(body, grid=grid, in_specs=in_specs, out_specs=out_specs, o...  180 us
    all_to_all x2, blocking collectives, exchange(): return lax.all_to_all(value, 'space', 0, 0, tiled=True)  91.9 us
    ppermute x6, waiting for transfers between devices, reduced(): other = lax.ppermute(own, 'space', [(i, i ^ step) for i in range(p.space)])  35.4 us
    all_to_all x4, waiting for transfers between devices, exchange(): return lax.all_to_all(value, 'space', 0, 0, tiled=True)  20.7 us
    ppermute x12, starting transfers between devices, around(): lax.ppermute(value, axis, [(i, (i + step) % size) for i in range(size)])  20.5 us
    all_to_all x4, starting transfers between devices, exchange(): return lax.all_to_all(value, 'space', 0, 0, tiled=True)  19.1 us
  transfers between devices with their start and end apart: 22, of which 7 were waited for; matrix products, arithmetic and copies ran while one was open for 2% of the time, Pallas kernels for 33%

profile of v3, /device:TPU:0, one launch (start us, length us, event | category | flops | bytes accessed | tf_op | source)
XLA Modules:
  0.0 387.2 jit_solution(12223185124311220475)
XLA Ops:
  0.6 6.6 %shard_map.229 = bf16[8,1,2,8,24,384]{5,4,3,2,1,0:T(8,128)(2,1)} custom-call(bf16[8,12,2,17280]{3,2,1,0:T(2,128)(2,1)} %stored_ref.7, bf16[128,192]{1,0:T(8,128)(2,1)} %constant.20.clone.table_ref.refs_6_, f32[128,1]{1,0:T(8,128)} %constant.22.clone.scale_ref), custom_call_target="tpu_custom_call" | custom-call | flops 452984832 | bytes 9044480 | tf_op jit(solution)/shard_map/pallas_call | solution.py:614
  7.2 5.2 %all-to-all-start.2 = ((bf16[8,1,2,8,24,384]{5,4,3,2,1,0:T(8,128)(2,1)}), bf16[8,1,2,8,24,384]{5,4,3,2,1,0:T(8,128)(2,1)}, u32[]{:S(2)}, u32[]{:S(2)}) async-start(bf16[8,1,2,8,24,384]{5,4,3,2,1,0:T(8,128)(2,1)} %shard_map.229), calls=%async_computation.2 | async-start | bytes 4718592 | tf_op jit(solution)/shard_map/all_to_all | solution.py:672
  12.4 8.4 %shard_map.227 = (bf16[2,12,192,384]{3,2,1,0:T(8,128)(2,1)}, f32[2,48,192]{2,1,0:T(8,128)}) custom-call(bf16[8,12,2,17280]{3,2,1,0:T(2,128)(2,1)} %stored_ref.6, bf16[2,8,384]{2,1,0:T(8,128)(2,1)} %constant.27.clone.sum_ref.refs_9_), custom_call_target="tpu_custom_call" | custom-call | flops 113246208 | bytes 10260480 | tf_op jit(solution)/shard_map/pallas_call | solution.py:614
  20.8 2.2 collective-permute-start.3
  23.0 2.6 collective-permute-start.4
  25.6 1.4 collective-permute-start.5
  27.0 0.8 pad_maximum_fusion
  27.8 0.6 reshape.32.refs_5_.refs_6_.refs_10_
  28.4 0.7 collective-permute-done.3.refs_1_
  29.1 3.9 collective-permute-done.4.refs_2_
  33.0 0.6 jit_solution_.3.refs_7_
  33.6 10.1 %shard_map.228 = bf16[8,1,2,8,24,384]{5,4,3,2,1,0:T(8,128)(2,1)} custom-call(f32[2,48,192]{2,1,0:T(8,128)} %get-tuple-element.23.refs_0_, f32[2,48,192]{2,1,0:T(8,128)} %collective-permute-done.3.refs_1_, f32[2,48,192]{2,1,0:T(8,128)} %collective-permute-done.4.refs_2_, f32[2,48,192]{2,1,0:T(8,128)} %collective-permute-done.5.refs_3_, ...), custom_call_target="tpu_custom_call" | custom-call | flops 452984832 | bytes 6282752 | tf_op jit(solution)/shard_map/pallas_call | solution.py:614
  43.7 4.4 %all-to-all-start.1 = ((bf16[8,1,2,8,24,384]{5,4,3,2,1,0:T(8,128)(2,1)}), bf16[8,1,2,8,24,384]{5,4,3,2,1,0:T(8,128)(2,1)}, u32[]{:S(2)}, u32[]{:S(2)}) async-start(bf16[8,1,2,8,24,384]{5,4,3,2,1,0:T(8,128)(2,1)} %shard_map.228), calls=%async_computation.1 | async-start | bytes 4718592 | tf_op jit(solution)/shard_map/all_to_all | solution.py:672
  48.1 8.4 %shard_map.224 = (bf16[2,12,192,384]{3,2,1,0:T(8,128)(2,1)}, f32[2,48,192]{2,1,0:T(8,128)}) custom-call(bf16[8,12,2,17280]{3,2,1,0:T(2,128)(2,1)} %stored_ref.6, bf16[2,8,384]{2,1,0:T(8,128)(2,1)} %constant.27.clone.sum_ref.refs_9_), custom_call_target="tpu_custom_call" | custom-call | flops 113246208 | bytes 10260480 | tf_op jit(solution)/shard_map/pallas_call | solution.py:614
  56.5 2.6 collective-permute-start
  59.1 1.6 collective-permute-start.1
  60.8 0.7 collective-permute-start.2
  61.5 6.6 %shard_map.225.refs_9_ = bf16[8,2,2,8,24,384]{5,4,3,2,1,0:T(8,128)(2,1)} custom-call(bf16[8,12,2,17280]{3,2,1,0:T(2,128)(2,1)} %stored_ref.7, bf16[128,192]{1,0:T(8,128)(2,1)} %constant.20.clone.table_ref.refs_6_, f32[128,1]{1,0:T(8,128)} %constant.22.clone.scale_ref), custom_call_target="tpu_custom_call" | custom-call | flops 452984832 | bytes 11403776 | tf_op jit(solution)/shard_map/pallas_call | solution.py:614
  68.1 10.1 %shard_map.226 = bf16[8,2,2,8,24,384]{5,4,3,2,1,0:T(8,128)(2,1)} custom-call(f32[2,48,192]{2,1,0:T(8,128)} %get-tuple-element.21.refs_0_, f32[2,48,192]{2,1,0:T(8,128)} %collective-permute-done.refs_1_, f32[2,48,192]{2,1,0:T(8,128)} %collective-permute-done.1.refs_2_, f32[2,48,192]{2,1,0:T(8,128)} %collective-permute-done.2.refs_3_, ...), custom_call_target="tpu_custom_call", output_to_operand_aliasing={{}: (9, {})} | custom-call | flops 452984832 | bytes 13360640 | tf_op jit(solution)/shard_map/pallas_call | solution.py:614
  78.2 4.8 %all-to-all-start = ((bf16[8,2,2,8,24,384]{5,4,3,2,1,0:T(8,128)(2,1)}), bf16[8,2,2,8,24,384]{5,4,3,2,1,0:T(8,128)(2,1)}, u32[]{:S(2)}, u32[]{:S(2)}) async-start(bf16[8,2,2,8,24,384]{5,4,3,2,1,0:T(8,128)(2,1)} %shard_map.226), calls=%async_computation | async-start | bytes 9437184 | tf_op jit(solution)/shard_map/all_to_all | solution.py:672
  83.0 33.9 %shard_map.230 = (bf16[8,2,2,12,16,384]{5,4,3,2,1,0:T(8,128)(2,1)}, f32[776,128]{1,0:T(8,128)}) custom-call(bf16[8,1,2,8,24,384]{5,4,3,2,1,0:T(8,128)(2,1)} %all-to-all-done.1.x_ref, bf16[8,1,2,8,24,384]{5,4,3,2,1,0:T(8,128)(2,1)} %all-to-all-done.2.g_ref, bf16[192,192]{1,0:T(8,128)(2,1)} %constant.25.clone.there_ref, ...), custom_call_target="tpu_custom_call" | custom-call | flops 10871635968 | bytes 10132480 | tf_op jit(solution)/shard_map/pallas_call | solution.py:614
  116.9 20.7 %all-to-all-done.x_ref.g_ref = bf16[8,2,2,8,24,384]{5,4,3,2,1,0:T(8,128)(2,1)} async-done(((bf16[8,2,2,8,24,384]{5,4,3,2,1,0:T(8,128)(2,1)}), bf16[8,2,2,8,24,384]{5,4,3,2,1,0:T(8,128)(2,1)}, u32[]{:S(2)}, u32[]{:S(2)}) %all-to-all-start) | async-done | bytes 4718624 | tf_op jit(solution)/shard_map/all_to_all | solution.py:672
  137.5 34.0 %shard_map.231 = (bf16[8,1,2,12,16,384]{5,4,3,2,1,0:T(8,128)(2,1)}, bf16[8,1,2,12,16,384]{5,4,3,2,1,0:T(8,128)(2,1)}, bf16[776,128]{1,0:T(8,128)(2,1)}) custom-call(bf16[8,2,2,8,24,384]{5,4,3,2,1,0:T(8,128)(2,1)} %all-to-all-done.x_ref.g_ref, bf16[8,2,2,8,24,384]{5,4,3,2,1,0:T(8,128)(2,1)} %all-to-all-done.x_ref.g_ref, ...), custom_call_target="tpu_custom_call" | custom-call | flops 10871635968 | bytes 15049728 | tf_op jit(solution)/shard_map/pallas_call | solution.py:614
  171.5 34.0 %all_to_all.30.refs_4_.refs_8_ = bf16[8,1,2,12,16,384]{5,4,3,2,1,0:T(8,128)(2,1)} all-to-all(bf16[8,1,2,12,16,384]{5,4,3,2,1,0:T(8,128)(2,1)} %get-tuple-element.28), channel_id=1, replica_groups=mesh['space'=8,'chan'=4] {'space'}, dimensions={0} | all-to-all | bytes 4718592 | tf_op jit(solution)/shard_map/all_to_all | solution.py:672
  205.5 57.9 %all_to_all.31.rows_ref.refs_4_.refs_8_ = bf16[8,2,2,12,16,384]{5,4,3,2,1,0:T(8,128)(2,1)} all-to-all(bf16[8,2,2,12,16,384]{5,4,3,2,1,0:T(8,128)(2,1)S(1)} %copy-done), channel_id=1, replica_groups=mesh['space'=8,'chan'=4] {'space'}, dimensions={0} | all-to-all | bytes 9437184 | tf_op jit(solution)/shard_map/all_to_all | solution.py:672
  263.4 4.8 %all-to-all-start.3 = ((bf16[8,1,2,12,16,384]{5,4,3,2,1,0:T(8,128)(2,1)}), bf16[8,1,2,12,16,384]{5,4,3,2,1,0:T(8,128)(2,1)}, u32[]{:S(2)}, u32[]{:S(2)}) async-start(bf16[8,1,2,12,16,384]{5,4,3,2,1,0:T(8,128)(2,1)} %get-tuple-element.26), calls=%async_computation.3 | async-start | bytes 4718592 | tf_op jit(solution)/shard_map/all_to_all | solution.py:672
  268.4 1.6 collective-permute-done.12
  270.0 1.7 collective-permute-start.13
  271.7 28.9 %collective-permute-done.13 = bf16[776,128]{1,0:T(8,128)(2,1)S(1)} collective-permute-done((bf16[776,128]{1,0:T(8,128)(2,1)S(1)}, bf16[776,128]{1,0:T(8,128)(2,1)S(1)}, u32[]{:S(2)}, u32[]{:S(2)}) %collective-permute-start.13) | collective-permute-done | bytes 198688 | tf_op jit(solution)/shard_map/ppermute | solution.py:688
  300.7 1.6 collective-permute-start.14
  302.3 4.9 %collective-permute-done.14 = bf16[776,128]{1,0:T(8,128)(2,1)S(1)} collective-permute-done((bf16[776,128]{1,0:T(8,128)(2,1)S(1)}, bf16[776,128]{1,0:T(8,128)(2,1)S(1)}, u32[]{:S(2)}, u32[]{:S(2)}) %collective-permute-start.14) | collective-permute-done | bytes 198688 | tf_op jit(solution)/shard_map/ppermute | solution.py:688
  307.2 0.7 copy-done.1
  308.0 0.8 fusion.1
  308.7 11.3 %shard_map.234 = (bf16[2,48,192]{2,1,0:T(8,128)(2,1)}, f32[2,384]{1,0:T(2,128)}) custom-call(f32[2,48,192]{2,1,0:T(8,128)} %get-tuple-element.21.refs_0_, f32[2,48,192]{2,1,0:T(8,128)} %collective-permute-done.refs_1_, f32[2,48,192]{2,1,0:T(8,128)} %collective-permute-done.1.refs_2_, f32[2,48,192]{2,1,0:T(8,128)} %collective-permute-done.2.refs_3_, ...), custom_call_target="tpu_custom_call" | custom-call | flops 452984832 | bytes 6334464 | tf_op jit(solution)/shard_map/pallas_call | solution.py:614
  320.0 11.3 %shard_map.235 = (bf16[2,48,192]{2,1,0:T(8,128)(2,1)}, f32[2,384]{1,0:T(2,128)}) custom-call(f32[2,48,192]{2,1,0:T(8,128)} %get-tuple-element.23.refs_0_, f32[2,48,192]{2,1,0:T(8,128)} %collective-permute-done.3.refs_1_, f32[2,48,192]{2,1,0:T(8,128)} %collective-permute-done.4.refs_2_, f32[2,48,192]{2,1,0:T(8,128)} %collective-permute-done.5.refs_3_, ...), custom_call_target="tpu_custom_call" | custom-call | flops 452984832 | bytes 8693760 | tf_op jit(solution)/shard_map/pallas_call | solution.py:614
  331.3 0.7 add.24
  332.0 1.3 fusion
  333.4 1.6 collective-permute-start.10
  334.9 3.4 collective-permute-start.11
  338.3 1.0 collective-permute-start.6
  340.4 7.7 %shard_map.232.refs_2_ = bf16[8,12,2,17280]{3,2,1,0:T(2,128)(2,1)} custom-call(bf16[8,2,2,12,16,384]{5,4,3,2,1,0:T(8,128)(2,1)} %all_to_all.31.rows_ref.refs_4_.refs_8_, bf16[192,128]{1,0:T(8,128)(2,1)} %constant.23.clone.table_ref.refs_1_), custom_call_target="tpu_custom_call" | custom-call | flops 452984832 | bytes 11403264 | tf_op jit(solution)/shard_map/pallas_call | solution.py:614
  348.1 1.3 add.26
  349.4 1.6 collective-permute-start.17
  350.9 7.7 %shard_map.233 = bf16[8,12,2,17280]{3,2,1,0:T(2,128)(2,1)} custom-call(bf16[8,1,2,12,16,384]{5,4,3,2,1,0:T(8,128)(2,1)} %all-to-all-done.3.refs_0_, bf16[192,128]{1,0:T(8,128)(2,1)} %constant.23.clone.table_ref.refs_1_, bf16[8,12,2,17280]{3,2,1,0:T(2,128)(2,1)} %shard_map.232.refs_2_), custom_call_target="tpu_custom_call", output_to_operand_aliasing={{}: (2, {})} | custom-call | flops 452984832 | bytes 15679488 | tf_op jit(solution)/shard_map/pallas_call | solution.py:614
  358.7 3.4 collective-permute-start.7
  362.1 0.7 add.27
  363.5 11.9 %shard_map.236.refs_13_ = bf16[8,12,2,17280]{3,2,1,0:T(2,128)(2,1)} custom-call(f32[2,48,192]{2,1,0:T(8,128)} %get-tuple-element.23.refs_0_, f32[2,48,192]{2,1,0:T(8,128)} %collective-permute-done.3.refs_1_, f32[2,48,192]{2,1,0:T(8,128)} %collective-permute-done.4.refs_2_, f32[2,48,192]{2,1,0:T(8,128)} %collective-permute-done.5.refs_3_, ...), custom_call_target="tpu_custom_call" | custom-call | flops 452984832 | bytes 15424512 | tf_op jit(solution)/shard_map/pallas_call | solution.py:614
  375.4 11.9 %shard_map.237 = bf16[8,12,2,17280]{3,2,1,0:T(2,128)(2,1)} custom-call(f32[2,48,192]{2,1,0:T(8,128)} %get-tuple-element.21.refs_0_, f32[2,48,192]{2,1,0:T(8,128)} %collective-permute-done.refs_1_, f32[2,48,192]{2,1,0:T(8,128)} %collective-permute-done.1.refs_2_, f32[2,48,192]{2,1,0:T(8,128)} %collective-permute-done.2.refs_3_, ...), custom_call_target="tpu_custom_call", output_to_operand_aliasing={{}: (13, {})} | custom-call | flops 452984832 | bytes 19700736 | tf_op jit(solution)/shard_map/pallas_call | solution.py:614
  (33 shorter events, 2.2 us)
Async XLA Ops:
  7.2 36.4 %all-to-all-start.2 = ((bf16[8,1,2,8,24,384]{5,4,3,2,1,0:T(8,128)(2,1)}), bf16[8,1,2,8,24,384]{5,4,3,2,1,0:T(8,128)(2,1)}, u32[]{:S(2)}, u32[]{:S(2)}) async-start(bf16[8,1,2,8,24,384]{5,4,3,2,1,0:T(8,128)(2,1)} %shard_map.229), calls=%async_computation.2 | async-start | bytes 4718592 | tf_op jit(solution)/shard_map/all_to_all | solution.py:672
  20.8 8.3 %collective-permute-start.3 = (f32[2,48,192]{2,1,0:T(8,128)}, f32[2,48,192]{2,1,0:T(8,128)}, u32[]{:S(2)}, u32[]{:S(2)}) collective-permute-start(f32[2,48,192]{2,1,0:T(8,128)} %get-tuple-element.23.refs_0_), channel_id=1, source_target_pairs={{0,1},{1,2},{2,3},{3,0},{4,5},{5,6},{6,7},{7,4},{8,9},{9,10},{10,1... | collective-permute-start | bytes 221192 | tf_op jit(solution)/shard_map/ppermute | solution.py:679
  23.0 9.9 %collective-permute-start.4 = (f32[2,48,192]{2,1,0:T(8,128)}, f32[2,48,192]{2,1,0:T(8,128)}, u32[]{:S(2)}, u32[]{:S(2)}) collective-permute-start(f32[2,48,192]{2,1,0:T(8,128)} %get-tuple-element.23.refs_0_), channel_id=1, source_target_pairs={{0,2},{1,3},{2,0},{3,1},{4,6},{5,7},{6,4},{7,5},{8,10},{9,11},{10,... | collective-permute-start | bytes 221192 | tf_op jit(solution)/shard_map/ppermute | solution.py:679
  25.6 7.4 %collective-permute-start.5 = (f32[2,48,192]{2,1,0:T(8,128)}, f32[2,48,192]{2,1,0:T(8,128)}, u32[]{:S(2)}, u32[]{:S(2)}) collective-permute-start(f32[2,48,192]{2,1,0:T(8,128)} %get-tuple-element.23.refs_0_), channel_id=1, source_target_pairs={{0,3},{1,0},{2,1},{3,2},{4,7},{5,4},{6,5},{7,6},{8,11},{9,8},{10,9... | collective-permute-start | bytes 221192 | tf_op jit(solution)/shard_map/ppermute | solution.py:679
  43.7 34.5 %all-to-all-start.1 = ((bf16[8,1,2,8,24,384]{5,4,3,2,1,0:T(8,128)(2,1)}), bf16[8,1,2,8,24,384]{5,4,3,2,1,0:T(8,128)(2,1)}, u32[]{:S(2)}, u32[]{:S(2)}) async-start(bf16[8,1,2,8,24,384]{5,4,3,2,1,0:T(8,128)(2,1)} %shard_map.228), calls=%async_computation.1 | async-start | bytes 4718592 | tf_op jit(solution)/shard_map/all_to_all | solution.py:672
  56.5 11.5 %collective-permute-start = (f32[2,48,192]{2,1,0:T(8,128)}, f32[2,48,192]{2,1,0:T(8,128)}, u32[]{:S(2)}, u32[]{:S(2)}) collective-permute-start(f32[2,48,192]{2,1,0:T(8,128)} %get-tuple-element.21.refs_0_), channel_id=1, source_target_pairs={{0,1},{1,2},{2,3},{3,0},{4,5},{5,6},{6,7},{7,4},{8,9},{9,10},{10,1... | collective-permute-start | bytes 221192 | tf_op jit(solution)/shard_map/ppermute | solution.py:679
  59.1 9.0 %collective-permute-start.1 = (f32[2,48,192]{2,1,0:T(8,128)}, f32[2,48,192]{2,1,0:T(8,128)}, u32[]{:S(2)}, u32[]{:S(2)}) collective-permute-start(f32[2,48,192]{2,1,0:T(8,128)} %get-tuple-element.21.refs_0_), channel_id=1, source_target_pairs={{0,2},{1,3},{2,0},{3,1},{4,6},{5,7},{6,4},{7,5},{8,10},{9,11},{10,... | collective-permute-start | bytes 221192 | tf_op jit(solution)/shard_map/ppermute | solution.py:679
  60.8 7.4 %collective-permute-start.2 = (f32[2,48,192]{2,1,0:T(8,128)}, f32[2,48,192]{2,1,0:T(8,128)}, u32[]{:S(2)}, u32[]{:S(2)}) collective-permute-start(f32[2,48,192]{2,1,0:T(8,128)} %get-tuple-element.21.refs_0_), channel_id=1, source_target_pairs={{0,3},{1,0},{2,1},{3,2},{4,7},{5,4},{6,5},{7,6},{8,11},{9,8},{10,9... | collective-permute-start | bytes 221192 | tf_op jit(solution)/shard_map/ppermute | solution.py:679
  78.2 59.3 %all-to-all-start = ((bf16[8,2,2,8,24,384]{5,4,3,2,1,0:T(8,128)(2,1)}), bf16[8,2,2,8,24,384]{5,4,3,2,1,0:T(8,128)(2,1)}, u32[]{:S(2)}, u32[]{:S(2)}) async-start(bf16[8,2,2,8,24,384]{5,4,3,2,1,0:T(8,128)(2,1)} %shard_map.226), calls=%async_computation | async-start | bytes 9437184 | tf_op jit(solution)/shard_map/all_to_all | solution.py:672
  171.5 34.0 %copy-start = (bf16[8,2,2,12,16,384]{5,4,3,2,1,0:T(8,128)(2,1)S(1)}, bf16[8,2,2,12,16,384]{5,4,3,2,1,0:T(8,128)(2,1)}, u32[]{:S(2)}) copy-start(bf16[8,2,2,12,16,384]{5,4,3,2,1,0:T(8,128)(2,1)} %get-tuple-element.27) | copy-start | bytes 14155780
  263.4 4.8 %copy-start.2 = (bf16[776,128]{1,0:T(8,128)(2,1)S(1)}, bf16[776,128]{1,0:T(8,128)(2,1)}, u32[]{:S(2)}) copy-start(bf16[776,128]{1,0:T(8,128)(2,1)} %get-tuple-element.31) | copy-start | bytes 595972
  263.4 87.5 %all-to-all-start.3 = ((bf16[8,1,2,12,16,384]{5,4,3,2,1,0:T(8,128)(2,1)}), bf16[8,1,2,12,16,384]{5,4,3,2,1,0:T(8,128)(2,1)}, u32[]{:S(2)}, u32[]{:S(2)}) async-start(bf16[8,1,2,12,16,384]{5,4,3,2,1,0:T(8,128)(2,1)} %get-tuple-element.26), calls=%async_computation.3 | async-start | bytes 4718592 | tf_op jit(solution)/shard_map/all_to_all | solution.py:672
  268.2 1.7 collective-permute-start.12
  270.0 30.7 %collective-permute-start.13 = (bf16[776,128]{1,0:T(8,128)(2,1)S(1)}, bf16[776,128]{1,0:T(8,128)(2,1)S(1)}, u32[]{:S(2)}, u32[]{:S(2)}) collective-permute-start(bf16[776,128]{1,0:T(8,128)(2,1)S(1)} %add_convert_fusion.1), channel_id=1, source_target_pairs={{0,8},{4,12},{8,0},{12,4},{16,24},{20,28},{24,16},{28,20},{1,9},{5... | collective-permute-start | bytes 595976 | tf_op jit(solution)/shard_map/ppermute | solution.py:688
  300.7 6.5 %collective-permute-start.14 = (bf16[776,128]{1,0:T(8,128)(2,1)S(1)}, bf16[776,128]{1,0:T(8,128)(2,1)S(1)}, u32[]{:S(2)}, u32[]{:S(2)}) collective-permute-start(bf16[776,128]{1,0:T(8,128)(2,1)S(1)} %add_convert_fusion), channel_id=1, source_target_pairs={{0,16},{4,20},{8,24},{12,28},{16,0},{20,4},{24,8},{28,12},{1,17},{... | collective-permute-start | bytes 595976 | tf_op jit(solution)/shard_map/ppermute | solution.py:688
  307.2 0.8 copy-start.1
  332.0 7.3 %collective-permute-start.15 = (f32[2,384]{1,0:T(2,128)S(1)}, f32[2,384]{1,0:T(2,128)S(1)}, u32[]{:S(2)}, u32[]{:S(2)}) collective-permute-start(f32[2,384]{1,0:T(2,128)S(1)} %add.24), channel_id=1, source_target_pairs={{0,4},{4,0},{8,12},{12,8},{16,20},{20,16},{24,28},{28,24},{1,5},{5... | collective-permute-start | bytes 9224 | tf_op jit(solution)/shard_map/ppermute | solution.py:688
  333.4 30.1 %collective-permute-start.10 = (bf16[2,48,192]{2,1,0:T(8,128)(2,1)}, bf16[2,48,192]{2,1,0:T(8,128)(2,1)}, u32[]{:S(2)}, u32[]{:S(2)}) collective-permute-start(bf16[2,48,192]{2,1,0:T(8,128)(2,1)} %get-tuple-element.30.refs_4_), channel_id=1, source_target_pairs={{0,2},{1,3},{2,0},{3,1},{4,6},{5,7},{6,4},{7,5},{8,10},{9,11},{10,... | collective-permute-start | bytes 110600 | tf_op jit(solution)/shard_map/ppermute | solution.py:679
  334.9 28.5 %collective-permute-start.11 = (bf16[2,48,192]{2,1,0:T(8,128)(2,1)}, bf16[2,48,192]{2,1,0:T(8,128)(2,1)}, u32[]{:S(2)}, u32[]{:S(2)}) collective-permute-start(bf16[2,48,192]{2,1,0:T(8,128)(2,1)} %get-tuple-element.30.refs_4_), channel_id=1, source_target_pairs={{0,3},{1,0},{2,1},{3,2},{4,7},{5,4},{6,5},{7,6},{8,11},{9,8},{10,9... | collective-permute-start | bytes 110600 | tf_op jit(solution)/shard_map/ppermute | solution.py:679
  338.3 25.2 %collective-permute-start.9 = (bf16[2,48,192]{2,1,0:T(8,128)(2,1)}, bf16[2,48,192]{2,1,0:T(8,128)(2,1)}, u32[]{:S(2)}, u32[]{:S(2)}) collective-permute-start(bf16[2,48,192]{2,1,0:T(8,128)(2,1)} %get-tuple-element.30.refs_4_), channel_id=1, source_target_pairs={{0,1},{1,2},{2,3},{3,0},{4,5},{5,6},{6,7},{7,4},{8,9},{9,10},{10,1... | collective-permute-start | bytes 110600 | tf_op jit(solution)/shard_map/ppermute | solution.py:679
  338.3 37.0 %collective-permute-start.6 = (bf16[2,48,192]{2,1,0:T(8,128)(2,1)}, bf16[2,48,192]{2,1,0:T(8,128)(2,1)}, u32[]{:S(2)}, u32[]{:S(2)}) collective-permute-start(bf16[2,48,192]{2,1,0:T(8,128)(2,1)} %get-tuple-element.29.refs_4_), channel_id=1, source_target_pairs={{0,1},{1,2},{2,3},{3,0},{4,5},{5,6},{6,7},{7,4},{8,9},{9,10},{10,1... | collective-permute-start | bytes 110600 | tf_op jit(solution)/shard_map/ppermute | solution.py:679
  339.9 8.3 %collective-permute-start.16 = (f32[2,384]{1,0:T(2,128)}, f32[2,384]{1,0:T(2,128)}, u32[]{:S(2)}, u32[]{:S(2)}) collective-permute-start(f32[2,384]{1,0:T(2,128)} %add.25), channel_id=1, source_target_pairs={{0,8},{4,12},{8,0},{12,4},{16,24},{20,28},{24,16},{28,20},{1,9},{5... | collective-permute-start | bytes 9224 | tf_op jit(solution)/shard_map/ppermute | solution.py:688
  349.4 9.3 %collective-permute-start.17 = (f32[2,384]{1,0:T(2,128)}, f32[2,384]{1,0:T(2,128)}, u32[]{:S(2)}, u32[]{:S(2)}) collective-permute-start(f32[2,384]{1,0:T(2,128)} %add.26), channel_id=1, source_target_pairs={{0,16},{4,20},{8,24},{12,28},{16,0},{20,4},{24,8},{28,12},{1,17},{... | collective-permute-start | bytes 9224 | tf_op jit(solution)/shard_map/ppermute | solution.py:688
  358.7 16.7 %collective-permute-start.7 = (bf16[2,48,192]{2,1,0:T(8,128)(2,1)}, bf16[2,48,192]{2,1,0:T(8,128)(2,1)}, u32[]{:S(2)}, u32[]{:S(2)}) collective-permute-start(bf16[2,48,192]{2,1,0:T(8,128)(2,1)} %get-tuple-element.29.refs_4_), channel_id=1, source_target_pairs={{0,2},{1,3},{2,0},{3,1},{4,6},{5,7},{6,4},{7,5},{8,10},{9,11},{10,... | collective-permute-start | bytes 110600 | tf_op jit(solution)/shard_map/ppermute | solution.py:679
  363.5 11.9 %collective-permute-start.8 = (bf16[2,48,192]{2,1,0:T(8,128)(2,1)}, bf16[2,48,192]{2,1,0:T(8,128)(2,1)}, u32[]{:S(2)}, u32[]{:S(2)}) collective-permute-start(bf16[2,48,192]{2,1,0:T(8,128)(2,1)} %get-tuple-element.29.refs_4_), channel_id=1, source_target_pairs={{0,3},{1,0},{2,1},{3,2},{4,7},{5,4},{6,5},{7,6},{8,11},{9,8},{10,9... | collective-permute-start | bytes 110600 | tf_op jit(solution)/shard_map/ppermute | solution.py:679

commit v4 on v3

--- a/solution.py
+++ b/solution.py
@@ -53,6 +53,8 @@
         self.turn = self.lon // PACK
         self.turn_pad = -(-self.turn // 16) * 16
         self.words = self.long // LANES
+        self.step = SLOTS if self.rows % SLOTS == 0 else self.rows
+        self.steps = self.rows // self.step
         self.word_pad = self.tiles * self.turn_pad
         self.channels = self.groups * width * chan
 
@@ -138,24 +140,28 @@
 
 
 def clear_tail(p, words_ref):
-    @pl.when(pl.program_id(0) == 0)
+    @pl.when(first_step())
     def _():
         tail = p.word_pad - p.words
         words_ref[:, :, p.words :, :] = jnp.zeros(words_ref.shape[:2] + (tail, LANES), single)
 
 
-def each_row(p, body):
-    side = SLOTS if p.rows % SLOTS == 0 else 1
-
-    def step(i, carry):
-        for slot in range(side):
-            body(i * side + slot, slot)
-        return carry
-
-    lax.fori_loop(0, p.rows // side, step, 0)
+def first_step():
+    return (pl.program_id(0) == 0) & (pl.program_id(1) == 0)
+
+
+def last_step():
+    return (pl.program_id(0) == pl.num_programs(0) - 1) & (
+        pl.program_id(1) == pl.num_programs(1) - 1
+    )
+
+
+def last_part():
+    return pl.program_id(1) == pl.num_programs(1) - 1
 
 
 def analyse(p, tokens, table, scale, turn_ref, h):
+    h = pl.program_id(1) * p.step + h
     spectrum = mul(table, tokens) * scale
     for c in range(p.tiles):
         for ri in range(2):
@@ -196,30 +202,26 @@
 
 def cotangent_kernel(p, stored_ref, table_ref, scale_ref, out_ref, words_ref, turn_ref):
     clear_tail(p, words_ref)
-
-    def row(h, slot):
-        spread(p, stored_ref, words_ref.at[slot], h)
-        tokens = gather_row(p, words_ref.at[slot])
+    for h in range(p.step):
+        spread(p, stored_ref, words_ref.at[h], h)
+        tokens = gather_row(p, words_ref.at[h])
         analyse(p, tokens, table_ref[...], scale_ref[...], turn_ref, h)
 
-    each_row(p, row)
-    send_turn(p, turn_ref, out_ref, p.modes, 2 * p.rows)
-
-
-def stats_kernel(p, stored_ref, sum_ref, tokens_ref, stat_ref, words_ref, rows_ref):
+    @pl.when(last_part())
+    def _():
+        send_turn(p, turn_ref, out_ref, p.modes, 2 * p.rows)
+
+
+def stats_kernel(p, stored_ref, sum_ref, tokens_ref, stat_ref, words_ref):
     clear_tail(p, words_ref)
     count = 2 * p.stack
-
-    def row(h, slot):
-        spread(p, stored_ref, words_ref.at[slot], h)
-        tokens = gather_row(p, words_ref.at[slot])
+    for h in range(p.step):
+        spread(p, stored_ref, words_ref.at[h], h)
+        tokens = gather_row(p, words_ref.at[h])
         tokens_ref[0, h] = tokens
         wide = tokens.astype(single)
-        rows_ref[h] = mul(sum_ref[0], tokens, NT) + summed(sum_ref[1], wide * wide)
-
-    each_row(p, row)
-    for h in range(p.rows):
-        stat_ref[0, h * count : (h + 1) * count, :] = rows_ref[h, :count, :]
+        rows = mul(sum_ref[0], tokens, NT) + summed(sum_ref[1], wide * wide)
+        stat_ref[0, h * count : (h + 1) * count, :] = rows[:count]
 
 
 def moments(p, stat_refs, rows_ref):
@@ -227,7 +229,7 @@
     total = stat_refs[0][0]
     for ref in stat_refs[1:]:
         total = total + ref[0]
-    for h in range(p.rows):
+    for h in range(p.step):
         part = total[h * count : (h + 1) * count] * (1.0 / p.channels)
         mean, square = part[: p.stack], part[p.stack :]
         inverse = lax.rsqrt(square - mean * mean + norm_epsilon)
@@ -243,7 +245,7 @@
     out_ref, rows_ref, turn_ref = refs[p.chan + 5 :]
     moments(p, stat_refs, rows_ref)
 
-    def row(h, slot):
+    for h in range(p.step):
         tiles = []
         for c, (mean, inverse) in enumerate(expand(p, rows_ref[h], wide_ref)):
             at = slice(c * LANES, (c + 1) * LANES)
@@ -252,8 +254,9 @@
         normed = jnp.concatenate(tiles, axis=1)
         analyse(p, normed, table_ref[...], scale_ref[...], turn_ref, h)
 
-    each_row(p, row)
-    send_turn(p, turn_ref, out_ref, p.modes, 2 * p.rows)
+    @pl.when(last_part())
+    def _():
+        send_turn(p, turn_ref, out_ref, p.modes, 2 * p.rows)
 
 
 def gelu_both(values):
@@ -498,27 +501,27 @@
 def mixed_kernel(p, rows_ref, table_ref, out_ref, words_ref):
     factor = 1.0 / math.sqrt(p.lon)
 
-    def row(h, slot):
+    for h in range(p.step):
         block = rows_ref[:, 0, 0, h].reshape(2 * MW, p.lanes)
         tokens = mul(table_ref[...], block) * factor
-        scatter_row(p, tokens, words_ref.at[slot], out_ref, h)
-
-    each_row(p, row)
-
-
-def slope_sums_kernel(p, *refs):
+        scatter_row(p, tokens, words_ref.at[h], out_ref, h)
+
+
+def slope_sums_kernel(p, follows, *refs):
     stat_refs = refs[: p.chan]
     rows_in_ref, tokens_ref, affine_ref, table_ref, wide_ref, sum_ref = refs[p.chan : p.chan + 6]
-    sums_ref, total_ref, param_ref, rows_ref, part_ref, dense_ref = refs[p.chan + 6 :]
+    refs = refs[p.chan + 6 :]
+    before_ref, refs = (refs[0], refs[1:]) if follows else (None, refs)
+    sums_ref, total_ref, param_ref, rows_ref, dense_ref = refs
     factor = 1.0 / math.sqrt(p.lon)
     count = 2 * p.stack
     moments(p, stat_refs, rows_ref)
 
-    @pl.when(pl.program_id(0) == 0)
+    @pl.when(first_step())
     def _():
         param_ref[...] = jnp.zeros_like(param_ref)
 
-    def row(h, slot):
+    for h in range(p.step):
         block = rows_in_ref[:, 0, 0, h].reshape(2 * MW, p.lanes)
         folds = (PACK * p.turn_pad // 8, 8, LANES)
         plain, scaled = [], []
@@ -532,21 +535,21 @@
             grad = normed_grad * affine_ref[0:1, at]
             plain.append(grad.astype(half))
             scaled.append((grad * centred).astype(half))
-        part_ref[h] = mul(sum_ref[0], jnp.concatenate(plain, axis=1), NT) + mul(
+        sums = mul(sum_ref[0], jnp.concatenate(plain, axis=1), NT) + mul(
             sum_ref[1], jnp.concatenate(scaled, axis=1), NT
         )
-
-    each_row(p, row)
-    for h in range(p.rows):
-        dense_ref[h * count : (h + 1) * count, :] = part_ref[h, :count, :]
+        dense_ref[h * count : (h + 1) * count, :] = sums[:count]
     sums_ref[0] = dense_ref[...].astype(half)
 
-    @pl.when(pl.program_id(0) == pl.num_programs(0) - 1)
+    @pl.when(last_step())
     def _():
         for kind in range(2):
-            total_ref[kind : kind + 1, :] = param_ref[8 * kind : 8 * kind + 8, :].sum(
-                0, keepdims=True
-            )
+            at = slice(kind, kind + 1)
+            total = param_ref[8 * kind : 8 * kind + 8, :].sum(0, keepdims=True)
+            if before_ref is not None:
+                total = total + before_ref[0, at, :]
+            for d in range(p.space):
+                total_ref[d, at, :] = total
 
 
 def input_grad_kernel(p, *refs):
@@ -559,12 +562,12 @@
     total = part_refs[0][0].astype(single)
     for ref in part_refs[1:]:
         total = total + ref[0].astype(single)
-    for h in range(p.rows):
+    for h in range(p.step):
         part_ref[h, :count, :] = total[h * count : (h + 1) * count] * (1.0 / p.channels)
         if count < 8:
             part_ref[h, count:, :] = jnp.zeros((8 - count, p.turn_pad * PACK), single)
 
-    def row(h, slot):
+    for h in range(p.step):
         block = rows_in_ref[:, 0, 0, h].reshape(2 * MW, p.lanes)
         spectrum = mul(table_ref[...], block)
         moment = expand(p, rows_ref[h], wide_ref)
@@ -577,9 +580,7 @@
             grad = spectrum[:, at] * factor * affine_ref[0:1, at]
             tiles.append(inverse * (grad - first - centred * second))
         grad = jnp.concatenate(tiles, axis=1)
-        scatter_row(p, grad, words_ref.at[slot], out_ref, h)
-
-    each_row(p, row)
+        scatter_row(p, grad, words_ref.at[h], out_ref, h)
 
 
 def whole_spec(value):
@@ -587,9 +588,9 @@
     return pl.BlockSpec(dims, lambda *_: (0,) * len(dims))
 
 
-def pack_spec(value, offset=0):
-    dims = (1,) + value.shape[1:]
-    return pl.BlockSpec(dims, lambda b, *_: (b + offset,) + (0,) * (len(dims) - 1))
+def part_spec(p, value):
+    dims = (1, value.shape[1] // p.steps) + value.shape[2:]
+    return pl.BlockSpec(dims, lambda b, r: (b, r) + (0,) * (len(dims) - 2))
 
 
 def peer_spec(value, which=0, wide=1):
@@ -597,10 +598,13 @@
     return pl.BlockSpec(dims, lambda b, *_: (0, which, b) + (0,) * (len(dims) - 3))
 
 
+def peer_part_spec(p, value, which=0):
+    dims = (value.shape[0], 1, 1, value.shape[3] // p.steps) + value.shape[4:]
+    return pl.BlockSpec(dims, lambda b, r: (0, which, b, r) + (0,) * (len(dims) - 4))
+
+
 def stored_spec(p, offset):
-    return pl.BlockSpec(
-        (p.stack, p.rows, p.groups, p.long), lambda b, *_: (b + offset, 0, 0, 0)
-    )
+    return pl.BlockSpec((p.stack, p.step, p.groups, p.long), lambda b, r: (b + offset, r, 0, 0))
 
 
 def call(body, grid, ins, in_specs, outs, out_specs, scratch, flops, aliases=None):
@@ -694,17 +698,17 @@
 def on_device(space, chan, members, gain, shift, w_first, b_first, w_second, b_second, cotangent):
     p = Plan(members, w_first.shape[-1], space, chan)
     size = p.packs // 2
-    grid = (size,)
+    grid = (size, p.steps)
     table, plain_scale, double_scale, mixed_table, slope_table = lon_tables(p)
     there_table, back_table = lat_tables(p)
     sum_table, wide_table = sum_tables(p)
     affine = jnp.concatenate([gain] * p.stack + [shift] * p.stack).reshape(2, p.lanes)
     tokens_rows = PACK * p.turn_pad
     dft_flops = 2 * size * p.rows * tokens_rows * 2 * MW * p.lanes
-    words = pltpu.VMEM((SLOTS, PACK, p.word_pad, LANES), single)
-    lines = pltpu.VMEM((SLOTS, p.stack, p.word_pad * p.groups, LANES), single)
+    words = pltpu.VMEM((p.step, PACK, p.word_pad, LANES), single)
+    lines = pltpu.VMEM((p.step, p.stack, p.word_pad * p.groups, LANES), single)
     turn_in = pltpu.VMEM((p.tiles, MW * 2 * p.rows, LANES), single)
-    rows_scratch = pltpu.VMEM((p.rows, 8, tokens_rows), single)
+    rows_scratch = pltpu.VMEM((p.step, 8, tokens_rows), single)
 
     def sent(wide):
         return jax.ShapeDtypeStruct((space, wide, size, p.modes, 2 * p.rows, p.lanes), half)
@@ -743,7 +747,7 @@
         return call(
             functools.partial(stats_kernel, p), grid, ins,
             [stored_spec(p, c * size), whole_spec(sum_table)],
-            outs, [pack_spec(o) for o in outs], [words, rows_scratch], dft_flops // 4,
+            outs, [part_spec(p, o) for o in outs], [words], dft_flops // 4,
         )
 
     def normalise_chunk(stats, tokens, before):
@@ -751,7 +755,7 @@
         out = sent(1 if before is None else 2)
         return out_call(
             functools.partial(normalise_kernel, p), (*stats, tokens, *tail),
-            [pack_spec(s) for s in stats] + [pack_spec(tokens)] + [whole_spec(v) for v in tail],
+            [part_spec(p, s) for s in (*stats, tokens)] + [whole_spec(v) for v in tail],
             out, peer_spec(out, out.shape[1] - 1), [rows_scratch, turn_in], dft_flops, before,
         )
 
@@ -795,25 +799,27 @@
     def mixed_chunk(c, rows_in, which, before):
         return out_call(
             functools.partial(mixed_kernel, p), (rows_in, mixed_table),
-            [peer_spec(rows_in, which), whole_spec(mixed_table)], stored, stored_spec(p, c * size),
+            [peer_part_spec(p, rows_in, which), whole_spec(mixed_table)], stored, stored_spec(p, c * size),
             [lines], dft_flops, before,
         )
 
-    def slope_sums_chunk(stats, rows_in, which, tokens):
+    def slope_sums_chunk(stats, rows_in, which, tokens, before):
         tail = (affine, slope_table, wide_table, sum_table)
+        tail += () if before is None else (before,)
         outs = [
             jax.ShapeDtypeStruct((size, count, tokens_rows), half),
-            jax.ShapeDtypeStruct((2, p.lanes), single),
+            jax.ShapeDtypeStruct((space, 2, p.lanes), single),
         ]
         return call(
-            functools.partial(slope_sums_kernel, p), grid,
+            functools.partial(slope_sums_kernel, p, before is not None), grid,
             (*stats, rows_in, tokens, *tail),
-            [pack_spec(s) for s in stats] + [peer_spec(rows_in, which), pack_spec(tokens)]
+            [part_spec(p, s) for s in stats]
+            + [peer_part_spec(p, rows_in, which), part_spec(p, tokens)]
             + [whole_spec(v) for v in tail],
-            outs, [pack_spec(outs[0]), whole_spec(outs[1])],
+            outs, [part_spec(p, outs[0]), whole_spec(outs[1])],
             [
-                pltpu.VMEM((16, p.lanes), single), rows_scratch, rows_scratch,
-                pltpu.VMEM((count, tokens_rows), single),
+                pltpu.VMEM((16, p.lanes), single), rows_scratch,
+                pltpu.VMEM((count // p.steps, tokens_rows), single),
             ],
             dft_flops,
         )
@@ -823,8 +829,9 @@
         return out_call(
             functools.partial(input_grad_kernel, p),
             (*stats, *parts, rows_in, tokens, *tail),
-            [pack_spec(s) for s in (*stats, *parts)]
-            + [peer_spec(rows_in, which), pack_spec(tokens)] + [whole_spec(v) for v in tail],
+            [part_spec(p, s) for s in (*stats, *parts)]
+            + [peer_part_spec(p, rows_in, which), part_spec(p, tokens)]
+            + [whole_spec(v) for v in tail],
             stored, stored_spec(p, c * size), [rows_scratch, rows_scratch, lines], dft_flops,
             before,
         )
@@ -845,11 +852,11 @@
     y1, dx1, totals = spectral_chunk(both1, 1, both1, totals)
     dx1 = exchange(dx1)
     y1 = exchange(y1)
-    sums, params0 = slope_sums_chunk(stats0, rows0, 1, tokens0)
+    sums, params = slope_sums_chunk(stats0, rows0, 1, tokens0, None)
     parts = channel_sums(sums)
     grad_input = input_grad_chunk(0, stats0, parts, rows0, 1, tokens0, None)
     mixed = mixed_chunk(0, rows0, 0, None)
-    sums, params1 = slope_sums_chunk(stats1, dx1, 0, tokens1)
+    sums, params = slope_sums_chunk(stats1, dx1, 0, tokens1, params)
     parts = channel_sums(sums)
     grad_input = input_grad_chunk(1, stats1, parts, dx1, 0, tokens1, grad_input)
     mixed = mixed_chunk(1, y1, 0, mixed)
@@ -857,8 +864,10 @@
     flat = reduced(p, totals, half)[:, : p.width]
     grads = flat[: 4 * size_w].reshape((2,) + w_first.shape)
     bias_grads = flat[4 * size_w : 4 * size_w + 4 * p.groups].reshape((2,) + b_first.shape)
-    params = reduced(p, params0 + params1, single)
-    params = params.reshape(2, p.stack, size_w).sum(1)
+    params = exchange(params).sum(0)
+    params = [
+        sum(params[kind, s * size_w : (s + 1) * size_w] for s in range(p.stack)) for kind in range(2)
+    ]
     return (
         mixed, grad_input, grads[0], bias_grads[0], grads[1], bias_grads[1], params[0], params[1]
     )

time: 388 us -> 351 us (0.905)
  blocking collectives: 91.9 us -> 33.9 us
  waiting for transfers between devices: 60.7 us -> 81.4 us
  starting transfers between devices: 45.1 us -> 50.7 us
    all_to_all x2 -> x1, blocking collectives: 91.9 us -> 33.9 us  [exchange(): return lax.all_to_all(value, 'space', 0, 0, tiled=True)]
    all_to_all x4 -> x6, waiting for transfers between devices: 20.7 us -> 41.4 us  [exchange(): return lax.all_to_all(value, 'space', 0, 0, tiled=True)]
    all_to_all x4 -> x6, starting transfers between devices: 19.1 us -> 27.3 us  [exchange(): return lax.all_to_all(value, 'space', 0, 0, tiled=True)]
    ppermute x6 -> x3, waiting for transfers between devices: 35.4 us -> 35.4 us  [reduced(): other = lax.ppermute(own, 'space', [(i, i ^ step) for i in range(p.space)])]
  transfers between devices with their start and end apart: 22 -> 21, of which waited for: 7 -> 7; matrix products, arithmetic and copies ran while one was open for 2% -> 1% of each run, Pallas kernels for 33% -> 46%
where the time goes in v4:
time: 351 us; the launch traced here: 349 us
  Pallas kernels  178 us (51%)
  waiting for transfers between devices  81.4 us (23%)
  starting transfers between devices  50.7 us (14%)
  blocking collectives  33.9 us (10%)
    pallas_call x14, Pallas kernels, _call(): pl.pallas_call(body, grid=grid, in_specs=in_specs, out_specs=out_specs, o...  178 us
    all_to_all x6, waiting for transfers between devices, exchange(): return lax.all_to_all(value, 'space', 0, 0, tiled=True)  41.4 us
    ppermute x3, waiting for transfers between devices, reduced(): other = lax.ppermute(own, 'space', [(i, i ^ step) for i in range(p.space)])  35.4 us
    all_to_all x1, blocking collectives, exchange(): return lax.all_to_all(value, 'space', 0, 0, tiled=True)  33.9 us
    all_to_all x6, starting transfers between devices, exchange(): return lax.all_to_all(value, 'space', 0, 0, tiled=True)  27.3 us
    ppermute x12, starting transfers between devices, around(): lax.ppermute(value, axis, [(i, (i + step) % size) for i in range(size)])  19.7 us
  transfers between devices with their start and end apart: 21, of which 7 were waited for; matrix products, arithmetic and copies ran while one was open for 1% of the time, Pallas kernels for 46%

profile of v4, /device:TPU:0, one launch (start us, length us, event | category | flops | bytes accessed | tf_op | source)
XLA Modules:
  0.0 349.5 jit_solution(9603354839508391257)
XLA Ops:
  0.6 7.5 %shard_map.229 = bf16[8,1,2,8,24,384]{5,4,3,2,1,0:T(8,128)(2,1)} custom-call(bf16[8,12,2,17280]{3,2,1,0:T(2,128)(2,1)} %stored_ref.7, bf16[128,192]{1,0:T(8,128)(2,1)} %constant.20.clone.table_ref.refs_6_, f32[128,1]{1,0:T(8,128)} %constant.22.clone.scale_ref), custom_call_target="tpu_custom_call" | custom-call | flops 452984832 | bytes 9044480 | tf_op jit(solution)/shard_map/pallas_call | solution.py:618
  8.2 5.2 %all-to-all-start.2 = ((bf16[8,1,2,8,24,384]{5,4,3,2,1,0:T(8,128)(2,1)}), bf16[8,1,2,8,24,384]{5,4,3,2,1,0:T(8,128)(2,1)}, u32[]{:S(2)}, u32[]{:S(2)}) async-start(bf16[8,1,2,8,24,384]{5,4,3,2,1,0:T(8,128)(2,1)} %shard_map.229), calls=%async_computation.2 | async-start | bytes 4718592 | tf_op jit(solution)/shard_map/all_to_all | solution.py:676
  13.3 7.6 %shard_map.227 = (bf16[2,12,192,384]{3,2,1,0:T(8,128)(2,1)}, f32[2,48,192]{2,1,0:T(8,128)}) custom-call(bf16[8,12,2,17280]{3,2,1,0:T(2,128)(2,1)} %stored_ref.6, bf16[2,8,384]{2,1,0:T(8,128)(2,1)} %constant.27.clone.sum_ref.refs_9_), custom_call_target="tpu_custom_call" | custom-call | flops 113246208 | bytes 10260480 | tf_op jit(solution)/shard_map/pallas_call | solution.py:618
  20.9 2.2 collective-permute-start.3
  23.2 2.6 collective-permute-start.4
  25.7 1.4 collective-permute-start.5
  27.1 0.8 pad_maximum_fusion
  27.9 0.6 reshape.31.refs_5_.refs_6_.refs_10_
  28.5 0.7 collective-permute-done.3.refs_1_
  29.2 3.9 %collective-permute-done.4.refs_2_ = f32[2,48,192]{2,1,0:T(8,128)} collective-permute-done((f32[2,48,192]{2,1,0:T(8,128)}, f32[2,48,192]{2,1,0:T(8,128)}, u32[]{:S(2)}, u32[]{:S(2)}) %collective-permute-start.4) | collective-permute-done | bytes 73760 | tf_op jit(solution)/shard_map/ppermute | solution.py:683
  33.1 0.6 jit_solution_.3.refs_7_
  33.7 10.2 %shard_map.228 = bf16[8,1,2,8,24,384]{5,4,3,2,1,0:T(8,128)(2,1)} custom-call(f32[2,48,192]{2,1,0:T(8,128)} %get-tuple-element.23.refs_0_, f32[2,48,192]{2,1,0:T(8,128)} %collective-permute-done.3.refs_1_, f32[2,48,192]{2,1,0:T(8,128)} %collective-permute-done.4.refs_2_, f32[2,48,192]{2,1,0:T(8,128)} %collective-permute-done.5.refs_3_, ...), custom_call_target="tpu_custom_call" | custom-call | flops 452984832 | bytes 6282752 | tf_op jit(solution)/shard_map/pallas_call | solution.py:618
  43.9 4.4 %all-to-all-start.1 = ((bf16[8,1,2,8,24,384]{5,4,3,2,1,0:T(8,128)(2,1)}), bf16[8,1,2,8,24,384]{5,4,3,2,1,0:T(8,128)(2,1)}, u32[]{:S(2)}, u32[]{:S(2)}) async-start(bf16[8,1,2,8,24,384]{5,4,3,2,1,0:T(8,128)(2,1)} %shard_map.228), calls=%async_computation.1 | async-start | bytes 4718592 | tf_op jit(solution)/shard_map/all_to_all | solution.py:676
  48.4 7.6 %shard_map.224 = (bf16[2,12,192,384]{3,2,1,0:T(8,128)(2,1)}, f32[2,48,192]{2,1,0:T(8,128)}) custom-call(bf16[8,12,2,17280]{3,2,1,0:T(2,128)(2,1)} %stored_ref.6, bf16[2,8,384]{2,1,0:T(8,128)(2,1)} %constant.27.clone.sum_ref.refs_9_), custom_call_target="tpu_custom_call" | custom-call | flops 113246208 | bytes 10260480 | tf_op jit(solution)/shard_map/pallas_call | solution.py:618
  55.9 2.6 collective-permute-start
  58.5 1.6 collective-permute-start.1
  60.2 0.8 collective-permute-start.2
  61.0 7.5 %shard_map.225.refs_9_ = bf16[8,2,2,8,24,384]{5,4,3,2,1,0:T(8,128)(2,1)} custom-call(bf16[8,12,2,17280]{3,2,1,0:T(2,128)(2,1)} %stored_ref.7, bf16[128,192]{1,0:T(8,128)(2,1)} %constant.20.clone.table_ref.refs_6_, f32[128,1]{1,0:T(8,128)} %constant.22.clone.scale_ref), custom_call_target="tpu_custom_call" | custom-call | flops 452984832 | bytes 11403776 | tf_op jit(solution)/shard_map/pallas_call | solution.py:618
  68.5 10.2 %shard_map.226 = bf16[8,2,2,8,24,384]{5,4,3,2,1,0:T(8,128)(2,1)} custom-call(f32[2,48,192]{2,1,0:T(8,128)} %get-tuple-element.21.refs_0_, f32[2,48,192]{2,1,0:T(8,128)} %collective-permute-done.refs_1_, f32[2,48,192]{2,1,0:T(8,128)} %collective-permute-done.1.refs_2_, f32[2,48,192]{2,1,0:T(8,128)} %collective-permute-done.2.refs_3_, ...), custom_call_target="tpu_custom_call", output_to_operand_aliasing={{}: (9, {})} | custom-call | flops 452984832 | bytes 13360640 | tf_op jit(solution)/shard_map/pallas_call | solution.py:618
  78.7 4.6 %all-to-all-start = ((bf16[8,2,2,8,24,384]{5,4,3,2,1,0:T(8,128)(2,1)}), bf16[8,2,2,8,24,384]{5,4,3,2,1,0:T(8,128)(2,1)}, u32[]{:S(2)}, u32[]{:S(2)}) async-start(bf16[8,2,2,8,24,384]{5,4,3,2,1,0:T(8,128)(2,1)} %shard_map.226), calls=%async_computation | async-start | bytes 9437184 | tf_op jit(solution)/shard_map/all_to_all | solution.py:676
  83.3 33.9 %shard_map.230 = (bf16[8,2,2,12,16,384]{5,4,3,2,1,0:T(8,128)(2,1)}, f32[776,128]{1,0:T(8,128)}) custom-call(bf16[8,1,2,8,24,384]{5,4,3,2,1,0:T(8,128)(2,1)} %all-to-all-done.1.x_ref, bf16[8,1,2,8,24,384]{5,4,3,2,1,0:T(8,128)(2,1)} %all-to-all-done.2.g_ref, bf16[192,192]{1,0:T(8,128)(2,1)} %constant.25.clone.there_ref, ...), custom_call_target="tpu_custom_call" | custom-call | flops 10871635968 | bytes 10132480 | tf_op jit(solution)/shard_map/pallas_call | solution.py:618
  117.2 20.8 %all-to-all-done.x_ref.g_ref = bf16[8,2,2,8,24,384]{5,4,3,2,1,0:T(8,128)(2,1)} async-done(((bf16[8,2,2,8,24,384]{5,4,3,2,1,0:T(8,128)(2,1)}), bf16[8,2,2,8,24,384]{5,4,3,2,1,0:T(8,128)(2,1)}, u32[]{:S(2)}, u32[]{:S(2)}) %all-to-all-start) | async-done | bytes 4718624 | tf_op jit(solution)/shard_map/all_to_all | solution.py:676
  138.0 4.8 %all-to-all-start.4 = ((bf16[8,2,2,12,16,384]{5,4,3,2,1,0:T(8,128)(2,1)}), bf16[8,2,2,12,16,384]{5,4,3,2,1,0:T(8,128)(2,1)}, u32[]{:S(2)}, u32[]{:S(2)}) async-start(bf16[8,2,2,12,16,384]{5,4,3,2,1,0:T(8,128)(2,1)} %get-tuple-element.27), calls=%async_computation.4 | async-start | bytes 9437184 | tf_op jit(solution)/shard_map/all_to_all | solution.py:676
  142.8 34.0 %shard_map.231 = (bf16[8,1,2,12,16,384]{5,4,3,2,1,0:T(8,128)(2,1)}, bf16[8,1,2,12,16,384]{5,4,3,2,1,0:T(8,128)(2,1)}, bf16[776,128]{1,0:T(8,128)(2,1)}) custom-call(bf16[8,2,2,8,24,384]{5,4,3,2,1,0:T(8,128)(2,1)} %all-to-all-done.x_ref.g_ref, bf16[8,2,2,8,24,384]{5,4,3,2,1,0:T(8,128)(2,1)} %all-to-all-done.x_ref.g_ref, ...), custom_call_target="tpu_custom_call" | custom-call | flops 10871635968 | bytes 15049728 | tf_op jit(solution)/shard_map/pallas_call | solution.py:618
  176.9 20.5 %all-to-all-done.4.rows_ref.refs_4_.refs_8_ = bf16[8,2,2,12,16,384]{5,4,3,2,1,0:T(8,128)(2,1)} async-done(((bf16[8,2,2,12,16,384]{5,4,3,2,1,0:T(8,128)(2,1)}), bf16[8,2,2,12,16,384]{5,4,3,2,1,0:T(8,128)(2,1)}, u32[]{:S(2)}, u32[]{:S(2)}) %all-to-all-start.4) | async-done | bytes 4718624 | tf_op jit(solution)/shard_map/all_to_all | solution.py:676
  197.4 33.9 %all_to_all.35.refs_4_.refs_8_ = bf16[8,1,2,12,16,384]{5,4,3,2,1,0:T(8,128)(2,1)} all-to-all(bf16[8,1,2,12,16,384]{5,4,3,2,1,0:T(8,128)(2,1)} %get-tuple-element.28), channel_id=1, replica_groups=mesh['space'=8,'chan'=4] {'space'}, dimensions={0} | all-to-all | bytes 4718592 | tf_op jit(solution)/shard_map/all_to_all | solution.py:676
  231.2 4.4 %all-to-all-start.3 = ((bf16[8,1,2,12,16,384]{5,4,3,2,1,0:T(8,128)(2,1)}), bf16[8,1,2,12,16,384]{5,4,3,2,1,0:T(8,128)(2,1)}, u32[]{:S(2)}, u32[]{:S(2)}) async-start(bf16[8,1,2,12,16,384]{5,4,3,2,1,0:T(8,128)(2,1)} %get-tuple-element.26), calls=%async_computation.3 | async-start | bytes 4718592 | tf_op jit(solution)/shard_map/all_to_all | solution.py:676
  235.6 0.4 collective-permute-start.12
  236.0 1.6 collective-permute-done.12
  237.6 1.7 collective-permute-start.13
  239.3 28.9 %collective-permute-done.13 = bf16[776,128]{1,0:T(8,128)(2,1)S(1)} collective-permute-done((bf16[776,128]{1,0:T(8,128)(2,1)S(1)}, bf16[776,128]{1,0:T(8,128)(2,1)S(1)}, u32[]{:S(2)}, u32[]{:S(2)}) %collective-permute-start.13) | collective-permute-done | bytes 198688 | tf_op jit(solution)/shard_map/ppermute | solution.py:692
  268.3 1.6 collective-permute-start.14
  269.9 4.9 %collective-permute-done.14 = bf16[776,128]{1,0:T(8,128)(2,1)S(1)} collective-permute-done((bf16[776,128]{1,0:T(8,128)(2,1)S(1)}, bf16[776,128]{1,0:T(8,128)(2,1)S(1)}, u32[]{:S(2)}, u32[]{:S(2)}) %collective-permute-start.14) | collective-permute-done | bytes 198688 | tf_op jit(solution)/shard_map/ppermute | solution.py:692
  274.8 0.6 fusion
  275.4 0.8 fusion.1
  276.2 10.6 %shard_map.234 = (bf16[2,48,192]{2,1,0:T(8,128)(2,1)}, f32[8,2,384]{2,1,0:T(2,128)}) custom-call(f32[2,48,192]{2,1,0:T(8,128)} %get-tuple-element.23.refs_0_, f32[2,48,192]{2,1,0:T(8,128)} %collective-permute-done.3.refs_1_, f32[2,48,192]{2,1,0:T(8,128)} %collective-permute-done.4.refs_2_, f32[2,48,192]{2,1,0:T(8,128)} %collective-permute-done.5.refs_3_, ...), custom_call_target="tpu_custom_call" | custom-call | flops 452984832 | bytes 8715264 | tf_op jit(solution)/shard_map/pallas_call | solution.py:618
  286.8 1.2 collective-permute-start.10
  288.0 2.9 collective-permute-start.11
  290.9 10.6 %shard_map.235 = (bf16[2,48,192]{2,1,0:T(8,128)(2,1)}, f32[8,2,384]{2,1,0:T(2,128)}) custom-call(f32[2,48,192]{2,1,0:T(8,128)} %get-tuple-element.21.refs_0_, f32[2,48,192]{2,1,0:T(8,128)} %collective-permute-done.refs_1_, f32[2,48,192]{2,1,0:T(8,128)} %collective-permute-done.1.refs_2_, f32[2,48,192]{2,1,0:T(8,128)} %collective-permute-done.2.refs_3_, ...), custom_call_target="tpu_custom_call" | custom-call | flops 452984832 | bytes 6380544 | tf_op jit(solution)/shard_map/pallas_call | solution.py:618
  301.5 1.3 collective-permute-start.6
  302.8 3.1 collective-permute-start.7
  305.9 7.8 %shard_map.232.refs_2_ = bf16[8,12,2,17280]{3,2,1,0:T(2,128)(2,1)} custom-call(bf16[8,2,2,12,16,384]{5,4,3,2,1,0:T(8,128)(2,1)} %all-to-all-done.4.rows_ref.refs_4_.refs_8_, bf16[192,128]{1,0:T(8,128)(2,1)} %constant.23.clone.table_ref.refs_1_), custom_call_target="tpu_custom_call" | custom-call | flops 452984832 | bytes 11403264 | tf_op jit(solution)/shard_map/pallas_call | solution.py:618
  313.7 3.9 %all-to-all-start.6 = ((f32[8,2,384]{2,1,0:T(2,128)}), f32[8,2,384]{2,1,0:T(2,128)}, u32[]{:S(2)}, u32[]{:S(2)}) async-start(f32[8,2,384]{2,1,0:T(2,128)} %get-tuple-element.33), calls=%async_computation.6 | async-start | bytes 49152 | tf_op jit(solution)/shard_map/all_to_all | solution.py:676
  317.6 7.8 %shard_map.233 = bf16[8,12,2,17280]{3,2,1,0:T(2,128)(2,1)} custom-call(bf16[8,1,2,12,16,384]{5,4,3,2,1,0:T(8,128)(2,1)} %all-to-all-done.3.refs_0_, bf16[192,128]{1,0:T(8,128)(2,1)} %constant.23.clone.table_ref.refs_1_, bf16[8,12,2,17280]{3,2,1,0:T(2,128)(2,1)} %shard_map.232.refs_2_), custom_call_target="tpu_custom_call", output_to_operand_aliasing={{}: (2, {})} | custom-call | flops 452984832 | bytes 15679488 | tf_op jit(solution)/shard_map/pallas_call | solution.py:618
  325.5 0.8 reduce_sum.9
  326.2 0.6 slice_add_fusion
  326.9 11.3 %shard_map.236.refs_13_ = bf16[8,12,2,17280]{3,2,1,0:T(2,128)(2,1)} custom-call(f32[2,48,192]{2,1,0:T(8,128)} %get-tuple-element.23.refs_0_, f32[2,48,192]{2,1,0:T(8,128)} %collective-permute-done.3.refs_1_, f32[2,48,192]{2,1,0:T(8,128)} %collective-permute-done.4.refs_2_, f32[2,48,192]{2,1,0:T(8,128)} %collective-permute-done.5.refs_3_, ...), custom_call_target="tpu_custom_call" | custom-call | flops 452984832 | bytes 15424512 | tf_op jit(solution)/shard_map/pallas_call | solution.py:618
  338.2 11.3 %shard_map.237 = bf16[8,12,2,17280]{3,2,1,0:T(2,128)(2,1)} custom-call(f32[2,48,192]{2,1,0:T(8,128)} %get-tuple-element.21.refs_0_, f32[2,48,192]{2,1,0:T(8,128)} %collective-permute-done.refs_1_, f32[2,48,192]{2,1,0:T(8,128)} %collective-permute-done.1.refs_2_, f32[2,48,192]{2,1,0:T(8,128)} %collective-permute-done.2.refs_3_, ...), custom_call_target="tpu_custom_call", output_to_operand_aliasing={{}: (13, {})} | custom-call | flops 452984832 | bytes 19700736 | tf_op jit(solution)/shard_map/pallas_call | solution.py:618
  (21 shorter events, 0.2 us)
Async XLA Ops:
  8.2 35.8 %all-to-all-start.2 = ((bf16[8,1,2,8,24,384]{5,4,3,2,1,0:T(8,128)(2,1)}), bf16[8,1,2,8,24,384]{5,4,3,2,1,0:T(8,128)(2,1)}, u32[]{:S(2)}, u32[]{:S(2)}) async-start(bf16[8,1,2,8,24,384]{5,4,3,2,1,0:T(8,128)(2,1)} %shard_map.229), calls=%async_computation.2 | async-start | bytes 4718592 | tf_op jit(solution)/shard_map/all_to_all | solution.py:676
  20.9 8.3 %collective-permute-start.3 = (f32[2,48,192]{2,1,0:T(8,128)}, f32[2,48,192]{2,1,0:T(8,128)}, u32[]{:S(2)}, u32[]{:S(2)}) collective-permute-start(f32[2,48,192]{2,1,0:T(8,128)} %get-tuple-element.23.refs_0_), channel_id=1, source_target_pairs={{0,1},{1,2},{2,3},{3,0},{4,5},{5,6},{6,7},{7,4},{8,9},{9,10},{10,1... | collective-permute-start | bytes 221192 | tf_op jit(solution)/shard_map/ppermute | solution.py:683
  23.2 9.9 %collective-permute-start.4 = (f32[2,48,192]{2,1,0:T(8,128)}, f32[2,48,192]{2,1,0:T(8,128)}, u32[]{:S(2)}, u32[]{:S(2)}) collective-permute-start(f32[2,48,192]{2,1,0:T(8,128)} %get-tuple-element.23.refs_0_), channel_id=1, source_target_pairs={{0,2},{1,3},{2,0},{3,1},{4,6},{5,7},{6,4},{7,5},{8,10},{9,11},{10,... | collective-permute-start | bytes 221192 | tf_op jit(solution)/shard_map/ppermute | solution.py:683
  25.7 7.4 %collective-permute-start.5 = (f32[2,48,192]{2,1,0:T(8,128)}, f32[2,48,192]{2,1,0:T(8,128)}, u32[]{:S(2)}, u32[]{:S(2)}) collective-permute-start(f32[2,48,192]{2,1,0:T(8,128)} %get-tuple-element.23.refs_0_), channel_id=1, source_target_pairs={{0,3},{1,0},{2,1},{3,2},{4,7},{5,4},{6,5},{7,6},{8,11},{9,8},{10,9... | collective-permute-start | bytes 221192 | tf_op jit(solution)/shard_map/ppermute | solution.py:683
  43.9 34.8 %all-to-all-start.1 = ((bf16[8,1,2,8,24,384]{5,4,3,2,1,0:T(8,128)(2,1)}), bf16[8,1,2,8,24,384]{5,4,3,2,1,0:T(8,128)(2,1)}, u32[]{:S(2)}, u32[]{:S(2)}) async-start(bf16[8,1,2,8,24,384]{5,4,3,2,1,0:T(8,128)(2,1)} %shard_map.228), calls=%async_computation.1 | async-start | bytes 4718592 | tf_op jit(solution)/shard_map/all_to_all | solution.py:676
  55.9 12.5 %collective-permute-start = (f32[2,48,192]{2,1,0:T(8,128)}, f32[2,48,192]{2,1,0:T(8,128)}, u32[]{:S(2)}, u32[]{:S(2)}) collective-permute-start(f32[2,48,192]{2,1,0:T(8,128)} %get-tuple-element.21.refs_0_), channel_id=1, source_target_pairs={{0,1},{1,2},{2,3},{3,0},{4,5},{5,6},{6,7},{7,4},{8,9},{9,10},{10,1... | collective-permute-start | bytes 221192 | tf_op jit(solution)/shard_map/ppermute | solution.py:683
  58.5 9.9 %collective-permute-start.1 = (f32[2,48,192]{2,1,0:T(8,128)}, f32[2,48,192]{2,1,0:T(8,128)}, u32[]{:S(2)}, u32[]{:S(2)}) collective-permute-start(f32[2,48,192]{2,1,0:T(8,128)} %get-tuple-element.21.refs_0_), channel_id=1, source_target_pairs={{0,2},{1,3},{2,0},{3,1},{4,6},{5,7},{6,4},{7,5},{8,10},{9,11},{10,... | collective-permute-start | bytes 221192 | tf_op jit(solution)/shard_map/ppermute | solution.py:683
  60.2 8.3 %collective-permute-start.2 = (f32[2,48,192]{2,1,0:T(8,128)}, f32[2,48,192]{2,1,0:T(8,128)}, u32[]{:S(2)}, u32[]{:S(2)}) collective-permute-start(f32[2,48,192]{2,1,0:T(8,128)} %get-tuple-element.21.refs_0_), channel_id=1, source_target_pairs={{0,3},{1,0},{2,1},{3,2},{4,7},{5,4},{6,5},{7,6},{8,11},{9,8},{10,9... | collective-permute-start | bytes 221192 | tf_op jit(solution)/shard_map/ppermute | solution.py:683
  78.7 59.3 %all-to-all-start = ((bf16[8,2,2,8,24,384]{5,4,3,2,1,0:T(8,128)(2,1)}), bf16[8,2,2,8,24,384]{5,4,3,2,1,0:T(8,128)(2,1)}, u32[]{:S(2)}, u32[]{:S(2)}) async-start(bf16[8,2,2,8,24,384]{5,4,3,2,1,0:T(8,128)(2,1)} %shard_map.226), calls=%async_computation | async-start | bytes 9437184 | tf_op jit(solution)/shard_map/all_to_all | solution.py:676
  138.0 59.3 %all-to-all-start.4 = ((bf16[8,2,2,12,16,384]{5,4,3,2,1,0:T(8,128)(2,1)}), bf16[8,2,2,12,16,384]{5,4,3,2,1,0:T(8,128)(2,1)}, u32[]{:S(2)}, u32[]{:S(2)}) async-start(bf16[8,2,2,12,16,384]{5,4,3,2,1,0:T(8,128)(2,1)} %get-tuple-element.27), calls=%async_computation.4 | async-start | bytes 9437184 | tf_op jit(solution)/shard_map/all_to_all | solution.py:676
  197.4 38.2 %copy-start = (bf16[776,128]{1,0:T(8,128)(2,1)S(1)}, bf16[776,128]{1,0:T(8,128)(2,1)}, u32[]{:S(2)}) copy-start(bf16[776,128]{1,0:T(8,128)(2,1)} %get-tuple-element.32) | copy-start | bytes 595972
  231.2 82.5 %all-to-all-start.3 = ((bf16[8,1,2,12,16,384]{5,4,3,2,1,0:T(8,128)(2,1)}), bf16[8,1,2,12,16,384]{5,4,3,2,1,0:T(8,128)(2,1)}, u32[]{:S(2)}, u32[]{:S(2)}) async-start(bf16[8,1,2,12,16,384]{5,4,3,2,1,0:T(8,128)(2,1)} %get-tuple-element.26), calls=%async_computation.3 | async-start | bytes 4718592 | tf_op jit(solution)/shard_map/all_to_all | solution.py:676
  235.6 1.9 collective-permute-start.12
  237.6 30.7 %collective-permute-start.13 = (bf16[776,128]{1,0:T(8,128)(2,1)S(1)}, bf16[776,128]{1,0:T(8,128)(2,1)S(1)}, u32[]{:S(2)}, u32[]{:S(2)}) collective-permute-start(bf16[776,128]{1,0:T(8,128)(2,1)S(1)} %add_convert_fusion.1), channel_id=1, source_target_pairs={{0,8},{4,12},{8,0},{12,4},{16,24},{20,28},{24,16},{28,20},{1,9},{5... | collective-permute-start | bytes 595976 | tf_op jit(solution)/shard_map/ppermute | solution.py:692
  268.3 6.5 %collective-permute-start.14 = (bf16[776,128]{1,0:T(8,128)(2,1)S(1)}, bf16[776,128]{1,0:T(8,128)(2,1)S(1)}, u32[]{:S(2)}, u32[]{:S(2)}) collective-permute-start(bf16[776,128]{1,0:T(8,128)(2,1)S(1)} %add_convert_fusion), channel_id=1, source_target_pairs={{0,16},{4,20},{8,24},{12,28},{16,0},{20,4},{24,8},{28,12},{1,17},{... | collective-permute-start | bytes 595976 | tf_op jit(solution)/shard_map/ppermute | solution.py:692
  286.8 40.1 %collective-permute-start.10 = (bf16[2,48,192]{2,1,0:T(8,128)(2,1)}, bf16[2,48,192]{2,1,0:T(8,128)(2,1)}, u32[]{:S(2)}, u32[]{:S(2)}) collective-permute-start(bf16[2,48,192]{2,1,0:T(8,128)(2,1)} %get-tuple-element.31.refs_4_), channel_id=1, source_target_pairs={{0,2},{1,3},{2,0},{3,1},{4,6},{5,7},{6,4},{7,5},{8,10},{9,11},{10,... | collective-permute-start | bytes 110600 | tf_op jit(solution)/shard_map/ppermute | solution.py:683
  288.0 38.9 %collective-permute-start.11 = (bf16[2,48,192]{2,1,0:T(8,128)(2,1)}, bf16[2,48,192]{2,1,0:T(8,128)(2,1)}, u32[]{:S(2)}, u32[]{:S(2)}) collective-permute-start(bf16[2,48,192]{2,1,0:T(8,128)(2,1)} %get-tuple-element.31.refs_4_), channel_id=1, source_target_pairs={{0,3},{1,0},{2,1},{3,2},{4,7},{5,4},{6,5},{7,6},{8,11},{9,8},{10,9... | collective-permute-start | bytes 110600 | tf_op jit(solution)/shard_map/ppermute | solution.py:683
  290.9 36.0 %collective-permute-start.9 = (bf16[2,48,192]{2,1,0:T(8,128)(2,1)}, bf16[2,48,192]{2,1,0:T(8,128)(2,1)}, u32[]{:S(2)}, u32[]{:S(2)}) collective-permute-start(bf16[2,48,192]{2,1,0:T(8,128)(2,1)} %get-tuple-element.31.refs_4_), channel_id=1, source_target_pairs={{0,1},{1,2},{2,3},{3,0},{4,5},{5,6},{6,7},{7,4},{8,9},{9,10},{10,1... | collective-permute-start | bytes 110600 | tf_op jit(solution)/shard_map/ppermute | solution.py:683
  301.5 36.7 %collective-permute-start.6 = (bf16[2,48,192]{2,1,0:T(8,128)(2,1)}, bf16[2,48,192]{2,1,0:T(8,128)(2,1)}, u32[]{:S(2)}, u32[]{:S(2)}) collective-permute-start(bf16[2,48,192]{2,1,0:T(8,128)(2,1)} %get-tuple-element.30.refs_4_), channel_id=1, source_target_pairs={{0,1},{1,2},{2,3},{3,0},{4,5},{5,6},{6,7},{7,4},{8,9},{9,10},{10,1... | collective-permute-start | bytes 110600 | tf_op jit(solution)/shard_map/ppermute | solution.py:683
  302.8 35.4 %collective-permute-start.7 = (bf16[2,48,192]{2,1,0:T(8,128)(2,1)}, bf16[2,48,192]{2,1,0:T(8,128)(2,1)}, u32[]{:S(2)}, u32[]{:S(2)}) collective-permute-start(bf16[2,48,192]{2,1,0:T(8,128)(2,1)} %get-tuple-element.30.refs_4_), channel_id=1, source_target_pairs={{0,2},{1,3},{2,0},{3,1},{4,6},{5,7},{6,4},{7,5},{8,10},{9,11},{10,... | collective-permute-start | bytes 110600 | tf_op jit(solution)/shard_map/ppermute | solution.py:683
  313.7 11.8 %all-to-all-start.6 = ((f32[8,2,384]{2,1,0:T(2,128)}), f32[8,2,384]{2,1,0:T(2,128)}, u32[]{:S(2)}, u32[]{:S(2)}) async-start(f32[8,2,384]{2,1,0:T(2,128)} %get-tuple-element.33), calls=%async_computation.6 | async-start | bytes 49152 | tf_op jit(solution)/shard_map/all_to_all | solution.py:676
  326.9 11.3 %collective-permute-start.8 = (bf16[2,48,192]{2,1,0:T(8,128)(2,1)}, bf16[2,48,192]{2,1,0:T(8,128)(2,1)}, u32[]{:S(2)}, u32[]{:S(2)}) collective-permute-start(bf16[2,48,192]{2,1,0:T(8,128)(2,1)} %get-tuple-element.30.refs_4_), channel_id=1, source_target_pairs={{0,3},{1,0},{2,1},{3,2},{4,7},{5,4},{6,5},{7,6},{8,11},{9,8},{10,9... | collective-permute-start | bytes 110600 | tf_op jit(solution)/shard_map/ppermute | solution.py:683

commit v5 on v4

--- a/solution.py
+++ b/solution.py
@@ -170,12 +170,24 @@
             ]
 
 
-def send_turn(p, turn_ref, out_ref, outer, inner, which=0):
+def send_turn(p, turn_ref, out_refs, outer, inner, which=0, me=None):
     count = outer * inner
-    for d in range(p.space):
+    for x in range(p.space):
         for c in range(p.tiles):
-            part = turn_ref[c, d * count : (d + 1) * count, :].reshape(outer, inner, LANES)
-            out_ref[d, which, 0, :, :, c * LANES : (c + 1) * LANES] = part.astype(half)
+            lanes = slice(c * LANES, (c + 1) * LANES)
+            if me is None:
+                part = turn_ref[c, x * count : (x + 1) * count, :]
+                out_refs[0][x, which, 0, :, :, lanes] = part.reshape(outer, inner, LANES).astype(half)
+            else:
+                at = pl.ds(pl.multiple_of((me ^ x) * count, 8), count)
+                part = turn_ref[c, at, :]
+                out_refs[x][which, 0, :, :, lanes] = part.reshape(outer, inner, LANES).astype(half)
+
+
+def peer_rows(p, refs, i):
+    if len(refs) == 1:
+        return refs[0][:, 0, 0, i].reshape(-1, p.lanes)
+    return jnp.concatenate([ref[0, 0, i] for ref in refs], axis=0)
 
 
 def split_three(value):
@@ -200,7 +212,9 @@
     return mul(table, high, NT) + mul(table, low, NT)
 
 
-def cotangent_kernel(p, stored_ref, table_ref, scale_ref, out_ref, words_ref, turn_ref):
+def cotangent_kernel(p, split, stored_ref, table_ref, scale_ref, *refs):
+    me, refs = (refs[0][0], refs[1:]) if split else (None, refs)
+    out_refs, (words_ref, turn_ref) = refs[:-2], refs[-2:]
     clear_tail(p, words_ref)
     for h in range(p.step):
         spread(p, stored_ref, words_ref.at[h], h)
@@ -209,7 +223,7 @@
 
     @pl.when(last_part())
     def _():
-        send_turn(p, turn_ref, out_ref, p.modes, 2 * p.rows)
+        send_turn(p, turn_ref, out_refs, p.modes, 2 * p.rows, 0, me)
 
 
 def stats_kernel(p, stored_ref, sum_ref, tokens_ref, stat_ref, words_ref):
@@ -239,10 +253,12 @@
             rows_ref[h, count:, :] = jnp.zeros((8 - count, p.turn_pad * PACK), single)
 
 
-def normalise_kernel(p, *refs):
+def normalise_kernel(p, split, *refs):
     stat_refs = refs[: p.chan]
     tokens_ref, affine_ref, table_ref, scale_ref, wide_ref = refs[p.chan : p.chan + 5]
-    out_ref, rows_ref, turn_ref = refs[p.chan + 5 :]
+    refs = refs[p.chan + 5 :]
+    me, refs = (refs[0][0], refs[1:]) if split else (None, refs)
+    out_refs, (rows_ref, turn_ref) = refs[:-2], refs[-2:]
     moments(p, stat_refs, rows_ref)
 
     for h in range(p.step):
@@ -256,7 +272,7 @@
 
     @pl.when(last_part())
     def _():
-        send_turn(p, turn_ref, out_ref, p.modes, 2 * p.rows)
+        send_turn(p, turn_ref, out_refs, p.modes, 2 * p.rows, 0, me)
 
 
 def gelu_both(values):
@@ -324,43 +340,39 @@
             out_ref[which : which + 1, ri * p.lanes : (ri + 1) * p.lanes] = row
 
 
-def spectral_kernel(
-    p,
-    step_modes,
-    joined,
-    x_ref,
-    g_ref,
-    there_ref,
-    back_ref,
-    w_first_ref,
-    w_second_ref,
-    b_first_ref,
-    b_second_ref,
-    *refs,
-):
-    before_ref = None
+def spectral_kernel(p, step_modes, peers, split, joined, *refs):
+    x_refs, g_refs, refs = refs[:peers], refs[peers : 2 * peers], refs[2 * peers :]
+    there_ref, back_ref, w_first_ref, w_second_ref, b_first_ref, b_second_ref = refs[:6]
+    refs = refs[6:]
+    me, before_ref = None, None
     if not joined:
         before_ref, refs = refs[0], refs[1:]
-    out_refs = refs[: 1 if joined else 2]
+    if split:
+        me, refs = refs[0][0], refs[1:]
+    y_refs, refs = refs[:1], refs[1:]
+    x_out_refs = y_refs
+    if not joined:
+        x_outs = p.space if split else 1
+        x_out_refs, refs = refs[:x_outs], refs[x_outs:]
     (
-    total_ref,
-    gb_ref,
-    bias_ref,
-    lat_ref,
-    hid_ref,
-    gpost_ref,
-    gpre_ref,
-    slope_ref,
-    gsh_ref,
-    shr_ref,
-    glat_ref,
-    turn_y_ref,
-    turn_x_ref,
-    acc1_ref,
-    acc2_ref,
-    w1_ref,
-    w2_ref,
-    ) = refs[len(out_refs) :]
+        total_ref,
+        gb_ref,
+        bias_ref,
+        lat_ref,
+        hid_ref,
+        gpost_ref,
+        gpre_ref,
+        slope_ref,
+        gsh_ref,
+        shr_ref,
+        glat_ref,
+        turn_y_ref,
+        turn_x_ref,
+        acc1_ref,
+        acc2_ref,
+        w1_ref,
+        w2_ref,
+    ) = refs
     pack, group = pl.program_id(0), pl.program_id(1)
     count = step_modes * p.lat
     factor = 1.0 / math.sqrt(p.lat)
@@ -374,9 +386,9 @@
         acc1_ref[...] = jnp.zeros_like(acc1_ref)
         acc2_ref[...] = jnp.zeros_like(acc2_ref)
 
-    def there(ref, into, offset):
+    def there(refs, into, offset):
         for m in range(step_modes):
-            block = ref[:, 0, 0, m].reshape(2 * p.lat, p.lanes)
+            block = peer_rows(p, refs, m)
             out = (mul(there_ref[...], block) * factor).astype(half)
             at = pl.ds(offset + m * p.lat, p.lat)
             into[at, : p.lanes] = out[: p.lat]
@@ -402,8 +414,8 @@
     def folded(value):
         return value.reshape(BAND // 8, 8, value.shape[1]).sum(0)
 
-    there(x_ref, lat_ref, base)
-    there(g_ref, gsh_ref, 0)
+    there(x_refs, lat_ref, base)
+    there(g_refs, gsh_ref, 0)
     every = [slice(low, low + COLUMNS) for low in range(0, 2 * p.lanes, COLUMNS)]
     lat = lat_ref[pl.ds(base, count), :]
     for columns in every:
@@ -450,8 +462,8 @@
 
     @pl.when(group == pl.num_programs(1) - 1)
     def _():
-        send_turn(p, turn_y_ref, out_refs[0], p.rows, 2 * p.modes)
-        send_turn(p, turn_x_ref, out_refs[-1], p.rows, 2 * p.modes, len(out_refs) % 2)
+        send_turn(p, turn_y_ref, y_refs, p.rows, 2 * p.modes)
+        send_turn(p, turn_x_ref, x_out_refs, p.rows, 2 * p.modes, 1 if joined else 0, me)
         acc1_ref[...] += mul(lat_ref[...], gpre_ref[...], TN)
         acc2_ref[...] += mul(hid_ref[...], gpost_ref[...], TN)
 
@@ -502,15 +514,16 @@
     factor = 1.0 / math.sqrt(p.lon)
 
     for h in range(p.step):
-        block = rows_ref[:, 0, 0, h].reshape(2 * MW, p.lanes)
+        block = peer_rows(p, (rows_ref,), h)
         tokens = mul(table_ref[...], block) * factor
         scatter_row(p, tokens, words_ref.at[h], out_ref, h)
 
 
-def slope_sums_kernel(p, follows, *refs):
-    stat_refs = refs[: p.chan]
-    rows_in_ref, tokens_ref, affine_ref, table_ref, wide_ref, sum_ref = refs[p.chan : p.chan + 6]
-    refs = refs[p.chan + 6 :]
+def slope_sums_kernel(p, peers, follows, *refs):
+    stat_refs, refs = refs[: p.chan], refs[p.chan :]
+    rows_in_refs, refs = refs[:peers], refs[peers:]
+    tokens_ref, affine_ref, table_ref, wide_ref, sum_ref = refs[:5]
+    refs = refs[5:]
     before_ref, refs = (refs[0], refs[1:]) if follows else (None, refs)
     sums_ref, total_ref, param_ref, rows_ref, dense_ref = refs
     factor = 1.0 / math.sqrt(p.lon)
@@ -522,7 +535,7 @@
         param_ref[...] = jnp.zeros_like(param_ref)
 
     for h in range(p.step):
-        block = rows_in_ref[:, 0, 0, h].reshape(2 * MW, p.lanes)
+        block = peer_rows(p, rows_in_refs, h)
         folds = (PACK * p.turn_pad // 8, 8, LANES)
         plain, scaled = [], []
         spectrum = mul(table_ref[...], block)
@@ -552,10 +565,10 @@
                 total_ref[d, at, :] = total
 
 
-def input_grad_kernel(p, *refs):
-    stat_refs, part_refs = refs[: p.chan], refs[p.chan : 2 * p.chan]
-    rows_in_ref, tokens_ref, affine_ref, table_ref, wide_ref = refs[2 * p.chan : 2 * p.chan + 5]
-    out_ref, rows_ref, part_ref, words_ref = refs[2 * p.chan + 5 :]
+def input_grad_kernel(p, peers, *refs):
+    stat_refs, part_refs, refs = refs[: p.chan], refs[p.chan : 2 * p.chan], refs[2 * p.chan :]
+    rows_in_refs, refs = refs[:peers], refs[peers:]
+    tokens_ref, affine_ref, table_ref, wide_ref, out_ref, rows_ref, part_ref, words_ref = refs
     factor = 1.0 / math.sqrt(p.lon)
     count = 2 * p.stack
     moments(p, stat_refs, rows_ref)
@@ -568,7 +581,7 @@
             part_ref[h, count:, :] = jnp.zeros((8 - count, p.turn_pad * PACK), single)
 
     for h in range(p.step):
-        block = rows_in_ref[:, 0, 0, h].reshape(2 * MW, p.lanes)
+        block = peer_rows(p, rows_in_refs, h)
         spectrum = mul(table_ref[...], block)
         moment = expand(p, rows_ref[h], wide_ref)
         means = expand(p, part_ref[h], wide_ref)
@@ -601,6 +614,16 @@
 def peer_part_spec(p, value, which=0):
     dims = (value.shape[0], 1, 1, value.shape[3] // p.steps) + value.shape[4:]
     return pl.BlockSpec(dims, lambda b, r: (0, which, b, r) + (0,) * (len(dims) - 4))
+
+
+def one_peer_spec(value, which=0):
+    dims = (1, 1) + value.shape[2:]
+    return pl.BlockSpec(dims, lambda b, *_: (which, b) + (0,) * (len(dims) - 2))
+
+
+def one_peer_part_spec(p, value):
+    dims = (1, 1, value.shape[2] // p.steps) + value.shape[3:]
+    return pl.BlockSpec(dims, lambda b, r: (0, b, r) + (0,) * (len(dims) - 3))
 
 
 def stored_spec(p, offset):
@@ -646,8 +669,15 @@
         jnp.asarray(plain_scale),
         jnp.asarray(double_scale),
         to_half(owner * twice),
-        to_half(owner),
+        owner,
     )
+
+
+def by_distance(p, table, inner):
+    at = np.arange(p.space * inner, dtype=np.int32)
+    source = ((at // inner) ^ lax.axis_index("space").astype(jnp.int32)) * inner + at % inner
+    chosen = (at[:, None] == source[None, :]).astype(half)
+    return mul(jnp.asarray(table, half), chosen).astype(half)
 
 
 def lat_tables(p):
@@ -655,7 +685,7 @@
     there = np.block([[cos_lat, sin_lat], [-sin_lat, cos_lat]])
     there = there.reshape(2 * p.lat, 2, p.space, p.rows).transpose(0, 2, 1, 3)
     back = np.block([[cos_lat.T, -sin_lat.T], [sin_lat.T, cos_lat.T]])
-    return jnp.asarray(there.reshape(2 * p.lat, 2 * p.lat), half), jnp.asarray(back, half)
+    return there.reshape(2 * p.lat, 2 * p.lat), jnp.asarray(back, half)
 
 
 def sum_tables(p):
@@ -672,6 +702,18 @@
     return jnp.asarray(sums, half), jnp.asarray(wide.reshape(24, 2 * p.lanes), half)
 
 
+def splits(space):
+    return (MW // space) % 4 == 0 and space & (space - 1) == 0
+
+
+def exchange_near(values):
+    count = len(values)
+    return tuple(
+        value if x == 0 else lax.ppermute(value, "space", [(i, i ^ x) for i in range(count)])
+        for x, value in enumerate(values)
+    )
+
+
 def exchange(value):
     return lax.all_to_all(value, "space", 0, 0, tiled=True)
 
@@ -699,8 +741,15 @@
     p = Plan(members, w_first.shape[-1], space, chan)
     size = p.packs // 2
     grid = (size, p.steps)
-    table, plain_scale, double_scale, mixed_table, slope_table = lon_tables(p)
-    there_table, back_table = lat_tables(p)
+    table, plain_scale, double_scale, mixed_table, slope_plain = lon_tables(p)
+    there_plain, back_table = lat_tables(p)
+    slope_table, there_table = jnp.asarray(slope_plain, half), jnp.asarray(there_plain, half)
+    split = splits(space)
+    if split:
+        slope_near = by_distance(p, slope_plain, 2 * p.modes)
+        there_near = by_distance(p, there_plain, 2 * p.rows)
+        me = lax.axis_index("space").astype(jnp.int32).reshape(1)
+    own_spec = pl.BlockSpec(memory_space=pltpu.SMEM)
     sum_table, wide_table = sum_tables(p)
     affine = jnp.concatenate([gain] * p.stack + [shift] * p.stack).reshape(2, p.lanes)
     tokens_rows = PACK * p.turn_pad
@@ -719,23 +768,32 @@
     count = 2 * p.stack * p.rows
     stored = jax.ShapeDtypeStruct(members.shape, half)
 
-    def out_call(body, ins, specs, out, out_spec, scratch, flops, before):
+    def out_call(body, ins, specs, outs, out_specs, scratch, flops, before):
         ins, specs = list(ins), list(specs)
         aliases = {}
         inner = body
         if before is not None:
-            place = len(ins)
-            inner = lambda *refs: body(*refs[:place], *refs[place + 1 :])
-            ins.append(before)
-            specs.append(pl.BlockSpec(memory_space=pl.ANY))
-            aliases = {place: 0}
-        return call(inner, grid, tuple(ins), specs, [out], [out_spec], scratch, flops, aliases)[0]
-
-    def cotangent_chunk(c, wide):
+            place, extra = len(ins), len(before)
+            inner = lambda *refs: body(*refs[:place], *refs[place + extra :])
+            ins += before
+            specs += [pl.BlockSpec(memory_space=pl.ANY)] * extra
+            aliases = {place + k: k for k in range(extra)}
+        return call(inner, grid, tuple(ins), specs, outs, out_specs, scratch, flops, aliases)
+
+    def spectra_out(wide, which, near):
+        if near:
+            one = jax.ShapeDtypeStruct(sent(wide).shape[1:], half)
+            return [one] * space, [one_peer_spec(one, which)] * space
+        return [sent(wide)], [peer_spec(sent(wide), which)]
+
+    def cotangent_chunk(c, wide, near):
+        outs, out_specs = spectra_out(wide, 0, near)
+        ins, specs = (cotangent, table, double_scale), [whole_spec(table), whole_spec(double_scale)]
+        if near:
+            ins, specs = (*ins, me), [*specs, own_spec]
         return out_call(
-            functools.partial(cotangent_kernel, p), (cotangent, table, double_scale),
-            [stored_spec(p, c * size), whole_spec(table), whole_spec(double_scale)],
-            sent(wide), peer_spec(sent(wide)), [words, turn_in], dft_flops, None,
+            functools.partial(cotangent_kernel, p, near), ins,
+            [stored_spec(p, c * size), *specs], outs, out_specs, [words, turn_in], dft_flops, None,
         )
 
     def stats_chunk(c):
@@ -750,31 +808,46 @@
             outs, [part_spec(p, o) for o in outs], [words], dft_flops // 4,
         )
 
-    def normalise_chunk(stats, tokens, before):
+    def normalise_chunk(stats, tokens, before, near):
         tail = (affine, table, plain_scale, wide_table)
-        out = sent(1 if before is None else 2)
+        ins = (*stats, tokens, *tail)
+        specs = [part_spec(p, s) for s in (*stats, tokens)] + [whole_spec(v) for v in tail]
+        if near:
+            ins, specs = (*ins, me), [*specs, own_spec]
+        which = 0 if before is None else 1
+        outs, out_specs = spectra_out(which + 1, which, near)
         return out_call(
-            functools.partial(normalise_kernel, p), (*stats, tokens, *tail),
-            [part_spec(p, s) for s in (*stats, tokens)] + [whole_spec(v) for v in tail],
-            out, peer_spec(out, out.shape[1] - 1), [rows_scratch, turn_in], dft_flops, before,
+            functools.partial(normalise_kernel, p, near), ins, specs,
+            outs, out_specs, [rows_scratch, turn_in], dft_flops, before,
         )
 
     step_modes = 2 if p.modes % 2 == 0 else 1
     wide_lanes = 2 * p.lanes
 
-    def spectral_chunk(x_in, x_which, g_in, before):
+    def spectral_chunk(x_in, x_which, g_in, before, near):
         joined = before is None
-        tail = (there_table, back_table, w_first, w_second, b_first, b_second)
+        tail = (there_near if near else there_table, back_table)
+        tail += (w_first, w_second, b_first, b_second)
         tail += () if joined else (before,)
+        specs = [whole_spec(v) for v in tail]
+        if near:
+            tail, specs = (*tail, me), [*specs, own_spec]
 
         def mode_spec(which):
+            lead = (1, 1) if near else (space, 1, 1)
+            at = (which,) if near else (0, which)
             return pl.BlockSpec(
-                (space, 1, 1, step_modes, 2 * p.rows, p.lanes),
-                lambda b, m: (0, which, b, m, 0, 0),
+                lead + (step_modes, 2 * p.rows, p.lanes), lambda b, m: at + (b, m, 0, 0)
             )
 
-        outs = [returned(2)] if joined else [returned(1), returned(1)]
+        peers = len(x_in)
+        outs = [returned(2 if joined else 1)]
         out_specs = [peer_spec(o, 0, o.shape[1]) for o in outs]
+        if near:
+            one = jax.ShapeDtypeStruct(returned(1).shape[1:], half)
+            outs, out_specs = outs + [one] * space, out_specs + [one_peer_spec(one)] * space
+        elif not joined:
+            outs, out_specs = outs * 2, out_specs * 2
         bias_rows = -(-4 * p.groups // 8) * 8
         totals = jax.ShapeDtypeStruct(
             (4 * p.groups * p.width + bias_rows, LANES), single if joined else half
@@ -784,9 +857,9 @@
         brief = pltpu.VMEM((step_modes * p.lat, wide_lanes), half)
         turn_out = pltpu.VMEM((p.tiles, p.lat * 2 * p.modes, LANES), single)
         return call(
-            functools.partial(spectral_kernel, p, step_modes, joined),
-            (size, p.modes // step_modes), (x_in, g_in, *tail),
-            [mode_spec(x_which), mode_spec(0)] + [whole_spec(v) for v in tail],
+            functools.partial(spectral_kernel, p, step_modes, peers, near, joined),
+            (size, p.modes // step_modes), (*x_in, *g_in, *tail),
+            [mode_spec(x_which)] * peers + [mode_spec(0)] * peers + specs,
             [*outs, totals],
             [*out_specs, whole_spec(totals)],
             [pltpu.VMEM((16, wide_lanes), single), pltpu.VMEM((2, wide_lanes), single)]
@@ -799,23 +872,28 @@
     def mixed_chunk(c, rows_in, which, before):
         return out_call(
             functools.partial(mixed_kernel, p), (rows_in, mixed_table),
-            [peer_part_spec(p, rows_in, which), whole_spec(mixed_table)], stored, stored_spec(p, c * size),
-            [lines], dft_flops, before,
+            [peer_part_spec(p, rows_in, which), whole_spec(mixed_table)],
+            [stored], [stored_spec(p, c * size)], [lines], dft_flops, before,
         )
 
+    def rows_specs(rows_in, which):
+        if len(rows_in) == 1:
+            return [peer_part_spec(p, rows_in[0], which)]
+        return [one_peer_part_spec(p, value) for value in rows_in]
+
     def slope_sums_chunk(stats, rows_in, which, tokens, before):
-        tail = (affine, slope_table, wide_table, sum_table)
+        near = len(rows_in) > 1
+        tail = (affine, slope_near if near else slope_table, wide_table, sum_table)
         tail += () if before is None else (before,)
         outs = [
             jax.ShapeDtypeStruct((size, count, tokens_rows), half),
             jax.ShapeDtypeStruct((space, 2, p.lanes), single),
         ]
         return call(
-            functools.partial(slope_sums_kernel, p, before is not None), grid,
-            (*stats, rows_in, tokens, *tail),
-            [part_spec(p, s) for s in stats]
-            + [peer_part_spec(p, rows_in, which), part_spec(p, tokens)]
-            + [whole_spec(v) for v in tail],
+            functools.partial(slope_sums_kernel, p, len(rows_in), before is not None),
+            grid, (*stats, *rows_in, tokens, *tail),
+            [part_spec(p, s) for s in stats] + rows_specs(rows_in, which)
+            + [part_spec(p, tokens)] + [whole_spec(v) for v in tail],
             outs, [part_spec(p, outs[0]), whole_spec(outs[1])],
             [
                 pltpu.VMEM((16, p.lanes), single), rows_scratch,
@@ -825,41 +903,45 @@
         )
 
     def input_grad_chunk(c, stats, parts, rows_in, which, tokens, before):
-        tail = (affine, slope_table, wide_table)
+        near = len(rows_in) > 1
+        tail = (affine, slope_near if near else slope_table, wide_table)
         return out_call(
-            functools.partial(input_grad_kernel, p),
-            (*stats, *parts, rows_in, tokens, *tail),
-            [part_spec(p, s) for s in (*stats, *parts)]
-            + [peer_part_spec(p, rows_in, which), part_spec(p, tokens)]
-            + [whole_spec(v) for v in tail],
-            stored, stored_spec(p, c * size), [rows_scratch, rows_scratch, lines], dft_flops,
+            functools.partial(input_grad_kernel, p, len(rows_in)),
+            (*stats, *parts, *rows_in, tokens, *tail),
+            [part_spec(p, s) for s in (*stats, *parts)] + rows_specs(rows_in, which)
+            + [part_spec(p, tokens)] + [whole_spec(v) for v in tail],
+            [stored], [stored_spec(p, c * size)], [rows_scratch, rows_scratch, lines], dft_flops,
             before,
         )
 
     def channel_sums(value):
         return around(value, "chan", chan)
 
-    g0 = exchange(cotangent_chunk(0, 1))
+    def moved(values, near):
+        return exchange_near(values) if near else (exchange(values[0]),)
+
+    g0 = moved(cotangent_chunk(0, 1, False), False)
     tokens0, sums = stats_chunk(0)
     stats0 = channel_sums(sums)
-    x0 = exchange(normalise_chunk(stats0, tokens0, None))
-    both1 = cotangent_chunk(1, 2)
+    x0 = moved(normalise_chunk(stats0, tokens0, None, False), False)
+    both1 = cotangent_chunk(1, 2, split)
     tokens1, sums = stats_chunk(1)
     stats1 = channel_sums(sums)
-    both1 = exchange(normalise_chunk(stats1, tokens1, both1))
-    out0, totals = spectral_chunk(x0, 0, g0, None)
+    both1 = moved(normalise_chunk(stats1, tokens1, both1, split), split)
+    out0, totals = spectral_chunk(x0, 0, g0, None, False)
     rows0 = exchange(out0)
-    y1, dx1, totals = spectral_chunk(both1, 1, both1, totals)
-    dx1 = exchange(dx1)
+    y1, *dx1, totals = spectral_chunk(both1, 1, both1, totals, split)
+    dx1 = moved(dx1, split)
     y1 = exchange(y1)
-    sums, params = slope_sums_chunk(stats0, rows0, 1, tokens0, None)
+    sums, params = slope_sums_chunk(stats0, (rows0,), 1, tokens0, None)
     parts = channel_sums(sums)
-    grad_input = input_grad_chunk(0, stats0, parts, rows0, 1, tokens0, None)
+    grad_input = input_grad_chunk(0, stats0, parts, (rows0,), 1, tokens0, None)
     mixed = mixed_chunk(0, rows0, 0, None)
     sums, params = slope_sums_chunk(stats1, dx1, 0, tokens1, params)
     parts = channel_sums(sums)
-    grad_input = input_grad_chunk(1, stats1, parts, dx1, 0, tokens1, grad_input)
-    mixed = mixed_chunk(1, y1, 0, mixed)
+    grad_input = input_grad_chunk(1, stats1, parts, dx1, 0, tokens1, grad_input)[0]
+    mixed = mixed_chunk(1, y1, 0, mixed)[0]
+
     size_w = p.groups * p.width
     flat = reduced(p, totals, half)[:, : p.width]
     grads = flat[: 4 * size_w].reshape((2,) + w_first.shape)

time: 351 us -> 389 us (1.11)
  waiting for transfers between devices: 81.4 us -> 107 us
  starting transfers between devices: 50.7 us -> 57.7 us
    ppermute x0 -> x14, waiting for transfers between devices: none -> 68.2 us  [exchange_near(): lax.ppermute(value, 'space', [(i, i ^ x) for i in range(count)])]
    all_to_all x6 -> x4, waiting for transfers between devices: 41.4 us -> 0.01 us  [exchange(): return lax.all_to_all(value, 'space', 0, 0, tiled=True)]
    ppermute x0 -> x14, starting transfers between devices: none -> 12.6 us  [exchange_near(): lax.ppermute(value, 'space', [(i, i ^ x) for i in range(count)])]
    all_to_all x6 -> x4, starting transfers between devices: 27.3 us -> 18.3 us  [exchange(): return lax.all_to_all(value, 'space', 0, 0, tiled=True)]
  transfers between devices with their start and end apart: 21 -> 33, of which waited for: 7 -> 10; matrix products, arithmetic and copies ran while one was open for 1% -> 2% of each run, Pallas kernels for 46% -> 33%
where the time goes in v5:
time: 389 us; the launch traced here: 387 us
  Pallas kernels  179 us (46%)
  waiting for transfers between devices  107 us (28%)
  starting transfers between devices  57.7 us (15%)
  blocking collectives  33.7 us (9%)
    pallas_call x14, Pallas kernels, _call(): pl.pallas_call(body, grid=grid, in_specs=in_specs, out_specs=out_specs, o...  179 us
    ppermute x14, waiting for transfers between devices, exchange_near(): lax.ppermute(value, 'space', [(i, i ^ x) for i in range(count)])  68.2 us
    ppermute x3, waiting for transfers between devices, reduced(): other = lax.ppermute(own, 'space', [(i, i ^ step) for i in range(p.space)])  33.8 us
    all_to_all x1, blocking collectives, exchange(): return lax.all_to_all(value, 'space', 0, 0, tiled=True)  33.7 us
    ppermute x12, starting transfers between devices, around(): lax.ppermute(value, axis, [(i, (i + step) % size) for i in range(size)])  23.2 us
    all_to_all x4, starting transfers between devices, exchange(): return lax.all_to_all(value, 'space', 0, 0, tiled=True)  18.3 us
    ppermute x14, starting transfers between devices, exchange_near(): lax.ppermute(value, 'space', [(i, i ^ x) for i in range(count)])  12.6 us
  transfers between devices with their start and end apart: 33, of which 10 were waited for; matrix products, arithmetic and copies ran while one was open for 2% of the time, Pallas kernels for 33%

profile of v5, /device:TPU:0, one launch (start us, length us, event | category | flops | bytes accessed | tf_op | source)
XLA Modules:
  0.0 386.8 jit_solution(1542760695075258811)
XLA Ops:
  0.6 7.5 %shard_map.301 = bf16[8,1,2,8,24,384]{5,4,3,2,1,0:T(8,128)(2,1)} custom-call(bf16[8,12,2,17280]{3,2,1,0:T(2,128)(2,1)} %stored_ref.7, bf16[128,192]{1,0:T(8,128)(2,1)} %constant.42.clone.table_ref.refs_6_, f32[128,1]{1,0:T(8,128)} %constant.44.clone.scale_ref), custom_call_target="tpu_custom_call" | custom-call | flops 452984832 | bytes 9044480 | tf_op jit(solution)/shard_map/pallas_call | solution.py:641
  8.2 5.2 %all-to-all-start.1 = ((bf16[8,1,2,8,24,384]{5,4,3,2,1,0:T(8,128)(2,1)}), bf16[8,1,2,8,24,384]{5,4,3,2,1,0:T(8,128)(2,1)}, u32[]{:S(2)}, u32[]{:S(2)}) async-start(bf16[8,1,2,8,24,384]{5,4,3,2,1,0:T(8,128)(2,1)} %shard_map.301), calls=%async_computation.1 | async-start | bytes 4718592 | tf_op jit(solution)/shard_map/all_to_all | solution.py:718
  13.3 7.6 %shard_map.299 = (bf16[2,12,192,384]{3,2,1,0:T(8,128)(2,1)}, f32[2,48,192]{2,1,0:T(8,128)}) custom-call(bf16[8,12,2,17280]{3,2,1,0:T(2,128)(2,1)} %stored_ref.6, bf16[2,8,384]{2,1,0:T(8,128)(2,1)} %constant.55.clone.sum_ref.refs_9_.refs_16_), custom_call_target="tpu_custom_call" | custom-call | flops 113246208 | bytes 10260480 | tf_op jit(solution)/shard_map/pallas_call | solution.py:641
  20.9 2.2 collective-permute-start.10
  23.2 2.6 collective-permute-start.11
  25.7 1.4 collective-permute-start.12
  27.1 0.8 pad_maximum_fusion
  29.2 3.9 collective-permute-done.11.refs_2_
  33.7 10.2 %shard_map.300 = bf16[8,1,2,8,24,384]{5,4,3,2,1,0:T(8,128)(2,1)} custom-call(f32[2,48,192]{2,1,0:T(8,128)} %get-tuple-element.62.refs_0_, f32[2,48,192]{2,1,0:T(8,128)} %collective-permute-done.10.refs_1_, f32[2,48,192]{2,1,0:T(8,128)} %collective-permute-done.11.refs_2_, f32[2,48,192]{2,1,0:T(8,128)} %collective-permute-done.12.refs_3_, ...), custom_call_target="tpu_custom_call" | custom-call | flops 452984832 | bytes 6282752 | tf_op jit(solution)/shard_map/pallas_call | solution.py:641
  43.9 33.7 %all_to_all.25.refs_0_ = bf16[8,1,2,8,24,384]{5,4,3,2,1,0:T(8,128)(2,1)} all-to-all(bf16[8,1,2,8,24,384]{5,4,3,2,1,0:T(8,128)(2,1)} %shard_map.300), channel_id=1, replica_groups=mesh['space'=8,'chan'=4] {'space'}, dimensions={0} | all-to-all | bytes 4718592 | tf_op jit(solution)/shard_map/all_to_all | solution.py:718
  77.7 33.8 %shard_map.302 = (bf16[8,2,2,12,16,384]{5,4,3,2,1,0:T(8,128)(2,1)}, f32[776,128]{1,0:T(8,128)}) custom-call(bf16[8,1,2,8,24,384]{5,4,3,2,1,0:T(8,128)(2,1)} %all_to_all.25.refs_0_, bf16[8,1,2,8,24,384]{5,4,3,2,1,0:T(8,128)(2,1)} %all-to-all-done.1.refs_1_, bf16[192,192]{1,0:T(8,128)(2,1)} %constant.48.clone.refs_2_, ...), custom_call_target="tpu_custom_call" | custom-call | flops 10871635968 | bytes 10132480 | tf_op jit(solution)/shard_map/pallas_call | solution.py:641
  111.5 4.6 %all-to-all-start.3 = ((bf16[8,2,2,12,16,384]{5,4,3,2,1,0:T(8,128)(2,1)}), bf16[8,2,2,12,16,384]{5,4,3,2,1,0:T(8,128)(2,1)}, u32[]{:S(2)}, u32[]{:S(2)}) async-start(bf16[8,2,2,12,16,384]{5,4,3,2,1,0:T(8,128)(2,1)} %get-tuple-element.66), calls=%async_computation.3 | async-start | bytes 9437184 | tf_op jit(solution)/shard_map/all_to_all | solution.py:718
  116.1 7.6 %shard_map.296 = (bf16[2,12,192,384]{3,2,1,0:T(8,128)(2,1)}, f32[2,48,192]{2,1,0:T(8,128)}) custom-call(bf16[8,12,2,17280]{3,2,1,0:T(2,128)(2,1)} %stored_ref.6, bf16[2,8,384]{2,1,0:T(8,128)(2,1)} %constant.55.clone.sum_ref.refs_9_.refs_16_), custom_call_target="tpu_custom_call" | custom-call | flops 113246208 | bytes 10260480 | tf_op jit(solution)/shard_map/pallas_call | solution.py:641
  123.7 2.6 collective-permute-start
  126.3 1.6 collective-permute-start.1
  127.9 0.8 collective-permute-start.2
  128.7 7.5 %shard_map.297 = (bf16[2,2,8,24,384]{4,3,2,1,0:T(8,128)(2,1)}, bf16[2,2,8,24,384]{4,3,2,1,0:T(8,128)(2,1)}, bf16[2,2,8,24,384]{4,3,2,1,0:T(8,128)(2,1)}, bf16[2,...) custom-call(bf16[8,12,2,17280]{3,2,1,0:T(2,128)(2,1)} %stored_ref.7,, ...), custom_call_target="tpu_custom_call" | custom-call | flops 452984832 | bytes 11403780 | tf_op jit(solution)/shard_map/pallas_call | solution.py:641
  136.2 10.3 %shard_map.298 = (bf16[2,2,8,24,384]{4,3,2,1,0:T(8,128)(2,1)}, bf16[2,2,8,24,384]{4,3,2,1,0:T(8,128)(2,1)}, bf16[2,2,8,24,384]{4,3,2,1,0:T(8,128)(2,1)}, bf16[2,...) custom-call(f32[2,48,192]{2,1,0:T(8,128)} %get-tuple-element.44.refs, ...), custom_call_target="tpu_custom_call", output_to_operand_aliasing={{0}: (10, {}), {1}: (11, {}), {2}: (12, {}), {3}: (13, {}),... | custom-call | flops 452984832 | bytes 13360644 | tf_op jit(solution)/shard_map/pallas_call | solution.py:641
  146.6 1.9 collective-permute-start.4
  148.6 1.8 collective-permute-start.6
  150.3 2.6 collective-permute-start.8
  153.0 30.1 %collective-permute-done.4.refs_2_.refs_10_ = bf16[2,2,8,24,384]{4,3,2,1,0:T(8,128)(2,1)S(1)} collective-permute-done((bf16[2,2,8,24,384]{4,3,2,1,0:T(8,128)(2,1)}, bf16[2,2,8,24,384]{4,3,2,1,0:T(8,128)(2,1)S(1)}, u32[]{:S(2)}, u32[]{:S(2)}) %collective-permute-start.4) | collective-permute-done | bytes 589856 | tf_op jit(solution)/shard_map/ppermute | solution.py:712
  183.1 0.9 copy-done.5
  184.8 1.7 fusion.refs_16_
  186.5 8.2 %collective-permute-done.5.refs_3_.refs_11_ = bf16[2,2,8,24,384]{4,3,2,1,0:T(8,128)(2,1)} collective-permute-done((bf16[2,2,8,24,384]{4,3,2,1,0:T(8,128)(2,1)}, bf16[2,2,8,24,384]{4,3,2,1,0:T(8,128)(2,1)}, u32[]{:S(2)}, u32[]{:S(2)}) %collective-permute-start.5) | collective-permute-done | bytes 589856 | tf_op jit(solution)/shard_map/ppermute | solution.py:712
  194.7 14.7 %collective-permute-done.8.refs_6_.refs_14_ = bf16[2,2,8,24,384]{4,3,2,1,0:T(8,128)(2,1)} collective-permute-done((bf16[2,2,8,24,384]{4,3,2,1,0:T(8,128)(2,1)}, bf16[2,2,8,24,384]{4,3,2,1,0:T(8,128)(2,1)}, u32[]{:S(2)}, u32[]{:S(2)}) %collective-permute-start.8) | collective-permute-done | bytes 589856 | tf_op jit(solution)/shard_map/ppermute | solution.py:712
  209.4 11.5 %collective-permute-done.9.refs_7_.refs_15_ = bf16[2,2,8,24,384]{4,3,2,1,0:T(8,128)(2,1)} collective-permute-done((bf16[2,2,8,24,384]{4,3,2,1,0:T(8,128)(2,1)}, bf16[2,2,8,24,384]{4,3,2,1,0:T(8,128)(2,1)}, u32[]{:S(2)}, u32[]{:S(2)}) %collective-permute-start.9) | collective-permute-done | bytes 589856 | tf_op jit(solution)/shard_map/ppermute | solution.py:712
  220.9 34.6 %shard_map.303 = (bf16[8,1,2,12,16,384]{5,4,3,2,1,0:T(8,128)(2,1)}, bf16[1,2,12,16,384]{4,3,2,1,0:T(8,128)(2,1)}, bf16[1,2,12,16,384]{4,3,2,1,0:T(8,128)(2,1)}, ...) custom-call(bf16[2,2,8,24,384]{4,3,2,1,0:T(8,128)(2,1)} %get-tuple-e, ...), custom_call_target="tpu_custom_call" | custom-call | flops 10871635968 | bytes 15049732 | tf_op jit(solution)/shard_map/pallas_call | solution.py:641
  255.5 4.5 %all-to-all-start.2 = ((bf16[8,1,2,12,16,384]{5,4,3,2,1,0:T(8,128)(2,1)}), bf16[8,1,2,12,16,384]{5,4,3,2,1,0:T(8,128)(2,1)}, u32[]{:S(2)}, u32[]{:S(2)}) async-start(bf16[8,1,2,12,16,384]{5,4,3,2,1,0:T(8,128)(2,1)} %get-tuple-element.65), calls=%async_computation.2 | async-start | bytes 4718592 | tf_op jit(solution)/shard_map/all_to_all | solution.py:718
  260.5 1.5 collective-permute-done.26
  262.1 1.7 collective-permute-start.27
  264.3 29.0 %collective-permute-done.27 = bf16[776,128]{1,0:T(8,128)(2,1)S(1)} collective-permute-done((bf16[776,128]{1,0:T(8,128)(2,1)S(1)}, bf16[776,128]{1,0:T(8,128)(2,1)S(1)}, u32[]{:S(2)}, u32[]{:S(2)}) %collective-permute-start.27) | collective-permute-done | bytes 198688 | tf_op jit(solution)/shard_map/ppermute | solution.py:734
  293.4 1.6 collective-permute-start.28
  296.2 3.3 collective-permute-done.28
  299.6 1.5 collective-permute-start.18
  301.1 3.4 collective-permute-start.19
  305.9 10.6 %shard_map.306 = (bf16[2,48,192]{2,1,0:T(8,128)(2,1)}, f32[8,2,384]{2,1,0:T(2,128)}) custom-call(f32[2,48,192]{2,1,0:T(8,128)} %get-tuple-element.62.refs_0_, f32[2,48,192]{2,1,0:T(8,128)} %collective-permute-done.10.refs_1_, f32[2,48,192]{2,1,0:T(8,128)} %collective-permute-done.11.refs_2_, f32[2,48,192]{2,1,0:T(8,128)} %collective-permute-done.12.refs_3_, ...), custom_call_target="tpu_custom_call" | custom-call | flops 452984832 | bytes 8715264 | tf_op jit(solution)/shard_map/pallas_call | solution.py:641
  316.4 2.6 collective-permute-start.23
  319.1 1.6 collective-permute-start.24
  320.7 3.7 collective-permute-done.17.refs_9_.refs_13_
  324.4 3.7 collective-permute-start.25
  328.1 10.8 %shard_map.307 = (bf16[2,48,192]{2,1,0:T(8,128)(2,1)}, f32[8,2,384]{2,1,0:T(2,128)}) custom-call(f32[2,48,192]{2,1,0:T(8,128)} %get-tuple-element.44.refs_0_, f32[2,48,192]{2,1,0:T(8,128)} %collective-permute-done.refs_1_, f32[2,48,192]{2,1,0:T(8,128)} %collective-permute-done.1.refs_2_, f32[2,48,192]{2,1,0:T(8,128)} %collective-permute-done.2.refs_3_, ...), custom_call_target="tpu_custom_call" | custom-call | flops 452984832 | bytes 6380544 | tf_op jit(solution)/shard_map/pallas_call | solution.py:641
  339.7 7.8 %shard_map.304.refs_2_ = bf16[8,12,2,17280]{3,2,1,0:T(2,128)(2,1)} custom-call(bf16[8,2,2,12,16,384]{5,4,3,2,1,0:T(8,128)(2,1)} %all-to-all-done.3.rows_ref.refs_4_.refs_8_, bf16[192,128]{1,0:T(8,128)(2,1)} %constant.45.clone.table_ref.refs_1_), custom_call_target="tpu_custom_call" | custom-call | flops 452984832 | bytes 11403264 | tf_op jit(solution)/shard_map/pallas_call | solution.py:641
  347.5 3.9 %all-to-all-start.4 = ((f32[8,2,384]{2,1,0:T(2,128)}), f32[8,2,384]{2,1,0:T(2,128)}, u32[]{:S(2)}, u32[]{:S(2)}) async-start(f32[8,2,384]{2,1,0:T(2,128)} %get-tuple-element.79), calls=%async_computation.4 | async-start | bytes 49152 | tf_op jit(solution)/shard_map/all_to_all | solution.py:718
  351.5 7.8 %shard_map.305 = bf16[8,12,2,17280]{3,2,1,0:T(2,128)(2,1)} custom-call(bf16[8,1,2,12,16,384]{5,4,3,2,1,0:T(8,128)(2,1)} %all-to-all-done.2.refs_0_, bf16[192,128]{1,0:T(8,128)(2,1)} %constant.45.clone.table_ref.refs_1_, bf16[8,12,2,17280]{3,2,1,0:T(2,128)(2,1)} %shard_map.304.refs_2_), custom_call_target="tpu_custom_call", output_to_operand_aliasing={{}: (2, {})} | custom-call | flops 452984832 | bytes 15679488 | tf_op jit(solution)/shard_map/pallas_call | solution.py:641
  360.7 3.2 collective-permute-start.22
  364.0 11.2 %shard_map.308.refs_20_ = bf16[8,12,2,17280]{3,2,1,0:T(2,128)(2,1)} custom-call(f32[2,48,192]{2,1,0:T(8,128)} %get-tuple-element.62.refs_0_, f32[2,48,192]{2,1,0:T(8,128)} %collective-permute-done.10.refs_1_, f32[2,48,192]{2,1,0:T(8,128)} %collective-permute-done.11.refs_2_, f32[2,48,192]{2,1,0:T(8,128)} %collective-permute-done.12.refs_3_, ...), custom_call_target="tpu_custom_call" | custom-call | flops 452984832 | bytes 15424512 | tf_op jit(solution)/shard_map/pallas_call | solution.py:641
  375.3 11.4 %shard_map.309 = bf16[8,12,2,17280]{3,2,1,0:T(2,128)(2,1)} custom-call(f32[2,48,192]{2,1,0:T(8,128)} %get-tuple-element.44.refs_0_, f32[2,48,192]{2,1,0:T(8,128)} %collective-permute-done.refs_1_, f32[2,48,192]{2,1,0:T(8,128)} %collective-permute-done.1.refs_2_, f32[2,48,192]{2,1,0:T(8,128)} %collective-permute-done.2.refs_3_, ...), custom_call_target="tpu_custom_call", output_to_operand_aliasing={{}: (20, {})} | custom-call | flops 452984832 | bytes 19700736 | tf_op jit(solution)/shard_map/pallas_call | solution.py:641
  (63 shorter events, 9.0 us)
Async XLA Ops:
  8.2 35.8 %all-to-all-start.1 = ((bf16[8,1,2,8,24,384]{5,4,3,2,1,0:T(8,128)(2,1)}), bf16[8,1,2,8,24,384]{5,4,3,2,1,0:T(8,128)(2,1)}, u32[]{:S(2)}, u32[]{:S(2)}) async-start(bf16[8,1,2,8,24,384]{5,4,3,2,1,0:T(8,128)(2,1)} %shard_map.301), calls=%async_computation.1 | async-start | bytes 4718592 | tf_op jit(solution)/shard_map/all_to_all | solution.py:718
  20.9 8.3 %collective-permute-start.10 = (f32[2,48,192]{2,1,0:T(8,128)}, f32[2,48,192]{2,1,0:T(8,128)}, u32[]{:S(2)}, u32[]{:S(2)}) collective-permute-start(f32[2,48,192]{2,1,0:T(8,128)} %get-tuple-element.62.refs_0_), channel_id=1, source_target_pairs={{0,1},{1,2},{2,3},{3,0},{4,5},{5,6},{6,7},{7,4},{8,9},{9,10},{10,1... | collective-permute-start | bytes 221192 | tf_op jit(solution)/shard_map/ppermute | solution.py:725
  23.2 9.9 %collective-permute-start.11 = (f32[2,48,192]{2,1,0:T(8,128)}, f32[2,48,192]{2,1,0:T(8,128)}, u32[]{:S(2)}, u32[]{:S(2)}) collective-permute-start(f32[2,48,192]{2,1,0:T(8,128)} %get-tuple-element.62.refs_0_), channel_id=1, source_target_pairs={{0,2},{1,3},{2,0},{3,1},{4,6},{5,7},{6,4},{7,5},{8,10},{9,11},{10,... | collective-permute-start | bytes 221192 | tf_op jit(solution)/shard_map/ppermute | solution.py:725
  25.7 7.4 %collective-permute-start.12 = (f32[2,48,192]{2,1,0:T(8,128)}, f32[2,48,192]{2,1,0:T(8,128)}, u32[]{:S(2)}, u32[]{:S(2)}) collective-permute-start(f32[2,48,192]{2,1,0:T(8,128)} %get-tuple-element.62.refs_0_), channel_id=1, source_target_pairs={{0,3},{1,0},{2,1},{3,2},{4,7},{5,4},{6,5},{7,6},{8,11},{9,8},{10,9... | collective-permute-start | bytes 221192 | tf_op jit(solution)/shard_map/ppermute | solution.py:725
  111.5 144.0 %all-to-all-start.3 = ((bf16[8,2,2,12,16,384]{5,4,3,2,1,0:T(8,128)(2,1)}), bf16[8,2,2,12,16,384]{5,4,3,2,1,0:T(8,128)(2,1)}, u32[]{:S(2)}, u32[]{:S(2)}) async-start(bf16[8,2,2,12,16,384]{5,4,3,2,1,0:T(8,128)(2,1)} %get-tuple-element.66), calls=%async_computation.3 | async-start | bytes 9437184 | tf_op jit(solution)/shard_map/all_to_all | solution.py:718
  123.7 12.5 %collective-permute-start = (f32[2,48,192]{2,1,0:T(8,128)}, f32[2,48,192]{2,1,0:T(8,128)}, u32[]{:S(2)}, u32[]{:S(2)}) collective-permute-start(f32[2,48,192]{2,1,0:T(8,128)} %get-tuple-element.44.refs_0_), channel_id=1, source_target_pairs={{0,1},{1,2},{2,3},{3,0},{4,5},{5,6},{6,7},{7,4},{8,9},{9,10},{10,1... | collective-permute-start | bytes 221192 | tf_op jit(solution)/shard_map/ppermute | solution.py:725
  126.3 9.9 %collective-permute-start.1 = (f32[2,48,192]{2,1,0:T(8,128)}, f32[2,48,192]{2,1,0:T(8,128)}, u32[]{:S(2)}, u32[]{:S(2)}) collective-permute-start(f32[2,48,192]{2,1,0:T(8,128)} %get-tuple-element.44.refs_0_), channel_id=1, source_target_pairs={{0,2},{1,3},{2,0},{3,1},{4,6},{5,7},{6,4},{7,5},{8,10},{9,11},{10,... | collective-permute-start | bytes 221192 | tf_op jit(solution)/shard_map/ppermute | solution.py:725
  127.9 8.3 %collective-permute-start.2 = (f32[2,48,192]{2,1,0:T(8,128)}, f32[2,48,192]{2,1,0:T(8,128)}, u32[]{:S(2)}, u32[]{:S(2)}) collective-permute-start(f32[2,48,192]{2,1,0:T(8,128)} %get-tuple-element.44.refs_0_), channel_id=1, source_target_pairs={{0,3},{1,0},{2,1},{3,2},{4,7},{5,4},{6,5},{7,6},{8,11},{9,8},{10,9... | collective-permute-start | bytes 221192 | tf_op jit(solution)/shard_map/ppermute | solution.py:725
  146.5 3.8 collective-permute-start.3
  146.6 36.4 %collective-permute-start.4 = (bf16[2,2,8,24,384]{4,3,2,1,0:T(8,128)(2,1)}, bf16[2,2,8,24,384]{4,3,2,1,0:T(8,128)(2,1)S(1)}, u32[]{:S(2)}, u32[]{:S(2)}) collective-permute-start(bf16[2,2,8,24,384]{4,3,2,1,0:T(8,128)(2,1)} %get-tuple-element.56), channel_id=1, source_target_pairs={{0,8},{4,12},{8,0},{12,4},{16,24},{20,28},{24,16},{28,20},{1,9},{5... | collective-permute-start | bytes 1769480 | tf_op jit(solution)/shard_map/ppermute | solution.py:712
  148.5 46.1 %collective-permute-start.5 = (bf16[2,2,8,24,384]{4,3,2,1,0:T(8,128)(2,1)}, bf16[2,2,8,24,384]{4,3,2,1,0:T(8,128)(2,1)}, u32[]{:S(2)}, u32[]{:S(2)}) collective-permute-start(bf16[2,2,8,24,384]{4,3,2,1,0:T(8,128)(2,1)} %get-tuple-element.57), channel_id=1, source_target_pairs={{0,12},{4,8},{8,4},{12,0},{16,28},{20,24},{24,20},{28,16},{1,13},{... | collective-permute-start | bytes 1769480 | tf_op jit(solution)/shard_map/ppermute | solution.py:712
  148.6 46.1 %collective-permute-start.6 = (bf16[2,2,8,24,384]{4,3,2,1,0:T(8,128)(2,1)}, bf16[2,2,8,24,384]{4,3,2,1,0:T(8,128)(2,1)}, u32[]{:S(2)}, u32[]{:S(2)}) collective-permute-start(bf16[2,2,8,24,384]{4,3,2,1,0:T(8,128)(2,1)} %get-tuple-element.58), channel_id=1, source_target_pairs={{0,16},{4,20},{8,24},{12,28},{16,0},{20,4},{24,8},{28,12},{1,17},{... | collective-permute-start | bytes 1769480 | tf_op jit(solution)/shard_map/ppermute | solution.py:712
  150.3 44.3 %collective-permute-start.7 = (bf16[2,2,8,24,384]{4,3,2,1,0:T(8,128)(2,1)}, bf16[2,2,8,24,384]{4,3,2,1,0:T(8,128)(2,1)}, u32[]{:S(2)}, u32[]{:S(2)}) collective-permute-start(bf16[2,2,8,24,384]{4,3,2,1,0:T(8,128)(2,1)} %get-tuple-element.59), channel_id=1, source_target_pairs={{0,20},{4,16},{8,28},{12,24},{16,4},{20,0},{24,12},{28,8},{1,21},{... | collective-permute-start | bytes 1769480 | tf_op jit(solution)/shard_map/ppermute | solution.py:712
  150.3 32.7 %copy-start.4 = (bf16[2,2,8,24,384]{4,3,2,1,0:T(8,128)(2,1)}, bf16[2,2,8,24,384]{4,3,2,1,0:T(8,128)(2,1)S(1)}, u32[]{:S(2)}) copy-start(bf16[2,2,8,24,384]{4,3,2,1,0:T(8,128)(2,1)S(1)} %collective-permute-done.3.refs_1_.refs_9_) | copy-start | bytes 1769476
  150.3 59.0 %collective-permute-start.8 = (bf16[2,2,8,24,384]{4,3,2,1,0:T(8,128)(2,1)}, bf16[2,2,8,24,384]{4,3,2,1,0:T(8,128)(2,1)}, u32[]{:S(2)}, u32[]{:S(2)}) collective-permute-start(bf16[2,2,8,24,384]{4,3,2,1,0:T(8,128)(2,1)} %get-tuple-element.60), channel_id=1, source_target_pairs={{0,24},{4,28},{8,16},{12,20},{16,8},{20,12},{24,0},{28,4},{1,25},{... | collective-permute-start | bytes 1769480 | tf_op jit(solution)/shard_map/ppermute | solution.py:712
  183.1 0.9 copy-start.5
  183.9 37.0 %collective-permute-start.9 = (bf16[2,2,8,24,384]{4,3,2,1,0:T(8,128)(2,1)}, bf16[2,2,8,24,384]{4,3,2,1,0:T(8,128)(2,1)}, u32[]{:S(2)}, u32[]{:S(2)}) collective-permute-start(bf16[2,2,8,24,384]{4,3,2,1,0:T(8,128)(2,1)} %get-tuple-element.61), channel_id=1, source_target_pairs={{0,28},{4,24},{8,20},{12,16},{16,12},{20,8},{24,4},{28,0},{1,29},{... | collective-permute-start | bytes 1769480 | tf_op jit(solution)/shard_map/ppermute | solution.py:712
  255.5 4.6 %copy-start.1 = (bf16[776,128]{1,0:T(8,128)(2,1)S(1)}, bf16[776,128]{1,0:T(8,128)(2,1)}, u32[]{:S(2)}) copy-start(bf16[776,128]{1,0:T(8,128)(2,1)} %get-tuple-element.78) | copy-start | bytes 595972
  255.5 8.3 %copy-start.2 = (s32[128]{0:T(128)S(1)}, s32[128]{0:T(128)}, u32[]{:S(2)}) copy-start(s32[128]{0:T(128)} %constant.49.clone) | copy-start | bytes 1540
  255.5 8.3 %copy-start.3 = (s32[128]{0:T(128)S(1)}, s32[128]{0:T(128)}, u32[]{:S(2)}) copy-start(s32[128]{0:T(128)} %constant.50.clone) | copy-start | bytes 1540
  255.5 8.3 %copy-start.7 = (bf16[1,2,12,16,384]{4,3,2,1,0:T(8,128)(2,1)S(1)}, bf16[1,2,12,16,384]{4,3,2,1,0:T(8,128)(2,1)}, u32[]{:S(2)}) copy-start(bf16[1,2,12,16,384]{4,3,2,1,0:T(8,128)(2,1)} %get-tuple-element.68) | copy-start | bytes 884740
  255.5 8.5 %copy-start.6 = (bf16[1,2,12,16,384]{4,3,2,1,0:T(8,128)(2,1)S(1)}, bf16[1,2,12,16,384]{4,3,2,1,0:T(8,128)(2,1)}, u32[]{:S(2)}) copy-start(bf16[1,2,12,16,384]{4,3,2,1,0:T(8,128)(2,1)} %get-tuple-element.69) | copy-start | bytes 884740
  255.5 39.4 %copy-start = (bf16[192,128]{1,0:T(8,128)(2,1)S(1)}, bf16[192,128]{1,0:T(8,128)(2,1)}, u32[]{:S(2)}) copy-start(bf16[192,128]{1,0:T(8,128)(2,1)} %constant.47.clone.refs_7_.refs_11_) | copy-start | bytes 147460
  255.5 92.0 %all-to-all-start.2 = ((bf16[8,1,2,12,16,384]{5,4,3,2,1,0:T(8,128)(2,1)}), bf16[8,1,2,12,16,384]{5,4,3,2,1,0:T(8,128)(2,1)}, u32[]{:S(2)}, u32[]{:S(2)}) async-start(bf16[8,1,2,12,16,384]{5,4,3,2,1,0:T(8,128)(2,1)} %get-tuple-element.65), calls=%async_computation.2 | async-start | bytes 4718592 | tf_op jit(solution)/shard_map/all_to_all | solution.py:718
  260.1 1.9 collective-permute-start.26
  262.1 31.2 %collective-permute-start.27 = (bf16[776,128]{1,0:T(8,128)(2,1)S(1)}, bf16[776,128]{1,0:T(8,128)(2,1)S(1)}, u32[]{:S(2)}, u32[]{:S(2)}) collective-permute-start(bf16[776,128]{1,0:T(8,128)(2,1)S(1)} %add_convert_fusion.1), channel_id=1, source_target_pairs={{0,8},{4,12},{8,0},{12,4},{16,24},{20,28},{24,16},{28,20},{1,9},{5... | collective-permute-start | bytes 595976 | tf_op jit(solution)/shard_map/ppermute | solution.py:734
  263.8 35.8 %collective-permute-start.13 = (bf16[1,2,12,16,384]{4,3,2,1,0:T(8,128)(2,1)S(1)}, bf16[1,2,12,16,384]{4,3,2,1,0:T(8,128)(2,1)}, u32[]{:S(2)}, u32[]{:S(2)}) collective-permute-start(bf16[1,2,12,16,384]{4,3,2,1,0:T(8,128)(2,1)S(1)} %copy-done.7), channel_id=1, source_target_pairs={{0,4},{4,0},{8,12},{12,8},{16,20},{20,16},{24,28},{28,24},{1,5},{5... | collective-permute-start | bytes 884744 | tf_op jit(solution)/shard_map/ppermute | solution.py:712
  264.0 37.1 %collective-permute-start.14 = (bf16[1,2,12,16,384]{4,3,2,1,0:T(8,128)(2,1)S(1)}, bf16[1,2,12,16,384]{4,3,2,1,0:T(8,128)(2,1)}, u32[]{:S(2)}, u32[]{:S(2)}) collective-permute-start(bf16[1,2,12,16,384]{4,3,2,1,0:T(8,128)(2,1)S(1)} %copy-done.6), channel_id=1, source_target_pairs={{0,8},{4,12},{8,0},{12,4},{16,24},{20,28},{24,16},{28,20},{1,9},{5... | collective-permute-start | bytes 884744 | tf_op jit(solution)/shard_map/ppermute | solution.py:712
  293.4 6.2 %collective-permute-start.28 = (bf16[776,128]{1,0:T(8,128)(2,1)S(1)}, bf16[776,128]{1,0:T(8,128)(2,1)S(1)}, u32[]{:S(2)}, u32[]{:S(2)}) collective-permute-start(bf16[776,128]{1,0:T(8,128)(2,1)S(1)} %add_convert_fusion), channel_id=1, source_target_pairs={{0,16},{4,20},{8,24},{12,28},{16,0},{20,4},{24,8},{28,12},{1,17},{... | collective-permute-start | bytes 595976 | tf_op jit(solution)/shard_map/ppermute | solution.py:734
  295.7 20.8 %collective-permute-start.15 = (bf16[1,2,12,16,384]{4,3,2,1,0:T(8,128)(2,1)}, bf16[1,2,12,16,384]{4,3,2,1,0:T(8,128)(2,1)}, u32[]{:S(2)}, u32[]{:S(2)}) collective-permute-start(bf16[1,2,12,16,384]{4,3,2,1,0:T(8,128)(2,1)} %get-tuple-element.70), channel_id=1, source_target_pairs={{0,12},{4,8},{8,4},{12,0},{16,28},{20,24},{24,20},{28,16},{1,13},{... | collective-permute-start | bytes 884744 | tf_op jit(solution)/shard_map/ppermute | solution.py:712
  295.7 23.4 %collective-permute-start.16 = (bf16[1,2,12,16,384]{4,3,2,1,0:T(8,128)(2,1)}, bf16[1,2,12,16,384]{4,3,2,1,0:T(8,128)(2,1)}, u32[]{:S(2)}, u32[]{:S(2)}) collective-permute-start(bf16[1,2,12,16,384]{4,3,2,1,0:T(8,128)(2,1)} %get-tuple-element.71), channel_id=1, source_target_pairs={{0,16},{4,20},{8,24},{12,28},{16,0},{20,4},{24,8},{28,12},{1,17},{... | collective-permute-start | bytes 884744 | tf_op jit(solution)/shard_map/ppermute | solution.py:712
  299.5 24.9 %collective-permute-start.17 = (bf16[1,2,12,16,384]{4,3,2,1,0:T(8,128)(2,1)}, bf16[1,2,12,16,384]{4,3,2,1,0:T(8,128)(2,1)}, u32[]{:S(2)}, u32[]{:S(2)}) collective-permute-start(bf16[1,2,12,16,384]{4,3,2,1,0:T(8,128)(2,1)} %get-tuple-element.72), channel_id=1, source_target_pairs={{0,20},{4,16},{8,28},{12,24},{16,4},{20,0},{24,12},{28,8},{1,21},{... | collective-permute-start | bytes 884744 | tf_op jit(solution)/shard_map/ppermute | solution.py:712
  299.6 28.5 %collective-permute-start.18 = (bf16[1,2,12,16,384]{4,3,2,1,0:T(8,128)(2,1)}, bf16[1,2,12,16,384]{4,3,2,1,0:T(8,128)(2,1)}, u32[]{:S(2)}, u32[]{:S(2)}) collective-permute-start(bf16[1,2,12,16,384]{4,3,2,1,0:T(8,128)(2,1)} %get-tuple-element.73), channel_id=1, source_target_pairs={{0,24},{4,28},{8,16},{12,20},{16,8},{20,12},{24,0},{28,4},{1,25},{... | collective-permute-start | bytes 884744 | tf_op jit(solution)/shard_map/ppermute | solution.py:712
  301.1 27.0 %collective-permute-start.19 = (bf16[1,2,12,16,384]{4,3,2,1,0:T(8,128)(2,1)}, bf16[1,2,12,16,384]{4,3,2,1,0:T(8,128)(2,1)}, u32[]{:S(2)}, u32[]{:S(2)}) collective-permute-start(bf16[1,2,12,16,384]{4,3,2,1,0:T(8,128)(2,1)} %get-tuple-element.74), channel_id=1, source_target_pairs={{0,28},{4,24},{8,20},{12,16},{16,12},{20,8},{24,4},{28,0},{1,29},{... | collective-permute-start | bytes 884744 | tf_op jit(solution)/shard_map/ppermute | solution.py:712
  316.4 44.3 %collective-permute-start.23 = (bf16[2,48,192]{2,1,0:T(8,128)(2,1)}, bf16[2,48,192]{2,1,0:T(8,128)(2,1)}, u32[]{:S(2)}, u32[]{:S(2)}) collective-permute-start(bf16[2,48,192]{2,1,0:T(8,128)(2,1)} %get-tuple-element.77.refs_4_), channel_id=1, source_target_pairs={{0,1},{1,2},{2,3},{3,0},{4,5},{5,6},{6,7},{7,4},{8,9},{9,10},{10,1... | collective-permute-start | bytes 110600 | tf_op jit(solution)/shard_map/ppermute | solution.py:725
  319.1 44.9 %collective-permute-start.24 = (bf16[2,48,192]{2,1,0:T(8,128)(2,1)}, bf16[2,48,192]{2,1,0:T(8,128)(2,1)}, u32[]{:S(2)}, u32[]{:S(2)}) collective-permute-start(bf16[2,48,192]{2,1,0:T(8,128)(2,1)} %get-tuple-element.77.refs_4_), channel_id=1, source_target_pairs={{0,2},{1,3},{2,0},{3,1},{4,6},{5,7},{6,4},{7,5},{8,10},{9,11},{10,... | collective-permute-start | bytes 110600 | tf_op jit(solution)/shard_map/ppermute | solution.py:725
  324.4 39.6 %collective-permute-start.25 = (bf16[2,48,192]{2,1,0:T(8,128)(2,1)}, bf16[2,48,192]{2,1,0:T(8,128)(2,1)}, u32[]{:S(2)}, u32[]{:S(2)}) collective-permute-start(bf16[2,48,192]{2,1,0:T(8,128)(2,1)} %get-tuple-element.77.refs_4_), channel_id=1, source_target_pairs={{0,3},{1,0},{2,1},{3,2},{4,7},{5,4},{6,5},{7,6},{8,11},{9,8},{10,9... | collective-permute-start | bytes 110600 | tf_op jit(solution)/shard_map/ppermute | solution.py:725
  338.9 36.4 %collective-permute-start.20 = (bf16[2,48,192]{2,1,0:T(8,128)(2,1)}, bf16[2,48,192]{2,1,0:T(8,128)(2,1)}, u32[]{:S(2)}, u32[]{:S(2)}) collective-permute-start(bf16[2,48,192]{2,1,0:T(8,128)(2,1)} %get-tuple-element.76.refs_4_), channel_id=1, source_target_pairs={{0,1},{1,2},{2,3},{3,0},{4,5},{5,6},{6,7},{7,4},{8,9},{9,10},{10,1... | collective-permute-start | bytes 110600 | tf_op jit(solution)/shard_map/ppermute | solution.py:725
  339.2 36.1 %collective-permute-start.21 = (bf16[2,48,192]{2,1,0:T(8,128)(2,1)}, bf16[2,48,192]{2,1,0:T(8,128)(2,1)}, u32[]{:S(2)}, u32[]{:S(2)}) collective-permute-start(bf16[2,48,192]{2,1,0:T(8,128)(2,1)} %get-tuple-element.76.refs_4_), channel_id=1, source_target_pairs={{0,2},{1,3},{2,0},{3,1},{4,6},{5,7},{6,4},{7,5},{8,10},{9,11},{10,... | collective-permute-start | bytes 110600 | tf_op jit(solution)/shard_map/ppermute | solution.py:725
  347.5 11.8 %all-to-all-start.4 = ((f32[8,2,384]{2,1,0:T(2,128)}), f32[8,2,384]{2,1,0:T(2,128)}, u32[]{:S(2)}, u32[]{:S(2)}) async-start(f32[8,2,384]{2,1,0:T(2,128)} %get-tuple-element.79), calls=%async_computation.4 | async-start | bytes 49152 | tf_op jit(solution)/shard_map/all_to_all | solution.py:718
  360.7 14.5 %collective-permute-start.22 = (bf16[2,48,192]{2,1,0:T(8,128)(2,1)}, bf16[2,48,192]{2,1,0:T(8,128)(2,1)}, u32[]{:S(2)}, u32[]{:S(2)}) collective-permute-start(bf16[2,48,192]{2,1,0:T(8,128)(2,1)} %get-tuple-element.76.refs_4_), channel_id=1, source_target_pairs={{0,3},{1,0},{2,1},{3,2},{4,7},{5,4},{6,5},{7,6},{8,11},{9,8},{10,9... | collective-permute-start | bytes 110600 | tf_op jit(solution)/shard_map/ppermute | solution.py:725

commit v6 on v5

--- a/solution.py
+++ b/solution.py
@@ -340,20 +340,14 @@
             out_ref[which : which + 1, ri * p.lanes : (ri + 1) * p.lanes] = row
 
 
-def spectral_kernel(p, step_modes, peers, split, joined, *refs):
+def spectral_kernel(p, step_modes, peers, y_near, x_near, follows, *refs):
     x_refs, g_refs, refs = refs[:peers], refs[peers : 2 * peers], refs[2 * peers :]
     there_ref, back_ref, w_first_ref, w_second_ref, b_first_ref, b_second_ref = refs[:6]
     refs = refs[6:]
-    me, before_ref = None, None
-    if not joined:
-        before_ref, refs = refs[0], refs[1:]
-    if split:
-        me, refs = refs[0][0], refs[1:]
-    y_refs, refs = refs[:1], refs[1:]
-    x_out_refs = y_refs
-    if not joined:
-        x_outs = p.space if split else 1
-        x_out_refs, refs = refs[:x_outs], refs[x_outs:]
+    before_ref, refs = (refs[0], refs[1:]) if follows else (None, refs)
+    me, refs = (refs[0][0], refs[1:]) if y_near or x_near else (None, refs)
+    y_count, x_count = (p.space if near else 1 for near in (y_near, x_near))
+    y_refs, x_out_refs, refs = refs[:y_count], refs[y_count : y_count + x_count], refs[y_count + x_count :]
     (
         total_ref,
         gb_ref,
@@ -462,8 +456,8 @@
 
     @pl.when(group == pl.num_programs(1) - 1)
     def _():
-        send_turn(p, turn_y_ref, y_refs, p.rows, 2 * p.modes)
-        send_turn(p, turn_x_ref, x_out_refs, p.rows, 2 * p.modes, 1 if joined else 0, me)
+        send_turn(p, turn_y_ref, y_refs, p.rows, 2 * p.modes, 0, me if y_near else None)
+        send_turn(p, turn_x_ref, x_out_refs, p.rows, 2 * p.modes, 0, me if x_near else None)
         acc1_ref[...] += mul(lat_ref[...], gpre_ref[...], TN)
         acc2_ref[...] += mul(hid_ref[...], gpost_ref[...], TN)
 
@@ -510,11 +504,12 @@
         keep(place, len(rows), jnp.concatenate(rows, axis=0))
 
 
-def mixed_kernel(p, rows_ref, table_ref, out_ref, words_ref):
+def mixed_kernel(p, peers, *refs):
+    rows_refs, (table_ref, out_ref, words_ref) = refs[:peers], refs[peers:]
     factor = 1.0 / math.sqrt(p.lon)
 
     for h in range(p.step):
-        block = peer_rows(p, (rows_ref,), h)
+        block = peer_rows(p, rows_refs, h)
         tokens = mul(table_ref[...], block) * factor
         scatter_row(p, tokens, words_ref.at[h], out_ref, h)
 
@@ -668,7 +663,7 @@
         to_half(turned.T),
         jnp.asarray(plain_scale),
         jnp.asarray(double_scale),
-        to_half(owner * twice),
+        owner * twice,
         owner,
     )
 
@@ -730,10 +725,18 @@
 def reduced(p, value, kind):
     step = 1
     while step < p.space:
+        wide = step > 1 and 4 * step <= p.space
         own = value.astype(kind)
-        other = lax.ppermute(own, "space", [(i, i ^ step) for i in range(p.space)])
-        value = own.astype(single) + other.astype(single)
-        step *= 2
+        near, far, both = (
+            lax.ppermute(own, "space", [(i, i ^ (step * k)) for i in range(p.space)])
+            if k == 1 or wide
+            else None
+            for k in (1, 2, 3)
+        )
+        value = own.astype(single) + near.astype(single)
+        if wide:
+            value = value + (far.astype(single) + both.astype(single))
+        step *= 4 if wide else 2
     return value
 
 
@@ -741,12 +744,14 @@
     p = Plan(members, w_first.shape[-1], space, chan)
     size = p.packs // 2
     grid = (size, p.steps)
-    table, plain_scale, double_scale, mixed_table, slope_plain = lon_tables(p)
+    table, plain_scale, double_scale, mixed_plain, slope_plain = lon_tables(p)
     there_plain, back_table = lat_tables(p)
     slope_table, there_table = jnp.asarray(slope_plain, half), jnp.asarray(there_plain, half)
+    mixed_table = jnp.asarray(mixed_plain, half)
     split = splits(space)
     if split:
         slope_near = by_distance(p, slope_plain, 2 * p.modes)
+        mixed_near = by_distance(p, mixed_plain, 2 * p.modes)
         there_near = by_distance(p, there_plain, 2 * p.rows)
         me = lax.axis_index("space").astype(jnp.int32).reshape(1)
     own_spec = pl.BlockSpec(memory_space=pltpu.SMEM)
@@ -762,8 +767,7 @@
     def sent(wide):
         return jax.ShapeDtypeStruct((space, wide, size, p.modes, 2 * p.rows, p.lanes), half)
 
-    def returned(wide):
-        return jax.ShapeDtypeStruct((space, wide, size, p.rows, 2 * p.modes, p.lanes), half)
+    returned = jax.ShapeDtypeStruct((space, 1, size, p.rows, 2 * p.modes, p.lanes), half)
 
     count = 2 * p.stack * p.rows
     stored = jax.ShapeDtypeStruct(members.shape, half)
@@ -824,40 +828,39 @@
     step_modes = 2 if p.modes % 2 == 0 else 1
     wide_lanes = 2 * p.lanes
 
-    def spectral_chunk(x_in, x_which, g_in, before, near):
-        joined = before is None
-        tail = (there_near if near else there_table, back_table)
+    def spectral_chunk(x_in, x_which, g_in, before, y_near, x_near):
+        peers = len(x_in)
+        tail = (there_near if peers > 1 else there_table, back_table)
         tail += (w_first, w_second, b_first, b_second)
-        tail += () if joined else (before,)
+        tail += () if before is None else (before,)
         specs = [whole_spec(v) for v in tail]
-        if near:
+        if y_near or x_near:
             tail, specs = (*tail, me), [*specs, own_spec]
 
         def mode_spec(which):
-            lead = (1, 1) if near else (space, 1, 1)
-            at = (which,) if near else (0, which)
+            lead = (1, 1) if peers > 1 else (space, 1, 1)
+            at = (which,) if peers > 1 else (0, which)
             return pl.BlockSpec(
                 lead + (step_modes, 2 * p.rows, p.lanes), lambda b, m: at + (b, m, 0, 0)
             )
 
-        peers = len(x_in)
-        outs = [returned(2 if joined else 1)]
-        out_specs = [peer_spec(o, 0, o.shape[1]) for o in outs]
-        if near:
-            one = jax.ShapeDtypeStruct(returned(1).shape[1:], half)
-            outs, out_specs = outs + [one] * space, out_specs + [one_peer_spec(one)] * space
-        elif not joined:
-            outs, out_specs = outs * 2, out_specs * 2
+        outs, out_specs = [], []
+        one = jax.ShapeDtypeStruct(returned.shape[1:], half)
+        for near in (y_near, x_near):
+            outs += [one] * space if near else [returned]
+            out_specs += [one_peer_spec(one)] * space if near else [peer_spec(returned)]
         bias_rows = -(-4 * p.groups // 8) * 8
         totals = jax.ShapeDtypeStruct(
-            (4 * p.groups * p.width + bias_rows, LANES), single if joined else half
+            (4 * p.groups * p.width + bias_rows, LANES), single if before is None else half
         )
         kept = pltpu.VMEM((p.modes * p.lat, wide_lanes), half)
         held = pltpu.VMEM((step_modes * p.lat, wide_lanes), single)
         brief = pltpu.VMEM((step_modes * p.lat, wide_lanes), half)
         turn_out = pltpu.VMEM((p.tiles, p.lat * 2 * p.modes, LANES), single)
         return call(
-            functools.partial(spectral_kernel, p, step_modes, peers, near, joined),
+            functools.partial(
+                spectral_kernel, p, step_modes, peers, y_near, x_near, before is not None
+            ),
             (size, p.modes // step_modes), (*x_in, *g_in, *tail),
             [mode_spec(x_which)] * peers + [mode_spec(0)] * peers + specs,
             [*outs, totals],
@@ -869,19 +872,20 @@
             12 * size * p.modes * p.lat * wide_lanes * wide_lanes,
         )
 
-    def mixed_chunk(c, rows_in, which, before):
+    def mixed_chunk(c, rows_in, before):
+        table_in = mixed_near if len(rows_in) > 1 else mixed_table
         return out_call(
-            functools.partial(mixed_kernel, p), (rows_in, mixed_table),
-            [peer_part_spec(p, rows_in, which), whole_spec(mixed_table)],
+            functools.partial(mixed_kernel, p, len(rows_in)), (*rows_in, table_in),
+            rows_specs(rows_in) + [whole_spec(table_in)],
             [stored], [stored_spec(p, c * size)], [lines], dft_flops, before,
         )
 
-    def rows_specs(rows_in, which):
+    def rows_specs(rows_in):
         if len(rows_in) == 1:
-            return [peer_part_spec(p, rows_in[0], which)]
+            return [peer_part_spec(p, rows_in[0])]
         return [one_peer_part_spec(p, value) for value in rows_in]
 
-    def slope_sums_chunk(stats, rows_in, which, tokens, before):
+    def slope_sums_chunk(stats, rows_in, tokens, before):
         near = len(rows_in) > 1
         tail = (affine, slope_near if near else slope_table, wide_table, sum_table)
         tail += () if before is None else (before,)
@@ -892,7 +896,7 @@
         return call(
             functools.partial(slope_sums_kernel, p, len(rows_in), before is not None),
             grid, (*stats, *rows_in, tokens, *tail),
-            [part_spec(p, s) for s in stats] + rows_specs(rows_in, which)
+            [part_spec(p, s) for s in stats] + rows_specs(rows_in)
             + [part_spec(p, tokens)] + [whole_spec(v) for v in tail],
             outs, [part_spec(p, outs[0]), whole_spec(outs[1])],
             [
@@ -902,13 +906,13 @@
             dft_flops,
         )
 
-    def input_grad_chunk(c, stats, parts, rows_in, which, tokens, before):
+    def input_grad_chunk(c, stats, parts, rows_in, tokens, before):
         near = len(rows_in) > 1
         tail = (affine, slope_near if near else slope_table, wide_table)
         return out_call(
             functools.partial(input_grad_kernel, p, len(rows_in)),
             (*stats, *parts, *rows_in, tokens, *tail),
-            [part_spec(p, s) for s in (*stats, *parts)] + rows_specs(rows_in, which)
+            [part_spec(p, s) for s in (*stats, *parts)] + rows_specs(rows_in)
             + [part_spec(p, tokens)] + [whole_spec(v) for v in tail],
             [stored], [stored_spec(p, c * size)], [rows_scratch, rows_scratch, lines], dft_flops,
             before,
@@ -928,19 +932,21 @@
     tokens1, sums = stats_chunk(1)
     stats1 = channel_sums(sums)
     both1 = moved(normalise_chunk(stats1, tokens1, both1, split), split)
-    out0, totals = spectral_chunk(x0, 0, g0, None, False)
-    rows0 = exchange(out0)
-    y1, *dx1, totals = spectral_chunk(both1, 1, both1, totals, split)
-    dx1 = moved(dx1, split)
-    y1 = exchange(y1)
-    sums, params = slope_sums_chunk(stats0, (rows0,), 1, tokens0, None)
+    cut = space if split else 1
+    *outs, totals = spectral_chunk(x0, 0, g0, None, split, False)
+    dx0 = moved(outs[cut:], False)
+    y0 = moved(outs[:cut], split)
+    *outs, totals = spectral_chunk(both1, 1, both1, totals, False, split)
+    dx1 = moved(outs[1:], split)
+    y1 = moved(outs[:1], False)
+    sums, params = slope_sums_chunk(stats0, dx0, tokens0, None)
     parts = channel_sums(sums)
-    grad_input = input_grad_chunk(0, stats0, parts, (rows0,), 1, tokens0, None)
-    mixed = mixed_chunk(0, rows0, 0, None)
-    sums, params = slope_sums_chunk(stats1, dx1, 0, tokens1, params)
+    grad_input = input_grad_chunk(0, stats0, parts, dx0, tokens0, None)
+    mixed = mixed_chunk(0, y0, None)
+    sums, params = slope_sums_chunk(stats1, dx1, tokens1, params)
     parts = channel_sums(sums)
-    grad_input = input_grad_chunk(1, stats1, parts, dx1, 0, tokens1, grad_input)[0]
-    mixed = mixed_chunk(1, y1, 0, mixed)[0]
+    grad_input = input_grad_chunk(1, stats1, parts, dx1, tokens1, grad_input)[0]
+    mixed = mixed_chunk(1, y1, mixed)[0]
 
     size_w = p.groups * p.width
     flat = reduced(p, totals, half)[:, : p.width]

time: 389 us -> 385 us (0.990)
  blocking collectives: 33.7 us -> 0 us
  waiting for transfers between devices: 107 us -> 126 us
  starting transfers between devices: 57.7 us -> 66.7 us
    ppermute x14 -> x21, waiting for transfers between devices: 68.2 us -> 121 us  [exchange_near(): lax.ppermute(value, 'space', [(i, i ^ x) for i in range(count)])]
    ppermute x3 -> x4, waiting for transfers between devices: 33.8 us -> 0.01 us  [reduced(): lax.ppermute(own, 'space', [(i, i ^ step * k) for i in range(p.space)])]
    all_to_all x1 -> x0, blocking collectives: 33.7 us -> none  [exchange(): return lax.all_to_all(value, 'space', 0, 0, tiled=True)]
    ppermute x14 -> x21, starting transfers between devices: 12.6 us -> 19.7 us  [exchange_near(): lax.ppermute(value, 'space', [(i, i ^ x) for i in range(count)])]
    all_to_all x4 -> x5, starting transfers between devices: 18.3 us -> 23.1 us  [exchange(): return lax.all_to_all(value, 'space', 0, 0, tiled=True)]
  transfers between devices with their start and end apart: 33 -> 42, of which waited for: 10 -> 11; matrix products, arithmetic and copies ran while one was open for 2% -> 2% of each run, Pallas kernels for 33% -> 42%
where the time goes in v6:
time: 385 us; the launch traced here: 383 us
  Pallas kernels  179 us (46%)
  waiting for transfers between devices  126 us (33%)
  starting transfers between devices  66.7 us (17%)
  other arithmetic  4.29 us (1%)
  local copies, waits for them, and re-layouts  3.88 us (1%)
    pallas_call x14, Pallas kernels, _call(): pl.pallas_call(body, grid=grid, in_specs=in_specs, out_specs=out_specs, o...  179 us
    ppermute x21, waiting for transfers between devices, exchange_near(): lax.ppermute(value, 'space', [(i, i ^ x) for i in range(count)])  121 us
    all_to_all x5, starting transfers between devices, exchange(): return lax.all_to_all(value, 'space', 0, 0, tiled=True)  23.1 us
    ppermute x12, starting transfers between devices, around(): lax.ppermute(value, axis, [(i, (i + step) % size) for i in range(size)])  19.9 us
    ppermute x21, starting transfers between devices, exchange_near(): lax.ppermute(value, 'space', [(i, i ^ x) for i in range(count)])  19.7 us
  transfers between devices with their start and end apart: 42, of which 11 were waited for; matrix products, arithmetic and copies ran while one was open for 2% of the time, Pallas kernels for 42%

profile of v6, /device:TPU:0, one launch (start us, length us, event | category | flops | bytes accessed | tf_op | source)
XLA Modules:
  0.0 382.9 jit_solution(14991115467335126235)
XLA Ops:
  0.6 7.5 %shard_map.337 = bf16[8,1,2,8,24,384]{5,4,3,2,1,0:T(8,128)(2,1)} custom-call(bf16[8,12,2,17280]{3,2,1,0:T(2,128)(2,1)} %stored_ref.7, bf16[128,192]{1,0:T(8,128)(2,1)} %constant.42.clone.table_ref.refs_6_, f32[128,1]{1,0:T(8,128)} %constant.44.clone.scale_ref), custom_call_target="tpu_custom_call" | custom-call | flops 452984832 | bytes 9044480 | tf_op jit(solution)/shard_map/pallas_call | solution.py:636
  8.2 5.2 %all-to-all-start.1 = ((bf16[8,1,2,8,24,384]{5,4,3,2,1,0:T(8,128)(2,1)}), bf16[8,1,2,8,24,384]{5,4,3,2,1,0:T(8,128)(2,1)}, u32[]{:S(2)}, u32[]{:S(2)}) async-start(bf16[8,1,2,8,24,384]{5,4,3,2,1,0:T(8,128)(2,1)} %shard_map.337), calls=%async_computation.1 | async-start | bytes 4718592 | tf_op jit(solution)/shard_map/all_to_all | solution.py:713
  13.3 7.6 %shard_map.335 = (bf16[2,12,192,384]{3,2,1,0:T(8,128)(2,1)}, f32[2,48,192]{2,1,0:T(8,128)}) custom-call(bf16[8,12,2,17280]{3,2,1,0:T(2,128)(2,1)} %stored_ref.6, bf16[2,8,384]{2,1,0:T(8,128)(2,1)} %constant.55.clone.sum_ref.refs_9_.refs_16_), custom_call_target="tpu_custom_call" | custom-call | flops 113246208 | bytes 10260480 | tf_op jit(solution)/shard_map/pallas_call | solution.py:636
  20.9 2.3 collective-permute-start.10
  23.2 2.6 collective-permute-start.11
  25.8 1.4 collective-permute-start.12
  29.3 3.9 %collective-permute-done.11.refs_2_ = f32[2,48,192]{2,1,0:T(8,128)} collective-permute-done((f32[2,48,192]{2,1,0:T(8,128)}, f32[2,48,192]{2,1,0:T(8,128)}, u32[]{:S(2)}, u32[]{:S(2)}) %collective-permute-start.11) | collective-permute-done | bytes 73760 | tf_op jit(solution)/shard_map/ppermute | solution.py:720
  33.8 10.2 %shard_map.336 = bf16[8,1,2,8,24,384]{5,4,3,2,1,0:T(8,128)(2,1)} custom-call(f32[2,48,192]{2,1,0:T(8,128)} %get-tuple-element.70.refs_0_, f32[2,48,192]{2,1,0:T(8,128)} %collective-permute-done.10.refs_1_, f32[2,48,192]{2,1,0:T(8,128)} %collective-permute-done.11.refs_2_, f32[2,48,192]{2,1,0:T(8,128)} %collective-permute-done.12.refs_3_, ...), custom_call_target="tpu_custom_call" | custom-call | flops 452984832 | bytes 6282752 | tf_op jit(solution)/shard_map/pallas_call | solution.py:636
  44.0 4.4 %all-to-all-start = ((bf16[8,1,2,8,24,384]{5,4,3,2,1,0:T(8,128)(2,1)}), bf16[8,1,2,8,24,384]{5,4,3,2,1,0:T(8,128)(2,1)}, u32[]{:S(2)}, u32[]{:S(2)}) async-start(bf16[8,1,2,8,24,384]{5,4,3,2,1,0:T(8,128)(2,1)} %shard_map.336), calls=%async_computation | async-start | bytes 4718592 | tf_op jit(solution)/shard_map/all_to_all | solution.py:713
  48.4 7.6 %shard_map.332 = (bf16[2,12,192,384]{3,2,1,0:T(8,128)(2,1)}, f32[2,48,192]{2,1,0:T(8,128)}) custom-call(bf16[8,12,2,17280]{3,2,1,0:T(2,128)(2,1)} %stored_ref.6, bf16[2,8,384]{2,1,0:T(8,128)(2,1)} %constant.55.clone.sum_ref.refs_9_.refs_16_), custom_call_target="tpu_custom_call" | custom-call | flops 113246208 | bytes 10260480 | tf_op jit(solution)/shard_map/pallas_call | solution.py:636
  56.0 2.6 collective-permute-start
  58.6 1.6 collective-permute-start.1
  61.0 7.5 %shard_map.333 = (bf16[2,2,8,24,384]{4,3,2,1,0:T(8,128)(2,1)}, bf16[2,2,8,24,384]{4,3,2,1,0:T(8,128)(2,1)}, bf16[2,2,8,24,384]{4,3,2,1,0:T(8,128)(2,1)}, bf16[2,...) custom-call(bf16[8,12,2,17280]{3,2,1,0:T(2,128)(2,1)} %stored_ref.7,, ...), custom_call_target="tpu_custom_call" | custom-call | flops 452984832 | bytes 11403780 | tf_op jit(solution)/shard_map/pallas_call | solution.py:636
  68.5 10.3 %shard_map.334 = (bf16[2,2,8,24,384]{4,3,2,1,0:T(8,128)(2,1)}, bf16[2,2,8,24,384]{4,3,2,1,0:T(8,128)(2,1)}, bf16[2,2,8,24,384]{4,3,2,1,0:T(8,128)(2,1)}, bf16[2,...) custom-call(f32[2,48,192]{2,1,0:T(8,128)} %get-tuple-element.52.refs, ...), custom_call_target="tpu_custom_call", output_to_operand_aliasing={{0}: (10, {}), {1}: (11, {}), {2}: (12, {}), {3}: (13, {}),... | custom-call | flops 452984832 | bytes 13360644 | tf_op jit(solution)/shard_map/pallas_call | solution.py:636
  78.8 1.9 collective-permute-start.4
  80.8 34.1 %shard_map.338 = (bf16[1,2,12,16,384]{4,3,2,1,0:T(8,128)(2,1)}, bf16[1,2,12,16,384]{4,3,2,1,0:T(8,128)(2,1)}, bf16[1,2,12,16,384]{4,3,2,1,0:T(8,128)(2,1)}, bf16...) custom-call(bf16[8,1,2,8,24,384]{5,4,3,2,1,0:T(8,128)(2,1)} %all-to-, ...), custom_call_target="tpu_custom_call" | custom-call | flops 10871635968 | bytes 10132484 | tf_op jit(solution)/shard_map/pallas_call | solution.py:636
  115.0 4.9 %all-to-all-start.3 = ((bf16[8,1,2,12,16,384]{5,4,3,2,1,0:T(8,128)(2,1)}), bf16[8,1,2,12,16,384]{5,4,3,2,1,0:T(8,128)(2,1)}, u32[]{:S(2)}, u32[]{:S(2)}) async-start(bf16[8,1,2,12,16,384]{5,4,3,2,1,0:T(8,128)(2,1)} %get-tuple-element.90), calls=%async_computation.3 | async-start | bytes 4718592 | tf_op jit(solution)/shard_map/all_to_all | solution.py:713
  119.8 1.4 collective-permute-start.5
  121.3 1.5 collective-permute-start.6
  123.0 1.5 collective-permute-start.8
  126.5 33.6 %collective-permute-done.5.refs_3_.refs_11_ = bf16[2,2,8,24,384]{4,3,2,1,0:T(8,128)(2,1)S(1)} collective-permute-done((bf16[2,2,8,24,384]{4,3,2,1,0:T(8,128)(2,1)S(1)}, bf16[2,2,8,24,384]{4,3,2,1,0:T(8,128)(2,1)S(1)}, u32[]{:S(2)}, u32[]{:S(2)}) %collective-permute-start.5) | collective-permute-done | bytes 589856 | tf_op jit(solution)/shard_map/ppermute | solution.py:707
  161.3 36.7 %collective-permute-done.7.refs_5_.refs_13_ = bf16[2,2,8,24,384]{4,3,2,1,0:T(8,128)(2,1)S(1)} collective-permute-done((bf16[2,2,8,24,384]{4,3,2,1,0:T(8,128)(2,1)S(1)}, bf16[2,2,8,24,384]{4,3,2,1,0:T(8,128)(2,1)S(1)}, u32[]{:S(2)}, u32[]{:S(2)}) %collective-permute-start.7) | collective-permute-done | bytes 589856 | tf_op jit(solution)/shard_map/ppermute | solution.py:707
  199.2 34.5 %shard_map.339 = (bf16[8,1,2,12,16,384]{5,4,3,2,1,0:T(8,128)(2,1)}, bf16[1,2,12,16,384]{4,3,2,1,0:T(8,128)(2,1)}, bf16[1,2,12,16,384]{4,3,2,1,0:T(8,128)(2,1)}, ...) custom-call(bf16[2,2,8,24,384]{4,3,2,1,0:T(8,128)(2,1)} %get-tuple-e, ...), custom_call_target="tpu_custom_call" | custom-call | flops 10871635968 | bytes 15049732 | tf_op jit(solution)/shard_map/pallas_call | solution.py:636
  233.9 4.5 %all-to-all-start.2 = ((bf16[8,1,2,12,16,384]{5,4,3,2,1,0:T(8,128)(2,1)}), bf16[8,1,2,12,16,384]{5,4,3,2,1,0:T(8,128)(2,1)}, u32[]{:S(2)}, u32[]{:S(2)}) async-start(bf16[8,1,2,12,16,384]{5,4,3,2,1,0:T(8,128)(2,1)} %get-tuple-element.73), calls=%async_computation.2 | async-start | bytes 4718592 | tf_op jit(solution)/shard_map/all_to_all | solution.py:713
  239.0 1.9 collective-permute-start.14
  241.1 1.5 collective-permute-start.16
  243.6 2.6 collective-permute-start.18
  246.2 27.7 %collective-permute-done.14.refs_2_ = bf16[1,2,12,16,384]{4,3,2,1,0:T(8,128)(2,1)} collective-permute-done((bf16[1,2,12,16,384]{4,3,2,1,0:T(8,128)(2,1)S(1)}, bf16[1,2,12,16,384]{4,3,2,1,0:T(8,128)(2,1)}, u32[]{:S(2)}, u32[]{:S(2)}) %collective-permute-start.14) | collective-permute-done | bytes 294944 | tf_op jit(solution)/shard_map/ppermute | solution.py:707
  274.7 4.4 %collective-permute-done.15.refs_3_ = bf16[1,2,12,16,384]{4,3,2,1,0:T(8,128)(2,1)} collective-permute-done((bf16[1,2,12,16,384]{4,3,2,1,0:T(8,128)(2,1)S(1)}, bf16[1,2,12,16,384]{4,3,2,1,0:T(8,128)(2,1)}, u32[]{:S(2)}, u32[]{:S(2)}) %collective-permute-start.15) | collective-permute-done | bytes 294944 | tf_op jit(solution)/shard_map/ppermute | solution.py:707
  279.8 1.4 collective-permute-start.35
  281.1 1.4 collective-permute-start.36
  283.3 4.2 %collective-permute-done.18.refs_6_ = bf16[1,2,12,16,384]{4,3,2,1,0:T(8,128)(2,1)} collective-permute-done((bf16[1,2,12,16,384]{4,3,2,1,0:T(8,128)(2,1)S(1)}, bf16[1,2,12,16,384]{4,3,2,1,0:T(8,128)(2,1)}, u32[]{:S(2)}, u32[]{:S(2)}) %collective-permute-start.18) | collective-permute-done | bytes 294944 | tf_op jit(solution)/shard_map/ppermute | solution.py:707
  287.6 5.2 %collective-permute-done.19.refs_7_ = bf16[1,2,12,16,384]{4,3,2,1,0:T(8,128)(2,1)} collective-permute-done((bf16[1,2,12,16,384]{4,3,2,1,0:T(8,128)(2,1)S(1)}, bf16[1,2,12,16,384]{4,3,2,1,0:T(8,128)(2,1)}, u32[]{:S(2)}, u32[]{:S(2)}) %collective-permute-start.19) | collective-permute-done | bytes 294944 | tf_op jit(solution)/shard_map/ppermute | solution.py:707
  293.3 7.8 %shard_map.340.refs_2_ = bf16[8,12,2,17280]{3,2,1,0:T(2,128)(2,1)} custom-call(bf16[1,2,12,16,384]{4,3,2,1,0:T(8,128)(2,1)} %get-tuple-element.74.refs_0_, bf16[1,2,12,16,384]{4,3,2,1,0:T(8,128)(2,1)} %collective-permute-done.13.refs_1_, bf16[1,2,12,16,384]{4,3,2,1,0:T(8,128)(2,1)} %collective-permute-done.14.refs_2_, ...), custom_call_target="tpu_custom_call" | custom-call | flops 452984832 | bytes 9043968 | tf_op jit(solution)/shard_map/pallas_call | solution.py:636
  301.1 1.8 collective-permute-start.22
  304.1 1.3 add_add_fusion
  306.3 1.4 collective-permute-done.21.refs_6_.refs_10_
  310.0 10.6 %shard_map.342 = (bf16[2,48,192]{2,1,0:T(8,128)(2,1)}, f32[8,2,384]{2,1,0:T(2,128)}) custom-call(f32[2,48,192]{2,1,0:T(8,128)} %get-tuple-element.70.refs_0_, f32[2,48,192]{2,1,0:T(8,128)} %collective-permute-done.10.refs_1_, f32[2,48,192]{2,1,0:T(8,128)} %collective-permute-done.11.refs_2_, f32[2,48,192]{2,1,0:T(8,128)} %collective-permute-done.12.refs_3_, ...), custom_call_target="tpu_custom_call" | custom-call | flops 452984832 | bytes 6355968 | tf_op jit(solution)/shard_map/pallas_call | solution.py:636
  320.6 1.5 collective-permute-start.30
  322.1 1.3 collective-permute-start.31
  323.3 6.5 %collective-permute-done.24.refs_9_.refs_13_ = bf16[1,2,12,16,384]{4,3,2,1,0:T(8,128)(2,1)} collective-permute-done((bf16[1,2,12,16,384]{4,3,2,1,0:T(8,128)(2,1)}, bf16[1,2,12,16,384]{4,3,2,1,0:T(8,128)(2,1)}, u32[]{:S(2)}, u32[]{:S(2)}) %collective-permute-start.24) | collective-permute-done | bytes 294944 | tf_op jit(solution)/shard_map/ppermute | solution.py:707
  329.9 2.1 collective-permute-start.32
  332.0 10.8 %shard_map.343 = (bf16[2,48,192]{2,1,0:T(8,128)(2,1)}, f32[8,2,384]{2,1,0:T(2,128)}) custom-call(f32[2,48,192]{2,1,0:T(8,128)} %get-tuple-element.52.refs_0_, f32[2,48,192]{2,1,0:T(8,128)} %collective-permute-done.refs_1_, f32[2,48,192]{2,1,0:T(8,128)} %collective-permute-done.1.refs_2_, f32[2,48,192]{2,1,0:T(8,128)} %collective-permute-done.2.refs_3_, ...), custom_call_target="tpu_custom_call" | custom-call | flops 452984832 | bytes 6380544 | tf_op jit(solution)/shard_map/pallas_call | solution.py:636
  343.7 4.2 %all-to-all-start.4 = ((f32[8,2,384]{2,1,0:T(2,128)}), f32[8,2,384]{2,1,0:T(2,128)}, u32[]{:S(2)}, u32[]{:S(2)}) async-start(f32[8,2,384]{2,1,0:T(2,128)} %get-tuple-element.95), calls=%async_computation.4 | async-start | bytes 49152 | tf_op jit(solution)/shard_map/all_to_all | solution.py:713
  347.8 7.8 %shard_map.341 = bf16[8,12,2,17280]{3,2,1,0:T(2,128)(2,1)} custom-call(bf16[8,1,2,12,16,384]{5,4,3,2,1,0:T(8,128)(2,1)} %all-to-all-done.2.refs_0_, bf16[192,128]{1,0:T(8,128)(2,1)} %constant.48.clone.refs_1_, bf16[8,12,2,17280]{3,2,1,0:T(2,128)(2,1)} %shard_map.340.refs_2_), custom_call_target="tpu_custom_call", output_to_operand_aliasing={{}: (2, {})} | custom-call | flops 452984832 | bytes 15679488 | tf_op jit(solution)/shard_map/pallas_call | solution.py:636
  357.1 3.0 collective-permute-start.29
  360.1 11.2 %shard_map.344.refs_20_ = bf16[8,12,2,17280]{3,2,1,0:T(2,128)(2,1)} custom-call(f32[2,48,192]{2,1,0:T(8,128)} %get-tuple-element.70.refs_0_, f32[2,48,192]{2,1,0:T(8,128)} %collective-permute-done.10.refs_1_, f32[2,48,192]{2,1,0:T(8,128)} %collective-permute-done.11.refs_2_, f32[2,48,192]{2,1,0:T(8,128)} %collective-permute-done.12.refs_3_, ...), custom_call_target="tpu_custom_call" | custom-call | flops 452984832 | bytes 13065216 | tf_op jit(solution)/shard_map/pallas_call | solution.py:636
  371.3 11.4 %shard_map.345 = bf16[8,12,2,17280]{3,2,1,0:T(2,128)(2,1)} custom-call(f32[2,48,192]{2,1,0:T(8,128)} %get-tuple-element.52.refs_0_, f32[2,48,192]{2,1,0:T(8,128)} %collective-permute-done.refs_1_, f32[2,48,192]{2,1,0:T(8,128)} %collective-permute-done.1.refs_2_, f32[2,48,192]{2,1,0:T(8,128)} %collective-permute-done.2.refs_3_, ...), custom_call_target="tpu_custom_call", output_to_operand_aliasing={{}: (20, {})} | custom-call | flops 452984832 | bytes 19700736 | tf_op jit(solution)/shard_map/pallas_call | solution.py:636
  (114 shorter events, 19.6 us)
Async XLA Ops:
  8.2 35.8 %all-to-all-start.1 = ((bf16[8,1,2,8,24,384]{5,4,3,2,1,0:T(8,128)(2,1)}), bf16[8,1,2,8,24,384]{5,4,3,2,1,0:T(8,128)(2,1)}, u32[]{:S(2)}, u32[]{:S(2)}) async-start(bf16[8,1,2,8,24,384]{5,4,3,2,1,0:T(8,128)(2,1)} %shard_map.337), calls=%async_computation.1 | async-start | bytes 4718592 | tf_op jit(solution)/shard_map/all_to_all | solution.py:713
  20.9 8.3 %collective-permute-start.10 = (f32[2,48,192]{2,1,0:T(8,128)}, f32[2,48,192]{2,1,0:T(8,128)}, u32[]{:S(2)}, u32[]{:S(2)}) collective-permute-start(f32[2,48,192]{2,1,0:T(8,128)} %get-tuple-element.70.refs_0_), channel_id=1, source_target_pairs={{0,1},{1,2},{2,3},{3,0},{4,5},{5,6},{6,7},{7,4},{8,9},{9,10},{10,1... | collective-permute-start | bytes 221192 | tf_op jit(solution)/shard_map/ppermute | solution.py:720
  23.2 9.9 %collective-permute-start.11 = (f32[2,48,192]{2,1,0:T(8,128)}, f32[2,48,192]{2,1,0:T(8,128)}, u32[]{:S(2)}, u32[]{:S(2)}) collective-permute-start(f32[2,48,192]{2,1,0:T(8,128)} %get-tuple-element.70.refs_0_), channel_id=1, source_target_pairs={{0,2},{1,3},{2,0},{3,1},{4,6},{5,7},{6,4},{7,5},{8,10},{9,11},{10,... | collective-permute-start | bytes 221192 | tf_op jit(solution)/shard_map/ppermute | solution.py:720
  25.8 7.4 %collective-permute-start.12 = (f32[2,48,192]{2,1,0:T(8,128)}, f32[2,48,192]{2,1,0:T(8,128)}, u32[]{:S(2)}, u32[]{:S(2)}) collective-permute-start(f32[2,48,192]{2,1,0:T(8,128)} %get-tuple-element.70.refs_0_), channel_id=1, source_target_pairs={{0,3},{1,0},{2,1},{3,2},{4,7},{5,4},{6,5},{7,6},{8,11},{9,8},{10,9... | collective-permute-start | bytes 221192 | tf_op jit(solution)/shard_map/ppermute | solution.py:720
  44.0 36.8 %all-to-all-start = ((bf16[8,1,2,8,24,384]{5,4,3,2,1,0:T(8,128)(2,1)}), bf16[8,1,2,8,24,384]{5,4,3,2,1,0:T(8,128)(2,1)}, u32[]{:S(2)}, u32[]{:S(2)}) async-start(bf16[8,1,2,8,24,384]{5,4,3,2,1,0:T(8,128)(2,1)} %shard_map.336), calls=%async_computation | async-start | bytes 4718592 | tf_op jit(solution)/shard_map/all_to_all | solution.py:713
  56.0 12.5 %collective-permute-start = (f32[2,48,192]{2,1,0:T(8,128)}, f32[2,48,192]{2,1,0:T(8,128)}, u32[]{:S(2)}, u32[]{:S(2)}) collective-permute-start(f32[2,48,192]{2,1,0:T(8,128)} %get-tuple-element.52.refs_0_), channel_id=1, source_target_pairs={{0,1},{1,2},{2,3},{3,0},{4,5},{5,6},{6,7},{7,4},{8,9},{9,10},{10,1... | collective-permute-start | bytes 221192 | tf_op jit(solution)/shard_map/ppermute | solution.py:720
  58.6 9.9 %collective-permute-start.1 = (f32[2,48,192]{2,1,0:T(8,128)}, f32[2,48,192]{2,1,0:T(8,128)}, u32[]{:S(2)}, u32[]{:S(2)}) collective-permute-start(f32[2,48,192]{2,1,0:T(8,128)} %get-tuple-element.52.refs_0_), channel_id=1, source_target_pairs={{0,2},{1,3},{2,0},{3,1},{4,6},{5,7},{6,4},{7,5},{8,10},{9,11},{10,... | collective-permute-start | bytes 221192 | tf_op jit(solution)/shard_map/ppermute | solution.py:720
  60.2 8.3 %collective-permute-start.2 = (f32[2,48,192]{2,1,0:T(8,128)}, f32[2,48,192]{2,1,0:T(8,128)}, u32[]{:S(2)}, u32[]{:S(2)}) collective-permute-start(f32[2,48,192]{2,1,0:T(8,128)} %get-tuple-element.52.refs_0_), channel_id=1, source_target_pairs={{0,3},{1,0},{2,1},{3,2},{4,7},{5,4},{6,5},{7,6},{8,11},{9,8},{10,9... | collective-permute-start | bytes 221192 | tf_op jit(solution)/shard_map/ppermute | solution.py:720
  78.8 44.2 %collective-permute-start.3 = (bf16[2,2,8,24,384]{4,3,2,1,0:T(8,128)(2,1)}, bf16[2,2,8,24,384]{4,3,2,1,0:T(8,128)(2,1)}, u32[]{:S(2)}, u32[]{:S(2)}) collective-permute-start(bf16[2,2,8,24,384]{4,3,2,1,0:T(8,128)(2,1)} %get-tuple-element.63), channel_id=1, source_target_pairs={{0,4},{4,0},{8,12},{12,8},{16,20},{20,16},{24,28},{28,24},{1,5},{5... | collective-permute-start | bytes 1769480 | tf_op jit(solution)/shard_map/ppermute | solution.py:707
  78.8 45.6 %collective-permute-start.4 = (bf16[2,2,8,24,384]{4,3,2,1,0:T(8,128)(2,1)}, bf16[2,2,8,24,384]{4,3,2,1,0:T(8,128)(2,1)}, u32[]{:S(2)}, u32[]{:S(2)}) collective-permute-start(bf16[2,2,8,24,384]{4,3,2,1,0:T(8,128)(2,1)} %get-tuple-element.64), channel_id=1, source_target_pairs={{0,8},{4,12},{8,0},{12,4},{16,24},{20,28},{24,16},{28,20},{1,9},{5... | collective-permute-start | bytes 1769480 | tf_op jit(solution)/shard_map/ppermute | solution.py:707
  114.9 10.8 %copy-start.9 = (s32[192]{0:T(256)S(1)}, s32[192]{0:T(256)}, u32[]{:S(2)}) copy-start(s32[192]{0:T(256)} %constant.52.clone) | copy-start | bytes 2308
  114.9 10.8 %copy-start.10 = (s32[192]{0:T(256)S(1)}, s32[192]{0:T(256)}, u32[]{:S(2)}) copy-start(s32[192]{0:T(256)} %constant.53.clone) | copy-start | bytes 2308
  115.0 118.9 %all-to-all-start.3 = ((bf16[8,1,2,12,16,384]{5,4,3,2,1,0:T(8,128)(2,1)}), bf16[8,1,2,12,16,384]{5,4,3,2,1,0:T(8,128)(2,1)}, u32[]{:S(2)}, u32[]{:S(2)}) async-start(bf16[8,1,2,12,16,384]{5,4,3,2,1,0:T(8,128)(2,1)} %get-tuple-element.90), calls=%async_computation.3 | async-start | bytes 4718592 | tf_op jit(solution)/shard_map/all_to_all | solution.py:713
  119.8 40.3 %collective-permute-start.5 = (bf16[2,2,8,24,384]{4,3,2,1,0:T(8,128)(2,1)S(1)}, bf16[2,2,8,24,384]{4,3,2,1,0:T(8,128)(2,1)S(1)}, u32[]{:S(2)}, u32[]{:S(2)}) collective-permute-start(bf16[2,2,8,24,384]{4,3,2,1,0:T(8,128)(2,1)S(1)} %copy-done), channel_id=1, source_target_pairs={{0,12},{4,8},{8,4},{12,0},{16,28},{20,24},{24,20},{28,16},{1,13},{... | collective-permute-start | bytes 1769480 | tf_op jit(solution)/shard_map/ppermute | solution.py:707
  121.3 40.1 %collective-permute-start.6 = (bf16[2,2,8,24,384]{4,3,2,1,0:T(8,128)(2,1)S(1)}, bf16[2,2,8,24,384]{4,3,2,1,0:T(8,128)(2,1)S(1)}, u32[]{:S(2)}, u32[]{:S(2)}) collective-permute-start(bf16[2,2,8,24,384]{4,3,2,1,0:T(8,128)(2,1)S(1)} %copy-done.1), channel_id=1, source_target_pairs={{0,16},{4,20},{8,24},{12,28},{16,0},{20,4},{24,8},{28,12},{1,17},{... | collective-permute-start | bytes 1769480 | tf_op jit(solution)/shard_map/ppermute | solution.py:707
  122.8 75.2 %collective-permute-start.7 = (bf16[2,2,8,24,384]{4,3,2,1,0:T(8,128)(2,1)S(1)}, bf16[2,2,8,24,384]{4,3,2,1,0:T(8,128)(2,1)S(1)}, u32[]{:S(2)}, u32[]{:S(2)}) collective-permute-start(bf16[2,2,8,24,384]{4,3,2,1,0:T(8,128)(2,1)S(1)} %copy-done.2), channel_id=1, source_target_pairs={{0,20},{4,16},{8,28},{12,24},{16,4},{20,0},{24,12},{28,8},{1,21},{... | collective-permute-start | bytes 1769480 | tf_op jit(solution)/shard_map/ppermute | solution.py:707
  123.0 75.0 %collective-permute-start.8 = (bf16[2,2,8,24,384]{4,3,2,1,0:T(8,128)(2,1)S(1)}, bf16[2,2,8,24,384]{4,3,2,1,0:T(8,128)(2,1)S(1)}, u32[]{:S(2)}, u32[]{:S(2)}) collective-permute-start(bf16[2,2,8,24,384]{4,3,2,1,0:T(8,128)(2,1)S(1)} %copy-done.3), channel_id=1, source_target_pairs={{0,24},{4,28},{8,16},{12,20},{16,8},{20,12},{24,0},{28,4},{1,25},{... | collective-permute-start | bytes 1769480 | tf_op jit(solution)/shard_map/ppermute | solution.py:707
  124.5 73.5 %collective-permute-start.9 = (bf16[2,2,8,24,384]{4,3,2,1,0:T(8,128)(2,1)S(1)}, bf16[2,2,8,24,384]{4,3,2,1,0:T(8,128)(2,1)S(1)}, u32[]{:S(2)}, u32[]{:S(2)}) collective-permute-start(bf16[2,2,8,24,384]{4,3,2,1,0:T(8,128)(2,1)S(1)} %copy-done.4), channel_id=1, source_target_pairs={{0,28},{4,24},{8,20},{12,16},{16,12},{20,8},{24,4},{28,0},{1,29},{... | collective-permute-start | bytes 1769480 | tf_op jit(solution)/shard_map/ppermute | solution.py:707
  160.2 37.9 %copy-start.13 = (bf16[2,2,8,24,384]{4,3,2,1,0:T(8,128)(2,1)}, bf16[2,2,8,24,384]{4,3,2,1,0:T(8,128)(2,1)S(1)}, u32[]{:S(2)}) copy-start(bf16[2,2,8,24,384]{4,3,2,1,0:T(8,128)(2,1)S(1)} %collective-permute-done.5.refs_3_.refs_11_) | copy-start | bytes 1769476
  161.3 36.7 %copy-start.14 = (bf16[2,2,8,24,384]{4,3,2,1,0:T(8,128)(2,1)}, bf16[2,2,8,24,384]{4,3,2,1,0:T(8,128)(2,1)S(1)}, u32[]{:S(2)}) copy-start(bf16[2,2,8,24,384]{4,3,2,1,0:T(8,128)(2,1)S(1)} %collective-permute-done.6.refs_4_.refs_12_) | copy-start | bytes 1769476
  233.9 40.0 %copy-start.18 = (bf16[1,2,12,16,384]{4,3,2,1,0:T(8,128)(2,1)S(1)}, bf16[1,2,12,16,384]{4,3,2,1,0:T(8,128)(2,1)}, u32[]{:S(2)}) copy-start(bf16[1,2,12,16,384]{4,3,2,1,0:T(8,128)(2,1)} %get-tuple-element.81) | copy-start | bytes 884740
  233.9 48.7 %copy-start.7 = (bf16[192,128]{1,0:T(8,128)(2,1)S(1)}, bf16[192,128]{1,0:T(8,128)(2,1)}, u32[]{:S(2)}) copy-start(bf16[192,128]{1,0:T(8,128)(2,1)} %constant.48.clone.refs_1_) | copy-start | bytes 147460
  233.9 109.8 %all-to-all-start.2 = ((bf16[8,1,2,12,16,384]{5,4,3,2,1,0:T(8,128)(2,1)}), bf16[8,1,2,12,16,384]{5,4,3,2,1,0:T(8,128)(2,1)}, u32[]{:S(2)}, u32[]{:S(2)}) async-start(bf16[8,1,2,12,16,384]{5,4,3,2,1,0:T(8,128)(2,1)} %get-tuple-element.73), calls=%async_computation.2 | async-start | bytes 4718592 | tf_op jit(solution)/shard_map/all_to_all | solution.py:713
  238.5 4.1 %collective-permute-start.33 = (bf16[776,128]{1,0:T(8,128)(2,1)S(1)}, bf16[776,128]{1,0:T(8,128)(2,1)S(1)}, u32[]{:S(2)}, u32[]{:S(2)}) collective-permute-start(bf16[776,128]{1,0:T(8,128)(2,1)S(1)} %copy-done.6), channel_id=1, source_target_pairs={{0,4},{4,0},{8,12},{12,8},{16,20},{20,16},{24,28},{28,24},{1,5},{5... | collective-permute-start | bytes 595976 | tf_op jit(solution)/shard_map/ppermute | solution.py:731
  238.9 4.7 %collective-permute-start.13 = (bf16[1,2,12,16,384]{4,3,2,1,0:T(8,128)(2,1)S(1)}, bf16[1,2,12,16,384]{4,3,2,1,0:T(8,128)(2,1)}, u32[]{:S(2)}, u32[]{:S(2)}) collective-permute-start(bf16[1,2,12,16,384]{4,3,2,1,0:T(8,128)(2,1)S(1)} %copy-done.24), channel_id=1, source_target_pairs={{0,4},{4,0},{8,12},{12,8},{16,20},{20,16},{24,28},{28,24},{1,5},{5... | collective-permute-start | bytes 884744 | tf_op jit(solution)/shard_map/ppermute | solution.py:707
  239.0 34.8 %collective-permute-start.14 = (bf16[1,2,12,16,384]{4,3,2,1,0:T(8,128)(2,1)S(1)}, bf16[1,2,12,16,384]{4,3,2,1,0:T(8,128)(2,1)}, u32[]{:S(2)}, u32[]{:S(2)}) collective-permute-start(bf16[1,2,12,16,384]{4,3,2,1,0:T(8,128)(2,1)S(1)} %copy-done.23), channel_id=1, source_target_pairs={{0,8},{4,12},{8,0},{12,4},{16,24},{20,28},{24,16},{28,20},{1,9},{5... | collective-permute-start | bytes 884744 | tf_op jit(solution)/shard_map/ppermute | solution.py:707
  241.0 38.1 %collective-permute-start.15 = (bf16[1,2,12,16,384]{4,3,2,1,0:T(8,128)(2,1)S(1)}, bf16[1,2,12,16,384]{4,3,2,1,0:T(8,128)(2,1)}, u32[]{:S(2)}, u32[]{:S(2)}) collective-permute-start(bf16[1,2,12,16,384]{4,3,2,1,0:T(8,128)(2,1)S(1)} %copy-done.22), channel_id=1, source_target_pairs={{0,12},{4,8},{8,4},{12,0},{16,28},{20,24},{24,20},{28,16},{1,13},{... | collective-permute-start | bytes 884744 | tf_op jit(solution)/shard_map/ppermute | solution.py:707
  241.1 38.7 %collective-permute-start.16 = (bf16[1,2,12,16,384]{4,3,2,1,0:T(8,128)(2,1)S(1)}, bf16[1,2,12,16,384]{4,3,2,1,0:T(8,128)(2,1)}, u32[]{:S(2)}, u32[]{:S(2)}) collective-permute-start(bf16[1,2,12,16,384]{4,3,2,1,0:T(8,128)(2,1)S(1)} %copy-done.21), channel_id=1, source_target_pairs={{0,16},{4,20},{8,24},{12,28},{16,0},{20,4},{24,8},{28,12},{1,17},{... | collective-permute-start | bytes 884744 | tf_op jit(solution)/shard_map/ppermute | solution.py:707
  242.5 38.6 %collective-permute-start.17 = (bf16[1,2,12,16,384]{4,3,2,1,0:T(8,128)(2,1)S(1)}, bf16[1,2,12,16,384]{4,3,2,1,0:T(8,128)(2,1)}, u32[]{:S(2)}, u32[]{:S(2)}) collective-permute-start(bf16[1,2,12,16,384]{4,3,2,1,0:T(8,128)(2,1)S(1)} %copy-done.20), channel_id=1, source_target_pairs={{0,20},{4,16},{8,28},{12,24},{16,4},{20,0},{24,12},{28,8},{1,21},{... | collective-permute-start | bytes 884744 | tf_op jit(solution)/shard_map/ppermute | solution.py:707
  243.6 44.0 %collective-permute-start.18 = (bf16[1,2,12,16,384]{4,3,2,1,0:T(8,128)(2,1)S(1)}, bf16[1,2,12,16,384]{4,3,2,1,0:T(8,128)(2,1)}, u32[]{:S(2)}, u32[]{:S(2)}) collective-permute-start(bf16[1,2,12,16,384]{4,3,2,1,0:T(8,128)(2,1)S(1)} %copy-done.19), channel_id=1, source_target_pairs={{0,24},{4,28},{8,16},{12,20},{16,8},{20,12},{24,0},{28,4},{1,25},{... | collective-permute-start | bytes 884744 | tf_op jit(solution)/shard_map/ppermute | solution.py:707
  273.9 18.8 %collective-permute-start.19 = (bf16[1,2,12,16,384]{4,3,2,1,0:T(8,128)(2,1)S(1)}, bf16[1,2,12,16,384]{4,3,2,1,0:T(8,128)(2,1)}, u32[]{:S(2)}, u32[]{:S(2)}) collective-permute-start(bf16[1,2,12,16,384]{4,3,2,1,0:T(8,128)(2,1)S(1)} %copy-done.18), channel_id=1, source_target_pairs={{0,28},{4,24},{8,20},{12,16},{16,12},{20,8},{24,4},{28,0},{1,29},{... | collective-permute-start | bytes 884744 | tf_op jit(solution)/shard_map/ppermute | solution.py:707
  279.1 22.0 %collective-permute-start.34 = (bf16[776,128]{1,0:T(8,128)(2,1)}, bf16[776,128]{1,0:T(8,128)(2,1)}, u32[]{:S(2)}, u32[]{:S(2)}) collective-permute-start(bf16[776,128]{1,0:T(8,128)(2,1)} %add_convert_fusion), channel_id=1, source_target_pairs={{0,8},{4,12},{8,0},{12,4},{16,24},{20,28},{24,16},{28,20},{1,9},{5... | collective-permute-start | bytes 595976 | tf_op jit(solution)/shard_map/ppermute | solution.py:731
  279.8 23.1 %collective-permute-start.35 = (bf16[776,128]{1,0:T(8,128)(2,1)}, bf16[776,128]{1,0:T(8,128)(2,1)}, u32[]{:S(2)}, u32[]{:S(2)}) collective-permute-start(bf16[776,128]{1,0:T(8,128)(2,1)} %add_convert_fusion), channel_id=1, source_target_pairs={{0,16},{4,20},{8,24},{12,28},{16,0},{20,4},{24,8},{28,12},{1,17},{... | collective-permute-start | bytes 595976 | tf_op jit(solution)/shard_map/ppermute | solution.py:731
  281.1 22.3 %collective-permute-start.36 = (bf16[776,128]{1,0:T(8,128)(2,1)}, bf16[776,128]{1,0:T(8,128)(2,1)}, u32[]{:S(2)}, u32[]{:S(2)}) collective-permute-start(bf16[776,128]{1,0:T(8,128)(2,1)} %add_convert_fusion), channel_id=1, source_target_pairs={{0,24},{4,28},{8,16},{12,20},{16,8},{20,12},{24,0},{28,4},{1,25},{... | collective-permute-start | bytes 595976 | tf_op jit(solution)/shard_map/ppermute | solution.py:731
  287.5 17.9 %collective-permute-start.20 = (bf16[1,2,12,16,384]{4,3,2,1,0:T(8,128)(2,1)}, bf16[1,2,12,16,384]{4,3,2,1,0:T(8,128)(2,1)}, u32[]{:S(2)}, u32[]{:S(2)}) collective-permute-start(bf16[1,2,12,16,384]{4,3,2,1,0:T(8,128)(2,1)} %get-tuple-element.83), channel_id=1, source_target_pairs={{0,4},{4,0},{8,12},{12,8},{16,20},{20,16},{24,28},{28,24},{1,5},{5... | collective-permute-start | bytes 884744 | tf_op jit(solution)/shard_map/ppermute | solution.py:707
  292.7 15.0 %collective-permute-start.21 = (bf16[1,2,12,16,384]{4,3,2,1,0:T(8,128)(2,1)}, bf16[1,2,12,16,384]{4,3,2,1,0:T(8,128)(2,1)}, u32[]{:S(2)}, u32[]{:S(2)}) collective-permute-start(bf16[1,2,12,16,384]{4,3,2,1,0:T(8,128)(2,1)} %get-tuple-element.84), channel_id=1, source_target_pairs={{0,8},{4,12},{8,0},{12,4},{16,24},{20,28},{24,16},{28,20},{1,9},{5... | collective-permute-start | bytes 884744 | tf_op jit(solution)/shard_map/ppermute | solution.py:707
  301.1 19.5 %collective-permute-start.22 = (bf16[1,2,12,16,384]{4,3,2,1,0:T(8,128)(2,1)}, bf16[1,2,12,16,384]{4,3,2,1,0:T(8,128)(2,1)}, u32[]{:S(2)}, u32[]{:S(2)}) collective-permute-start(bf16[1,2,12,16,384]{4,3,2,1,0:T(8,128)(2,1)} %get-tuple-element.85), channel_id=1, source_target_pairs={{0,12},{4,8},{8,4},{12,0},{16,28},{20,24},{24,20},{28,16},{1,13},{... | collective-permute-start | bytes 884744 | tf_op jit(solution)/shard_map/ppermute | solution.py:707
  302.9 19.2 %collective-permute-start.23 = (bf16[1,2,12,16,384]{4,3,2,1,0:T(8,128)(2,1)}, bf16[1,2,12,16,384]{4,3,2,1,0:T(8,128)(2,1)}, u32[]{:S(2)}, u32[]{:S(2)}) collective-permute-start(bf16[1,2,12,16,384]{4,3,2,1,0:T(8,128)(2,1)} %get-tuple-element.86), channel_id=1, source_target_pairs={{0,16},{4,20},{8,24},{12,28},{16,0},{20,4},{24,8},{28,12},{1,17},{... | collective-permute-start | bytes 884744 | tf_op jit(solution)/shard_map/ppermute | solution.py:707
  303.4 26.4 %collective-permute-start.24 = (bf16[1,2,12,16,384]{4,3,2,1,0:T(8,128)(2,1)}, bf16[1,2,12,16,384]{4,3,2,1,0:T(8,128)(2,1)}, u32[]{:S(2)}, u32[]{:S(2)}) collective-permute-start(bf16[1,2,12,16,384]{4,3,2,1,0:T(8,128)(2,1)} %get-tuple-element.87), channel_id=1, source_target_pairs={{0,20},{4,16},{8,28},{12,24},{16,4},{20,0},{24,12},{28,8},{1,21},{... | collective-permute-start | bytes 884744 | tf_op jit(solution)/shard_map/ppermute | solution.py:707
  305.4 26.5 %collective-permute-start.25 = (bf16[1,2,12,16,384]{4,3,2,1,0:T(8,128)(2,1)}, bf16[1,2,12,16,384]{4,3,2,1,0:T(8,128)(2,1)}, u32[]{:S(2)}, u32[]{:S(2)}) collective-permute-start(bf16[1,2,12,16,384]{4,3,2,1,0:T(8,128)(2,1)} %get-tuple-element.88), channel_id=1, source_target_pairs={{0,24},{4,28},{8,16},{12,20},{16,8},{20,12},{24,0},{28,4},{1,25},{... | collective-permute-start | bytes 884744 | tf_op jit(solution)/shard_map/ppermute | solution.py:707
  307.7 24.3 %collective-permute-start.26 = (bf16[1,2,12,16,384]{4,3,2,1,0:T(8,128)(2,1)}, bf16[1,2,12,16,384]{4,3,2,1,0:T(8,128)(2,1)}, u32[]{:S(2)}, u32[]{:S(2)}) collective-permute-start(bf16[1,2,12,16,384]{4,3,2,1,0:T(8,128)(2,1)} %get-tuple-element.89), channel_id=1, source_target_pairs={{0,28},{4,24},{8,20},{12,16},{16,12},{20,8},{24,4},{28,0},{1,29},{... | collective-permute-start | bytes 884744 | tf_op jit(solution)/shard_map/ppermute | solution.py:707
  320.6 36.5 %collective-permute-start.30 = (bf16[2,48,192]{2,1,0:T(8,128)(2,1)}, bf16[2,48,192]{2,1,0:T(8,128)(2,1)}, u32[]{:S(2)}, u32[]{:S(2)}) collective-permute-start(bf16[2,48,192]{2,1,0:T(8,128)(2,1)} %get-tuple-element.93.refs_4_), channel_id=1, source_target_pairs={{0,1},{1,2},{2,3},{3,0},{4,5},{5,6},{6,7},{7,4},{8,9},{9,10},{10,1... | collective-permute-start | bytes 110600 | tf_op jit(solution)/shard_map/ppermute | solution.py:720
  322.1 38.0 %collective-permute-start.31 = (bf16[2,48,192]{2,1,0:T(8,128)(2,1)}, bf16[2,48,192]{2,1,0:T(8,128)(2,1)}, u32[]{:S(2)}, u32[]{:S(2)}) collective-permute-start(bf16[2,48,192]{2,1,0:T(8,128)(2,1)} %get-tuple-element.93.refs_4_), channel_id=1, source_target_pairs={{0,2},{1,3},{2,0},{3,1},{4,6},{5,7},{6,4},{7,5},{8,10},{9,11},{10,... | collective-permute-start | bytes 110600 | tf_op jit(solution)/shard_map/ppermute | solution.py:720
  329.9 30.2 %collective-permute-start.32 = (bf16[2,48,192]{2,1,0:T(8,128)(2,1)}, bf16[2,48,192]{2,1,0:T(8,128)(2,1)}, u32[]{:S(2)}, u32[]{:S(2)}) collective-permute-start(bf16[2,48,192]{2,1,0:T(8,128)(2,1)} %get-tuple-element.93.refs_4_), channel_id=1, source_target_pairs={{0,3},{1,0},{2,1},{3,2},{4,7},{5,4},{6,5},{7,6},{8,11},{9,8},{10,9... | collective-permute-start | bytes 110600 | tf_op jit(solution)/shard_map/ppermute | solution.py:720
  342.8 28.6 %collective-permute-start.27 = (bf16[2,48,192]{2,1,0:T(8,128)(2,1)}, bf16[2,48,192]{2,1,0:T(8,128)(2,1)}, u32[]{:S(2)}, u32[]{:S(2)}) collective-permute-start(bf16[2,48,192]{2,1,0:T(8,128)(2,1)} %get-tuple-element.92.refs_4_), channel_id=1, source_target_pairs={{0,1},{1,2},{2,3},{3,0},{4,5},{5,6},{6,7},{7,4},{8,9},{9,10},{10,1... | collective-permute-start | bytes 110600 | tf_op jit(solution)/shard_map/ppermute | solution.py:720
  342.8 28.5 %collective-permute-start.28 = (bf16[2,48,192]{2,1,0:T(8,128)(2,1)}, bf16[2,48,192]{2,1,0:T(8,128)(2,1)}, u32[]{:S(2)}, u32[]{:S(2)}) collective-permute-start(bf16[2,48,192]{2,1,0:T(8,128)(2,1)} %get-tuple-element.92.refs_4_), channel_id=1, source_target_pairs={{0,2},{1,3},{2,0},{3,1},{4,6},{5,7},{6,4},{7,5},{8,10},{9,11},{10,... | collective-permute-start | bytes 110600 | tf_op jit(solution)/shard_map/ppermute | solution.py:720
  343.7 12.0 %all-to-all-start.4 = ((f32[8,2,384]{2,1,0:T(2,128)}), f32[8,2,384]{2,1,0:T(2,128)}, u32[]{:S(2)}, u32[]{:S(2)}) async-start(f32[8,2,384]{2,1,0:T(2,128)} %get-tuple-element.95), calls=%async_computation.4 | async-start | bytes 49152 | tf_op jit(solution)/shard_map/all_to_all | solution.py:713
  357.1 14.3 %collective-permute-start.29 = (bf16[2,48,192]{2,1,0:T(8,128)(2,1)}, bf16[2,48,192]{2,1,0:T(8,128)(2,1)}, u32[]{:S(2)}, u32[]{:S(2)}) collective-permute-start(bf16[2,48,192]{2,1,0:T(8,128)(2,1)} %get-tuple-element.92.refs_4_), channel_id=1, source_target_pairs={{0,3},{1,0},{2,1},{3,2},{4,7},{5,4},{6,5},{7,6},{8,11},{9,8},{10,9... | collective-permute-start | bytes 110600 | tf_op jit(solution)/shard_map/ppermute | solution.py:720
  (19 other events, 121.9 us)

commit v7 on v6

--- a/solution.py
+++ b/solution.py
@@ -146,6 +146,13 @@
         words_ref[:, :, p.words :, :] = jnp.zeros(words_ref.shape[:2] + (tail, LANES), single)
 
 
+def pipelined(p, fetch, use):
+    ahead = fetch(0)
+    for h in range(p.step):
+        now, ahead = ahead, fetch(h + 1) if h + 1 < p.step else None
+        use(h, now)
+
+
 def first_step():
     return (pl.program_id(0) == 0) & (pl.program_id(1) == 0)
 
@@ -216,10 +223,15 @@
     me, refs = (refs[0][0], refs[1:]) if split else (None, refs)
     out_refs, (words_ref, turn_ref) = refs[:-2], refs[-2:]
     clear_tail(p, words_ref)
-    for h in range(p.step):
+
+    def fetch(h):
         spread(p, stored_ref, words_ref.at[h], h)
-        tokens = gather_row(p, words_ref.at[h])
+        return gather_row(p, words_ref.at[h])
+
+    def use(h, tokens):
         analyse(p, tokens, table_ref[...], scale_ref[...], turn_ref, h)
+
+    pipelined(p, fetch, use)
 
     @pl.when(last_part())
     def _():
@@ -229,13 +241,18 @@
 def stats_kernel(p, stored_ref, sum_ref, tokens_ref, stat_ref, words_ref):
     clear_tail(p, words_ref)
     count = 2 * p.stack
-    for h in range(p.step):
+
+    def fetch(h):
         spread(p, stored_ref, words_ref.at[h], h)
-        tokens = gather_row(p, words_ref.at[h])
+        return gather_row(p, words_ref.at[h])
+
+    def use(h, tokens):
         tokens_ref[0, h] = tokens
         wide = tokens.astype(single)
         rows = mul(sum_ref[0], tokens, NT) + summed(sum_ref[1], wide * wide)
         stat_ref[0, h * count : (h + 1) * count, :] = rows[:count]
+
+    pipelined(p, fetch, use)
 
 
 def moments(p, stat_refs, rows_ref):
@@ -261,14 +278,16 @@
     out_refs, (rows_ref, turn_ref) = refs[:-2], refs[-2:]
     moments(p, stat_refs, rows_ref)
 
-    for h in range(p.step):
+    def use(h, pairs):
         tiles = []
-        for c, (mean, inverse) in enumerate(expand(p, rows_ref[h], wide_ref)):
+        for c, (mean, inverse) in enumerate(pairs):
             at = slice(c * LANES, (c + 1) * LANES)
             centred = (tokens_ref[0, h, :, at].astype(single) - mean) * inverse
             tiles.append((centred * affine_ref[0:1, at] + affine_ref[1:2, at]).astype(half))
         normed = jnp.concatenate(tiles, axis=1)
         analyse(p, normed, table_ref[...], scale_ref[...], turn_ref, h)
+
+    pipelined(p, lambda h: expand(p, rows_ref[h], wide_ref), use)
 
     @pl.when(last_part())
     def _():
@@ -508,10 +527,10 @@
     rows_refs, (table_ref, out_ref, words_ref) = refs[:peers], refs[peers:]
     factor = 1.0 / math.sqrt(p.lon)
 
-    for h in range(p.step):
-        block = peer_rows(p, rows_refs, h)
-        tokens = mul(table_ref[...], block) * factor
-        scatter_row(p, tokens, words_ref.at[h], out_ref, h)
+    def fetch(h):
+        return mul(table_ref[...], peer_rows(p, rows_refs, h)) * factor
+
+    pipelined(p, fetch, lambda h, tokens: scatter_row(p, tokens, words_ref.at[h], out_ref, h))
 
 
 def slope_sums_kernel(p, peers, follows, *refs):
@@ -529,12 +548,15 @@
     def _():
         param_ref[...] = jnp.zeros_like(param_ref)
 
-    for h in range(p.step):
-        block = peer_rows(p, rows_in_refs, h)
+    def fetch(h):
+        spectrum = mul(table_ref[...], peer_rows(p, rows_in_refs, h))
+        return spectrum, expand(p, rows_ref[h], wide_ref)
+
+    def use(h, fetched):
         folds = (PACK * p.turn_pad // 8, 8, LANES)
         plain, scaled = [], []
-        spectrum = mul(table_ref[...], block)
-        for c, (mean, inverse) in enumerate(expand(p, rows_ref[h], wide_ref)):
+        spectrum, pairs = fetched
+        for c, (mean, inverse) in enumerate(pairs):
             at = slice(c * LANES, (c + 1) * LANES)
             normed_grad = spectrum[:, at] * factor
             centred = (tokens_ref[0, h, :, at].astype(single) - mean) * inverse
@@ -547,6 +569,8 @@
             sum_ref[1], jnp.concatenate(scaled, axis=1), NT
         )
         dense_ref[h * count : (h + 1) * count, :] = sums[:count]
+
+    pipelined(p, fetch, use)
     sums_ref[0] = dense_ref[...].astype(half)
 
     @pl.when(last_step())
@@ -575,11 +599,12 @@
         if count < 8:
             part_ref[h, count:, :] = jnp.zeros((8 - count, p.turn_pad * PACK), single)
 
-    for h in range(p.step):
-        block = peer_rows(p, rows_in_refs, h)
-        spectrum = mul(table_ref[...], block)
-        moment = expand(p, rows_ref[h], wide_ref)
-        means = expand(p, part_ref[h], wide_ref)
+    def fetch(h):
+        spectrum = mul(table_ref[...], peer_rows(p, rows_in_refs, h))
+        return spectrum, expand(p, rows_ref[h], wide_ref), expand(p, part_ref[h], wide_ref)
+
+    def use(h, fetched):
+        spectrum, moment, means = fetched
         tiles = []
         for c in range(p.tiles):
             at = slice(c * LANES, (c + 1) * LANES)
@@ -589,6 +614,8 @@
             tiles.append(inverse * (grad - first - centred * second))
         grad = jnp.concatenate(tiles, axis=1)
         scatter_row(p, grad, words_ref.at[h], out_ref, h)
+
+    pipelined(p, fetch, use)
 
 
 def whole_spec(value):

time: 385 us -> 382 us (level)
  Pallas kernels: 179 us -> 172 us
    pallas_call x14, Pallas kernels: 179 us -> 172 us  [_call(): pl.pallas_call(body, grid=grid, in_specs=in_specs, out_specs=out_specs, o...]
  transfers between devices with their start and end apart: 42 -> 42, of which waited for: 11 -> 12; matrix products, arithmetic and copies ran while one was open for 2% -> 2% of each run, Pallas kernels for 42% -> 40%
where the time goes in v7:
time: 382 us; the launch traced here: 379 us
  Pallas kernels  172 us (45%)
  waiting for transfers between devices  128 us (34%)
  starting transfers between devices  67.4 us (18%)
  other arithmetic  4.29 us (1%)
  local copies, waits for them, and re-layouts  3.88 us (1%)
    pallas_call x14, Pallas kernels, _call(): pl.pallas_call(body, grid=grid, in_specs=in_specs, out_specs=out_specs, o...  172 us
    ppermute x21, waiting for transfers between devices, exchange_near(): lax.ppermute(value, 'space', [(i, i ^ x) for i in range(count)])  123 us
    all_to_all x5, starting transfers between devices, exchange(): return lax.all_to_all(value, 'space', 0, 0, tiled=True)  23.1 us
    ppermute x12, starting transfers between devices, around(): lax.ppermute(value, axis, [(i, (i + step) % size) for i in range(size)])  20.7 us
    ppermute x21, starting transfers between devices, exchange_near(): lax.ppermute(value, 'space', [(i, i ^ x) for i in range(count)])  19.7 us
  transfers between devices with their start and end apart: 42, of which 12 were waited for; matrix products, arithmetic and copies ran while one was open for 2% of the time, Pallas kernels for 40%

profile of v7, /device:TPU:0, one launch (start us, length us, event | category | flops | bytes accessed | tf_op | source)
XLA Modules:
  0.0 379.3 jit_solution(1126181553175351370)
XLA Ops:
  0.6 7.5 %shard_map.337 = bf16[8,1,2,8,24,384]{5,4,3,2,1,0:T(8,128)(2,1)} custom-call(bf16[8,12,2,17280]{3,2,1,0:T(2,128)(2,1)} %stored_ref.7, bf16[128,192]{1,0:T(8,128)(2,1)} %constant.42.clone.table_ref.refs_6_, f32[128,1]{1,0:T(8,128)} %constant.44.clone.scale_ref), custom_call_target="tpu_custom_call" | custom-call | flops 452984832 | bytes 9044480 | tf_op jit(solution)/shard_map/pallas_call | solution.py:663
  8.1 5.2 %all-to-all-start.1 = ((bf16[8,1,2,8,24,384]{5,4,3,2,1,0:T(8,128)(2,1)}), bf16[8,1,2,8,24,384]{5,4,3,2,1,0:T(8,128)(2,1)}, u32[]{:S(2)}, u32[]{:S(2)}) async-start(bf16[8,1,2,8,24,384]{5,4,3,2,1,0:T(8,128)(2,1)} %shard_map.337), calls=%async_computation.1 | async-start | bytes 4718592 | tf_op jit(solution)/shard_map/all_to_all | solution.py:740
  13.3 7.6 %shard_map.335 = (bf16[2,12,192,384]{3,2,1,0:T(8,128)(2,1)}, f32[2,48,192]{2,1,0:T(8,128)}) custom-call(bf16[8,12,2,17280]{3,2,1,0:T(2,128)(2,1)} %stored_ref.6, bf16[2,8,384]{2,1,0:T(8,128)(2,1)} %constant.55.clone.sum_ref.refs_9_.refs_16_), custom_call_target="tpu_custom_call" | custom-call | flops 113246208 | bytes 10260480 | tf_op jit(solution)/shard_map/pallas_call | solution.py:663
  20.9 2.3 collective-permute-start.10
  23.1 2.6 collective-permute-start.11
  25.7 1.3 collective-permute-start.12
  29.2 3.9 %collective-permute-done.11.refs_2_ = f32[2,48,192]{2,1,0:T(8,128)} collective-permute-done((f32[2,48,192]{2,1,0:T(8,128)}, f32[2,48,192]{2,1,0:T(8,128)}, u32[]{:S(2)}, u32[]{:S(2)}) %collective-permute-start.11) | collective-permute-done | bytes 73760 | tf_op jit(solution)/shard_map/ppermute | solution.py:747
  33.7 8.7 %shard_map.336 = bf16[8,1,2,8,24,384]{5,4,3,2,1,0:T(8,128)(2,1)} custom-call(f32[2,48,192]{2,1,0:T(8,128)} %get-tuple-element.70.refs_0_, f32[2,48,192]{2,1,0:T(8,128)} %collective-permute-done.10.refs_1_, f32[2,48,192]{2,1,0:T(8,128)} %collective-permute-done.11.refs_2_, f32[2,48,192]{2,1,0:T(8,128)} %collective-permute-done.12.refs_3_, ...), custom_call_target="tpu_custom_call" | custom-call | flops 452984832 | bytes 6282752 | tf_op jit(solution)/shard_map/pallas_call | solution.py:663
  42.8 4.4 %all-to-all-start = ((bf16[8,1,2,8,24,384]{5,4,3,2,1,0:T(8,128)(2,1)}), bf16[8,1,2,8,24,384]{5,4,3,2,1,0:T(8,128)(2,1)}, u32[]{:S(2)}, u32[]{:S(2)}) async-start(bf16[8,1,2,8,24,384]{5,4,3,2,1,0:T(8,128)(2,1)} %shard_map.336), calls=%async_computation | async-start | bytes 4718592 | tf_op jit(solution)/shard_map/all_to_all | solution.py:740
  47.2 7.6 %shard_map.332 = (bf16[2,12,192,384]{3,2,1,0:T(8,128)(2,1)}, f32[2,48,192]{2,1,0:T(8,128)}) custom-call(bf16[8,12,2,17280]{3,2,1,0:T(2,128)(2,1)} %stored_ref.6, bf16[2,8,384]{2,1,0:T(8,128)(2,1)} %constant.55.clone.sum_ref.refs_9_.refs_16_), custom_call_target="tpu_custom_call" | custom-call | flops 113246208 | bytes 10260480 | tf_op jit(solution)/shard_map/pallas_call | solution.py:663
  54.8 2.2 collective-permute-start
  57.0 2.6 collective-permute-start.1
  59.6 1.3 collective-permute-start.2
  60.9 7.4 %shard_map.333 = (bf16[2,2,8,24,384]{4,3,2,1,0:T(8,128)(2,1)}, bf16[2,2,8,24,384]{4,3,2,1,0:T(8,128)(2,1)}, bf16[2,2,8,24,384]{4,3,2,1,0:T(8,128)(2,1)}, bf16[2,...) custom-call(bf16[8,12,2,17280]{3,2,1,0:T(2,128)(2,1)} %stored_ref.7,, ...), custom_call_target="tpu_custom_call" | custom-call | flops 452984832 | bytes 11403780 | tf_op jit(solution)/shard_map/pallas_call | solution.py:663
  68.4 8.7 %shard_map.334 = (bf16[2,2,8,24,384]{4,3,2,1,0:T(8,128)(2,1)}, bf16[2,2,8,24,384]{4,3,2,1,0:T(8,128)(2,1)}, bf16[2,2,8,24,384]{4,3,2,1,0:T(8,128)(2,1)}, bf16[2,...) custom-call(f32[2,48,192]{2,1,0:T(8,128)} %get-tuple-element.52.refs, ...), custom_call_target="tpu_custom_call", output_to_operand_aliasing={{0}: (10, {}), {1}: (11, {}), {2}: (12, {}), {3}: (13, {}),... | custom-call | flops 452984832 | bytes 13360644 | tf_op jit(solution)/shard_map/pallas_call | solution.py:663
  77.2 1.9 collective-permute-start.4
  79.1 34.1 %shard_map.338 = (bf16[1,2,12,16,384]{4,3,2,1,0:T(8,128)(2,1)}, bf16[1,2,12,16,384]{4,3,2,1,0:T(8,128)(2,1)}, bf16[1,2,12,16,384]{4,3,2,1,0:T(8,128)(2,1)}, bf16...) custom-call(bf16[8,1,2,8,24,384]{5,4,3,2,1,0:T(8,128)(2,1)} %all-to-, ...), custom_call_target="tpu_custom_call" | custom-call | flops 10871635968 | bytes 10132484 | tf_op jit(solution)/shard_map/pallas_call | solution.py:663
  113.3 4.9 %all-to-all-start.3 = ((bf16[8,1,2,12,16,384]{5,4,3,2,1,0:T(8,128)(2,1)}), bf16[8,1,2,12,16,384]{5,4,3,2,1,0:T(8,128)(2,1)}, u32[]{:S(2)}, u32[]{:S(2)}) async-start(bf16[8,1,2,12,16,384]{5,4,3,2,1,0:T(8,128)(2,1)} %get-tuple-element.90), calls=%async_computation.3 | async-start | bytes 4718592 | tf_op jit(solution)/shard_map/all_to_all | solution.py:740
  118.2 1.4 collective-permute-start.5
  119.6 1.5 collective-permute-start.6
  121.4 1.5 collective-permute-start.8
  124.9 33.6 %collective-permute-done.5.refs_3_.refs_11_ = bf16[2,2,8,24,384]{4,3,2,1,0:T(8,128)(2,1)S(1)} collective-permute-done((bf16[2,2,8,24,384]{4,3,2,1,0:T(8,128)(2,1)S(1)}, bf16[2,2,8,24,384]{4,3,2,1,0:T(8,128)(2,1)S(1)}, u32[]{:S(2)}, u32[]{:S(2)}) %collective-permute-start.5) | collective-permute-done | bytes 589856 | tf_op jit(solution)/shard_map/ppermute | solution.py:734
  159.7 36.7 %collective-permute-done.7.refs_5_.refs_13_ = bf16[2,2,8,24,384]{4,3,2,1,0:T(8,128)(2,1)S(1)} collective-permute-done((bf16[2,2,8,24,384]{4,3,2,1,0:T(8,128)(2,1)S(1)}, bf16[2,2,8,24,384]{4,3,2,1,0:T(8,128)(2,1)S(1)}, u32[]{:S(2)}, u32[]{:S(2)}) %collective-permute-start.7) | collective-permute-done | bytes 589856 | tf_op jit(solution)/shard_map/ppermute | solution.py:734
  197.6 34.5 %shard_map.339 = (bf16[8,1,2,12,16,384]{5,4,3,2,1,0:T(8,128)(2,1)}, bf16[1,2,12,16,384]{4,3,2,1,0:T(8,128)(2,1)}, bf16[1,2,12,16,384]{4,3,2,1,0:T(8,128)(2,1)}, ...) custom-call(bf16[2,2,8,24,384]{4,3,2,1,0:T(8,128)(2,1)} %get-tuple-e, ...), custom_call_target="tpu_custom_call" | custom-call | flops 10871635968 | bytes 15049732 | tf_op jit(solution)/shard_map/pallas_call | solution.py:663
  232.3 4.5 %all-to-all-start.2 = ((bf16[8,1,2,12,16,384]{5,4,3,2,1,0:T(8,128)(2,1)}), bf16[8,1,2,12,16,384]{5,4,3,2,1,0:T(8,128)(2,1)}, u32[]{:S(2)}, u32[]{:S(2)}) async-start(bf16[8,1,2,12,16,384]{5,4,3,2,1,0:T(8,128)(2,1)} %get-tuple-element.73), calls=%async_computation.2 | async-start | bytes 4718592 | tf_op jit(solution)/shard_map/all_to_all | solution.py:740
  237.4 1.9 collective-permute-start.14
  239.4 1.5 collective-permute-start.16
  241.9 2.6 collective-permute-start.18
  244.5 27.7 %collective-permute-done.14.refs_2_ = bf16[1,2,12,16,384]{4,3,2,1,0:T(8,128)(2,1)} collective-permute-done((bf16[1,2,12,16,384]{4,3,2,1,0:T(8,128)(2,1)S(1)}, bf16[1,2,12,16,384]{4,3,2,1,0:T(8,128)(2,1)}, u32[]{:S(2)}, u32[]{:S(2)}) %collective-permute-start.14) | collective-permute-done | bytes 294944 | tf_op jit(solution)/shard_map/ppermute | solution.py:734
  273.0 4.4 %collective-permute-done.15.refs_3_ = bf16[1,2,12,16,384]{4,3,2,1,0:T(8,128)(2,1)} collective-permute-done((bf16[1,2,12,16,384]{4,3,2,1,0:T(8,128)(2,1)S(1)}, bf16[1,2,12,16,384]{4,3,2,1,0:T(8,128)(2,1)}, u32[]{:S(2)}, u32[]{:S(2)}) %collective-permute-start.15) | collective-permute-done | bytes 294944 | tf_op jit(solution)/shard_map/ppermute | solution.py:734
  278.1 1.4 collective-permute-start.35
  279.5 1.4 collective-permute-start.36
  281.7 4.2 %collective-permute-done.18.refs_6_ = bf16[1,2,12,16,384]{4,3,2,1,0:T(8,128)(2,1)} collective-permute-done((bf16[1,2,12,16,384]{4,3,2,1,0:T(8,128)(2,1)S(1)}, bf16[1,2,12,16,384]{4,3,2,1,0:T(8,128)(2,1)}, u32[]{:S(2)}, u32[]{:S(2)}) %collective-permute-start.18) | collective-permute-done | bytes 294944 | tf_op jit(solution)/shard_map/ppermute | solution.py:734
  285.9 5.2 %collective-permute-done.19.refs_7_ = bf16[1,2,12,16,384]{4,3,2,1,0:T(8,128)(2,1)} collective-permute-done((bf16[1,2,12,16,384]{4,3,2,1,0:T(8,128)(2,1)S(1)}, bf16[1,2,12,16,384]{4,3,2,1,0:T(8,128)(2,1)}, u32[]{:S(2)}, u32[]{:S(2)}) %collective-permute-start.19) | collective-permute-done | bytes 294944 | tf_op jit(solution)/shard_map/ppermute | solution.py:734
  291.6 7.8 %shard_map.340.refs_2_ = bf16[8,12,2,17280]{3,2,1,0:T(2,128)(2,1)} custom-call(bf16[1,2,12,16,384]{4,3,2,1,0:T(8,128)(2,1)} %get-tuple-element.74.refs_0_, bf16[1,2,12,16,384]{4,3,2,1,0:T(8,128)(2,1)} %collective-permute-done.13.refs_1_, bf16[1,2,12,16,384]{4,3,2,1,0:T(8,128)(2,1)} %collective-permute-done.14.refs_2_, ...), custom_call_target="tpu_custom_call" | custom-call | flops 452984832 | bytes 9043968 | tf_op jit(solution)/shard_map/pallas_call | solution.py:663
  299.4 1.8 collective-permute-start.22
  302.5 1.3 add_add_fusion
  304.6 1.4 collective-permute-done.21.refs_6_.refs_10_
  308.4 8.9 %shard_map.342 = (bf16[2,48,192]{2,1,0:T(8,128)(2,1)}, f32[8,2,384]{2,1,0:T(2,128)}) custom-call(f32[2,48,192]{2,1,0:T(8,128)} %get-tuple-element.70.refs_0_, f32[2,48,192]{2,1,0:T(8,128)} %collective-permute-done.10.refs_1_, f32[2,48,192]{2,1,0:T(8,128)} %collective-permute-done.11.refs_2_, f32[2,48,192]{2,1,0:T(8,128)} %collective-permute-done.12.refs_3_, ...), custom_call_target="tpu_custom_call" | custom-call | flops 452984832 | bytes 6355968 | tf_op jit(solution)/shard_map/pallas_call | solution.py:663
  318.3 1.6 collective-permute-start.31
  319.9 8.3 %collective-permute-done.24.refs_9_.refs_13_ = bf16[1,2,12,16,384]{4,3,2,1,0:T(8,128)(2,1)} collective-permute-done((bf16[1,2,12,16,384]{4,3,2,1,0:T(8,128)(2,1)}, bf16[1,2,12,16,384]{4,3,2,1,0:T(8,128)(2,1)}, u32[]{:S(2)}, u32[]{:S(2)}) %collective-permute-start.24) | collective-permute-done | bytes 294944 | tf_op jit(solution)/shard_map/ppermute | solution.py:734
  328.2 1.9 collective-permute-start.32
  330.2 9.1 %shard_map.343 = (bf16[2,48,192]{2,1,0:T(8,128)(2,1)}, f32[8,2,384]{2,1,0:T(2,128)}) custom-call(f32[2,48,192]{2,1,0:T(8,128)} %get-tuple-element.52.refs_0_, f32[2,48,192]{2,1,0:T(8,128)} %collective-permute-done.refs_1_, f32[2,48,192]{2,1,0:T(8,128)} %collective-permute-done.1.refs_2_, f32[2,48,192]{2,1,0:T(8,128)} %collective-permute-done.2.refs_3_, ...), custom_call_target="tpu_custom_call" | custom-call | flops 452984832 | bytes 6380544 | tf_op jit(solution)/shard_map/pallas_call | solution.py:663
  340.1 4.2 %all-to-all-start.4 = ((f32[8,2,384]{2,1,0:T(2,128)}), f32[8,2,384]{2,1,0:T(2,128)}, u32[]{:S(2)}, u32[]{:S(2)}) async-start(f32[8,2,384]{2,1,0:T(2,128)} %get-tuple-element.95), calls=%async_computation.4 | async-start | bytes 49152 | tf_op jit(solution)/shard_map/all_to_all | solution.py:740
  344.3 7.8 %shard_map.341 = bf16[8,12,2,17280]{3,2,1,0:T(2,128)(2,1)} custom-call(bf16[8,1,2,12,16,384]{5,4,3,2,1,0:T(8,128)(2,1)} %all-to-all-done.2.refs_0_, bf16[192,128]{1,0:T(8,128)(2,1)} %constant.48.clone.refs_1_, bf16[8,12,2,17280]{3,2,1,0:T(2,128)(2,1)} %shard_map.340.refs_2_), custom_call_target="tpu_custom_call", output_to_operand_aliasing={{}: (2, {})} | custom-call | flops 452984832 | bytes 15679488 | tf_op jit(solution)/shard_map/pallas_call | solution.py:663
  353.5 3.1 collective-permute-start.29
  356.6 11.2 %shard_map.344.refs_20_ = bf16[8,12,2,17280]{3,2,1,0:T(2,128)(2,1)} custom-call(f32[2,48,192]{2,1,0:T(8,128)} %get-tuple-element.70.refs_0_, f32[2,48,192]{2,1,0:T(8,128)} %collective-permute-done.10.refs_1_, f32[2,48,192]{2,1,0:T(8,128)} %collective-permute-done.11.refs_2_, f32[2,48,192]{2,1,0:T(8,128)} %collective-permute-done.12.refs_3_, ...), custom_call_target="tpu_custom_call" | custom-call | flops 452984832 | bytes 13065216 | tf_op jit(solution)/shard_map/pallas_call | solution.py:663
  367.8 11.3 %shard_map.345 = bf16[8,12,2,17280]{3,2,1,0:T(2,128)(2,1)} custom-call(f32[2,48,192]{2,1,0:T(8,128)} %get-tuple-element.52.refs_0_, f32[2,48,192]{2,1,0:T(8,128)} %collective-permute-done.refs_1_, f32[2,48,192]{2,1,0:T(8,128)} %collective-permute-done.1.refs_2_, f32[2,48,192]{2,1,0:T(8,128)} %collective-permute-done.2.refs_3_, ...), custom_call_target="tpu_custom_call", output_to_operand_aliasing={{}: (20, {})} | custom-call | flops 452984832 | bytes 19700736 | tf_op jit(solution)/shard_map/pallas_call | solution.py:663
  (114 shorter events, 20.1 us)
Async XLA Ops:
  8.1 34.7 %all-to-all-start.1 = ((bf16[8,1,2,8,24,384]{5,4,3,2,1,0:T(8,128)(2,1)}), bf16[8,1,2,8,24,384]{5,4,3,2,1,0:T(8,128)(2,1)}, u32[]{:S(2)}, u32[]{:S(2)}) async-start(bf16[8,1,2,8,24,384]{5,4,3,2,1,0:T(8,128)(2,1)} %shard_map.337), calls=%async_computation.1 | async-start | bytes 4718592 | tf_op jit(solution)/shard_map/all_to_all | solution.py:740
  20.9 8.3 %collective-permute-start.10 = (f32[2,48,192]{2,1,0:T(8,128)}, f32[2,48,192]{2,1,0:T(8,128)}, u32[]{:S(2)}, u32[]{:S(2)}) collective-permute-start(f32[2,48,192]{2,1,0:T(8,128)} %get-tuple-element.70.refs_0_), channel_id=1, source_target_pairs={{0,1},{1,2},{2,3},{3,0},{4,5},{5,6},{6,7},{7,4},{8,9},{9,10},{10,1... | collective-permute-start | bytes 221192 | tf_op jit(solution)/shard_map/ppermute | solution.py:747
  23.1 9.9 %collective-permute-start.11 = (f32[2,48,192]{2,1,0:T(8,128)}, f32[2,48,192]{2,1,0:T(8,128)}, u32[]{:S(2)}, u32[]{:S(2)}) collective-permute-start(f32[2,48,192]{2,1,0:T(8,128)} %get-tuple-element.70.refs_0_), channel_id=1, source_target_pairs={{0,2},{1,3},{2,0},{3,1},{4,6},{5,7},{6,4},{7,5},{8,10},{9,11},{10,... | collective-permute-start | bytes 221192 | tf_op jit(solution)/shard_map/ppermute | solution.py:747
  25.7 7.4 %collective-permute-start.12 = (f32[2,48,192]{2,1,0:T(8,128)}, f32[2,48,192]{2,1,0:T(8,128)}, u32[]{:S(2)}, u32[]{:S(2)}) collective-permute-start(f32[2,48,192]{2,1,0:T(8,128)} %get-tuple-element.70.refs_0_), channel_id=1, source_target_pairs={{0,3},{1,0},{2,1},{3,2},{4,7},{5,4},{6,5},{7,6},{8,11},{9,8},{10,9... | collective-permute-start | bytes 221192 | tf_op jit(solution)/shard_map/ppermute | solution.py:747
  42.8 36.3 %all-to-all-start = ((bf16[8,1,2,8,24,384]{5,4,3,2,1,0:T(8,128)(2,1)}), bf16[8,1,2,8,24,384]{5,4,3,2,1,0:T(8,128)(2,1)}, u32[]{:S(2)}, u32[]{:S(2)}) async-start(bf16[8,1,2,8,24,384]{5,4,3,2,1,0:T(8,128)(2,1)} %shard_map.336), calls=%async_computation | async-start | bytes 4718592 | tf_op jit(solution)/shard_map/all_to_all | solution.py:740
  54.8 13.5 %collective-permute-start = (f32[2,48,192]{2,1,0:T(8,128)}, f32[2,48,192]{2,1,0:T(8,128)}, u32[]{:S(2)}, u32[]{:S(2)}) collective-permute-start(f32[2,48,192]{2,1,0:T(8,128)} %get-tuple-element.52.refs_0_), channel_id=1, source_target_pairs={{0,1},{1,2},{2,3},{3,0},{4,5},{5,6},{6,7},{7,4},{8,9},{9,10},{10,1... | collective-permute-start | bytes 221192 | tf_op jit(solution)/shard_map/ppermute | solution.py:747
  57.0 11.4 %collective-permute-start.1 = (f32[2,48,192]{2,1,0:T(8,128)}, f32[2,48,192]{2,1,0:T(8,128)}, u32[]{:S(2)}, u32[]{:S(2)}) collective-permute-start(f32[2,48,192]{2,1,0:T(8,128)} %get-tuple-element.52.refs_0_), channel_id=1, source_target_pairs={{0,2},{1,3},{2,0},{3,1},{4,6},{5,7},{6,4},{7,5},{8,10},{9,11},{10,... | collective-permute-start | bytes 221192 | tf_op jit(solution)/shard_map/ppermute | solution.py:747
  59.6 8.8 %collective-permute-start.2 = (f32[2,48,192]{2,1,0:T(8,128)}, f32[2,48,192]{2,1,0:T(8,128)}, u32[]{:S(2)}, u32[]{:S(2)}) collective-permute-start(f32[2,48,192]{2,1,0:T(8,128)} %get-tuple-element.52.refs_0_), channel_id=1, source_target_pairs={{0,3},{1,0},{2,1},{3,2},{4,7},{5,4},{6,5},{7,6},{8,11},{9,8},{10,9... | collective-permute-start | bytes 221192 | tf_op jit(solution)/shard_map/ppermute | solution.py:747
  77.1 44.2 %collective-permute-start.3 = (bf16[2,2,8,24,384]{4,3,2,1,0:T(8,128)(2,1)}, bf16[2,2,8,24,384]{4,3,2,1,0:T(8,128)(2,1)}, u32[]{:S(2)}, u32[]{:S(2)}) collective-permute-start(bf16[2,2,8,24,384]{4,3,2,1,0:T(8,128)(2,1)} %get-tuple-element.63), channel_id=1, source_target_pairs={{0,4},{4,0},{8,12},{12,8},{16,20},{20,16},{24,28},{28,24},{1,5},{5... | collective-permute-start | bytes 1769480 | tf_op jit(solution)/shard_map/ppermute | solution.py:734
  77.2 45.6 %collective-permute-start.4 = (bf16[2,2,8,24,384]{4,3,2,1,0:T(8,128)(2,1)}, bf16[2,2,8,24,384]{4,3,2,1,0:T(8,128)(2,1)}, u32[]{:S(2)}, u32[]{:S(2)}) collective-permute-start(bf16[2,2,8,24,384]{4,3,2,1,0:T(8,128)(2,1)} %get-tuple-element.64), channel_id=1, source_target_pairs={{0,8},{4,12},{8,0},{12,4},{16,24},{20,28},{24,16},{28,20},{1,9},{5... | collective-permute-start | bytes 1769480 | tf_op jit(solution)/shard_map/ppermute | solution.py:734
  113.3 10.8 %copy-start.9 = (s32[192]{0:T(256)S(1)}, s32[192]{0:T(256)}, u32[]{:S(2)}) copy-start(s32[192]{0:T(256)} %constant.52.clone) | copy-start | bytes 2308
  113.3 10.8 %copy-start.10 = (s32[192]{0:T(256)S(1)}, s32[192]{0:T(256)}, u32[]{:S(2)}) copy-start(s32[192]{0:T(256)} %constant.53.clone) | copy-start | bytes 2308
  113.3 118.9 %all-to-all-start.3 = ((bf16[8,1,2,12,16,384]{5,4,3,2,1,0:T(8,128)(2,1)}), bf16[8,1,2,12,16,384]{5,4,3,2,1,0:T(8,128)(2,1)}, u32[]{:S(2)}, u32[]{:S(2)}) async-start(bf16[8,1,2,12,16,384]{5,4,3,2,1,0:T(8,128)(2,1)} %get-tuple-element.90), calls=%async_computation.3 | async-start | bytes 4718592 | tf_op jit(solution)/shard_map/all_to_all | solution.py:740
  118.2 40.3 %collective-permute-start.5 = (bf16[2,2,8,24,384]{4,3,2,1,0:T(8,128)(2,1)S(1)}, bf16[2,2,8,24,384]{4,3,2,1,0:T(8,128)(2,1)S(1)}, u32[]{:S(2)}, u32[]{:S(2)}) collective-permute-start(bf16[2,2,8,24,384]{4,3,2,1,0:T(8,128)(2,1)S(1)} %copy-done), channel_id=1, source_target_pairs={{0,12},{4,8},{8,4},{12,0},{16,28},{20,24},{24,20},{28,16},{1,13},{... | collective-permute-start | bytes 1769480 | tf_op jit(solution)/shard_map/ppermute | solution.py:734
  119.6 40.1 %collective-permute-start.6 = (bf16[2,2,8,24,384]{4,3,2,1,0:T(8,128)(2,1)S(1)}, bf16[2,2,8,24,384]{4,3,2,1,0:T(8,128)(2,1)S(1)}, u32[]{:S(2)}, u32[]{:S(2)}) collective-permute-start(bf16[2,2,8,24,384]{4,3,2,1,0:T(8,128)(2,1)S(1)} %copy-done.1), channel_id=1, source_target_pairs={{0,16},{4,20},{8,24},{12,28},{16,0},{20,4},{24,8},{28,12},{1,17},{... | collective-permute-start | bytes 1769480 | tf_op jit(solution)/shard_map/ppermute | solution.py:734
  121.1 75.2 %collective-permute-start.7 = (bf16[2,2,8,24,384]{4,3,2,1,0:T(8,128)(2,1)S(1)}, bf16[2,2,8,24,384]{4,3,2,1,0:T(8,128)(2,1)S(1)}, u32[]{:S(2)}, u32[]{:S(2)}) collective-permute-start(bf16[2,2,8,24,384]{4,3,2,1,0:T(8,128)(2,1)S(1)} %copy-done.2), channel_id=1, source_target_pairs={{0,20},{4,16},{8,28},{12,24},{16,4},{20,0},{24,12},{28,8},{1,21},{... | collective-permute-start | bytes 1769480 | tf_op jit(solution)/shard_map/ppermute | solution.py:734
  121.4 75.0 %collective-permute-start.8 = (bf16[2,2,8,24,384]{4,3,2,1,0:T(8,128)(2,1)S(1)}, bf16[2,2,8,24,384]{4,3,2,1,0:T(8,128)(2,1)S(1)}, u32[]{:S(2)}, u32[]{:S(2)}) collective-permute-start(bf16[2,2,8,24,384]{4,3,2,1,0:T(8,128)(2,1)S(1)} %copy-done.3), channel_id=1, source_target_pairs={{0,24},{4,28},{8,16},{12,20},{16,8},{20,12},{24,0},{28,4},{1,25},{... | collective-permute-start | bytes 1769480 | tf_op jit(solution)/shard_map/ppermute | solution.py:734
  122.8 73.5 %collective-permute-start.9 = (bf16[2,2,8,24,384]{4,3,2,1,0:T(8,128)(2,1)S(1)}, bf16[2,2,8,24,384]{4,3,2,1,0:T(8,128)(2,1)S(1)}, u32[]{:S(2)}, u32[]{:S(2)}) collective-permute-start(bf16[2,2,8,24,384]{4,3,2,1,0:T(8,128)(2,1)S(1)} %copy-done.4), channel_id=1, source_target_pairs={{0,28},{4,24},{8,20},{12,16},{16,12},{20,8},{24,4},{28,0},{1,29},{... | collective-permute-start | bytes 1769480 | tf_op jit(solution)/shard_map/ppermute | solution.py:734
  158.5 37.9 %copy-start.13 = (bf16[2,2,8,24,384]{4,3,2,1,0:T(8,128)(2,1)}, bf16[2,2,8,24,384]{4,3,2,1,0:T(8,128)(2,1)S(1)}, u32[]{:S(2)}) copy-start(bf16[2,2,8,24,384]{4,3,2,1,0:T(8,128)(2,1)S(1)} %collective-permute-done.5.refs_3_.refs_11_) | copy-start | bytes 1769476
  159.7 36.7 %copy-start.14 = (bf16[2,2,8,24,384]{4,3,2,1,0:T(8,128)(2,1)}, bf16[2,2,8,24,384]{4,3,2,1,0:T(8,128)(2,1)S(1)}, u32[]{:S(2)}) copy-start(bf16[2,2,8,24,384]{4,3,2,1,0:T(8,128)(2,1)S(1)} %collective-permute-done.6.refs_4_.refs_12_) | copy-start | bytes 1769476
  232.2 40.0 %copy-start.18 = (bf16[1,2,12,16,384]{4,3,2,1,0:T(8,128)(2,1)S(1)}, bf16[1,2,12,16,384]{4,3,2,1,0:T(8,128)(2,1)}, u32[]{:S(2)}) copy-start(bf16[1,2,12,16,384]{4,3,2,1,0:T(8,128)(2,1)} %get-tuple-element.81) | copy-start | bytes 884740
  232.2 48.7 %copy-start.7 = (bf16[192,128]{1,0:T(8,128)(2,1)S(1)}, bf16[192,128]{1,0:T(8,128)(2,1)}, u32[]{:S(2)}) copy-start(bf16[192,128]{1,0:T(8,128)(2,1)} %constant.48.clone.refs_1_) | copy-start | bytes 147460
  232.3 107.8 %all-to-all-start.2 = ((bf16[8,1,2,12,16,384]{5,4,3,2,1,0:T(8,128)(2,1)}), bf16[8,1,2,12,16,384]{5,4,3,2,1,0:T(8,128)(2,1)}, u32[]{:S(2)}, u32[]{:S(2)}) async-start(bf16[8,1,2,12,16,384]{5,4,3,2,1,0:T(8,128)(2,1)} %get-tuple-element.73), calls=%async_computation.2 | async-start | bytes 4718592 | tf_op jit(solution)/shard_map/all_to_all | solution.py:740
  236.8 4.1 %collective-permute-start.33 = (bf16[776,128]{1,0:T(8,128)(2,1)S(1)}, bf16[776,128]{1,0:T(8,128)(2,1)S(1)}, u32[]{:S(2)}, u32[]{:S(2)}) collective-permute-start(bf16[776,128]{1,0:T(8,128)(2,1)S(1)} %copy-done.6), channel_id=1, source_target_pairs={{0,4},{4,0},{8,12},{12,8},{16,20},{20,16},{24,28},{28,24},{1,5},{5... | collective-permute-start | bytes 595976 | tf_op jit(solution)/shard_map/ppermute | solution.py:758
  237.2 4.7 %collective-permute-start.13 = (bf16[1,2,12,16,384]{4,3,2,1,0:T(8,128)(2,1)S(1)}, bf16[1,2,12,16,384]{4,3,2,1,0:T(8,128)(2,1)}, u32[]{:S(2)}, u32[]{:S(2)}) collective-permute-start(bf16[1,2,12,16,384]{4,3,2,1,0:T(8,128)(2,1)S(1)} %copy-done.24), channel_id=1, source_target_pairs={{0,4},{4,0},{8,12},{12,8},{16,20},{20,16},{24,28},{28,24},{1,5},{5... | collective-permute-start | bytes 884744 | tf_op jit(solution)/shard_map/ppermute | solution.py:734
  237.4 34.8 %collective-permute-start.14 = (bf16[1,2,12,16,384]{4,3,2,1,0:T(8,128)(2,1)S(1)}, bf16[1,2,12,16,384]{4,3,2,1,0:T(8,128)(2,1)}, u32[]{:S(2)}, u32[]{:S(2)}) collective-permute-start(bf16[1,2,12,16,384]{4,3,2,1,0:T(8,128)(2,1)S(1)} %copy-done.23), channel_id=1, source_target_pairs={{0,8},{4,12},{8,0},{12,4},{16,24},{20,28},{24,16},{28,20},{1,9},{5... | collective-permute-start | bytes 884744 | tf_op jit(solution)/shard_map/ppermute | solution.py:734
  239.3 38.1 %collective-permute-start.15 = (bf16[1,2,12,16,384]{4,3,2,1,0:T(8,128)(2,1)S(1)}, bf16[1,2,12,16,384]{4,3,2,1,0:T(8,128)(2,1)}, u32[]{:S(2)}, u32[]{:S(2)}) collective-permute-start(bf16[1,2,12,16,384]{4,3,2,1,0:T(8,128)(2,1)S(1)} %copy-done.22), channel_id=1, source_target_pairs={{0,12},{4,8},{8,4},{12,0},{16,28},{20,24},{24,20},{28,16},{1,13},{... | collective-permute-start | bytes 884744 | tf_op jit(solution)/shard_map/ppermute | solution.py:734
  239.4 38.7 %collective-permute-start.16 = (bf16[1,2,12,16,384]{4,3,2,1,0:T(8,128)(2,1)S(1)}, bf16[1,2,12,16,384]{4,3,2,1,0:T(8,128)(2,1)}, u32[]{:S(2)}, u32[]{:S(2)}) collective-permute-start(bf16[1,2,12,16,384]{4,3,2,1,0:T(8,128)(2,1)S(1)} %copy-done.21), channel_id=1, source_target_pairs={{0,16},{4,20},{8,24},{12,28},{16,0},{20,4},{24,8},{28,12},{1,17},{... | collective-permute-start | bytes 884744 | tf_op jit(solution)/shard_map/ppermute | solution.py:734
  240.9 38.6 %collective-permute-start.17 = (bf16[1,2,12,16,384]{4,3,2,1,0:T(8,128)(2,1)S(1)}, bf16[1,2,12,16,384]{4,3,2,1,0:T(8,128)(2,1)}, u32[]{:S(2)}, u32[]{:S(2)}) collective-permute-start(bf16[1,2,12,16,384]{4,3,2,1,0:T(8,128)(2,1)S(1)} %copy-done.20), channel_id=1, source_target_pairs={{0,20},{4,16},{8,28},{12,24},{16,4},{20,0},{24,12},{28,8},{1,21},{... | collective-permute-start | bytes 884744 | tf_op jit(solution)/shard_map/ppermute | solution.py:734
  241.9 44.0 %collective-permute-start.18 = (bf16[1,2,12,16,384]{4,3,2,1,0:T(8,128)(2,1)S(1)}, bf16[1,2,12,16,384]{4,3,2,1,0:T(8,128)(2,1)}, u32[]{:S(2)}, u32[]{:S(2)}) collective-permute-start(bf16[1,2,12,16,384]{4,3,2,1,0:T(8,128)(2,1)S(1)} %copy-done.19), channel_id=1, source_target_pairs={{0,24},{4,28},{8,16},{12,20},{16,8},{20,12},{24,0},{28,4},{1,25},{... | collective-permute-start | bytes 884744 | tf_op jit(solution)/shard_map/ppermute | solution.py:734
  272.2 18.8 %collective-permute-start.19 = (bf16[1,2,12,16,384]{4,3,2,1,0:T(8,128)(2,1)S(1)}, bf16[1,2,12,16,384]{4,3,2,1,0:T(8,128)(2,1)}, u32[]{:S(2)}, u32[]{:S(2)}) collective-permute-start(bf16[1,2,12,16,384]{4,3,2,1,0:T(8,128)(2,1)S(1)} %copy-done.18), channel_id=1, source_target_pairs={{0,28},{4,24},{8,20},{12,16},{16,12},{20,8},{24,4},{28,0},{1,29},{... | collective-permute-start | bytes 884744 | tf_op jit(solution)/shard_map/ppermute | solution.py:734
  277.4 22.0 %collective-permute-start.34 = (bf16[776,128]{1,0:T(8,128)(2,1)}, bf16[776,128]{1,0:T(8,128)(2,1)}, u32[]{:S(2)}, u32[]{:S(2)}) collective-permute-start(bf16[776,128]{1,0:T(8,128)(2,1)} %add_convert_fusion), channel_id=1, source_target_pairs={{0,8},{4,12},{8,0},{12,4},{16,24},{20,28},{24,16},{28,20},{1,9},{5... | collective-permute-start | bytes 595976 | tf_op jit(solution)/shard_map/ppermute | solution.py:758
  278.1 23.1 %collective-permute-start.35 = (bf16[776,128]{1,0:T(8,128)(2,1)}, bf16[776,128]{1,0:T(8,128)(2,1)}, u32[]{:S(2)}, u32[]{:S(2)}) collective-permute-start(bf16[776,128]{1,0:T(8,128)(2,1)} %add_convert_fusion), channel_id=1, source_target_pairs={{0,16},{4,20},{8,24},{12,28},{16,0},{20,4},{24,8},{28,12},{1,17},{... | collective-permute-start | bytes 595976 | tf_op jit(solution)/shard_map/ppermute | solution.py:758
  279.5 22.3 %collective-permute-start.36 = (bf16[776,128]{1,0:T(8,128)(2,1)}, bf16[776,128]{1,0:T(8,128)(2,1)}, u32[]{:S(2)}, u32[]{:S(2)}) collective-permute-start(bf16[776,128]{1,0:T(8,128)(2,1)} %add_convert_fusion), channel_id=1, source_target_pairs={{0,24},{4,28},{8,16},{12,20},{16,8},{20,12},{24,0},{28,4},{1,25},{... | collective-permute-start | bytes 595976 | tf_op jit(solution)/shard_map/ppermute | solution.py:758
  285.9 17.9 %collective-permute-start.20 = (bf16[1,2,12,16,384]{4,3,2,1,0:T(8,128)(2,1)}, bf16[1,2,12,16,384]{4,3,2,1,0:T(8,128)(2,1)}, u32[]{:S(2)}, u32[]{:S(2)}) collective-permute-start(bf16[1,2,12,16,384]{4,3,2,1,0:T(8,128)(2,1)} %get-tuple-element.83), channel_id=1, source_target_pairs={{0,4},{4,0},{8,12},{12,8},{16,20},{20,16},{24,28},{28,24},{1,5},{5... | collective-permute-start | bytes 884744 | tf_op jit(solution)/shard_map/ppermute | solution.py:734
  291.1 15.0 %collective-permute-start.21 = (bf16[1,2,12,16,384]{4,3,2,1,0:T(8,128)(2,1)}, bf16[1,2,12,16,384]{4,3,2,1,0:T(8,128)(2,1)}, u32[]{:S(2)}, u32[]{:S(2)}) collective-permute-start(bf16[1,2,12,16,384]{4,3,2,1,0:T(8,128)(2,1)} %get-tuple-element.84), channel_id=1, source_target_pairs={{0,8},{4,12},{8,0},{12,4},{16,24},{20,28},{24,16},{28,20},{1,9},{5... | collective-permute-start | bytes 884744 | tf_op jit(solution)/shard_map/ppermute | solution.py:734
  299.4 17.9 %collective-permute-start.22 = (bf16[1,2,12,16,384]{4,3,2,1,0:T(8,128)(2,1)}, bf16[1,2,12,16,384]{4,3,2,1,0:T(8,128)(2,1)}, u32[]{:S(2)}, u32[]{:S(2)}) collective-permute-start(bf16[1,2,12,16,384]{4,3,2,1,0:T(8,128)(2,1)} %get-tuple-element.85), channel_id=1, source_target_pairs={{0,12},{4,8},{8,4},{12,0},{16,28},{20,24},{24,20},{28,16},{1,13},{... | collective-permute-start | bytes 884744 | tf_op jit(solution)/shard_map/ppermute | solution.py:734
  301.2 17.0 %collective-permute-start.23 = (bf16[1,2,12,16,384]{4,3,2,1,0:T(8,128)(2,1)}, bf16[1,2,12,16,384]{4,3,2,1,0:T(8,128)(2,1)}, u32[]{:S(2)}, u32[]{:S(2)}) collective-permute-start(bf16[1,2,12,16,384]{4,3,2,1,0:T(8,128)(2,1)} %get-tuple-element.86), channel_id=1, source_target_pairs={{0,16},{4,20},{8,24},{12,28},{16,0},{20,4},{24,8},{28,12},{1,17},{... | collective-permute-start | bytes 884744 | tf_op jit(solution)/shard_map/ppermute | solution.py:734
  301.8 26.4 %collective-permute-start.24 = (bf16[1,2,12,16,384]{4,3,2,1,0:T(8,128)(2,1)}, bf16[1,2,12,16,384]{4,3,2,1,0:T(8,128)(2,1)}, u32[]{:S(2)}, u32[]{:S(2)}) collective-permute-start(bf16[1,2,12,16,384]{4,3,2,1,0:T(8,128)(2,1)} %get-tuple-element.87), channel_id=1, source_target_pairs={{0,20},{4,16},{8,28},{12,24},{16,4},{20,0},{24,12},{28,8},{1,21},{... | collective-permute-start | bytes 884744 | tf_op jit(solution)/shard_map/ppermute | solution.py:734
  303.8 26.4 %collective-permute-start.25 = (bf16[1,2,12,16,384]{4,3,2,1,0:T(8,128)(2,1)}, bf16[1,2,12,16,384]{4,3,2,1,0:T(8,128)(2,1)}, u32[]{:S(2)}, u32[]{:S(2)}) collective-permute-start(bf16[1,2,12,16,384]{4,3,2,1,0:T(8,128)(2,1)} %get-tuple-element.88), channel_id=1, source_target_pairs={{0,24},{4,28},{8,16},{12,20},{16,8},{20,12},{24,0},{28,4},{1,25},{... | collective-permute-start | bytes 884744 | tf_op jit(solution)/shard_map/ppermute | solution.py:734
  306.1 24.1 %collective-permute-start.26 = (bf16[1,2,12,16,384]{4,3,2,1,0:T(8,128)(2,1)}, bf16[1,2,12,16,384]{4,3,2,1,0:T(8,128)(2,1)}, u32[]{:S(2)}, u32[]{:S(2)}) collective-permute-start(bf16[1,2,12,16,384]{4,3,2,1,0:T(8,128)(2,1)} %get-tuple-element.89), channel_id=1, source_target_pairs={{0,28},{4,24},{8,20},{12,16},{16,12},{20,8},{24,4},{28,0},{1,29},{... | collective-permute-start | bytes 884744 | tf_op jit(solution)/shard_map/ppermute | solution.py:734
  317.3 36.2 %collective-permute-start.30 = (bf16[2,48,192]{2,1,0:T(8,128)(2,1)}, bf16[2,48,192]{2,1,0:T(8,128)(2,1)}, u32[]{:S(2)}, u32[]{:S(2)}) collective-permute-start(bf16[2,48,192]{2,1,0:T(8,128)(2,1)} %get-tuple-element.93.refs_4_), channel_id=1, source_target_pairs={{0,1},{1,2},{2,3},{3,0},{4,5},{5,6},{6,7},{7,4},{8,9},{9,10},{10,1... | collective-permute-start | bytes 110600 | tf_op jit(solution)/shard_map/ppermute | solution.py:747
  318.3 38.4 %collective-permute-start.31 = (bf16[2,48,192]{2,1,0:T(8,128)(2,1)}, bf16[2,48,192]{2,1,0:T(8,128)(2,1)}, u32[]{:S(2)}, u32[]{:S(2)}) collective-permute-start(bf16[2,48,192]{2,1,0:T(8,128)(2,1)} %get-tuple-element.93.refs_4_), channel_id=1, source_target_pairs={{0,2},{1,3},{2,0},{3,1},{4,6},{5,7},{6,4},{7,5},{8,10},{9,11},{10,... | collective-permute-start | bytes 110600 | tf_op jit(solution)/shard_map/ppermute | solution.py:747
  328.2 28.4 %collective-permute-start.32 = (bf16[2,48,192]{2,1,0:T(8,128)(2,1)}, bf16[2,48,192]{2,1,0:T(8,128)(2,1)}, u32[]{:S(2)}, u32[]{:S(2)}) collective-permute-start(bf16[2,48,192]{2,1,0:T(8,128)(2,1)} %get-tuple-element.93.refs_4_), channel_id=1, source_target_pairs={{0,3},{1,0},{2,1},{3,2},{4,7},{5,4},{6,5},{7,6},{8,11},{9,8},{10,9... | collective-permute-start | bytes 110600 | tf_op jit(solution)/shard_map/ppermute | solution.py:747
  339.3 28.5 %collective-permute-start.27 = (bf16[2,48,192]{2,1,0:T(8,128)(2,1)}, bf16[2,48,192]{2,1,0:T(8,128)(2,1)}, u32[]{:S(2)}, u32[]{:S(2)}) collective-permute-start(bf16[2,48,192]{2,1,0:T(8,128)(2,1)} %get-tuple-element.92.refs_4_), channel_id=1, source_target_pairs={{0,1},{1,2},{2,3},{3,0},{4,5},{5,6},{6,7},{7,4},{8,9},{9,10},{10,1... | collective-permute-start | bytes 110600 | tf_op jit(solution)/shard_map/ppermute | solution.py:747
  339.4 28.3 %collective-permute-start.28 = (bf16[2,48,192]{2,1,0:T(8,128)(2,1)}, bf16[2,48,192]{2,1,0:T(8,128)(2,1)}, u32[]{:S(2)}, u32[]{:S(2)}) collective-permute-start(bf16[2,48,192]{2,1,0:T(8,128)(2,1)} %get-tuple-element.92.refs_4_), channel_id=1, source_target_pairs={{0,2},{1,3},{2,0},{3,1},{4,6},{5,7},{6,4},{7,5},{8,10},{9,11},{10,... | collective-permute-start | bytes 110600 | tf_op jit(solution)/shard_map/ppermute | solution.py:747
  340.1 12.0 %all-to-all-start.4 = ((f32[8,2,384]{2,1,0:T(2,128)}), f32[8,2,384]{2,1,0:T(2,128)}, u32[]{:S(2)}, u32[]{:S(2)}) async-start(f32[8,2,384]{2,1,0:T(2,128)} %get-tuple-element.95), calls=%async_computation.4 | async-start | bytes 49152 | tf_op jit(solution)/shard_map/all_to_all | solution.py:740
  353.5 14.3 %collective-permute-start.29 = (bf16[2,48,192]{2,1,0:T(8,128)(2,1)}, bf16[2,48,192]{2,1,0:T(8,128)(2,1)}, u32[]{:S(2)}, u32[]{:S(2)}) collective-permute-start(bf16[2,48,192]{2,1,0:T(8,128)(2,1)} %get-tuple-element.92.refs_4_), channel_id=1, source_target_pairs={{0,3},{1,0},{2,1},{3,2},{4,7},{5,4},{6,5},{7,6},{8,11},{9,8},{10,9... | collective-permute-start | bytes 110600 | tf_op jit(solution)/shard_map/ppermute | solution.py:747
  (19 other events, 121.9 us)

commit v8 on v7

--- a/solution.py
+++ b/solution.py
@@ -272,8 +272,8 @@
 
 def normalise_kernel(p, split, *refs):
     stat_refs = refs[: p.chan]
-    tokens_ref, affine_ref, table_ref, scale_ref, wide_ref = refs[p.chan : p.chan + 5]
-    refs = refs[p.chan + 5 :]
+    tokens_ref, affine_ref, table_ref, wide_ref = refs[p.chan : p.chan + 4]
+    refs = refs[p.chan + 4 :]
     me, refs = (refs[0][0], refs[1:]) if split else (None, refs)
     out_refs, (rows_ref, turn_ref) = refs[:-2], refs[-2:]
     moments(p, stat_refs, rows_ref)
@@ -285,7 +285,7 @@
             centred = (tokens_ref[0, h, :, at].astype(single) - mean) * inverse
             tiles.append((centred * affine_ref[0:1, at] + affine_ref[1:2, at]).astype(half))
         normed = jnp.concatenate(tiles, axis=1)
-        analyse(p, normed, table_ref[...], scale_ref[...], turn_ref, h)
+        analyse(p, normed, table_ref[...], 1.0 / math.sqrt(p.lon), turn_ref, h)
 
     pipelined(p, lambda h: expand(p, rows_ref[h], wide_ref), use)
 
@@ -771,7 +771,7 @@
     p = Plan(members, w_first.shape[-1], space, chan)
     size = p.packs // 2
     grid = (size, p.steps)
-    table, plain_scale, double_scale, mixed_plain, slope_plain = lon_tables(p)
+    table, _, double_scale, mixed_plain, slope_plain = lon_tables(p)
     there_plain, back_table = lat_tables(p)
     slope_table, there_table = jnp.asarray(slope_plain, half), jnp.asarray(there_plain, half)
     mixed_table = jnp.asarray(mixed_plain, half)
@@ -840,7 +840,7 @@
         )
 
     def normalise_chunk(stats, tokens, before, near):
-        tail = (affine, table, plain_scale, wide_table)
+        tail = (affine, table, wide_table)
         ins = (*stats, tokens, *tail)
         specs = [part_spec(p, s) for s in (*stats, tokens)] + [whole_spec(v) for v in tail]
         if near:

time: 382 us -> 381 us (level)
  no operation moved by 1% of the time
where the time goes in v8:
time: 381 us; the launch traced here: 379 us
  Pallas kernels  172 us (45%)
  waiting for transfers between devices  129 us (34%)
  starting transfers between devices  67.4 us (18%)
  other arithmetic  4.29 us (1%)
    pallas_call x14, Pallas kernels, _call(): pl.pallas_call(body, grid=grid, in_specs=in_specs, out_specs=out_specs, o...  172 us
    ppermute x21, waiting for transfers between devices, exchange_near(): lax.ppermute(value, 'space', [(i, i ^ x) for i in range(count)])  123 us
    all_to_all x5, starting transfers between devices, exchange(): return lax.all_to_all(value, 'space', 0, 0, tiled=True)  23.1 us
    ppermute x12, starting transfers between devices, around(): lax.ppermute(value, axis, [(i, (i + step) % size) for i in range(size)])  20.6 us
    ppermute x21, starting transfers between devices, exchange_near(): lax.ppermute(value, 'space', [(i, i ^ x) for i in range(count)])  19.7 us
  transfers between devices with their start and end apart: 42, of which 12 were waited for; matrix products, arithmetic and copies ran while one was open for 2% of the time, Pallas kernels for 40%

profile of v8, /device:TPU:0, one launch (start us, length us, event | category | flops | bytes accessed | tf_op | source)
XLA Modules:
  0.0 379.2 jit_solution(14954983821925521407)
XLA Ops:
  0.6 7.5 %shard_map.328 = bf16[8,1,2,8,24,384]{5,4,3,2,1,0:T(8,128)(2,1)} custom-call(bf16[8,12,2,17280]{3,2,1,0:T(2,128)(2,1)} %stored_ref.7, bf16[128,192]{1,0:T(8,128)(2,1)} %constant.40.clone.table_ref.refs_6_, f32[128,1]{1,0:T(8,128)} %constant.41.clone.scale_ref), custom_call_target="tpu_custom_call" | custom-call | flops 452984832 | bytes 9044480 | tf_op jit(solution)/shard_map/pallas_call | solution.py:663
  8.1 5.2 %all-to-all-start.1 = ((bf16[8,1,2,8,24,384]{5,4,3,2,1,0:T(8,128)(2,1)}), bf16[8,1,2,8,24,384]{5,4,3,2,1,0:T(8,128)(2,1)}, u32[]{:S(2)}, u32[]{:S(2)}) async-start(bf16[8,1,2,8,24,384]{5,4,3,2,1,0:T(8,128)(2,1)} %shard_map.328), calls=%async_computation.1 | async-start | bytes 4718592 | tf_op jit(solution)/shard_map/all_to_all | solution.py:740
  13.3 7.6 %shard_map.326 = (bf16[2,12,192,384]{3,2,1,0:T(8,128)(2,1)}, f32[2,48,192]{2,1,0:T(8,128)}) custom-call(bf16[8,12,2,17280]{3,2,1,0:T(2,128)(2,1)} %stored_ref.6, bf16[2,8,384]{2,1,0:T(8,128)(2,1)} %constant.52.clone.sum_ref.refs_9_.refs_16_), custom_call_target="tpu_custom_call" | custom-call | flops 113246208 | bytes 10260480 | tf_op jit(solution)/shard_map/pallas_call | solution.py:663
  20.9 2.3 collective-permute-start.10
  23.1 2.6 collective-permute-start.11
  25.7 1.3 collective-permute-start.12
  29.2 3.9 %collective-permute-done.11.refs_2_ = f32[2,48,192]{2,1,0:T(8,128)} collective-permute-done((f32[2,48,192]{2,1,0:T(8,128)}, f32[2,48,192]{2,1,0:T(8,128)}, u32[]{:S(2)}, u32[]{:S(2)}) %collective-permute-start.11) | collective-permute-done | bytes 73760 | tf_op jit(solution)/shard_map/ppermute | solution.py:747
  33.1 8.6 %shard_map.327 = bf16[8,1,2,8,24,384]{5,4,3,2,1,0:T(8,128)(2,1)} custom-call(f32[2,48,192]{2,1,0:T(8,128)} %get-tuple-element.70.refs_0_, f32[2,48,192]{2,1,0:T(8,128)} %collective-permute-done.10.refs_1_, f32[2,48,192]{2,1,0:T(8,128)} %collective-permute-done.11.refs_2_, f32[2,48,192]{2,1,0:T(8,128)} %collective-permute-done.12.refs_3_, ...), custom_call_target="tpu_custom_call" | custom-call | flops 452984832 | bytes 6282240 | tf_op jit(solution)/shard_map/pallas_call | solution.py:663
  42.8 4.4 %all-to-all-start = ((bf16[8,1,2,8,24,384]{5,4,3,2,1,0:T(8,128)(2,1)}), bf16[8,1,2,8,24,384]{5,4,3,2,1,0:T(8,128)(2,1)}, u32[]{:S(2)}, u32[]{:S(2)}) async-start(bf16[8,1,2,8,24,384]{5,4,3,2,1,0:T(8,128)(2,1)} %shard_map.327), calls=%async_computation | async-start | bytes 4718592 | tf_op jit(solution)/shard_map/all_to_all | solution.py:740
  47.2 7.6 %shard_map.323 = (bf16[2,12,192,384]{3,2,1,0:T(8,128)(2,1)}, f32[2,48,192]{2,1,0:T(8,128)}) custom-call(bf16[8,12,2,17280]{3,2,1,0:T(2,128)(2,1)} %stored_ref.6, bf16[2,8,384]{2,1,0:T(8,128)(2,1)} %constant.52.clone.sum_ref.refs_9_.refs_16_), custom_call_target="tpu_custom_call" | custom-call | flops 113246208 | bytes 10260480 | tf_op jit(solution)/shard_map/pallas_call | solution.py:663
  54.8 2.2 collective-permute-start
  57.0 2.6 collective-permute-start.1
  59.6 1.3 collective-permute-start.2
  60.9 7.4 %shard_map.324 = (bf16[2,2,8,24,384]{4,3,2,1,0:T(8,128)(2,1)}, bf16[2,2,8,24,384]{4,3,2,1,0:T(8,128)(2,1)}, bf16[2,2,8,24,384]{4,3,2,1,0:T(8,128)(2,1)}, bf16[2,...) custom-call(bf16[8,12,2,17280]{3,2,1,0:T(2,128)(2,1)} %stored_ref.7,, ...), custom_call_target="tpu_custom_call" | custom-call | flops 452984832 | bytes 11403780 | tf_op jit(solution)/shard_map/pallas_call | solution.py:663
  68.4 8.6 %shard_map.325 = (bf16[2,2,8,24,384]{4,3,2,1,0:T(8,128)(2,1)}, bf16[2,2,8,24,384]{4,3,2,1,0:T(8,128)(2,1)}, bf16[2,2,8,24,384]{4,3,2,1,0:T(8,128)(2,1)}, bf16[2,...) custom-call(f32[2,48,192]{2,1,0:T(8,128)} %get-tuple-element.52.refs, ...), custom_call_target="tpu_custom_call", output_to_operand_aliasing={{0}: (9, {}), {1}: (10, {}), {2}: (11, {}), {3}: (12, {}), ... | custom-call | flops 452984832 | bytes 13360132 | tf_op jit(solution)/shard_map/pallas_call | solution.py:663
  77.1 1.9 collective-permute-start.4
  79.0 34.1 %shard_map.329 = (bf16[1,2,12,16,384]{4,3,2,1,0:T(8,128)(2,1)}, bf16[1,2,12,16,384]{4,3,2,1,0:T(8,128)(2,1)}, bf16[1,2,12,16,384]{4,3,2,1,0:T(8,128)(2,1)}, bf16...) custom-call(bf16[8,1,2,8,24,384]{5,4,3,2,1,0:T(8,128)(2,1)} %all-to-, ...), custom_call_target="tpu_custom_call" | custom-call | flops 10871635968 | bytes 10132484 | tf_op jit(solution)/shard_map/pallas_call | solution.py:663
  113.2 4.9 %all-to-all-start.3 = ((bf16[8,1,2,12,16,384]{5,4,3,2,1,0:T(8,128)(2,1)}), bf16[8,1,2,12,16,384]{5,4,3,2,1,0:T(8,128)(2,1)}, u32[]{:S(2)}, u32[]{:S(2)}) async-start(bf16[8,1,2,12,16,384]{5,4,3,2,1,0:T(8,128)(2,1)} %get-tuple-element.90), calls=%async_computation.3 | async-start | bytes 4718592 | tf_op jit(solution)/shard_map/all_to_all | solution.py:740
  118.1 1.4 collective-permute-start.5
  119.5 1.5 collective-permute-start.6
  121.3 1.5 collective-permute-start.8
  124.8 33.6 %collective-permute-done.5.refs_3_.refs_11_ = bf16[2,2,8,24,384]{4,3,2,1,0:T(8,128)(2,1)S(1)} collective-permute-done((bf16[2,2,8,24,384]{4,3,2,1,0:T(8,128)(2,1)S(1)}, bf16[2,2,8,24,384]{4,3,2,1,0:T(8,128)(2,1)S(1)}, u32[]{:S(2)}, u32[]{:S(2)}) %collective-permute-start.5) | collective-permute-done | bytes 589856 | tf_op jit(solution)/shard_map/ppermute | solution.py:734
  159.6 36.7 %collective-permute-done.7.refs_5_.refs_13_ = bf16[2,2,8,24,384]{4,3,2,1,0:T(8,128)(2,1)S(1)} collective-permute-done((bf16[2,2,8,24,384]{4,3,2,1,0:T(8,128)(2,1)S(1)}, bf16[2,2,8,24,384]{4,3,2,1,0:T(8,128)(2,1)S(1)}, u32[]{:S(2)}, u32[]{:S(2)}) %collective-permute-start.7) | collective-permute-done | bytes 589856 | tf_op jit(solution)/shard_map/ppermute | solution.py:734
  197.5 34.5 %shard_map.330 = (bf16[8,1,2,12,16,384]{5,4,3,2,1,0:T(8,128)(2,1)}, bf16[1,2,12,16,384]{4,3,2,1,0:T(8,128)(2,1)}, bf16[1,2,12,16,384]{4,3,2,1,0:T(8,128)(2,1)}, ...) custom-call(bf16[2,2,8,24,384]{4,3,2,1,0:T(8,128)(2,1)} %get-tuple-e, ...), custom_call_target="tpu_custom_call" | custom-call | flops 10871635968 | bytes 15049732 | tf_op jit(solution)/shard_map/pallas_call | solution.py:663
  232.1 4.5 %all-to-all-start.2 = ((bf16[8,1,2,12,16,384]{5,4,3,2,1,0:T(8,128)(2,1)}), bf16[8,1,2,12,16,384]{5,4,3,2,1,0:T(8,128)(2,1)}, u32[]{:S(2)}, u32[]{:S(2)}) async-start(bf16[8,1,2,12,16,384]{5,4,3,2,1,0:T(8,128)(2,1)} %get-tuple-element.73), calls=%async_computation.2 | async-start | bytes 4718592 | tf_op jit(solution)/shard_map/all_to_all | solution.py:740
  237.3 1.9 collective-permute-start.14
  239.3 1.5 collective-permute-start.16
  241.8 2.6 collective-permute-start.18
  244.4 27.7 %collective-permute-done.14.refs_2_ = bf16[1,2,12,16,384]{4,3,2,1,0:T(8,128)(2,1)} collective-permute-done((bf16[1,2,12,16,384]{4,3,2,1,0:T(8,128)(2,1)S(1)}, bf16[1,2,12,16,384]{4,3,2,1,0:T(8,128)(2,1)}, u32[]{:S(2)}, u32[]{:S(2)}) %collective-permute-start.14) | collective-permute-done | bytes 294944 | tf_op jit(solution)/shard_map/ppermute | solution.py:734
  272.9 4.4 %collective-permute-done.15.refs_3_ = bf16[1,2,12,16,384]{4,3,2,1,0:T(8,128)(2,1)} collective-permute-done((bf16[1,2,12,16,384]{4,3,2,1,0:T(8,128)(2,1)S(1)}, bf16[1,2,12,16,384]{4,3,2,1,0:T(8,128)(2,1)}, u32[]{:S(2)}, u32[]{:S(2)}) %collective-permute-start.15) | collective-permute-done | bytes 294944 | tf_op jit(solution)/shard_map/ppermute | solution.py:734
  278.0 1.4 collective-permute-start.35
  279.4 1.4 collective-permute-start.36
  281.6 4.2 %collective-permute-done.18.refs_6_ = bf16[1,2,12,16,384]{4,3,2,1,0:T(8,128)(2,1)} collective-permute-done((bf16[1,2,12,16,384]{4,3,2,1,0:T(8,128)(2,1)S(1)}, bf16[1,2,12,16,384]{4,3,2,1,0:T(8,128)(2,1)}, u32[]{:S(2)}, u32[]{:S(2)}) %collective-permute-start.18) | collective-permute-done | bytes 294944 | tf_op jit(solution)/shard_map/ppermute | solution.py:734
  285.8 5.2 %collective-permute-done.19.refs_7_ = bf16[1,2,12,16,384]{4,3,2,1,0:T(8,128)(2,1)} collective-permute-done((bf16[1,2,12,16,384]{4,3,2,1,0:T(8,128)(2,1)S(1)}, bf16[1,2,12,16,384]{4,3,2,1,0:T(8,128)(2,1)}, u32[]{:S(2)}, u32[]{:S(2)}) %collective-permute-start.19) | collective-permute-done | bytes 294944 | tf_op jit(solution)/shard_map/ppermute | solution.py:734
  291.5 7.8 %shard_map.331.refs_2_ = bf16[8,12,2,17280]{3,2,1,0:T(2,128)(2,1)} custom-call(bf16[1,2,12,16,384]{4,3,2,1,0:T(8,128)(2,1)} %get-tuple-element.74.refs_0_, bf16[1,2,12,16,384]{4,3,2,1,0:T(8,128)(2,1)} %collective-permute-done.13.refs_1_, bf16[1,2,12,16,384]{4,3,2,1,0:T(8,128)(2,1)} %collective-permute-done.14.refs_2_, ...), custom_call_target="tpu_custom_call" | custom-call | flops 452984832 | bytes 9043968 | tf_op jit(solution)/shard_map/pallas_call | solution.py:663
  299.3 1.8 collective-permute-start.22
  302.4 1.3 add_add_fusion
  304.5 1.4 collective-permute-done.21.refs_6_.refs_10_
  308.3 8.9 %shard_map.333 = (bf16[2,48,192]{2,1,0:T(8,128)(2,1)}, f32[8,2,384]{2,1,0:T(2,128)}) custom-call(f32[2,48,192]{2,1,0:T(8,128)} %get-tuple-element.70.refs_0_, f32[2,48,192]{2,1,0:T(8,128)} %collective-permute-done.10.refs_1_, f32[2,48,192]{2,1,0:T(8,128)} %collective-permute-done.11.refs_2_, f32[2,48,192]{2,1,0:T(8,128)} %collective-permute-done.12.refs_3_, ...), custom_call_target="tpu_custom_call" | custom-call | flops 452984832 | bytes 6355968 | tf_op jit(solution)/shard_map/pallas_call | solution.py:663
  318.1 1.6 collective-permute-start.31
  319.7 8.4 %collective-permute-done.24.refs_9_.refs_13_ = bf16[1,2,12,16,384]{4,3,2,1,0:T(8,128)(2,1)} collective-permute-done((bf16[1,2,12,16,384]{4,3,2,1,0:T(8,128)(2,1)}, bf16[1,2,12,16,384]{4,3,2,1,0:T(8,128)(2,1)}, u32[]{:S(2)}, u32[]{:S(2)}) %collective-permute-start.24) | collective-permute-done | bytes 294944 | tf_op jit(solution)/shard_map/ppermute | solution.py:734
  328.1 1.9 collective-permute-start.32
  330.0 9.1 %shard_map.334 = (bf16[2,48,192]{2,1,0:T(8,128)(2,1)}, f32[8,2,384]{2,1,0:T(2,128)}) custom-call(f32[2,48,192]{2,1,0:T(8,128)} %get-tuple-element.52.refs_0_, f32[2,48,192]{2,1,0:T(8,128)} %collective-permute-done.refs_1_, f32[2,48,192]{2,1,0:T(8,128)} %collective-permute-done.1.refs_2_, f32[2,48,192]{2,1,0:T(8,128)} %collective-permute-done.2.refs_3_, ...), custom_call_target="tpu_custom_call" | custom-call | flops 452984832 | bytes 6380544 | tf_op jit(solution)/shard_map/pallas_call | solution.py:663
  340.1 4.2 %all-to-all-start.4 = ((f32[8,2,384]{2,1,0:T(2,128)}), f32[8,2,384]{2,1,0:T(2,128)}, u32[]{:S(2)}, u32[]{:S(2)}) async-start(f32[8,2,384]{2,1,0:T(2,128)} %get-tuple-element.95), calls=%async_computation.4 | async-start | bytes 49152 | tf_op jit(solution)/shard_map/all_to_all | solution.py:740
  344.3 7.8 %shard_map.332 = bf16[8,12,2,17280]{3,2,1,0:T(2,128)(2,1)} custom-call(bf16[8,1,2,12,16,384]{5,4,3,2,1,0:T(8,128)(2,1)} %all-to-all-done.2.refs_0_, bf16[192,128]{1,0:T(8,128)(2,1)} %constant.45.clone.refs_1_, bf16[8,12,2,17280]{3,2,1,0:T(2,128)(2,1)} %shard_map.331.refs_2_), custom_call_target="tpu_custom_call", output_to_operand_aliasing={{}: (2, {})} | custom-call | flops 452984832 | bytes 15679488 | tf_op jit(solution)/shard_map/pallas_call | solution.py:663
  353.5 3.0 collective-permute-start.29
  356.5 11.2 %shard_map.335.refs_20_ = bf16[8,12,2,17280]{3,2,1,0:T(2,128)(2,1)} custom-call(f32[2,48,192]{2,1,0:T(8,128)} %get-tuple-element.70.refs_0_, f32[2,48,192]{2,1,0:T(8,128)} %collective-permute-done.10.refs_1_, f32[2,48,192]{2,1,0:T(8,128)} %collective-permute-done.11.refs_2_, f32[2,48,192]{2,1,0:T(8,128)} %collective-permute-done.12.refs_3_, ...), custom_call_target="tpu_custom_call" | custom-call | flops 452984832 | bytes 13065216 | tf_op jit(solution)/shard_map/pallas_call | solution.py:663
  367.7 11.3 %shard_map.336 = bf16[8,12,2,17280]{3,2,1,0:T(2,128)(2,1)} custom-call(f32[2,48,192]{2,1,0:T(8,128)} %get-tuple-element.52.refs_0_, f32[2,48,192]{2,1,0:T(8,128)} %collective-permute-done.refs_1_, f32[2,48,192]{2,1,0:T(8,128)} %collective-permute-done.1.refs_2_, f32[2,48,192]{2,1,0:T(8,128)} %collective-permute-done.2.refs_3_, ...), custom_call_target="tpu_custom_call", output_to_operand_aliasing={{}: (20, {})} | custom-call | flops 452984832 | bytes 19700736 | tf_op jit(solution)/shard_map/pallas_call | solution.py:663
  (113 shorter events, 20.3 us)
Async XLA Ops:
  8.1 34.7 %all-to-all-start.1 = ((bf16[8,1,2,8,24,384]{5,4,3,2,1,0:T(8,128)(2,1)}), bf16[8,1,2,8,24,384]{5,4,3,2,1,0:T(8,128)(2,1)}, u32[]{:S(2)}, u32[]{:S(2)}) async-start(bf16[8,1,2,8,24,384]{5,4,3,2,1,0:T(8,128)(2,1)} %shard_map.328), calls=%async_computation.1 | async-start | bytes 4718592 | tf_op jit(solution)/shard_map/all_to_all | solution.py:740
  20.9 8.3 %collective-permute-start.10 = (f32[2,48,192]{2,1,0:T(8,128)}, f32[2,48,192]{2,1,0:T(8,128)}, u32[]{:S(2)}, u32[]{:S(2)}) collective-permute-start(f32[2,48,192]{2,1,0:T(8,128)} %get-tuple-element.70.refs_0_), channel_id=1, source_target_pairs={{0,1},{1,2},{2,3},{3,0},{4,5},{5,6},{6,7},{7,4},{8,9},{9,10},{10,1... | collective-permute-start | bytes 221192 | tf_op jit(solution)/shard_map/ppermute | solution.py:747
  23.1 9.9 %collective-permute-start.11 = (f32[2,48,192]{2,1,0:T(8,128)}, f32[2,48,192]{2,1,0:T(8,128)}, u32[]{:S(2)}, u32[]{:S(2)}) collective-permute-start(f32[2,48,192]{2,1,0:T(8,128)} %get-tuple-element.70.refs_0_), channel_id=1, source_target_pairs={{0,2},{1,3},{2,0},{3,1},{4,6},{5,7},{6,4},{7,5},{8,10},{9,11},{10,... | collective-permute-start | bytes 221192 | tf_op jit(solution)/shard_map/ppermute | solution.py:747
  25.7 7.4 %collective-permute-start.12 = (f32[2,48,192]{2,1,0:T(8,128)}, f32[2,48,192]{2,1,0:T(8,128)}, u32[]{:S(2)}, u32[]{:S(2)}) collective-permute-start(f32[2,48,192]{2,1,0:T(8,128)} %get-tuple-element.70.refs_0_), channel_id=1, source_target_pairs={{0,3},{1,0},{2,1},{3,2},{4,7},{5,4},{6,5},{7,6},{8,11},{9,8},{10,9... | collective-permute-start | bytes 221192 | tf_op jit(solution)/shard_map/ppermute | solution.py:747
  42.8 36.2 %all-to-all-start = ((bf16[8,1,2,8,24,384]{5,4,3,2,1,0:T(8,128)(2,1)}), bf16[8,1,2,8,24,384]{5,4,3,2,1,0:T(8,128)(2,1)}, u32[]{:S(2)}, u32[]{:S(2)}) async-start(bf16[8,1,2,8,24,384]{5,4,3,2,1,0:T(8,128)(2,1)} %shard_map.327), calls=%async_computation | async-start | bytes 4718592 | tf_op jit(solution)/shard_map/all_to_all | solution.py:740
  54.8 13.5 %collective-permute-start = (f32[2,48,192]{2,1,0:T(8,128)}, f32[2,48,192]{2,1,0:T(8,128)}, u32[]{:S(2)}, u32[]{:S(2)}) collective-permute-start(f32[2,48,192]{2,1,0:T(8,128)} %get-tuple-element.52.refs_0_), channel_id=1, source_target_pairs={{0,1},{1,2},{2,3},{3,0},{4,5},{5,6},{6,7},{7,4},{8,9},{9,10},{10,1... | collective-permute-start | bytes 221192 | tf_op jit(solution)/shard_map/ppermute | solution.py:747
  57.0 11.4 %collective-permute-start.1 = (f32[2,48,192]{2,1,0:T(8,128)}, f32[2,48,192]{2,1,0:T(8,128)}, u32[]{:S(2)}, u32[]{:S(2)}) collective-permute-start(f32[2,48,192]{2,1,0:T(8,128)} %get-tuple-element.52.refs_0_), channel_id=1, source_target_pairs={{0,2},{1,3},{2,0},{3,1},{4,6},{5,7},{6,4},{7,5},{8,10},{9,11},{10,... | collective-permute-start | bytes 221192 | tf_op jit(solution)/shard_map/ppermute | solution.py:747
  59.6 8.8 %collective-permute-start.2 = (f32[2,48,192]{2,1,0:T(8,128)}, f32[2,48,192]{2,1,0:T(8,128)}, u32[]{:S(2)}, u32[]{:S(2)}) collective-permute-start(f32[2,48,192]{2,1,0:T(8,128)} %get-tuple-element.52.refs_0_), channel_id=1, source_target_pairs={{0,3},{1,0},{2,1},{3,2},{4,7},{5,4},{6,5},{7,6},{8,11},{9,8},{10,9... | collective-permute-start | bytes 221192 | tf_op jit(solution)/shard_map/ppermute | solution.py:747
  77.0 44.2 %collective-permute-start.3 = (bf16[2,2,8,24,384]{4,3,2,1,0:T(8,128)(2,1)}, bf16[2,2,8,24,384]{4,3,2,1,0:T(8,128)(2,1)}, u32[]{:S(2)}, u32[]{:S(2)}) collective-permute-start(bf16[2,2,8,24,384]{4,3,2,1,0:T(8,128)(2,1)} %get-tuple-element.63), channel_id=1, source_target_pairs={{0,4},{4,0},{8,12},{12,8},{16,20},{20,16},{24,28},{28,24},{1,5},{5... | collective-permute-start | bytes 1769480 | tf_op jit(solution)/shard_map/ppermute | solution.py:734
  77.1 45.6 %collective-permute-start.4 = (bf16[2,2,8,24,384]{4,3,2,1,0:T(8,128)(2,1)}, bf16[2,2,8,24,384]{4,3,2,1,0:T(8,128)(2,1)}, u32[]{:S(2)}, u32[]{:S(2)}) collective-permute-start(bf16[2,2,8,24,384]{4,3,2,1,0:T(8,128)(2,1)} %get-tuple-element.64), channel_id=1, source_target_pairs={{0,8},{4,12},{8,0},{12,4},{16,24},{20,28},{24,16},{28,20},{1,9},{5... | collective-permute-start | bytes 1769480 | tf_op jit(solution)/shard_map/ppermute | solution.py:734
  113.2 10.8 %copy-start.9 = (s32[192]{0:T(256)S(1)}, s32[192]{0:T(256)}, u32[]{:S(2)}) copy-start(s32[192]{0:T(256)} %constant.49.clone) | copy-start | bytes 2308
  113.2 10.8 %copy-start.10 = (s32[192]{0:T(256)S(1)}, s32[192]{0:T(256)}, u32[]{:S(2)}) copy-start(s32[192]{0:T(256)} %constant.50.clone) | copy-start | bytes 2308
  113.2 118.9 %all-to-all-start.3 = ((bf16[8,1,2,12,16,384]{5,4,3,2,1,0:T(8,128)(2,1)}), bf16[8,1,2,12,16,384]{5,4,3,2,1,0:T(8,128)(2,1)}, u32[]{:S(2)}, u32[]{:S(2)}) async-start(bf16[8,1,2,12,16,384]{5,4,3,2,1,0:T(8,128)(2,1)} %get-tuple-element.90), calls=%async_computation.3 | async-start | bytes 4718592 | tf_op jit(solution)/shard_map/all_to_all | solution.py:740
  118.1 40.3 %collective-permute-start.5 = (bf16[2,2,8,24,384]{4,3,2,1,0:T(8,128)(2,1)S(1)}, bf16[2,2,8,24,384]{4,3,2,1,0:T(8,128)(2,1)S(1)}, u32[]{:S(2)}, u32[]{:S(2)}) collective-permute-start(bf16[2,2,8,24,384]{4,3,2,1,0:T(8,128)(2,1)S(1)} %copy-done), channel_id=1, source_target_pairs={{0,12},{4,8},{8,4},{12,0},{16,28},{20,24},{24,20},{28,16},{1,13},{... | collective-permute-start | bytes 1769480 | tf_op jit(solution)/shard_map/ppermute | solution.py:734
  119.5 40.1 %collective-permute-start.6 = (bf16[2,2,8,24,384]{4,3,2,1,0:T(8,128)(2,1)S(1)}, bf16[2,2,8,24,384]{4,3,2,1,0:T(8,128)(2,1)S(1)}, u32[]{:S(2)}, u32[]{:S(2)}) collective-permute-start(bf16[2,2,8,24,384]{4,3,2,1,0:T(8,128)(2,1)S(1)} %copy-done.1), channel_id=1, source_target_pairs={{0,16},{4,20},{8,24},{12,28},{16,0},{20,4},{24,8},{28,12},{1,17},{... | collective-permute-start | bytes 1769480 | tf_op jit(solution)/shard_map/ppermute | solution.py:734
  121.0 75.2 %collective-permute-start.7 = (bf16[2,2,8,24,384]{4,3,2,1,0:T(8,128)(2,1)S(1)}, bf16[2,2,8,24,384]{4,3,2,1,0:T(8,128)(2,1)S(1)}, u32[]{:S(2)}, u32[]{:S(2)}) collective-permute-start(bf16[2,2,8,24,384]{4,3,2,1,0:T(8,128)(2,1)S(1)} %copy-done.2), channel_id=1, source_target_pairs={{0,20},{4,16},{8,28},{12,24},{16,4},{20,0},{24,12},{28,8},{1,21},{... | collective-permute-start | bytes 1769480 | tf_op jit(solution)/shard_map/ppermute | solution.py:734
  121.3 75.0 %collective-permute-start.8 = (bf16[2,2,8,24,384]{4,3,2,1,0:T(8,128)(2,1)S(1)}, bf16[2,2,8,24,384]{4,3,2,1,0:T(8,128)(2,1)S(1)}, u32[]{:S(2)}, u32[]{:S(2)}) collective-permute-start(bf16[2,2,8,24,384]{4,3,2,1,0:T(8,128)(2,1)S(1)} %copy-done.3), channel_id=1, source_target_pairs={{0,24},{4,28},{8,16},{12,20},{16,8},{20,12},{24,0},{28,4},{1,25},{... | collective-permute-start | bytes 1769480 | tf_op jit(solution)/shard_map/ppermute | solution.py:734
  122.7 73.5 %collective-permute-start.9 = (bf16[2,2,8,24,384]{4,3,2,1,0:T(8,128)(2,1)S(1)}, bf16[2,2,8,24,384]{4,3,2,1,0:T(8,128)(2,1)S(1)}, u32[]{:S(2)}, u32[]{:S(2)}) collective-permute-start(bf16[2,2,8,24,384]{4,3,2,1,0:T(8,128)(2,1)S(1)} %copy-done.4), channel_id=1, source_target_pairs={{0,28},{4,24},{8,20},{12,16},{16,12},{20,8},{24,4},{28,0},{1,29},{... | collective-permute-start | bytes 1769480 | tf_op jit(solution)/shard_map/ppermute | solution.py:734
  158.4 37.9 %copy-start.13 = (bf16[2,2,8,24,384]{4,3,2,1,0:T(8,128)(2,1)}, bf16[2,2,8,24,384]{4,3,2,1,0:T(8,128)(2,1)S(1)}, u32[]{:S(2)}) copy-start(bf16[2,2,8,24,384]{4,3,2,1,0:T(8,128)(2,1)S(1)} %collective-permute-done.5.refs_3_.refs_11_) | copy-start | bytes 1769476
  159.6 36.7 %copy-start.14 = (bf16[2,2,8,24,384]{4,3,2,1,0:T(8,128)(2,1)}, bf16[2,2,8,24,384]{4,3,2,1,0:T(8,128)(2,1)S(1)}, u32[]{:S(2)}) copy-start(bf16[2,2,8,24,384]{4,3,2,1,0:T(8,128)(2,1)S(1)} %collective-permute-done.6.refs_4_.refs_12_) | copy-start | bytes 1769476
  232.1 40.0 %copy-start.18 = (bf16[1,2,12,16,384]{4,3,2,1,0:T(8,128)(2,1)S(1)}, bf16[1,2,12,16,384]{4,3,2,1,0:T(8,128)(2,1)}, u32[]{:S(2)}) copy-start(bf16[1,2,12,16,384]{4,3,2,1,0:T(8,128)(2,1)} %get-tuple-element.81) | copy-start | bytes 884740
  232.1 48.7 %copy-start.7 = (bf16[192,128]{1,0:T(8,128)(2,1)S(1)}, bf16[192,128]{1,0:T(8,128)(2,1)}, u32[]{:S(2)}) copy-start(bf16[192,128]{1,0:T(8,128)(2,1)} %constant.45.clone.refs_1_) | copy-start | bytes 147460
  232.1 107.9 %all-to-all-start.2 = ((bf16[8,1,2,12,16,384]{5,4,3,2,1,0:T(8,128)(2,1)}), bf16[8,1,2,12,16,384]{5,4,3,2,1,0:T(8,128)(2,1)}, u32[]{:S(2)}, u32[]{:S(2)}) async-start(bf16[8,1,2,12,16,384]{5,4,3,2,1,0:T(8,128)(2,1)} %get-tuple-element.73), calls=%async_computation.2 | async-start | bytes 4718592 | tf_op jit(solution)/shard_map/all_to_all | solution.py:740
  236.7 4.1 %collective-permute-start.33 = (bf16[776,128]{1,0:T(8,128)(2,1)S(1)}, bf16[776,128]{1,0:T(8,128)(2,1)S(1)}, u32[]{:S(2)}, u32[]{:S(2)}) collective-permute-start(bf16[776,128]{1,0:T(8,128)(2,1)S(1)} %copy-done.6), channel_id=1, source_target_pairs={{0,4},{4,0},{8,12},{12,8},{16,20},{20,16},{24,28},{28,24},{1,5},{5... | collective-permute-start | bytes 595976 | tf_op jit(solution)/shard_map/ppermute | solution.py:758
  237.1 4.7 %collective-permute-start.13 = (bf16[1,2,12,16,384]{4,3,2,1,0:T(8,128)(2,1)S(1)}, bf16[1,2,12,16,384]{4,3,2,1,0:T(8,128)(2,1)}, u32[]{:S(2)}, u32[]{:S(2)}) collective-permute-start(bf16[1,2,12,16,384]{4,3,2,1,0:T(8,128)(2,1)S(1)} %copy-done.24), channel_id=1, source_target_pairs={{0,4},{4,0},{8,12},{12,8},{16,20},{20,16},{24,28},{28,24},{1,5},{5... | collective-permute-start | bytes 884744 | tf_op jit(solution)/shard_map/ppermute | solution.py:734
  237.3 34.8 %collective-permute-start.14 = (bf16[1,2,12,16,384]{4,3,2,1,0:T(8,128)(2,1)S(1)}, bf16[1,2,12,16,384]{4,3,2,1,0:T(8,128)(2,1)}, u32[]{:S(2)}, u32[]{:S(2)}) collective-permute-start(bf16[1,2,12,16,384]{4,3,2,1,0:T(8,128)(2,1)S(1)} %copy-done.23), channel_id=1, source_target_pairs={{0,8},{4,12},{8,0},{12,4},{16,24},{20,28},{24,16},{28,20},{1,9},{5... | collective-permute-start | bytes 884744 | tf_op jit(solution)/shard_map/ppermute | solution.py:734
  239.2 38.1 %collective-permute-start.15 = (bf16[1,2,12,16,384]{4,3,2,1,0:T(8,128)(2,1)S(1)}, bf16[1,2,12,16,384]{4,3,2,1,0:T(8,128)(2,1)}, u32[]{:S(2)}, u32[]{:S(2)}) collective-permute-start(bf16[1,2,12,16,384]{4,3,2,1,0:T(8,128)(2,1)S(1)} %copy-done.22), channel_id=1, source_target_pairs={{0,12},{4,8},{8,4},{12,0},{16,28},{20,24},{24,20},{28,16},{1,13},{... | collective-permute-start | bytes 884744 | tf_op jit(solution)/shard_map/ppermute | solution.py:734
  239.3 38.7 %collective-permute-start.16 = (bf16[1,2,12,16,384]{4,3,2,1,0:T(8,128)(2,1)S(1)}, bf16[1,2,12,16,384]{4,3,2,1,0:T(8,128)(2,1)}, u32[]{:S(2)}, u32[]{:S(2)}) collective-permute-start(bf16[1,2,12,16,384]{4,3,2,1,0:T(8,128)(2,1)S(1)} %copy-done.21), channel_id=1, source_target_pairs={{0,16},{4,20},{8,24},{12,28},{16,0},{20,4},{24,8},{28,12},{1,17},{... | collective-permute-start | bytes 884744 | tf_op jit(solution)/shard_map/ppermute | solution.py:734
  240.8 38.6 %collective-permute-start.17 = (bf16[1,2,12,16,384]{4,3,2,1,0:T(8,128)(2,1)S(1)}, bf16[1,2,12,16,384]{4,3,2,1,0:T(8,128)(2,1)}, u32[]{:S(2)}, u32[]{:S(2)}) collective-permute-start(bf16[1,2,12,16,384]{4,3,2,1,0:T(8,128)(2,1)S(1)} %copy-done.20), channel_id=1, source_target_pairs={{0,20},{4,16},{8,28},{12,24},{16,4},{20,0},{24,12},{28,8},{1,21},{... | collective-permute-start | bytes 884744 | tf_op jit(solution)/shard_map/ppermute | solution.py:734
  241.8 44.0 %collective-permute-start.18 = (bf16[1,2,12,16,384]{4,3,2,1,0:T(8,128)(2,1)S(1)}, bf16[1,2,12,16,384]{4,3,2,1,0:T(8,128)(2,1)}, u32[]{:S(2)}, u32[]{:S(2)}) collective-permute-start(bf16[1,2,12,16,384]{4,3,2,1,0:T(8,128)(2,1)S(1)} %copy-done.19), channel_id=1, source_target_pairs={{0,24},{4,28},{8,16},{12,20},{16,8},{20,12},{24,0},{28,4},{1,25},{... | collective-permute-start | bytes 884744 | tf_op jit(solution)/shard_map/ppermute | solution.py:734
  272.1 18.8 %collective-permute-start.19 = (bf16[1,2,12,16,384]{4,3,2,1,0:T(8,128)(2,1)S(1)}, bf16[1,2,12,16,384]{4,3,2,1,0:T(8,128)(2,1)}, u32[]{:S(2)}, u32[]{:S(2)}) collective-permute-start(bf16[1,2,12,16,384]{4,3,2,1,0:T(8,128)(2,1)S(1)} %copy-done.18), channel_id=1, source_target_pairs={{0,28},{4,24},{8,20},{12,16},{16,12},{20,8},{24,4},{28,0},{1,29},{... | collective-permute-start | bytes 884744 | tf_op jit(solution)/shard_map/ppermute | solution.py:734
  277.3 22.0 %collective-permute-start.34 = (bf16[776,128]{1,0:T(8,128)(2,1)}, bf16[776,128]{1,0:T(8,128)(2,1)}, u32[]{:S(2)}, u32[]{:S(2)}) collective-permute-start(bf16[776,128]{1,0:T(8,128)(2,1)} %add_convert_fusion), channel_id=1, source_target_pairs={{0,8},{4,12},{8,0},{12,4},{16,24},{20,28},{24,16},{28,20},{1,9},{5... | collective-permute-start | bytes 595976 | tf_op jit(solution)/shard_map/ppermute | solution.py:758
  278.0 23.1 %collective-permute-start.35 = (bf16[776,128]{1,0:T(8,128)(2,1)}, bf16[776,128]{1,0:T(8,128)(2,1)}, u32[]{:S(2)}, u32[]{:S(2)}) collective-permute-start(bf16[776,128]{1,0:T(8,128)(2,1)} %add_convert_fusion), channel_id=1, source_target_pairs={{0,16},{4,20},{8,24},{12,28},{16,0},{20,4},{24,8},{28,12},{1,17},{... | collective-permute-start | bytes 595976 | tf_op jit(solution)/shard_map/ppermute | solution.py:758
  279.4 22.3 %collective-permute-start.36 = (bf16[776,128]{1,0:T(8,128)(2,1)}, bf16[776,128]{1,0:T(8,128)(2,1)}, u32[]{:S(2)}, u32[]{:S(2)}) collective-permute-start(bf16[776,128]{1,0:T(8,128)(2,1)} %add_convert_fusion), channel_id=1, source_target_pairs={{0,24},{4,28},{8,16},{12,20},{16,8},{20,12},{24,0},{28,4},{1,25},{... | collective-permute-start | bytes 595976 | tf_op jit(solution)/shard_map/ppermute | solution.py:758
  285.8 17.9 %collective-permute-start.20 = (bf16[1,2,12,16,384]{4,3,2,1,0:T(8,128)(2,1)}, bf16[1,2,12,16,384]{4,3,2,1,0:T(8,128)(2,1)}, u32[]{:S(2)}, u32[]{:S(2)}) collective-permute-start(bf16[1,2,12,16,384]{4,3,2,1,0:T(8,128)(2,1)} %get-tuple-element.83), channel_id=1, source_target_pairs={{0,4},{4,0},{8,12},{12,8},{16,20},{20,16},{24,28},{28,24},{1,5},{5... | collective-permute-start | bytes 884744 | tf_op jit(solution)/shard_map/ppermute | solution.py:734
  291.0 15.0 %collective-permute-start.21 = (bf16[1,2,12,16,384]{4,3,2,1,0:T(8,128)(2,1)}, bf16[1,2,12,16,384]{4,3,2,1,0:T(8,128)(2,1)}, u32[]{:S(2)}, u32[]{:S(2)}) collective-permute-start(bf16[1,2,12,16,384]{4,3,2,1,0:T(8,128)(2,1)} %get-tuple-element.84), channel_id=1, source_target_pairs={{0,8},{4,12},{8,0},{12,4},{16,24},{20,28},{24,16},{28,20},{1,9},{5... | collective-permute-start | bytes 884744 | tf_op jit(solution)/shard_map/ppermute | solution.py:734
  299.3 17.9 %collective-permute-start.22 = (bf16[1,2,12,16,384]{4,3,2,1,0:T(8,128)(2,1)}, bf16[1,2,12,16,384]{4,3,2,1,0:T(8,128)(2,1)}, u32[]{:S(2)}, u32[]{:S(2)}) collective-permute-start(bf16[1,2,12,16,384]{4,3,2,1,0:T(8,128)(2,1)} %get-tuple-element.85), channel_id=1, source_target_pairs={{0,12},{4,8},{8,4},{12,0},{16,28},{20,24},{24,20},{28,16},{1,13},{... | collective-permute-start | bytes 884744 | tf_op jit(solution)/shard_map/ppermute | solution.py:734
  301.1 17.0 %collective-permute-start.23 = (bf16[1,2,12,16,384]{4,3,2,1,0:T(8,128)(2,1)}, bf16[1,2,12,16,384]{4,3,2,1,0:T(8,128)(2,1)}, u32[]{:S(2)}, u32[]{:S(2)}) collective-permute-start(bf16[1,2,12,16,384]{4,3,2,1,0:T(8,128)(2,1)} %get-tuple-element.86), channel_id=1, source_target_pairs={{0,16},{4,20},{8,24},{12,28},{16,0},{20,4},{24,8},{28,12},{1,17},{... | collective-permute-start | bytes 884744 | tf_op jit(solution)/shard_map/ppermute | solution.py:734
  301.7 26.4 %collective-permute-start.24 = (bf16[1,2,12,16,384]{4,3,2,1,0:T(8,128)(2,1)}, bf16[1,2,12,16,384]{4,3,2,1,0:T(8,128)(2,1)}, u32[]{:S(2)}, u32[]{:S(2)}) collective-permute-start(bf16[1,2,12,16,384]{4,3,2,1,0:T(8,128)(2,1)} %get-tuple-element.87), channel_id=1, source_target_pairs={{0,20},{4,16},{8,28},{12,24},{16,4},{20,0},{24,12},{28,8},{1,21},{... | collective-permute-start | bytes 884744 | tf_op jit(solution)/shard_map/ppermute | solution.py:734
  303.7 26.3 %collective-permute-start.25 = (bf16[1,2,12,16,384]{4,3,2,1,0:T(8,128)(2,1)}, bf16[1,2,12,16,384]{4,3,2,1,0:T(8,128)(2,1)}, u32[]{:S(2)}, u32[]{:S(2)}) collective-permute-start(bf16[1,2,12,16,384]{4,3,2,1,0:T(8,128)(2,1)} %get-tuple-element.88), channel_id=1, source_target_pairs={{0,24},{4,28},{8,16},{12,20},{16,8},{20,12},{24,0},{28,4},{1,25},{... | collective-permute-start | bytes 884744 | tf_op jit(solution)/shard_map/ppermute | solution.py:734
  306.0 24.1 %collective-permute-start.26 = (bf16[1,2,12,16,384]{4,3,2,1,0:T(8,128)(2,1)}, bf16[1,2,12,16,384]{4,3,2,1,0:T(8,128)(2,1)}, u32[]{:S(2)}, u32[]{:S(2)}) collective-permute-start(bf16[1,2,12,16,384]{4,3,2,1,0:T(8,128)(2,1)} %get-tuple-element.89), channel_id=1, source_target_pairs={{0,28},{4,24},{8,20},{12,16},{16,12},{20,8},{24,4},{28,0},{1,29},{... | collective-permute-start | bytes 884744 | tf_op jit(solution)/shard_map/ppermute | solution.py:734
  317.2 36.3 %collective-permute-start.30 = (bf16[2,48,192]{2,1,0:T(8,128)(2,1)}, bf16[2,48,192]{2,1,0:T(8,128)(2,1)}, u32[]{:S(2)}, u32[]{:S(2)}) collective-permute-start(bf16[2,48,192]{2,1,0:T(8,128)(2,1)} %get-tuple-element.93.refs_4_), channel_id=1, source_target_pairs={{0,1},{1,2},{2,3},{3,0},{4,5},{5,6},{6,7},{7,4},{8,9},{9,10},{10,1... | collective-permute-start | bytes 110600 | tf_op jit(solution)/shard_map/ppermute | solution.py:747
  318.1 38.3 %collective-permute-start.31 = (bf16[2,48,192]{2,1,0:T(8,128)(2,1)}, bf16[2,48,192]{2,1,0:T(8,128)(2,1)}, u32[]{:S(2)}, u32[]{:S(2)}) collective-permute-start(bf16[2,48,192]{2,1,0:T(8,128)(2,1)} %get-tuple-element.93.refs_4_), channel_id=1, source_target_pairs={{0,2},{1,3},{2,0},{3,1},{4,6},{5,7},{6,4},{7,5},{8,10},{9,11},{10,... | collective-permute-start | bytes 110600 | tf_op jit(solution)/shard_map/ppermute | solution.py:747
  328.1 28.4 %collective-permute-start.32 = (bf16[2,48,192]{2,1,0:T(8,128)(2,1)}, bf16[2,48,192]{2,1,0:T(8,128)(2,1)}, u32[]{:S(2)}, u32[]{:S(2)}) collective-permute-start(bf16[2,48,192]{2,1,0:T(8,128)(2,1)} %get-tuple-element.93.refs_4_), channel_id=1, source_target_pairs={{0,3},{1,0},{2,1},{3,2},{4,7},{5,4},{6,5},{7,6},{8,11},{9,8},{10,9... | collective-permute-start | bytes 110600 | tf_op jit(solution)/shard_map/ppermute | solution.py:747
  339.2 28.5 %collective-permute-start.27 = (bf16[2,48,192]{2,1,0:T(8,128)(2,1)}, bf16[2,48,192]{2,1,0:T(8,128)(2,1)}, u32[]{:S(2)}, u32[]{:S(2)}) collective-permute-start(bf16[2,48,192]{2,1,0:T(8,128)(2,1)} %get-tuple-element.92.refs_4_), channel_id=1, source_target_pairs={{0,1},{1,2},{2,3},{3,0},{4,5},{5,6},{6,7},{7,4},{8,9},{9,10},{10,1... | collective-permute-start | bytes 110600 | tf_op jit(solution)/shard_map/ppermute | solution.py:747
  339.3 28.3 %collective-permute-start.28 = (bf16[2,48,192]{2,1,0:T(8,128)(2,1)}, bf16[2,48,192]{2,1,0:T(8,128)(2,1)}, u32[]{:S(2)}, u32[]{:S(2)}) collective-permute-start(bf16[2,48,192]{2,1,0:T(8,128)(2,1)} %get-tuple-element.92.refs_4_), channel_id=1, source_target_pairs={{0,2},{1,3},{2,0},{3,1},{4,6},{5,7},{6,4},{7,5},{8,10},{9,11},{10,... | collective-permute-start | bytes 110600 | tf_op jit(solution)/shard_map/ppermute | solution.py:747
  340.1 12.0 %all-to-all-start.4 = ((f32[8,2,384]{2,1,0:T(2,128)}), f32[8,2,384]{2,1,0:T(2,128)}, u32[]{:S(2)}, u32[]{:S(2)}) async-start(f32[8,2,384]{2,1,0:T(2,128)} %get-tuple-element.95), calls=%async_computation.4 | async-start | bytes 49152 | tf_op jit(solution)/shard_map/all_to_all | solution.py:740
  353.5 14.2 %collective-permute-start.29 = (bf16[2,48,192]{2,1,0:T(8,128)(2,1)}, bf16[2,48,192]{2,1,0:T(8,128)(2,1)}, u32[]{:S(2)}, u32[]{:S(2)}) collective-permute-start(bf16[2,48,192]{2,1,0:T(8,128)(2,1)} %get-tuple-element.92.refs_4_), channel_id=1, source_target_pairs={{0,3},{1,0},{2,1},{3,2},{4,7},{5,4},{6,5},{7,6},{8,11},{9,8},{10,9... | collective-permute-start | bytes 110600 | tf_op jit(solution)/shard_map/ppermute | solution.py:747
  (19 other events, 121.9 us)
